TPU v7x, 32 devices: a whole 2x2x4 slice. The times are simulated.
32 devices in a mesh: dp: 16 (over z, y, core), tensor: 2 (over x).
Axes of the slice: x: 2, y: 2, z: 4, core: 2. Of those that a mesh axis runs over, the one named last changes fastest.
Arguments:
- tokens: bfloat16 [8192, 1024], P(('dp', 'tensor')), may hold values from -6 to 6
- cotangent: bfloat16 [8192, 1024], P(('dp', 'tensor')), may hold values from -6 to 6
- deal_slot: int32 [8192], P(('dp', 'tensor')), may hold values from 0 to 255, as said below
- back_slot: int32 [8192], P(('dp', 'tensor')), may hold values from 0 to 255, as said below
- lengths: int32 [16, 4], P('dp'), may hold values from 1 to 256, 512 in all within a row
- time_step: int32 [1], replicated, may hold values from 0 to 4999
- time_table: bfloat16 [5000, 1024], P(None, 'dp'), may hold values from -3 to 3
- w_qkv: bfloat16 [2, 3, 1024, 1024], P(None, None, 'dp', 'tensor'), may hold values from -0.1875 to 0.1875
- b_qv: float32 [2, 2, 1024], P(None, None, 'tensor'), may hold values from -2 to 2
- w_out: bfloat16 [2, 1024, 1024], P(None, 'tensor', 'dp'), may hold values from -1.5 to 1.5
- out_bias: float32 [2, 2, 1024], replicated, may hold values from -2 to 2
- ln_gain: float32 [2, 2, 1024], replicated, may hold values from 0.5 to 1.5
- ln_shift: float32 [2, 2, 1024], replicated, may hold values from -2 to 2
- w_ff1: bfloat16 [2, 1024, 4096], P(None, 'dp', 'tensor'), may hold values from -0.1875 to 0.1875
- b_ff1: float32 [2, 4096], P(None, 'tensor'), may hold values from -2 to 2
- w_ff2: bfloat16 [2, 4096, 1024], P(None, 'tensor', 'dp'), may hold values from -0.09375 to 0.09375
Outputs:
- encoded: bfloat16 [8192, 1024], P(('dp', 'tensor'))
- grad_tokens: bfloat16 [8192, 1024], P(('dp', 'tensor'))
- grad_time_row: float32 [1024], replicated
- grad_w_qkv: float32 [2, 3, 1024, 1024], P(None, None, 'dp', 'tensor')
- grad_b_qv: float32 [2, 2, 1024], P(None, None, 'tensor')
- grad_w_out: float32 [2, 1024, 1024], P(None, 'tensor', 'dp')
- grad_out_bias: float32 [2, 2, 1024], replicated
- grad_ln_gain: float32 [2, 2, 1024], replicated
- grad_ln_shift: float32 [2, 2, 1024], replicated
- grad_w_ff1: float32 [2, 1024, 4096], P(None, 'dp', 'tensor')
- grad_b_ff1: float32 [2, 4096], P(None, 'tensor')
- grad_w_ff2: float32 [2, 4096, 1024], P(None, 'tensor', 'dp')
Inputs may be any that keep to these rules, and one draw needn't show every extreme that they name: `deal_slot`: the 256 entries of each device form a permutation of 0 to 255. `back_slot`: on each device's 256 entries, the inverse of deal_slot. Each group's 4 lengths sum to 512; the longest is exactly 256.
All inputs are finite; a program needn't handle non-finite values.
Results may differ from a plain program's by a relative error of at most 0.038.
Values may be sent and summed in bfloat16 or wider, within the bound.
No kernel may reach another device: no remote copies, remote signals or barrier semaphores. Data moves between devices by JAX's collectives and lax.ppermute only.
A program may use at most 192 MiB of HBM per device.

v0:
```python
import math

import jax
import jax.numpy as jnp
from jax import lax
from jax.sharding import PartitionSpec as P

D = 1024
HEADS = 16
FF = 4096


def layer_norm(summed, scaling, offset_vec):
    centre = jnp.mean(summed, axis=-1, keepdims=True)
    spread = summed - centre
    variance = jnp.mean(spread * spread, axis=-1, keepdims=True)
    return spread * lax.rsqrt(variance + 1e-05) * scaling + offset_vec


def gelu_slope(hidden_pre):
    normal_cdf = 0.5 * (1.0 + lax.erf(hidden_pre * 0.7071067811865476))
    return normal_cdf + hidden_pre * jnp.exp(-0.5 * hidden_pre * hidden_pre) * 0.3989422804014327


def contract_rows(left, right):
    return lax.dot_general(
        left, right, (((0,), (0,)), ((), ())), preferred_element_type=jnp.float32
    )


def times_transposed(left, right):
    return lax.dot_general(
        left, right, (((1,), (1,)), ((), ())), preferred_element_type=jnp.float32
    )


def owner_swap(first, second):
    return (
        lax.all_to_all(first, "dp", split_axis=0, concat_axis=0, tiled=True),
        lax.all_to_all(second, "dp", split_axis=0, concat_axis=0, tiled=True),
    )


def rows_in(local_rows, make):
    return make(lax.all_gather(local_rows, "tensor", axis=0, tiled=True), jnp.int32(0))


def branch_sum(source, weight, row_count):

    def term(first_row, term_rows):
        return jnp.dot(source, weight, preferred_element_type=jnp.float32)

    return lax.psum_scatter(
        term(jnp.int32(0), row_count * lax.axis_size("tensor")).astype(jnp.bfloat16),
        "tensor",
        scatter_dimension=0,
        tiled=True,
    ).astype(jnp.float32)


def grad_rows(grad_local, weight):

    def make(portion, first_row):
        return (portion, times_transposed(portion, weight))

    return make(lax.all_gather(grad_local, "tensor", axis=0, tiled=True), jnp.int32(0))


def grads_in(term, row_count):
    return lax.psum_scatter(
        term(jnp.int32(0), row_count * lax.axis_size("tensor")).astype(jnp.bfloat16),
        "tensor",
        scatter_dimension=0,
        tiled=True,
    ).astype(jnp.float32)


def masked_scores(query_block, key_rows, segment_block, segment, score_scale):
    scores = (
        jnp.einsum("qhe,khe->hqk", query_block, key_rows, preferred_element_type=jnp.float32)
        * score_scale
    )
    allowed = segment_block[:, None] == segment[None, :]
    return jnp.where(allowed[None], scores, -1e30)


def attend_forward(queries, key_rows, values, segment, score_scale):
    group_rows, head_count, head_size = queries.shape
    block_rows = min(512, group_rows)
    blocks = group_rows // block_rows

    def block_step(running, block_inputs):
        query_block, segment_block = block_inputs
        scores = masked_scores(query_block, key_rows, segment_block, segment, score_scale)
        highest = jnp.max(scores, axis=-1, keepdims=True)
        weights = jnp.exp(scores - highest)
        summed = jnp.sum(weights, axis=-1, keepdims=True)
        probabilities = (weights / summed).astype(jnp.bfloat16)
        mixture = jnp.einsum(
            "hqk,khe->qhe", probabilities, values, preferred_element_type=jnp.float32
        )
        return (running, (mixture.astype(jnp.bfloat16), (highest + jnp.log(summed))[..., 0]))

    _, (mixture, log_total) = lax.scan(
        block_step,
        None,
        (
            queries.reshape(blocks, block_rows, head_count, head_size),
            segment.reshape(blocks, block_rows),
        ),
    )
    return (mixture.reshape(group_rows, head_count * head_size), log_total)


def attend_backward(queries, key_rows, values, segment, log_total, grad_mixture, score_scale):
    group_rows, head_count, head_size = queries.shape
    block_rows = min(512, group_rows)
    blocks = group_rows // block_rows

    def block_step(running, block_inputs):
        grad_keys, grad_values = running
        query_block, segment_block, total_block, grad_block = block_inputs
        scores = masked_scores(query_block, key_rows, segment_block, segment, score_scale)
        probabilities = jnp.exp(scores - total_block[..., None])
        grad_probs = jnp.einsum(
            "qhe,khe->hqk", grad_block, values, preferred_element_type=jnp.float32
        )
        centre = jnp.sum(probabilities * grad_probs, axis=-1, keepdims=True)
        grad_scores = (probabilities * (grad_probs - centre)).astype(jnp.bfloat16)
        grad_query = (
            jnp.einsum("hqk,khe->qhe", grad_scores, key_rows, preferred_element_type=jnp.float32)
            * score_scale
        )
        grad_keys = (
            grad_keys
            + jnp.einsum(
                "hqk,qhe->khe", grad_scores, query_block, preferred_element_type=jnp.float32
            )
            * score_scale
        )
        grad_values = grad_values + jnp.einsum(
            "hqk,qhe->khe",
            probabilities.astype(jnp.bfloat16),
            grad_block,
            preferred_element_type=jnp.float32,
        )
        return ((grad_keys, grad_values), grad_query)

    zeros = jnp.zeros(key_rows.shape, jnp.float32)
    (grad_keys, grad_values), grad_query = lax.scan(
        block_step,
        (zeros, zeros),
        (
            queries.reshape(blocks, block_rows, head_count, head_size),
            segment.reshape(blocks, block_rows),
            log_total,
            grad_mixture.reshape(blocks, block_rows, head_count, head_size),
        ),
    )
    return (
        grad_query.reshape(group_rows, head_count * head_size),
        grad_keys.reshape(group_rows, head_count * head_size),
        grad_values.reshape(group_rows, head_count * head_size),
    )


def body(
    tokens,
    cotangent,
    deal_slot,
    back_slot,
    lengths,
    time_step,
    time_table,
    w_qkv,
    b_qv,
    w_out,
    out_bias,
    ln_gain,
    ln_shift,
    w_ff1,
    b_ff1,
    w_ff2,
):
    rows_dev = tokens.shape[0]
    group_rows = rows_dev * lax.axis_size("tensor")
    tensor_index = lax.axis_index("tensor")
    head_size = D // HEADS
    score_scale = 1.0 / math.sqrt(head_size)
    layer_total = w_qkv.shape[0]
    inner_width = w_qkv.shape[3]
    head_count = inner_width // head_size
    hidden_local = w_ff1.shape[2]
    own_rows, upstream_rows = owner_swap(
        jnp.take(tokens, back_slot, axis=0), jnp.take(cotangent, back_slot, axis=0)
    )
    seq_ends = jnp.cumsum(lengths[0])
    positions = jnp.arange(group_rows, dtype=jnp.int32)
    segment = jnp.sum((positions[:, None] >= seq_ends[None, :]).astype(jnp.int32), axis=1)
    time_piece = lax.dynamic_index_in_dim(time_table, time_step[0], 0, keepdims=False)
    stream = own_rows.astype(jnp.float32)
    saved = []
    for layer_num in range(layer_total):
        w_query, w_proj, w_first, w_second, time_row = (
            lax.all_gather(w_qkv[layer_num], "dp", axis=1, tiled=True),
            lax.all_gather(w_out[layer_num], "dp", axis=1, tiled=True),
            lax.all_gather(w_ff1[layer_num], "dp", axis=0, tiled=True),
            lax.all_gather(w_ff2[layer_num], "dp", axis=1, tiled=True),
            lax.all_gather(time_piece, "dp", axis=0, tiled=True),
        )
        if layer_num == 0:
            stream = stream + time_row.astype(jnp.float32)
        bias_qv = b_qv[layer_num]

        def make_qkv(portion, first_row, w_query=w_query, bias_qv=bias_qv):
            projected = jnp.einsum(
                "rd,cde->rce", portion, w_query, preferred_element_type=jnp.float32
            )
            queries = (projected[:, 0] + bias_qv[0]).astype(jnp.bfloat16)
            key_rows = projected[:, 1].astype(jnp.bfloat16)
            values = (projected[:, 2] + bias_qv[1]).astype(jnp.bfloat16)
            return (portion, jnp.stack([queries, key_rows, values], axis=1))

        input_rows, qkv_rows = rows_in(stream.astype(jnp.bfloat16), make_qkv)
        head_out, log_total = attend_forward(
            qkv_rows[:, 0].reshape(group_rows, head_count, head_size),
            qkv_rows[:, 1].reshape(group_rows, head_count, head_size),
            qkv_rows[:, 2].reshape(group_rows, head_count, head_size),
            segment,
            score_scale,
        )
        proj_full = w_proj
        out_rows = head_out
        attended = branch_sum(head_out, w_proj, rows_dev)
        middle = stream + attended + out_bias[layer_num, 0]
        normed = layer_norm(middle, ln_gain[layer_num, 0], ln_shift[layer_num, 0])
        bias_hidden = b_ff1[layer_num]

        def make_hidden(portion, first_row, w_first=w_first, bias_hidden=bias_hidden):
            return (
                portion,
                jnp.dot(portion, w_first, preferred_element_type=jnp.float32) + bias_hidden,
            )

        normed_rows, hidden_pre = rows_in(normed.astype(jnp.bfloat16), make_hidden)
        activated = jax.nn.gelu(hidden_pre, approximate=False).astype(jnp.bfloat16)
        second_sum = normed + branch_sum(activated, w_second, rows_dev) + out_bias[layer_num, 1]
        saved.append(
            (
                w_query,
                proj_full,
                w_first,
                w_second,
                input_rows,
                qkv_rows,
                head_out,
                out_rows,
                log_total,
                middle,
                normed_rows,
                hidden_pre,
                activated,
                second_sum,
            )
        )
        stream = layer_norm(second_sum, ln_gain[layer_num, 1], ln_shift[layer_num, 1])
    encoded_own = stream.astype(jnp.bfloat16)
    gradient = upstream_rows.astype(jnp.float32)
    matrix_grads = [None] * layer_total
    vector_grads = [None] * layer_total
    for layer_num in reversed(range(layer_total)):
        (
            w_query,
            proj_full,
            w_first,
            w_second,
            input_rows,
            qkv_rows,
            head_out,
            out_rows,
            log_total,
            middle,
            normed_rows,
            hidden_pre,
            activated,
            second_sum,
        ) = saved[layer_num]
        _, pull_second = jax.vjp(
            layer_norm, second_sum, ln_gain[layer_num, 1], ln_shift[layer_num, 1]
        )
        grad_second, gain_second, shift_second = pull_second(gradient)
        branch_grad = grad_second.astype(jnp.bfloat16)
        branch_all, grad_act = grad_rows(branch_grad, w_second)
        grad_second_w = contract_rows(activated, branch_all)
        grad_pre = (grad_act * gelu_slope(hidden_pre)).astype(jnp.bfloat16)
        grad_first_w = contract_rows(normed_rows, grad_pre)
        grad_hidden_bias = jnp.sum(grad_pre.astype(jnp.float32), axis=0)

        def hidden_term(first_row, term_rows, grad_pre=grad_pre, w_first=w_first):
            return times_transposed(grad_pre, w_first)

        grad_normed = grad_second + grads_in(hidden_term, rows_dev)
        _, pull_first = jax.vjp(layer_norm, middle, ln_gain[layer_num, 0], ln_shift[layer_num, 0])
        grad_middle, gain_first, shift_first = pull_first(grad_normed)
        attend_grad = grad_middle.astype(jnp.bfloat16)
        attend_all, grad_heads_wide = grad_rows(attend_grad, proj_full)
        grad_heads = grad_heads_wide.astype(jnp.bfloat16)
        grad_proj = contract_rows(head_out, attend_all)
        grad_query, grad_keys, grad_values = attend_backward(
            qkv_rows[:, 0].reshape(group_rows, head_count, head_size),
            qkv_rows[:, 1].reshape(group_rows, head_count, head_size),
            qkv_rows[:, 2].reshape(group_rows, head_count, head_size),
            segment,
            log_total,
            grad_heads.reshape(group_rows, head_count, head_size),
            score_scale,
        )
        grad_qkv = jnp.stack([grad_query, grad_keys, grad_values], axis=1).astype(jnp.bfloat16)
        grad_query_w = jnp.einsum(
            "rd,rce->cde", input_rows, grad_qkv, preferred_element_type=jnp.float32
        )
        qkv_sums = jnp.sum(grad_qkv.astype(jnp.float32), axis=0)

        def proj_term(first_row, term_rows, grad_qkv=grad_qkv, w_query=w_query):
            return jnp.einsum("rce,cde->rd", grad_qkv, w_query, preferred_element_type=jnp.float32)

        gradient = grad_middle + grads_in(proj_term, rows_dev)
        matrix_grads[layer_num] = (
            lax.psum_scatter(
                grad_query_w.astype(jnp.bfloat16), "dp", scatter_dimension=1, tiled=True
            ).astype(jnp.float32),
            lax.psum_scatter(
                grad_proj.astype(jnp.bfloat16), "dp", scatter_dimension=1, tiled=True
            ).astype(jnp.float32),
            lax.psum_scatter(
                grad_first_w.astype(jnp.bfloat16), "dp", scatter_dimension=0, tiled=True
            ).astype(jnp.float32),
            lax.psum_scatter(
                grad_second_w.astype(jnp.bfloat16), "dp", scatter_dimension=1, tiled=True
            ).astype(jnp.float32),
        )
        qv_place = lax.dynamic_update_slice_in_dim(
            jnp.zeros((2, D), jnp.float32),
            jnp.stack([qkv_sums[0], qkv_sums[2]]),
            tensor_index * inner_width,
            1,
        )
        hidden_place = lax.dynamic_update_slice_in_dim(
            jnp.zeros((FF,), jnp.float32), grad_hidden_bias, tensor_index * hidden_local, 0
        )
        vector_grads[layer_num] = (
            qv_place,
            hidden_place,
            jnp.stack([jnp.sum(grad_middle, axis=0), jnp.sum(grad_second, axis=0)]),
            jnp.stack([gain_first, gain_second]),
            jnp.stack([shift_first, shift_second]),
        )
    time_grad = jnp.sum(gradient, axis=0)
    totals = lax.psum(
        (
            jnp.stack([part[0] for part in vector_grads]),
            jnp.stack([part[1] for part in vector_grads]),
            jnp.stack([part[2] for part in vector_grads]),
            jnp.stack([part[3] for part in vector_grads]),
            jnp.stack([part[4] for part in vector_grads]),
            time_grad,
        ),
        ("dp", "tensor"),
    )
    returned_out, returned_grad = owner_swap(encoded_own, gradient.astype(jnp.bfloat16))
    encoded = jnp.take(returned_out, deal_slot, axis=0)
    grad_tokens = jnp.take(returned_grad, deal_slot, axis=0)
    grad_b_qv = lax.dynamic_slice_in_dim(totals[0], tensor_index * inner_width, inner_width, 2)
    grad_b_ff1 = lax.dynamic_slice_in_dim(totals[1], tensor_index * hidden_local, hidden_local, 1)
    grad_w_qkv = jnp.stack([part[0] for part in matrix_grads])
    grad_w_out = jnp.stack([part[1] for part in matrix_grads])
    grad_w_ff1 = jnp.stack([part[2] for part in matrix_grads])
    grad_w_ff2 = jnp.stack([part[3] for part in matrix_grads])
    return (
        encoded,
        grad_tokens,
        totals[5],
        grad_w_qkv,
        grad_b_qv,
        grad_w_out,
        totals[2],
        totals[3],
        totals[4],
        grad_w_ff1,
        grad_b_ff1,
        grad_w_ff2,
    )


def solution(mesh):
    return jax.shard_map(
        body,
        mesh=mesh,
        in_specs=(
            P(("dp", "tensor"), None),
            P(("dp", "tensor"), None),
            P(("dp", "tensor")),
            P(("dp", "tensor")),
            P("dp", None),
            P(),
            P(None, "dp"),
            P(None, None, "dp", "tensor"),
            P(None, None, "tensor"),
            P(None, "tensor", "dp"),
            P(),
            P(),
            P(),
            P(None, "dp", "tensor"),
            P(None, "tensor"),
            P(None, "tensor", "dp"),
        ),
        out_specs=(
            P(("dp", "tensor"), None),
            P(("dp", "tensor"), None),
            P(),
            P(None, None, "dp", "tensor"),
            P(None, None, "tensor"),
            P(None, "tensor", "dp"),
            P(),
            P(),
            P(),
            P(None, "dp", "tensor"),
            P(None, "tensor"),
            P(None, "tensor", "dp"),
        ),
        check_vma=False,
    )
```

profile of v0, /device:TPU:0, one launch (start us, length us, event | category | flops | bytes accessed | tf_op | source)
XLA Modules:
  0.0 1636.0 jit_solution(17389165604657745869)
XLA Ops:
  23.5 34.4 %all-reduce = bf16[1024]{0:T(1024)(128)(2,1)S(1)} all-reduce(bf16[1024]{0:T(1024)(128)(2,1)S(1)} %dynamic-update-slice), channel_id=2, replica_groups=mesh['dp'=16,'tensor'=2] {'dp'}, use_global_device_ids=true, to_apply=%add | all-reduce | flops 1024 | bytes 4096
  77.6 48.0 %all-gather.42.cloned.1.call-done = bf16[1,3,1024,512]{3,2,1,0:T(8,128)(2,1)} async-done(((bf16[1,3,64,512]{3,2,1,0:T(8,128)(2,1)}), bf16[1,3,1024,512]{3,2,1,0:T(8,128)(2,1)}) %all-gather.42.cloned.1.call-update) | async-done | bytes 3145744 | tf_op jit(solution)/shard_map/all_gather | solution.py:205
  136.9 28.3 %all-gather.44.cloned.1.call-done = bf16[1,512,1024]{1,2,0:T(8,128)(2,1)} async-done(((bf16[1,512,64]{1,2,0:T(8,128)(2,1)}), bf16[1,512,1024]{1,2,0:T(8,128)(2,1)}) %all-gather.44.cloned.1.call-update) | async-done | bytes 1048592 | tf_op jit(solution)/shard_map/all_gather | solution.py:206
  193.8 47.2 %all-gather.46.cloned.1.call-done = bf16[1,1024,2048]{2,1,0:T(8,128)(2,1)} async-done(((bf16[1,64,2048]{2,1,0:T(8,128)(2,1)}), bf16[1,1024,2048]{2,1,0:T(8,128)(2,1)}) %all-gather.46.cloned.1.call-update) | async-done | bytes 4194320 | tf_op jit(solution)/shard_map/all_gather | solution.py:207
  241.0 21.9 %all-gather.28.cloned.1.call-done = bf16[512,1024]{1,0:T(8,128)(2,1)} async-done(((bf16[256,1024]{1,0:T(8,128)(2,1)}), bf16[512,1024]{1,0:T(8,128)(2,1)}) %all-gather.28.cloned.1.call-update) | async-done | bytes 1048592 | tf_op jit(solution)/shard_map/all_gather | solution.py:45
  277.5 39.0 %all-gather.48.cloned.1.call-done = bf16[1,2048,1024]{1,2,0:T(8,128)(2,1)} async-done(((bf16[1,2048,64]{1,2,0:T(8,128)(2,1)}), bf16[1,2048,1024]{1,2,0:T(8,128)(2,1)}) %all-gather.48.cloned.1.call-update) | async-done | bytes 4194320 | tf_op jit(solution)/shard_map/all_gather | solution.py:208
  346.0 43.1 %all-gather.50.cloned.1.call-done = bf16[1,3,1024,512]{3,2,1,0:T(8,128)(2,1)} async-done(((bf16[1,3,64,512]{3,2,1,0:T(8,128)(2,1)}), bf16[1,3,1024,512]{3,2,1,0:T(8,128)(2,1)}) %all-gather.50.cloned.1.call-update) | async-done | bytes 3145744 | tf_op jit(solution)/shard_map/all_gather | solution.py:205
  389.1 22.1 %all-gather.30.cloned.1.call-done = bf16[512,1024]{1,0:T(8,128)(2,1)} async-done(((bf16[256,1024]{1,0:T(8,128)(2,1)}), bf16[512,1024]{1,0:T(8,128)(2,1)}) %all-gather.30.cloned.1.call-update) | async-done | bytes 1048592 | tf_op jit(solution)/shard_map/all_gather | solution.py:45
  422.2 29.1 %all-gather.52.cloned.1.call-done = bf16[1,512,1024]{1,2,0:T(8,128)(2,1)} async-done(((bf16[1,512,64]{1,2,0:T(8,128)(2,1)}), bf16[1,512,1024]{1,2,0:T(8,128)(2,1)}) %all-gather.52.cloned.1.call-update) | async-done | bytes 1048592 | tf_op jit(solution)/shard_map/all_gather | solution.py:206
  477.4 50.0 %all-gather.54.cloned.1.call-done = bf16[1,1024,2048]{2,1,0:T(8,128)(2,1)} async-done(((bf16[1,64,2048]{2,1,0:T(8,128)(2,1)}), bf16[1,1024,2048]{2,1,0:T(8,128)(2,1)}) %all-gather.54.cloned.1.call-update) | async-done | bytes 4194320 | tf_op jit(solution)/shard_map/all_gather | solution.py:207
  527.4 21.9 %all-gather.32.cloned.1.call-done = bf16[512,1024]{1,0:T(8,128)(2,1)} async-done(((bf16[256,1024]{1,0:T(8,128)(2,1)}), bf16[512,1024]{1,0:T(8,128)(2,1)}) %all-gather.32.cloned.1.call-update) | async-done | bytes 1048592 | tf_op jit(solution)/shard_map/all_gather | solution.py:45
  563.9 38.8 %all-gather.56.cloned.1.call-done = bf16[1,2048,1024]{1,2,0:T(8,128)(2,1)} async-done(((bf16[1,2048,64]{1,2,0:T(8,128)(2,1)}), bf16[1,2048,1024]{1,2,0:T(8,128)(2,1)}) %all-gather.56.cloned.1.call-update) | async-done | bytes 4194320 | tf_op jit(solution)/shard_map/all_gather | solution.py:208
  637.2 21.2 %all-gather.34.cloned.1.call-done = bf16[512,1024]{1,0:T(8,128)(2,1)} async-done(((bf16[256,1024]{1,0:T(8,128)(2,1)}), bf16[512,1024]{1,0:T(8,128)(2,1)}) %all-gather.34.cloned.1.call-update) | async-done | bytes 1048592 | tf_op jit(solution)/shard_map/all_gather | solution.py:66
  669.6 20.4 %reduce-scatter.23.cloned.1.call-done = bf16[256,1024]{1,0:T(8,128)(2,1)} async-done(((bf16[512,1024]{1,0:T(8,128)(2,1)}), bf16[256,1024]{1,0:T(8,128)(2,1)}) %reduce-scatter.23.cloned.1.call-update) | async-done | bytes 524304 | tf_op jit(solution)/shard_map/reduce_scatter | solution.py:70
  695.9 21.4 %all-gather.36.cloned.1.call-done = bf16[512,1024]{1,0:T(8,128)(2,1)} async-done(((bf16[256,1024]{1,0:T(8,128)(2,1)}), bf16[512,1024]{1,0:T(8,128)(2,1)}) %all-gather.36.cloned.1.call-update) | async-done | bytes 1048592 | tf_op jit(solution)/shard_map/all_gather | solution.py:66
  770.4 21.0 %all-gather.38.cloned.1.call-done = bf16[512,1024]{1,0:T(8,128)(2,1)} async-done(((bf16[256,1024]{1,0:T(8,128)(2,1)}), bf16[512,1024]{1,0:T(8,128)(2,1)}) %all-gather.38.cloned.1.call-update) | async-done | bytes 1048592 | tf_op jit(solution)/shard_map/all_gather | solution.py:66
  827.7 21.2 %all-gather.40.cloned.1.call-done = bf16[512,1024]{1,0:T(8,128)(2,1)} async-done(((bf16[256,1024]{1,0:T(8,128)(2,1)}), bf16[512,1024]{1,0:T(8,128)(2,1)}) %all-gather.40.cloned.1.call-update) | async-done | bytes 1048592 | tf_op jit(solution)/shard_map/all_gather | solution.py:66
  975.6 41.3 %reduce-scatter.31.cloned.1.call-done = bf16[512,64]{0,1:T(8,128)(2,1)} async-done(((bf16[512,1024]{0,1:T(8,128)(2,1)}), bf16[512,64]{0,1:T(8,128)(2,1)}) %reduce-scatter.31.cloned.1.call-update) | async-done | bytes 65552 | tf_op jit(solution)/shard_map/reduce_scatter | solution.py:332
  1018.5 128.2 %all-reduce.8.cloned.1.call-done = (f32[1024]{0:T(1024)}, f32[2,2,1024]{2,1,0:T(2,128)}, f32[2,2,1024]{2,1,0:T(2,128)}, f32[2,2,1024]{2,1,0:T(2,128)}, f32[2,2,1024]{2,1,0:T(2,128)}, /*index=5*/f32[2,4096]{1,0:T(2,128)}) async-done(((f32[1024]{0:T(1024)}, f32[2,2,1024]{2,1,0:T(2,128)}, f32[2,2,1024]{2,1,0:T(2,128)}, f32[2,2,1024]{2,1,0:T(2,128)}, f32[2,2,1024]{2,1,0:T(2,128)}, ...) | async-done | bytes 102416 | tf_op jit(solution)/shard_map/psum | solution.py:359
  1151.6 72.3 %reduce-scatter.41.cloned.1.call-done = bf16[2048,64]{0,1:T(8,128)(2,1)} async-done(((bf16[2048,1024]{0,1:T(8,128)(2,1)}), bf16[2048,64]{0,1:T(8,128)(2,1)}) %reduce-scatter.41.cloned.1.call-update) | async-done | bytes 262160 | tf_op jit(solution)/shard_map/reduce_scatter | solution.py:338
  1223.9 75.8 %reduce-scatter.39.cloned.1.call-done = bf16[2048,64]{0,1:T(8,128)(2,1)} async-done(((bf16[2048,1024]{0,1:T(8,128)(2,1)}), bf16[2048,64]{0,1:T(8,128)(2,1)}) %reduce-scatter.39.cloned.1.call-update) | async-done | bytes 262160 | tf_op jit(solution)/shard_map/reduce_scatter | solution.py:338
  1301.8 73.1 %reduce-scatter.37.cloned.1.call-done = bf16[64,2048]{1,0:T(8,128)(2,1)} async-done(((bf16[1024,2048]{1,0:T(8,128)(2,1)}), bf16[64,2048]{1,0:T(8,128)(2,1)}) %reduce-scatter.37.cloned.1.call-update) | async-done | bytes 262160 | tf_op jit(solution)/shard_map/reduce_scatter | solution.py:335
  1374.9 75.8 %reduce-scatter.35.cloned.1.call-done = bf16[64,2048]{1,0:T(8,128)(2,1)} async-done(((bf16[1024,2048]{1,0:T(8,128)(2,1)}), bf16[64,2048]{1,0:T(8,128)(2,1)}) %reduce-scatter.35.cloned.1.call-update) | async-done | bytes 262160 | tf_op jit(solution)/shard_map/reduce_scatter | solution.py:335
  1452.8 171.2 %all-reduce.10.cloned.1.call-done = (bf16[3,1024,512]{2,0,1:T(4,128)(2,1)}, bf16[3,1024,512]{2,0,1:T(4,128)(2,1)}) async-done(((bf16[3,1024,512]{2,0,1:T(4,128)(2,1)}, bf16[3,1024,512]{2,0,1:T(4,128)(2,1)}), (bf16[3,1024,512]{2,0,1:T(4,128)(2,1)}, bf16[3,1024,512]{2,0,1:T(4,128)(2,1)})) %all-reduce.10.cloned.1.call-update) | async-done | bytes 6291472
  (385 shorter events, 451.4 us)
Async XLA Ops:
  59.8 105.4 %all-gather.44.cloned.1.call-start = ((), (), s32[]{:S(2)}) async-start(), calls=%async_computation.41 | async-start | bytes 1114112 | tf_op jit(solution)/shard_map/all_gather | solution.py:206
  60.5 127.1 %reduce-scatter.15.cloned.1.call-start = ((), (), s32[]{:S(2)}) async-start(), calls=%async_computation.19 | async-start | bytes 1572864 | tf_op jit(solution)/shard_map/reduce_scatter | solution.py:53
  168.2 72.8 %all-gather.46.cloned.1.call-start = ((), (), s32[]{:S(2)}) async-start(), calls=%async_computation.42 | async-start | bytes 4456448 | tf_op jit(solution)/shard_map/all_gather | solution.py:207
  169.2 93.7 %all-gather.28.cloned.1.call-start = ((), (), s32[]{:S(2)}) async-start(), calls=%async_computation.20 | async-start | bytes 1572864 | tf_op jit(solution)/shard_map/all_gather | solution.py:45
  192.6 123.9 %all-gather.48.cloned.1.call-start = ((), (), s32[]{:S(2)}) async-start(), calls=%async_computation.43 | async-start | bytes 4456448 | tf_op jit(solution)/shard_map/all_gather | solution.py:208
  193.5 148.2 %reduce-scatter.17.cloned.1.call-start = ((), (), s32[]{:S(2)}) async-start(), calls=%async_computation.21 | async-start | bytes 1572864 | tf_op jit(solution)/shard_map/reduce_scatter | solution.py:53
  323.4 87.8 %all-gather.30.cloned.1.call-start = ((), (), s32[]{:S(2)}) async-start(), calls=%async_computation.22 | async-start | bytes 1572864 | tf_op jit(solution)/shard_map/all_gather | solution.py:45
  344.6 106.7 %all-gather.52.cloned.1.call-start = ((), (), s32[]{:S(2)}) async-start(), calls=%async_computation.45 | async-start | bytes 1114112 | tf_op jit(solution)/shard_map/all_gather | solution.py:206
  345.4 128.3 %reduce-scatter.19.cloned.1.call-start = ((), (), s32[]{:S(2)}) async-start(), calls=%async_computation.23 | async-start | bytes 1572864 | tf_op jit(solution)/shard_map/reduce_scatter | solution.py:53
  454.3 73.1 %all-gather.54.cloned.1.call-start = ((), (), s32[]{:S(2)}) async-start(), calls=%async_computation.46 | async-start | bytes 4456448 | tf_op jit(solution)/shard_map/all_gather | solution.py:207
  455.1 94.2 %all-gather.32.cloned.1.call-start = ((), (), s32[]{:S(2)}) async-start(), calls=%async_computation.24 | async-start | bytes 1572864 | tf_op jit(solution)/shard_map/all_gather | solution.py:45
  476.6 126.1 %all-gather.56.cloned.1.call-start = ((), (), s32[]{:S(2)}) async-start(), calls=%async_computation.47 | async-start | bytes 4456448 | tf_op jit(solution)/shard_map/all_gather | solution.py:208
  477.2 150.7 %reduce-scatter.21.cloned.1.call-start = ((), (), s32[]{:S(2)}) async-start(), calls=%async_computation.25 | async-start | bytes 1572864 | tf_op jit(solution)/shard_map/reduce_scatter | solution.py:53
  695.8 68.9 %reduce-scatter.25.cloned.1.call-start = ((), (), s32[]{:S(2)}) async-start(), calls=%async_computation.29 | async-start | bytes 1572864 | tf_op jit(solution)/shard_map/reduce_scatter | solution.py:70
  827.5 67.4 %reduce-scatter.29.cloned.1.call-start = ((), (), s32[]{:S(2)}) async-start(), calls=%async_computation.33 | async-start | bytes 1572864 | tf_op jit(solution)/shard_map/reduce_scatter | solution.py:70
  874.4 101.2 %reduce-scatter.33.cloned.1.call-start = ((), (), s32[]{:S(2)}) async-start(), calls=%async_computation.35 | async-start | bytes 1114112 | tf_op jit(solution)/shard_map/reduce_scatter | solution.py:332
  877.7 139.1 %reduce-scatter.31.cloned.1.call-start = ((), (), s32[]{:S(2)}) async-start(), calls=%async_computation.34 | async-start | bytes 1114112 | tf_op jit(solution)/shard_map/reduce_scatter | solution.py:332
  882.6 264.0 %all-reduce.8.cloned.1.call-start = ((), (), s32[]{:S(2)}) async-start(), calls=%async_computation.48 | async-start | bytes 204800 | tf_op jit(solution)/shard_map/psum | solution.py:359
  898.2 325.7 %reduce-scatter.41.cloned.1.call-start = ((), (), s32[]{:S(2)}) async-start(), calls=%async_computation.39 | async-start | bytes 4456448 | tf_op jit(solution)/shard_map/reduce_scatter | solution.py:338
  904.7 395.0 %reduce-scatter.39.cloned.1.call-start = ((), (), s32[]{:S(2)}) async-start(), calls=%async_computation.38 | async-start | bytes 4456448 | tf_op jit(solution)/shard_map/reduce_scatter | solution.py:338
  912.0 462.9 %reduce-scatter.37.cloned.1.call-start = ((), (), s32[]{:S(2)}) async-start(), calls=%async_computation.37 | async-start | bytes 4456448 | tf_op jit(solution)/shard_map/reduce_scatter | solution.py:335
  919.2 531.5 %reduce-scatter.35.cloned.1.call-start = ((), (), s32[]{:S(2)}) async-start(), calls=%async_computation.36 | async-start | bytes 4456448 | tf_op jit(solution)/shard_map/reduce_scatter | solution.py:335
  926.4 697.5 %all-reduce.10.cloned.1.call-start = ((), (), s32[]{:S(2)}) async-start(), calls=%async_computation.49 | async-start | bytes 16777216
  970.2 179.0 %all-to-all-start.3 = ((bf16[16,16,1024]{2,1,0:T(8,128)(2,1)}), bf16[16,16,1024]{2,1,0:T(8,128)(2,1)S(1)}, u32[]{:S(2)}, u32[]{:S(2)}) async-start(bf16[16,16,1024]{2,1,0:T(8,128)(2,1)} %bitcast.62), calls=%async_computation.11 | async-start | bytes 1048576 | tf_op jit(solution)/shard_map/all_to_all | solution.py:40
  (82 other events, 3899.4 us)
Sparse Core Ops, SparseCore 0:
  80.4 45.2 all-gather.41
  128.4 36.7 all-gather.43
  190.4 50.5 all-gather.45
  265.9 50.5 all-gather.47
  343.8 45.2 all-gather.49
  413.4 37.9 all-gather.51
  476.7 50.7 all-gather.53
  552.1 50.5 all-gather.55
  637.1 21.3 all-gather.33
  669.6 20.3 reduce-scatter.22
  696.0 21.2 all-gather.35
  744.4 20.3 reduce-scatter.24
  770.0 21.2 all-gather.37
  802.6 20.3 reduce-scatter.26
  827.6 21.2 all-gather.39
  874.6 20.3 reduce-scatter.28
  899.1 57.3 reduce-scatter.32
  960.4 56.4 reduce-scatter.30
  1024.3 122.3 all-reduce.7
  1150.5 73.3 reduce-scatter.40
  1228.2 71.3 reduce-scatter.38
  1303.4 71.4 reduce-scatter.36
  1379.2 71.4 reduce-scatter.34
  1454.5 169.3 all-reduce.9
  (8 shorter events, 153.8 us)
where the time goes:
time: 1650 us; the launch traced here: 1640 us
  waiting for transfers between devices  1280 us (78%)
  matrix products  159 us (10%)
  other arithmetic  58.8 us (4%)
  local copies, waits for them, and re-layouts  56.5 us (3%)
  blocking collectives  34.4 us (2%)
  starting transfers between devices  24.8 us (2%)
  between operations  17.8 us (1%)
    unnamed x33, waiting for transfers between devices  174 us
    reduce_scatter x2, waiting for transfers between devices, body(): lax.psum_scatter(grad_first_w.astype(jnp.bfloat16), 'dp', scatter_dimensi...  149 us
    reduce_scatter x2, waiting for transfers between devices, body(): lax.psum_scatter(grad_second_w.astype(jnp.bfloat16), 'dp', scatter_dimens...  148 us
    psum x1, waiting for transfers between devices, body(): lax.psum((jnp.stack([part[0] for part in vector_grads]), jnp.stack([part[...  128 us
    all_gather x2, waiting for transfers between devices, body(): lax.all_gather(w_ff1[layer_num], 'dp', axis=0, tiled=True)  97.3 us
    all_gather x2, waiting for transfers between devices, body(): lax.all_gather(w_qkv[layer_num], 'dp', axis=1, tiled=True)  91.1 us
    all_gather x4, waiting for transfers between devices, grad_rows(): lax.all_gather(grad_local, 'tensor', axis=0, tiled=True)  84.8 us
    all_gather x4, waiting for transfers between devices, rows_in(): lax.all_gather(local_rows, 'tensor', axis=0, tiled=True)  82.3 us
  transfers between devices with their start and end apart: 36, of which 32 were waited for; matrix products, arithmetic and copies ran while one was open for 8% of the time, Pallas kernels for 0%

commit v1 on v0

v1 whole, which is shorter than its diff:
```python
import math

import jax
import jax.numpy as jnp
import numpy as np
from jax import lax
from jax.sharding import PartitionSpec as P

D = 1024
HEADS = 16
FF = 4096
HEAD = D // HEADS
F32 = jnp.float32
BF16 = jnp.bfloat16


def layer_norm(summed, scaling, offset_vec):
    centre = jnp.mean(summed, axis=-1, keepdims=True)
    spread = summed - centre
    variance = jnp.mean(spread * spread, axis=-1, keepdims=True)
    return spread * lax.rsqrt(variance + 1e-05) * scaling + offset_vec


def gelu_slope(hidden_pre):
    normal_cdf = 0.5 * (1.0 + lax.erf(hidden_pre * 0.7071067811865476))
    return normal_cdf + hidden_pre * jnp.exp(-0.5 * hidden_pre * hidden_pre) * 0.3989422804014327


def dot(left, right):
    return jnp.dot(left, right, preferred_element_type=F32)


def contract_rows(left, right):
    return lax.dot_general(left, right, (((0,), (0,)), ((), ())), preferred_element_type=F32)


def times_transposed(left, right):
    return lax.dot_general(left, right, (((1,), (1,)), ((), ())), preferred_element_type=F32)


class Wires:
    def __init__(self, dp_size, tensor_size):
        self.dp_size, self.tensor_size = dp_size, tensor_size
        chips = dp_size // 2
        self.chips = chips
        order = list(range(0, chips, 2)) + list(range(chips - 1, 0, -2))
        place = {chip: spot for spot, chip in enumerate(order)}
        ring, sources = [], np.zeros((dp_size, chips), np.int32)
        for device in range(dp_size):
            chip, core = divmod(device, 2)
            way = 1 if core == 0 else -1
            ring.append((device, 2 * order[(place[chip] + way) % chips] + core))
            sources[device] = [order[(place[chip] - way * s) % chips] for s in range(chips)]
        self.ring = ring
        self.swap = [(d, d ^ 1) for d in range(dp_size)]
        dp_index = lax.axis_index("dp")
        self.core = dp_index % 2
        self.source = lax.dynamic_index_in_dim(jnp.asarray(sources), dp_index, 0, keepdims=False)

    def hop(self, array):
        return lax.ppermute(array, "dp", self.ring)

    def partner(self, array):
        return lax.ppermute(array, "dp", self.swap)

    def across(self, array):
        return lax.ppermute(array, "tensor", [(0, 1), (1, 0)])

    def half(self, array, axis, mine):
        width = array.shape[axis] // 2
        index = self.core if mine else 1 - self.core
        return lax.dynamic_slice_in_dim(array, index * width, width, axis)

    def ordered(self, mine, other, axis):
        return jnp.where(
            self.core == 0,
            jnp.concatenate([mine, other], axis),
            jnp.concatenate([other, mine], axis),
        )

    def gather_halves(self, shard, cuts, extra=None):
        mine, other = shard
        rows = mine.shape[0]
        got = self.partner(other)
        piece = self.ordered(mine, got, 0)
        chip_rows = 2 * rows
        if extra is not None:
            tail = jnp.zeros((8, piece.shape[1]), piece.dtype)
            pair = self.ordered(extra, self.partner(extra), 0)
            tail = lax.dynamic_update_slice(tail, pair[None, :], (0, 0))
            piece = jnp.concatenate([piece, tail], 0)
        wholes = [jnp.zeros((self.chips * chip_rows, b - a), piece.dtype) for a, b in cuts]
        vector = None if extra is None else jnp.zeros((self.chips, chip_rows), piece.dtype)
        for step in range(self.chips):
            if step:
                piece = self.hop(piece)
            chip = self.source[step]
            wholes = [
                lax.dynamic_update_slice(whole, piece[:chip_rows, a:b], (chip * chip_rows, 0))
                for whole, (a, b) in zip(wholes, cuts)
            ]
            if extra is not None:
                vector = lax.dynamic_update_slice(
                    vector, piece[chip_rows : chip_rows + 1, :chip_rows], (chip, 0)
                )
        halves = [(whole, self.partner(whole)) for whole in wholes]
        return halves if extra is None else (halves, vector.reshape(-1))

    def reduce_halves(self, sums):
        chip_rows = sums[0].shape[0] // self.chips
        widths = [part.shape[1] for part in sums]

        def portion(step):
            start = self.source[(step + 1) % self.chips] * chip_rows
            return [lax.dynamic_slice_in_dim(part, start, chip_rows, 0) for part in sums]

        total = jnp.concatenate(portion(0), 1)
        for step in range(1, self.chips):
            came = self.hop(total.astype(BF16)).astype(F32)
            total = came + jnp.concatenate(portion(step), 1).astype(F32)
        mine = self.half(total, 0, True)
        other = self.partner(self.half(total, 0, False).astype(BF16)).astype(F32)
        edges = np.cumsum([0] + widths)
        return [(mine[:, a:b], other[:, a:b]) for a, b in zip(edges[:-1], edges[1:])]

    def rows_in(self, local_rows):
        if self.tensor_size == 2:
            return [local_rows, self.across(local_rows)]
        return [lax.all_gather(local_rows, "tensor", axis=0, tiled=True)]

    def rows_out(self, term, count):
        if self.tensor_size == 2:
            came = self.across(term(1).astype(BF16))
            return term(0) + came.astype(F32)
        return lax.psum_scatter(
            term(0).astype(BF16), "tensor", scatter_dimension=0, tiled=True
        ).astype(F32)

    def butterfly(self, array, axis, size):
        bit = 1
        while bit < size:
            array = array + lax.ppermute(array, axis, [(i, i ^ bit) for i in range(size)])
            bit *= 2
        return array


def owner_swap(rows):
    return lax.all_to_all(rows, "dp", split_axis=0, concat_axis=0, tiled=True)


def masked_scores(query_block, key_rows, segment_block, segment, score_scale):
    scores = (
        jnp.einsum("qhe,khe->hqk", query_block, key_rows, preferred_element_type=F32) * score_scale
    )
    allowed = segment_block[:, None] == segment[None, :]
    return jnp.where(allowed[None], scores, -1e30)


def attend_forward(queries, key_rows, values, segment, score_scale):
    group_rows, head_count, head_size = queries.shape
    block_rows = min(512, group_rows)
    blocks = group_rows // block_rows

    def block_step(query_block, segment_block):
        scores = masked_scores(query_block, key_rows, segment_block, segment, score_scale)
        highest = jnp.max(scores, axis=-1, keepdims=True)
        weights = jnp.exp(scores - highest)
        summed = jnp.sum(weights, axis=-1, keepdims=True)
        probabilities = (weights / summed).astype(BF16)
        mixture = jnp.einsum("hqk,khe->qhe", probabilities, values, preferred_element_type=F32)
        return (mixture.astype(BF16), (highest + jnp.log(summed))[..., 0])

    if blocks == 1:
        mixture, log_total = block_step(queries, segment)
        log_total = log_total[None]
    else:
        _, (mixture, log_total) = lax.scan(
            lambda running, inputs: (running, block_step(*inputs)),
            None,
            (
                queries.reshape(blocks, block_rows, head_count, head_size),
                segment.reshape(blocks, block_rows),
            ),
        )
    return (mixture.reshape(group_rows, head_count * head_size), log_total)


def attend_backward(queries, key_rows, values, segment, log_total, grad_mixture, score_scale):
    group_rows, head_count, head_size = queries.shape
    block_rows = min(512, group_rows)
    blocks = group_rows // block_rows

    def block_step(query_block, segment_block, total_block, grad_block):
        scores = masked_scores(query_block, key_rows, segment_block, segment, score_scale)
        probabilities = jnp.exp(scores - total_block[..., None])
        grad_probs = jnp.einsum("qhe,khe->hqk", grad_block, values, preferred_element_type=F32)
        centre = jnp.sum(probabilities * grad_probs, axis=-1, keepdims=True)
        grad_scores = (probabilities * (grad_probs - centre)).astype(BF16)
        grad_query = (
            jnp.einsum("hqk,khe->qhe", grad_scores, key_rows, preferred_element_type=F32)
            * score_scale
        )
        grad_keys = (
            jnp.einsum("hqk,qhe->khe", grad_scores, query_block, preferred_element_type=F32)
            * score_scale
        )
        grad_values = jnp.einsum(
            "hqk,qhe->khe", probabilities.astype(BF16), grad_block, preferred_element_type=F32
        )
        return grad_query, grad_keys, grad_values

    if blocks == 1:
        grad_query, grad_keys, grad_values = block_step(
            queries, segment, log_total[0], grad_mixture
        )
    else:

        def step(running, inputs):
            grad_query, more_keys, more_values = block_step(*inputs)
            return (running[0] + more_keys, running[1] + more_values), grad_query

        zeros = jnp.zeros(key_rows.shape, F32)
        (grad_keys, grad_values), grad_query = lax.scan(
            step,
            (zeros, zeros),
            (
                queries.reshape(blocks, block_rows, head_count, head_size),
                segment.reshape(blocks, block_rows),
                log_total,
                grad_mixture.reshape(blocks, block_rows, head_count, head_size),
            ),
        )
    wide = (group_rows, head_count * head_size)
    return [
        part.astype(BF16).reshape(wide) for part in (grad_query, grad_keys, grad_values)
    ]


def join(blocks):
    return blocks[0] if len(blocks) == 1 else jnp.concatenate(blocks, 0)


def body(
    tokens,
    cotangent,
    deal_slot,
    back_slot,
    lengths,
    time_step,
    time_table,
    w_qkv,
    b_qv,
    w_out,
    out_bias,
    ln_gain,
    ln_shift,
    w_ff1,
    b_ff1,
    w_ff2,
):
    wires = Wires(lax.axis_size("dp"), lax.axis_size("tensor"))
    rows_dev = tokens.shape[0]
    group_rows = rows_dev * wires.tensor_size
    tensor_index = lax.axis_index("tensor")
    score_scale = 1.0 / math.sqrt(HEAD)
    layer_total = w_qkv.shape[0]
    inner = w_qkv.shape[3] // 2
    hidden = w_ff1.shape[2] // 2
    heads = inner // HEAD
    both = (True, False)

    time_piece = lax.dynamic_index_in_dim(time_table, time_step[0], 0, keepdims=False)
    weights = []
    for layer in range(layer_total):
        attn, feed = [], []
        for mine in both:
            qkv = wires.half(w_qkv[layer], 2, mine)
            attn.append(
                jnp.concatenate(
                    [qkv[0], qkv[1], qkv[2], wires.half(w_out[layer], 0, mine).T], axis=1
                )
            )
            feed.append(
                jnp.concatenate(
                    [wires.half(w_ff1[layer], 1, mine), wires.half(w_ff2[layer], 0, mine).T], axis=1
                )
            )
        attn_cuts = ((0, 3 * inner), (3 * inner, 4 * inner))
        feed_cuts = ((0, hidden), (hidden, 2 * hidden))
        if layer == 0:
            (qkv_w, out_w), time_row = wires.gather_halves(attn, attn_cuts, time_piece)
        else:
            qkv_w, out_w = wires.gather_halves(attn, attn_cuts)
        first_w, second_w = wires.gather_halves(feed, feed_cuts)
        weights.append((qkv_w, out_w, first_w, second_w))

    own_rows = owner_swap(jnp.take(tokens, back_slot, axis=0))
    upstream_rows = owner_swap(jnp.take(cotangent, back_slot, axis=0))
    seq_ends = jnp.cumsum(lengths[0])
    positions = jnp.arange(group_rows, dtype=jnp.int32)
    if wires.tensor_size == 2:
        positions = (positions + tensor_index * rows_dev) % group_rows
    segment = jnp.sum((positions[:, None] >= seq_ends[None, :]).astype(jnp.int32), axis=1)

    def split_heads(array):
        return array.reshape(group_rows, heads, HEAD)

    stream = own_rows.astype(F32) + time_row.astype(F32)
    saved = []
    for layer in range(layer_total):
        qkv_w, out_w, first_w, second_w = weights[layer]
        input_rows = join(wires.rows_in(stream.astype(BF16)))
        attention = []
        for half, mine in enumerate(both):
            bias_q = wires.half(b_qv[layer, 0], 0, mine)
            bias_v = wires.half(b_qv[layer, 1], 0, mine)
            projected = dot(input_rows, qkv_w[half])
            queries = split_heads((projected[:, :inner] + bias_q).astype(BF16))
            key_rows = split_heads(projected[:, inner : 2 * inner].astype(BF16))
            values = split_heads((projected[:, 2 * inner :] + bias_v).astype(BF16))
            head_out, log_total = attend_forward(queries, key_rows, values, segment, score_scale)
            attention.append((queries, key_rows, values, head_out, log_total))

        def attended_term(block):
            rows = group_rows if wires.tensor_size != 2 else rows_dev
            return sum(
                times_transposed(part[3][block * rows : (block + 1) * rows], out_w[half])
                for half, part in enumerate(attention)
            )

        middle = stream + wires.rows_out(attended_term, rows_dev) + out_bias[layer, 0]
        normed = layer_norm(middle, ln_gain[layer, 0], ln_shift[layer, 0])
        normed_blocks = wires.rows_in(normed.astype(BF16))
        hidden_blocks, act_blocks = [], []
        for block in normed_blocks:
            pre = [
                dot(block, first_w[half]) + wires.half(b_ff1[layer], 0, mine)
                for half, mine in enumerate(both)
            ]
            hidden_blocks.append(pre)
            act_blocks.append([jax.nn.gelu(f, approximate=False).astype(BF16) for f in pre])

        def feed_term(block):
            return sum(times_transposed(act_blocks[block][half], second_w[half]) for half in (0, 1))

        second_sum = normed + wires.rows_out(feed_term, rows_dev) + out_bias[layer, 1]
        saved.append(
            (input_rows, attention, middle, normed_blocks, hidden_blocks, act_blocks, second_sum)
        )
        stream = layer_norm(second_sum, ln_gain[layer, 1], ln_shift[layer, 1])
    returned_out = owner_swap(stream.astype(BF16))
    encoded = jnp.take(returned_out, deal_slot, axis=0)

    def both_cores(term):
        came = wires.partner(term(1).astype(BF16))
        return (term(0) + came.astype(F32)).astype(BF16)

    gradient = upstream_rows.astype(F32)
    matrix_grads = [None] * layer_total
    vector_grads = [None] * layer_total
    for layer in reversed(range(layer_total)):
        qkv_w, out_w, first_w, second_w = weights[layer]
        input_rows, attention, middle, normed_blocks, hidden_blocks, act_blocks, second_sum = saved[
            layer
        ]
        _, pull_second = jax.vjp(layer_norm, second_sum, ln_gain[layer, 1], ln_shift[layer, 1])
        grad_second, gain_second, shift_second = pull_second(gradient)
        branch_blocks = wires.rows_in(grad_second.astype(BF16))
        grad_pre = [
            [
                (dot(branch, second_w[half]) * gelu_slope(pre[half])).astype(BF16)
                for half in (0, 1)
            ]
            for branch, pre in zip(branch_blocks, hidden_blocks)
        ]

        def hidden_term(block):
            return sum(times_transposed(grad_pre[block][half], first_w[half]) for half in (0, 1))

        grad_normed = grad_second + wires.rows_out(hidden_term, rows_dev)
        grad_first_w = both_cores(
            lambda half: contract_rows(join(normed_blocks), join([b[half] for b in grad_pre]))
        )
        grad_second_w = both_cores(
            lambda half: contract_rows(join(branch_blocks), join([b[half] for b in act_blocks]))
        )
        feed_grads = wires.reduce_halves([grad_first_w, grad_second_w])
        grad_hidden_bias = [
            sum(jnp.sum(b[half].astype(F32), axis=0) for b in grad_pre) for half in (0, 1)
        ]
        _, pull_first = jax.vjp(layer_norm, middle, ln_gain[layer, 0], ln_shift[layer, 0])
        grad_middle, gain_first, shift_first = pull_first(grad_normed)
        attend_all = join(wires.rows_in(grad_middle.astype(BF16)))
        grad_qkv = []
        for half in (0, 1):
            queries, key_rows, values, head_out, log_total = attention[half]
            grad_heads = dot(attend_all, out_w[half]).astype(BF16)
            grad_qkv.append(
                attend_backward(
                    queries,
                    key_rows,
                    values,
                    segment,
                    log_total,
                    split_heads(grad_heads),
                    score_scale,
                )
            )
        grad_wide = [jnp.concatenate(parts, axis=1) for parts in grad_qkv]

        def proj_term(block):
            rows = group_rows if wires.tensor_size != 2 else rows_dev
            return sum(
                times_transposed(grad_wide[half][block * rows : (block + 1) * rows], qkv_w[half])
                for half in (0, 1)
            )

        gradient = grad_middle + wires.rows_out(proj_term, rows_dev)
        grad_proj = both_cores(lambda half: contract_rows(attend_all, attention[half][3]))
        grad_query_w = both_cores(lambda half: contract_rows(input_rows, grad_wide[half]))
        attn_grads = wires.reduce_halves([grad_query_w, grad_proj])
        qkv_pair, out_pair = attn_grads
        first_pair, second_pair = feed_grads
        rows = qkv_pair[0].shape[0]
        matrix_grads[layer] = (
            wires.ordered(
                *(part.reshape(rows, 3, inner).transpose(1, 0, 2) for part in qkv_pair), 2
            ),
            wires.ordered(out_pair[0].T, out_pair[1].T, 0),
            wires.ordered(first_pair[0], first_pair[1], 1),
            wires.ordered(second_pair[0].T, second_pair[1].T, 0),
        )
        qkv_sums = [jnp.sum(part.astype(F32), axis=0).reshape(3, inner) for part in grad_wide]
        vector_grads[layer] = (
            wires.ordered(qkv_sums[0], qkv_sums[1], 1)[jnp.array([0, 2])],
            wires.ordered(grad_hidden_bias[0], grad_hidden_bias[1], 0),
            jnp.stack([jnp.sum(grad_middle, axis=0), jnp.sum(grad_second, axis=0)]),
            jnp.stack([gain_first, gain_second]),
            jnp.stack([shift_first, shift_second]),
        )
    returned_grad = owner_swap(gradient.astype(BF16))
    grad_tokens = jnp.take(returned_grad, deal_slot, axis=0)
    time_grad = jnp.sum(gradient, axis=0)
    local = [jnp.stack([part[i] for part in vector_grads]) for i in range(5)]
    flat = jnp.concatenate([part.reshape(-1) for part in local[:2] + [time_grad] + local[2:]])
    flat = wires.butterfly(flat, "dp", wires.dp_size)
    border = local[0].size + local[1].size
    shared = wires.butterfly(flat[border:], "tensor", wires.tensor_size)
    grad_b_qv = flat[: local[0].size].reshape(local[0].shape)
    grad_b_ff1 = flat[local[0].size : border].reshape(local[1].shape)
    time_grad = shared[:D]
    rest = shared[D:].reshape(3, layer_total, 2, D)
    return (
        encoded,
        grad_tokens,
        time_grad,
        jnp.stack([part[0] for part in matrix_grads]),
        grad_b_qv,
        jnp.stack([part[1] for part in matrix_grads]),
        rest[0],
        rest[1],
        rest[2],
        jnp.stack([part[2] for part in matrix_grads]),
        grad_b_ff1,
        jnp.stack([part[3] for part in matrix_grads]),
    )


def solution(mesh):
    return jax.shard_map(
        body,
        mesh=mesh,
        in_specs=(
            P(("dp", "tensor"), None),
            P(("dp", "tensor"), None),
            P(("dp", "tensor")),
            P(("dp", "tensor")),
            P("dp", None),
            P(),
            P(None, "dp"),
            P(None, None, "dp", "tensor"),
            P(None, None, "tensor"),
            P(None, "tensor", "dp"),
            P(),
            P(),
            P(),
            P(None, "dp", "tensor"),
            P(None, "tensor"),
            P(None, "tensor", "dp"),
        ),
        out_specs=(
            P(("dp", "tensor"), None),
            P(("dp", "tensor"), None),
            P(),
            P(None, None, "dp", "tensor"),
            P(None, None, "tensor"),
            P(None, "tensor", "dp"),
            P(),
            P(),
            P(),
            P(None, "dp", "tensor"),
            P(None, "tensor"),
            P(None, "tensor", "dp"),
        ),
        check_vma=False,
    )
```

time: 1650 us -> 709 us (0.43)
  waiting for transfers between devices: 1280 us -> 140 us
  starting transfers between devices: 24.8 us -> 128 us
  local copies, waits for them, and re-layouts: 56.5 us -> 156 us
  matrix products: 159 us -> 196 us
  blocking collectives: 34.4 us -> 0 us
    all_gather x16 -> x0, waiting for transfers between devices: 491 us -> none  [the longest x2 97.3 us: body(): lax.all_gather(w_ff1[layer_num], 'dp', axis=0, tiled=True)]
    reduce_scatter x14 -> x0, waiting for transfers between devices: 477 us -> none  [the longest x2 149 us: body(): lax.psum_scatter(grad_first_w.astype(jnp.bfloat16), 'dp', scatter_dimensi...]
    unnamed x33 -> x0, waiting for transfers between devices: 174 us -> none
    ppermute x0 -> x102, waiting for transfers between devices: none -> 140 us  [the longest x16 63.4 us: across(): return lax.ppermute(array, 'tensor', [(0, 1), (1, 0)])]
    psum x1 -> x0, waiting for transfers between devices: 128 us -> none  [body(): lax.psum((jnp.stack([part[0] for part in vector_grads]), jnp.stack([part[...]
    ppermute x0 -> x102, starting transfers between devices: none -> 106 us  [the longest x56 75.3 us: hop(): return lax.ppermute(array, 'dp', self.ring)]
    dynamic_update_slice x2 -> x58, local copies, waits for them, and re-layouts: 0.03 us -> 71.5 us  [the longest x50 71.3 us: gather_halves(): lax.dynamic_update_slice(whole, piece[:chip_rows, a:b], (chip * chip_rows...]
    unnamed x1 -> x0, blocking collectives: 34.4 us -> none
  transfers between devices with their start and end apart: 36 -> 106, of which waited for: 32 -> 36; matrix products, arithmetic and copies ran while one was open for 8% -> 53% of each run, Pallas kernels for 0% -> 0%
where the time goes in v1:
time: 709 us; the launch traced here: 699 us
  matrix products  196 us (28%)
  local copies, waits for them, and re-layouts  156 us (22%)
  waiting for transfers between devices  140 us (20%)
  starting transfers between devices  128 us (18%)
  other arithmetic  53.2 us (8%)
  between operations  26.1 us (4%)
    dot_general x24, matrix products, dot(): return jnp.dot(left, right, preferred_element_type=F32)  77.6 us
    ppermute x56, starting transfers between devices, hop(): return lax.ppermute(array, 'dp', self.ring)  75.3 us
    dynamic_update_slice x50, local copies, waits for them, and re-layouts, gather_halves(): lax.dynamic_update_slice(whole, piece[:chip_rows, a:b], (chip * chip_rows...  71.3 us
    ppermute x16, waiting for transfers between devices, across(): return lax.ppermute(array, 'tensor', [(0, 1), (1, 0)])  63.4 us
    ppermute x56, waiting for transfers between devices, hop(): return lax.ppermute(array, 'dp', self.ring)  60.7 us
    dot_general x32, matrix products, times_transposed(): lax.dot_general(left, right, (((1,), (1,)), ((), ())), preferred_element_...  55.1 us
    dot_general x16, matrix products, contract_rows(): lax.dot_general(left, right, (((0,), (0,)), ((), ())), preferred_element_...  37.2 us
    unnamed x500, local copies, waits for them, and re-layouts  23.4 us
  transfers between devices with their start and end apart: 106, of which 36 were waited for; matrix products, arithmetic and copies ran while one was open for 53% of the time, Pallas kernels for 0%

profile of v1, /device:TPU:0, one launch (start us, length us, event | category | flops | bytes accessed | tf_op | source)
XLA Modules:
  0.0 698.8 jit_solution(4279177142325024606)
XLA Ops:
  9.1 7.0 %all-to-all-start.2 = ((bf16[16,16,1024]{2,1,0:T(8,128)(2,1)}), bf16[16,16,1024]{2,1,0:T(8,128)(2,1)S(1)}, u32[]{:S(2)}, u32[]{:S(2)}) async-start(bf16[16,16,1024]{2,1,0:T(8,128)(2,1)} %bitcast.98), calls=%async_computation.2 | async-start | bytes 1048576 | tf_op jit(solution)/shard_map/all_to_all | solution.py:148
  133.4 4.5 collective-permute-start.33
  166.1 5.7 collective-permute-done.9
  234.8 4.6 collective-permute-done.23
  252.2 12.3 %fusion.91 = (bf16[256,1024]{1,0:T(8,128)(2,1)S(1)}, f32[256,1024]{1,0:T(8,128)}) fusion(f32[1024]{0:T(1024)S(1)} %bitcast.578, bf16[256,1024]{1,0:T(8,128)(2,1)S(1)} %fusion.227, bf16[1024,1024]{1,0:T(8,128)(2,1)S(1)} %collective-permute-done.21), kind=kOutput, calls=%fused_computation.195 | convolution fusion | flops 554172416 | bytes 4198400 | tf_op jit(solution)/shard_map/dot_general | solution.py:30
  273.2 6.3 collective-permute-done.25
  301.5 8.8 %collective-permute-done.36 = bf16[256,1024]{1,0:T(8,128)(2,1)S(1)} collective-permute-done((bf16[256,1024]{1,0:T(8,128)(2,1)S(1)}, bf16[256,1024]{1,0:T(8,128)(2,1)S(1)}, u32[]{:S(2)}, u32[]{:S(2)}) %collective-permute-start.36) | collective-permute-done | bytes 524320 | tf_op jit(solution)/shard_map/ppermute | solution.py:67
  312.0 5.8 fusion.100
  320.8 5.6 fusion.106
  326.4 5.6 fusion.109
  338.1 5.4 fusion.103
  351.9 6.6 all-to-all-start.1
  366.6 7.5 %collective-permute-done.49 = bf16[256,1024]{1,0:T(8,128)(2,1)S(1)} collective-permute-done((bf16[256,1024]{1,0:T(8,128)(2,1)S(1)}, bf16[256,1024]{1,0:T(8,128)(2,1)S(1)}, u32[]{:S(2)}, u32[]{:S(2)}) %collective-permute-start.49) | collective-permute-done | bytes 524320 | tf_op jit(solution)/shard_map/ppermute | solution.py:67
  393.7 4.3 collective-permute-done.50
  407.3 6.9 collective-permute-done.51
  441.3 5.9 collective-permute-done.52
  550.1 4.7 all-to-all-start.3
  560.1 8.7 %collective-permute-done.59 = f32[19456]{0:T(1024)S(1)} collective-permute-done((f32[19456]{0:T(1024)S(1)}, f32[19456]{0:T(1024)S(1)}, u32[]{:S(2)}, u32[]{:S(2)}) %collective-permute-start.59) | collective-permute-done | bytes 77856 | tf_op jit(solution)/shard_map/ppermute | solution.py:142
  625.1 5.9 collective-permute-done.65
  633.5 5.9 collective-permute-done.66
  649.3 8.2 %collective-permute-done.68 = bf16[128,1024]{0,1:T(8,128)(2,1)S(1)} collective-permute-done((bf16[128,1024]{0,1:T(8,128)(2,1)S(1)}, bf16[128,1024]{0,1:T(8,128)(2,1)S(1)}, u32[]{:S(2)}, u32[]{:S(2)}) %collective-permute-start.68) | collective-permute-done | bytes 262176 | tf_op jit(solution)/shard_map/ppermute | solution.py:61
  665.3 4.3 collective-permute-done.88
  674.5 5.5 collective-permute-done.89
  683.1 7.2 %collective-permute-done.90 = bf16[128,2048]{0,1:T(8,128)(2,1)S(1)} collective-permute-done((bf16[128,2048]{0,1:T(8,128)(2,1)}, bf16[128,2048]{0,1:T(8,128)(2,1)S(1)}, u32[]{:S(2)}, u32[]{:S(2)}) %collective-permute-start.90) | collective-permute-done | bytes 524320 | tf_op jit(solution)/shard_map/ppermute | solution.py:61
  (1098 shorter events, 519.5 us)
Async XLA Ops:
  2.4 42.6 %collective-permute-start = (bf16[64]{0:T(256)(128)(2,1)}, bf16[64]{0:T(256)(128)(2,1)}, u32[]{:S(2)}, u32[]{:S(2)}) collective-permute-start(bf16[64]{0:T(256)(128)(2,1)} %bitcast.3), channel_id=1, source_target_pairs={{0,2},{2,0},{4,6},{6,4},{8,10},{10,8},{12,14},{14,12},{16,18},{18,... | collective-permute-start | bytes 392 | tf_op jit(solution)/shard_map/ppermute | solution.py:64
  4.9 41.0 %collective-permute-start.26 = (bf16[64,1024]{1,0:T(8,128)(2,1)S(1)}, bf16[64,1024]{1,0:T(8,128)(2,1)S(1)}, u32[]{:S(2)}, u32[]{:S(2)}) collective-permute-start(bf16[64,1024]{1,0:T(8,128)(2,1)S(1)} %pad_maximum_fusion.31), channel_id=1, source_target_pairs={{0,2},{2,0},{4,6},{6,4},{8,10},{10,8},{12,14},{14,12},{16,18},{18,... | collective-permute-start | bytes 393224 | tf_op jit(solution)/shard_map/ppermute | solution.py:64
  5.1 42.9 %collective-permute-start.1 = (bf16[64,1024]{1,0:T(8,128)(2,1)S(1)}, bf16[64,1024]{1,0:T(8,128)(2,1)S(1)}, u32[]{:S(2)}, u32[]{:S(2)}) collective-permute-start(bf16[64,1024]{1,0:T(8,128)(2,1)S(1)} %pad_maximum_fusion.30), channel_id=1, source_target_pairs={{0,2},{2,0},{4,6},{6,4},{8,10},{10,8},{12,14},{14,12},{16,18},{18,... | collective-permute-start | bytes 393224 | tf_op jit(solution)/shard_map/ppermute | solution.py:64
  9.1 90.8 %all-to-all-start.2 = ((bf16[16,16,1024]{2,1,0:T(8,128)(2,1)}), bf16[16,16,1024]{2,1,0:T(8,128)(2,1)S(1)}, u32[]{:S(2)}, u32[]{:S(2)}) async-start(bf16[16,16,1024]{2,1,0:T(8,128)(2,1)} %bitcast.98), calls=%async_computation.2 | async-start | bytes 1048576 | tf_op jit(solution)/shard_map/all_to_all | solution.py:148
  16.6 39.1 %collective-permute-start.13 = (bf16[64,2048]{1,0:T(8,128)(2,1)S(1)}, bf16[64,2048]{1,0:T(8,128)(2,1)S(1)}, u32[]{:S(2)}, u32[]{:S(2)}) collective-permute-start(bf16[64,2048]{1,0:T(8,128)(2,1)S(1)} %pad_maximum_fusion.26), channel_id=1, source_target_pairs={{0,2},{2,0},{4,6},{6,4},{8,10},{10,8},{12,14},{14,12},{16,18},{18,... | collective-permute-start | bytes 786440 | tf_op jit(solution)/shard_map/ppermute | solution.py:64
  17.0 36.2 %collective-permute-start.37 = (bf16[64,2048]{1,0:T(8,128)(2,1)S(1)}, bf16[64,2048]{1,0:T(8,128)(2,1)S(1)}, u32[]{:S(2)}, u32[]{:S(2)}) collective-permute-start(bf16[64,2048]{1,0:T(8,128)(2,1)S(1)} %pad_maximum_fusion.27), channel_id=1, source_target_pairs={{0,2},{2,0},{4,6},{6,4},{8,10},{10,8},{12,14},{14,12},{16,18},{18,... | collective-permute-start | bytes 786440 | tf_op jit(solution)/shard_map/ppermute | solution.py:64
  99.9 56.4 %all-to-all-start = ((bf16[16,16,1024]{2,1,0:T(8,128)(2,1)}), bf16[16,16,1024]{2,1,0:T(8,128)(2,1)}, u32[]{:S(2)}, u32[]{:S(2)}) async-start(bf16[16,16,1024]{2,1,0:T(8,128)(2,1)} %bitcast.465), calls=%async_computation | async-start | bytes 1048576 | tf_op jit(solution)/shard_map/all_to_all | solution.py:148
  151.8 145.2 %collective-permute-start.35 = (bf16[1024,256]{1,0:T(8,128)(2,1)S(1)}, bf16[1024,256]{1,0:T(8,128)(2,1)}, u32[]{:S(2)}, u32[]{:S(2)}) collective-permute-start(bf16[1024,256]{1,0:T(8,128)(2,1)S(1)} %slice_dynamic-update-slice_fusion.48), channel_id=1, source_target_pairs={{0,2},{2,0},{4,6},{6,4},{8,10},{10,8},{12,14},{14,12},{16,18},{18,... | collective-permute-start | bytes 1572872 | tf_op jit(solution)/shard_map/ppermute | solution.py:64
  156.3 56.9 %collective-permute-start.11 = (bf16[1024,256]{1,0:T(8,128)(2,1)}, bf16[1024,256]{1,0:T(8,128)(2,1)}, u32[]{:S(2)}, u32[]{:S(2)}) collective-permute-start(bf16[1024,256]{1,0:T(8,128)(2,1)} %slice_dynamic-update-slice_fusion.56), channel_id=1, source_target_pairs={{0,2},{2,0},{4,6},{6,4},{8,10},{10,8},{12,14},{14,12},{16,18},{18,... | collective-permute-start | bytes 1572872 | tf_op jit(solution)/shard_map/ppermute | solution.py:64
  160.6 38.3 %collective-permute-start.10 = (bf16[1024,768]{1,0:T(8,128)(2,1)}, bf16[1024,768]{1,0:T(8,128)(2,1)}, u32[]{:S(2)}, u32[]{:S(2)}) collective-permute-start(bf16[1024,768]{1,0:T(8,128)(2,1)} %slice_dynamic-update-slice_fusion.40), channel_id=1, source_target_pairs={{0,2},{2,0},{4,6},{6,4},{8,10},{10,8},{12,14},{14,12},{16,18},{18,... | collective-permute-start | bytes 4718600 | tf_op jit(solution)/shard_map/ppermute | solution.py:64
  190.0 44.7 %collective-permute-start.43 = (bf16[128,2048]{1,0:T(8,128)(2,1)}, bf16[128,2048]{1,0:T(8,128)(2,1)}, u32[]{:S(2)}, u32[]{:S(2)}) collective-permute-start(bf16[128,2048]{1,0:T(8,128)(2,1)} %collective-permute-done.42), channel_id=1, source_target_pairs={{0,8},{2,6},{4,0},{6,14},{8,16},{10,2},{12,4},{14,22},{16,24},{18,... | collective-permute-start | bytes 1572872 | tf_op jit(solution)/shard_map/ppermute | solution.py:61
  234.7 38.5 %collective-permute-start.34 = (bf16[1024,768]{1,0:T(8,128)(2,1)}, bf16[1024,768]{1,0:T(8,128)(2,1)S(1)}, u32[]{:S(2)}, u32[]{:S(2)}) collective-permute-start(bf16[1024,768]{1,0:T(8,128)(2,1)} %slice_dynamic-update-slice_fusion.32), channel_id=1, source_target_pairs={{0,2},{2,0},{4,6},{6,4},{8,10},{10,8},{12,14},{14,12},{16,18},{18,... | collective-permute-start | bytes 4718600 | tf_op jit(solution)/shard_map/ppermute | solution.py:64
  272.7 59.3 %collective-permute-start.46 = (bf16[1024,1024]{1,0:T(8,128)(2,1)}, bf16[1024,1024]{1,0:T(8,128)(2,1)}, u32[]{:S(2)}, u32[]{:S(2)}) collective-permute-start(bf16[1024,1024]{1,0:T(8,128)(2,1)} %get-tuple-element.167), channel_id=1, source_target_pairs={{0,2},{2,0},{4,6},{6,4},{8,10},{10,8},{12,14},{14,12},{16,18},{18,... | collective-permute-start | bytes 6291464 | tf_op jit(solution)/shard_map/ppermute | solution.py:64
  272.7 53.7 %collective-permute-start.45 = (bf16[1024,1024]{1,0:T(8,128)(2,1)}, bf16[1024,1024]{1,0:T(8,128)(2,1)}, u32[]{:S(2)}, u32[]{:S(2)}) collective-permute-start(bf16[1024,1024]{1,0:T(8,128)(2,1)} %get-tuple-element.168), channel_id=1, source_target_pairs={{0,2},{2,0},{4,6},{6,4},{8,10},{10,8},{12,14},{14,12},{16,18},{18,... | collective-permute-start | bytes 6291464 | tf_op jit(solution)/shard_map/ppermute | solution.py:64
  351.9 51.3 %all-to-all-start.1 = ((bf16[16,16,1024]{2,1,0:T(8,128)(2,1)}), bf16[16,16,1024]{2,1,0:T(8,128)(2,1)S(1)}, u32[]{:S(2)}, u32[]{:S(2)}) async-start(bf16[16,16,1024]{2,1,0:T(8,128)(2,1)} %bitcast.466), calls=%async_computation.1 | async-start | bytes 1048576 | tf_op jit(solution)/shard_map/all_to_all | solution.py:148
  390.6 68.8 %collective-permute-start.93 = (bf16[1024,1024]{0,1:T(8,128)(2,1)}, bf16[1024,1024]{0,1:T(8,128)(2,1)}, u32[]{:S(2)}, u32[]{:S(2)}) collective-permute-start(bf16[1024,1024]{0,1:T(8,128)(2,1)} %convolution_convert_fusion), channel_id=1, source_target_pairs={{0,2},{2,0},{4,6},{6,4},{8,10},{10,8},{12,14},{14,12},{16,18},{18,... | collective-permute-start | bytes 6291464 | tf_op jit(solution)/shard_map/ppermute | solution.py:64
  393.2 69.3 %collective-permute-start.92 = (bf16[1024,1024]{0,1:T(8,128)(2,1)}, bf16[1024,1024]{0,1:T(8,128)(2,1)}, u32[]{:S(2)}, u32[]{:S(2)}) collective-permute-start(bf16[1024,1024]{0,1:T(8,128)(2,1)} %convolution_convert_fusion.1), channel_id=1, source_target_pairs={{0,2},{2,0},{4,6},{6,4},{8,10},{10,8},{12,14},{14,12},{16,18},{18,... | collective-permute-start | bytes 6291464 | tf_op jit(solution)/shard_map/ppermute | solution.py:64
  437.7 46.5 %collective-permute-start.72 = (bf16[1024,768]{0,1:T(8,128)(2,1)}, bf16[1024,768]{0,1:T(8,128)(2,1)}, u32[]{:S(2)}, u32[]{:S(2)}) collective-permute-start(bf16[1024,768]{0,1:T(8,128)(2,1)} %convolution_convert_fusion.4), channel_id=1, source_target_pairs={{0,2},{2,0},{4,6},{6,4},{8,10},{10,8},{12,14},{14,12},{16,18},{18,... | collective-permute-start | bytes 4718600 | tf_op jit(solution)/shard_map/ppermute | solution.py:64
  479.4 110.7 %collective-permute-start.83 = (bf16[1024,1024]{0,1:T(8,128)(2,1)}, bf16[1024,1024]{0,1:T(8,128)(2,1)}, u32[]{:S(2)}, u32[]{:S(2)}) collective-permute-start(bf16[1024,1024]{0,1:T(8,128)(2,1)} %convolution_convert_fusion.2), channel_id=1, source_target_pairs={{0,2},{2,0},{4,6},{6,4},{8,10},{10,8},{12,14},{14,12},{16,18},{18,... | collective-permute-start | bytes 6291464 | tf_op jit(solution)/shard_map/ppermute | solution.py:64
  482.0 112.5 %collective-permute-start.82 = (bf16[1024,1024]{0,1:T(8,128)(2,1)}, bf16[1024,1024]{0,1:T(8,128)(2,1)}, u32[]{:S(2)}, u32[]{:S(2)}) collective-permute-start(bf16[1024,1024]{0,1:T(8,128)(2,1)} %convolution_convert_fusion.3), channel_id=1, source_target_pairs={{0,2},{2,0},{4,6},{6,4},{8,10},{10,8},{12,14},{14,12},{16,18},{18,... | collective-permute-start | bytes 6291464 | tf_op jit(solution)/shard_map/ppermute | solution.py:64
  497.2 45.2 %collective-permute-start.96 = (bf16[128,2048]{0,1:T(8,128)(2,1)}, bf16[128,2048]{0,1:T(8,128)(2,1)}, u32[]{:S(2)}, u32[]{:S(2)}) collective-permute-start(bf16[128,2048]{0,1:T(8,128)(2,1)} %add_convert_fusion.10), channel_id=1, source_target_pairs={{0,8},{2,6},{4,0},{6,14},{8,16},{10,2},{12,4},{14,22},{16,24},{18,... | collective-permute-start | bytes 1572872 | tf_op jit(solution)/shard_map/ppermute | solution.py:61
  502.0 33.0 %collective-permute-start.76 = (bf16[128,1024]{0,1:T(8,128)(2,1)}, bf16[128,1024]{0,1:T(8,128)(2,1)}, u32[]{:S(2)}, u32[]{:S(2)}) collective-permute-start(bf16[128,1024]{0,1:T(8,128)(2,1)} %add_convert_fusion.27), channel_id=1, source_target_pairs={{0,8},{2,6},{4,0},{6,14},{8,16},{10,2},{12,4},{14,22},{16,24},{18,... | collective-permute-start | bytes 786440 | tf_op jit(solution)/shard_map/ppermute | solution.py:61
  543.8 67.9 %collective-permute-start.62 = (bf16[1024,768]{0,1:T(8,128)(2,1)}, bf16[1024,768]{0,1:T(8,128)(2,1)}, u32[]{:S(2)}, u32[]{:S(2)}) collective-permute-start(bf16[1024,768]{0,1:T(8,128)(2,1)} %convolution_convert_fusion.5), channel_id=1, source_target_pairs={{0,2},{2,0},{4,6},{6,4},{8,10},{10,8},{12,14},{14,12},{16,18},{18,... | collective-permute-start | bytes 4718600 | tf_op jit(solution)/shard_map/ppermute | solution.py:64
  550.1 56.5 %all-to-all-start.3 = ((bf16[16,16,1024]{2,1,0:T(8,128)(2,1)}), bf16[16,16,1024]{2,1,0:T(8,128)(2,1)S(1)}, u32[]{:S(2)}, u32[]{:S(2)}) async-start(bf16[16,16,1024]{2,1,0:T(8,128)(2,1)} %bitcast.128), calls=%async_computation.3 | async-start | bytes 1048576 | tf_op jit(solution)/shard_map/all_to_all | solution.py:148
  (325 other events, 3579.9 us)

commit v2 on v1

v2 whole, which is shorter than its diff:
```python
import math

import jax
import jax.numpy as jnp
import numpy as np
from jax import lax
from jax.experimental import pallas as pl
from jax.experimental.pallas import tpu as pltpu
from jax.sharding import PartitionSpec as P

D = 1024
HEADS = 16
FF = 4096
HEAD = D // HEADS
F32 = jnp.float32
BF16 = jnp.bfloat16


def layer_norm(summed, scaling, offset_vec):
    centre = jnp.mean(summed, axis=-1, keepdims=True)
    spread = summed - centre
    variance = jnp.mean(spread * spread, axis=-1, keepdims=True)
    return spread * lax.rsqrt(variance + 1e-05) * scaling + offset_vec


def dot(left, right):
    return jnp.dot(left, right, preferred_element_type=F32)


def contract_rows(left, right):
    return lax.dot_general(left, right, (((0,), (0,)), ((), ())), preferred_element_type=F32)


def times_transposed(left, right):
    return lax.dot_general(left, right, (((1,), (1,)), ((), ())), preferred_element_type=F32)


class Wires:
    def __init__(self, dp_size, tensor_size):
        self.dp_size, self.tensor_size = dp_size, tensor_size
        chips = dp_size // 2
        self.chips = chips
        order = list(range(0, chips, 2)) + list(range(chips - 1, 0, -2))
        place = {chip: spot for spot, chip in enumerate(order)}
        ring, sources = [], np.zeros((dp_size, chips), np.int32)
        for device in range(dp_size):
            chip, core = divmod(device, 2)
            way = 1 if core == 0 else -1
            ring.append((device, 2 * order[(place[chip] + way) % chips] + core))
            sources[device] = [order[(place[chip] - way * s) % chips] for s in range(chips)]
        self.ring = ring
        self.swap = [(d, d ^ 1) for d in range(dp_size)]
        dp_index = lax.axis_index("dp")
        self.core = dp_index % 2
        self.source = lax.dynamic_index_in_dim(jnp.asarray(sources), dp_index, 0, keepdims=False)

    def hop(self, array):
        return lax.ppermute(array, "dp", self.ring)

    def partner(self, array):
        return lax.ppermute(array, "dp", self.swap)

    def across(self, array):
        return lax.ppermute(array, "tensor", [(0, 1), (1, 0)])

    def half(self, array, axis, mine):
        width = array.shape[axis] // 2
        index = self.core if mine else 1 - self.core
        return lax.dynamic_slice_in_dim(array, index * width, width, axis)

    def ordered(self, mine, other, axis):
        return jnp.where(
            self.core == 0,
            jnp.concatenate([mine, other], axis),
            jnp.concatenate([other, mine], axis),
        )

    def gather_halves(self, shard, cuts, extra=None):
        mine, other = shard
        got = self.partner(other)
        piece = self.ordered(mine, got, 0)
        chip_rows = piece.shape[0]
        if extra is not None:
            tail = jnp.zeros((8, piece.shape[1]), piece.dtype)
            pair = self.ordered(extra, self.partner(extra), 0)
            tail = lax.dynamic_update_slice(tail, pair[None, :], (0, 0))
            piece = jnp.concatenate([piece, tail], 0)
        piece = yield piece
        pieces = [piece]
        for _ in range(1, self.chips):
            piece = yield self.hop(piece)
            pieces.append(piece)
        wholes, vector = place_pieces(self.source, pieces, chip_rows, cuts)
        halves = [(whole, self.partner(whole)) for whole in wholes]
        if extra is None:
            return halves
        return halves, vector[:, 0, :chip_rows].reshape(-1)

    def reduce_halves(self, terms):
        came = [self.partner(term(1).astype(BF16)) for term in terms]
        came = yield came
        sums = [(term(0) + part.astype(F32)).astype(BF16) for term, part in zip(terms, came)]
        chip_rows = sums[0].shape[0] // self.chips
        widths = [part.shape[1] for part in sums]

        def portion(step):
            start = self.source[(step + 1) % self.chips] * chip_rows
            return [lax.dynamic_slice_in_dim(part, start, chip_rows, 0) for part in sums]

        total = jnp.concatenate(portion(0), 1)
        for step in range(1, self.chips):
            came = yield self.hop(total.astype(BF16))
            total = came.astype(F32) + jnp.concatenate(portion(step), 1).astype(F32)
        mine = self.half(total, 0, True)
        other = self.partner(self.half(total, 0, False).astype(BF16)).astype(F32)
        edges = np.cumsum([0] + widths)
        return [(mine[:, a:b], other[:, a:b]) for a, b in zip(edges[:-1], edges[1:])]

    def rows_in(self, local_rows, beside):
        beside = beside or Beside(0.0)
        local_rows = beside.tick(local_rows)
        if self.tensor_size == 2:
            return [local_rows, beside.tick(self.across(local_rows))]
        return [beside.tick(lax.all_gather(local_rows, "tensor", axis=0, tiled=True))]

    def rows_out(self, term, beside):
        if self.tensor_size == 2:
            came = self.across(beside.tick(term(1).astype(BF16)))
            return term(0) + beside.tick(came).astype(F32)
        whole = beside.tick(term(0).astype(BF16))
        return beside.tick(
            lax.psum_scatter(whole, "tensor", scatter_dimension=0, tiled=True)
        ).astype(F32)

    def butterfly(self, array, axis, size):
        bit = 1
        while bit < size:
            array = array + lax.ppermute(array, axis, [(i, i ^ bit) for i in range(size)])
            bit *= 2
        return array


class Task:
    def __init__(self, steps, load):
        self.steps, self.load, self.done, self.result = steps, load, False, None
        self.pending = None
        self.advance(None, first=True)

    def advance(self, arrived, first=False):
        try:
            self.pending = next(self.steps) if first else self.steps.send(arrived)
        except StopIteration as stop:
            self.done, self.result = True, stop.value

    def finish(self):
        while not self.done:
            self.advance(self.pending)
        return self.result


class Beside:
    def __init__(self, most):
        self.most, self.tasks = most, []

    def add(self, task):
        self.tasks.append(task)
        return task

    def lead(self, first, second):
        step = 0
        while not first.done:
            chosen = [first, second] if step % 2 else [first]
            arrived = lax.optimization_barrier([task.pending for task in chosen])
            for task, part in zip(chosen, arrived):
                task.advance(part)
            step += 1
        return first.result

    def tick(self, value):
        self.tasks = [task for task in self.tasks if not task.done]
        chosen, load = [], 0.0
        for task in self.tasks:
            if not chosen or load + task.load <= self.most:
                chosen.append(task)
                load += task.load
        if not chosen:
            return value
        value, arrived = lax.optimization_barrier((value, [task.pending for task in chosen]))
        for task, part in zip(chosen, arrived):
            task.advance(part)
        return value


def place_pieces(source, pieces, chip_rows, cuts):
    count, width = len(pieces), pieces[0].shape[1]
    aligned = all(a % 128 == 0 and b % 128 == 0 for a, b in cuts)
    ranges = cuts if aligned else ((0, width),)
    spare = pieces[0].shape[0] - chip_rows

    def kernel(source_ref, *refs):
        ins, outs, sems = refs[:count], refs[count:-1], refs[-1]
        copies = []
        for i, piece in enumerate(ins):
            rows = pl.ds(pl.multiple_of(source_ref[i] * chip_rows, chip_rows), chip_rows)
            for j, (a, b) in enumerate(ranges):
                copies.append(
                    pltpu.make_async_copy(
                        piece.at[0:chip_rows, a:b], outs[j].at[rows, :], sems.at[i, j]
                    )
                )
            if spare:
                copies.append(
                    pltpu.make_async_copy(
                        piece.at[chip_rows : chip_rows + spare, 0:128],
                        outs[-1].at[source_ref[i]],
                        sems.at[i, len(ranges)],
                    )
                )
        for copy in copies:
            copy.start()
        for copy in copies:
            copy.wait()

    shapes = [jax.ShapeDtypeStruct((count * chip_rows, b - a), BF16) for a, b in ranges]
    if spare:
        shapes.append(jax.ShapeDtypeStruct((count, spare, 128), BF16))
    size = count * pieces[0].size * 2
    outs = pl.pallas_call(
        kernel,
        out_shape=shapes,
        in_specs=[pl.BlockSpec(memory_space=pltpu.SMEM)]
        + [pl.BlockSpec(memory_space=pl.ANY)] * count,
        out_specs=[pl.BlockSpec(memory_space=pltpu.VMEM)] * len(shapes),
        scratch_shapes=[pltpu.SemaphoreType.DMA((count, len(shapes)))],
        compiler_params=pltpu.CompilerParams(vmem_limit_bytes=16 << 20),
        cost_estimate=pl.CostEstimate(flops=0, bytes_accessed=2 * size, transcendentals=0),
        name="place_pieces",
    )(source, *pieces)
    vector = outs[-1] if spare else None
    wholes = outs[: len(ranges)]
    if not aligned:
        wholes = [wholes[0][:, a:b] for a, b in cuts]
    return wholes, vector


def owner_swap(rows):
    return lax.all_to_all(rows, "dp", split_axis=0, concat_axis=0, tiled=True)


def erf(x):
    x = jnp.clip(x, -3.7439211627767994, 3.7439211627767994)
    s = x * x
    top = jnp.full_like(s, 0.00022905065861350646)
    for c in (0.0034082910107109506, 0.050955695062380861, 0.18520832239976145, 1.128379143519084):
        top = top * s + c
    low = jnp.full_like(s, -1.1791602954361697e-7)
    for c in (
        0.000023547966471313185,
        0.0010179625278914885,
        0.014070470171167667,
        0.11098505178285362,
        0.49746925110067538,
        1.0,
    ):
        low = low * s + c
    return x * top / low


def whole_spec(shape):
    return pl.BlockSpec(shape, lambda *_: (0,) * len(shape))


def attend_forward(blocks, weight, bias, segment):
    rows = sum(block.shape[0] for block in blocks)
    inner = weight.shape[1] // 3
    heads = inner // HEAD
    step = min(512, rows)
    scale = 1.0 / math.sqrt(HEAD)

    def kernel(*refs):
        xs = refs[: len(blocks)]
        w_ref, bias_ref, col_ref, row_ref, qkv_ref, out_ref, log_ref = refs[len(blocks) :]
        start = 0
        for x in xs:
            size = x.shape[0]
            projected = dot(x[...], w_ref[...]) + bias_ref[...]
            qkv_ref[start : start + size, :] = projected.astype(BF16)
            start += size
        for first in range(0, rows, step):
            part = slice(first, first + step)
            far = jnp.where(col_ref[...] == row_ref[:, part], 0.0, -1e30)
            mixed = []
            for h in range(heads):
                lanes = [slice(i * inner + h * HEAD, i * inner + (h + 1) * HEAD) for i in range(3)]
                scores = times_transposed(qkv_ref[:, lanes[1]], qkv_ref[part, lanes[0]])
                scores = scores * scale + far
                highest = jnp.max(scores, axis=0, keepdims=True)
                powers = jnp.exp(scores - highest)
                summed = jnp.sum(powers, axis=0, keepdims=True)
                mixture = contract_rows(qkv_ref[:, lanes[2]], powers.astype(BF16))
                mixed.append(mixture * (1.0 / summed))
                log_ref[h : h + 1, part] = highest + jnp.log(summed)
            out_ref[part, :] = jnp.concatenate(mixed, 0).T.astype(BF16)

    flops = 2 * rows * (D * 3 * inner + 2 * rows * inner)
    return pl.pallas_call(
        kernel,
        out_shape=[
            jax.ShapeDtypeStruct((rows, 3 * inner), BF16),
            jax.ShapeDtypeStruct((rows, inner), BF16),
            jax.ShapeDtypeStruct((heads, rows), F32),
        ],
        compiler_params=pltpu.CompilerParams(vmem_limit_bytes=56 << 20),
        cost_estimate=pl.CostEstimate(
            flops=flops, bytes_accessed=2 * (rows + 3 * inner) * D, transcendentals=heads * rows**2
        ),
        name="attend_forward",
    )(*blocks, weight, bias[None], segment[:, None], segment[None])


def attend_backward(blocks, weight, qkv, mixture, log_total, segment):
    rows = sum(block.shape[0] for block in blocks)
    inner = weight.shape[1]
    heads = inner // HEAD
    step = min(512, rows)
    scale = 1.0 / math.sqrt(HEAD)

    def kernel(*refs):
        xs = refs[: len(blocks)]
        (w_ref, qkv_ref, mix_ref, log_ref, col_ref, row_ref) = refs[len(blocks) : len(blocks) + 6]
        grad_ref, sum_ref, dout_ref = refs[len(blocks) + 6 :]
        start = 0
        for x in xs:
            size = x.shape[0]
            dout_ref[start : start + size, :] = dot(x[...], w_ref[...]).astype(BF16)
            start += size
        ones = jnp.ones((8, HEAD), F32)
        keys = [jnp.zeros((rows, HEAD), F32)] * heads
        values = [jnp.zeros((rows, HEAD), F32)] * heads
        for first in range(0, rows, step):
            part = slice(first, first + step)
            far = jnp.where(col_ref[...] == row_ref[:, part], 0.0, -1e30)
            queries = []
            for h in range(heads):
                lanes = [slice(i * inner + h * HEAD, i * inner + (h + 1) * HEAD) for i in range(3)]
                query, key = qkv_ref[part, lanes[0]], qkv_ref[:, lanes[1]]
                dout = dout_ref[part, lanes[0]]
                scores = times_transposed(key, query) * scale + far
                weights = jnp.exp(scores - log_ref[h : h + 1, part])
                product = dout.astype(F32) * mix_ref[part, lanes[0]].astype(F32)
                centre = lax.dot_general(
                    ones,
                    product,
                    (((1,), (1,)), ((), ())),
                    precision=lax.Precision.HIGHEST,
                    preferred_element_type=F32,
                )[0:1]
                grad_weights = times_transposed(qkv_ref[:, lanes[2]], dout)
                grad_scores = (weights * (grad_weights - centre)).astype(BF16)
                queries.append(contract_rows(key, grad_scores))
                keys[h] = keys[h] + dot(grad_scores, query)
                values[h] = values[h] + dot(weights.astype(BF16), dout)
            grad_ref[part, 0:inner] = (jnp.concatenate(queries, 0).T * scale).astype(BF16)
        for h in range(heads):
            grad_ref[:, inner + h * HEAD : inner + (h + 1) * HEAD] = (keys[h] * scale).astype(BF16)
            grad_ref[:, 2 * inner + h * HEAD : 2 * inner + (h + 1) * HEAD] = values[h].astype(BF16)
        sum_ref[...] = jnp.sum(grad_ref[...].astype(F32), axis=0, keepdims=True)

    flops = 2 * rows * (D * inner + 5 * rows * inner)
    return pl.pallas_call(
        kernel,
        out_shape=[
            jax.ShapeDtypeStruct((rows, 3 * inner), BF16),
            jax.ShapeDtypeStruct((1, 3 * inner), F32),
        ],
        scratch_shapes=[pltpu.VMEM((rows, inner), BF16)],
        compiler_params=pltpu.CompilerParams(vmem_limit_bytes=56 << 20),
        cost_estimate=pl.CostEstimate(
            flops=flops, bytes_accessed=2 * (rows + inner) * D, transcendentals=heads * rows**2
        ),
        name="attend_backward",
    )(*blocks, weight, qkv, mixture, log_total, segment[:, None], segment[None])


def feed(source, first, second, side, block, rows_all, filled, out_type, forward):
    rows = source.shape[0]
    hidden = first[0].shape[1]
    tile = min(512, hidden)
    tiles = hidden // tile
    row_tile = min(256, rows)
    inner_count = 2 if forward else 1
    given = 0 if filled is None else inner_count

    def kernel(x_ref, a_own, a_part, b_own, b_part, side_ref, *refs):
        refs = refs[given:]
        out_ref, inner_refs, refs = refs[0], refs[1 : 1 + inner_count], refs[1 + inner_count :]
        total_ref = refs[-1]
        index = pl.program_id(1)

        def run(a_ref, b_ref):
            pre = dot(x_ref[...], a_ref[...])
            if forward:
                pre = pre + side_ref[...]
                cdf = 0.5 + 0.5 * erf(pre * 0.7071067811865476)
                bell = jnp.exp(-0.5 * pre * pre) * 0.3989422804014327
                kept = (pre * cdf).astype(BF16)
                inner_refs[0][...] = kept
                inner_refs[1][...] = (cdf + pre * bell).astype(BF16)
            else:
                kept = (pre * side_ref[...].astype(F32)).astype(BF16)
                inner_refs[0][...] = kept
                refs[0][...] = jnp.sum(kept.astype(F32), axis=0, keepdims=True)[None]
            term = times_transposed(kept, b_ref[...])

            @pl.when(index == 0)
            def _():
                total_ref[...] = term

            @pl.when(index > 0)
            def _():
                total_ref[...] += term

        @pl.when(index < tiles)
        def _():
            run(a_own, b_own)

        @pl.when(index >= tiles)
        def _():
            run(a_part, b_part)

        @pl.when(index == 2 * tiles - 1)
        def _():
            out_ref[...] = total_ref[...].astype(out_type)

    shift = block * (rows // row_tile)
    own = pl.BlockSpec((D, tile), lambda r, i: (0, jnp.minimum(i, tiles - 1)))
    part = pl.BlockSpec((D, tile), lambda r, i: (0, jnp.maximum(i - tiles, 0)))
    over = pl.BlockSpec((row_tile, tile), lambda r, i: (r + shift, i))
    source_spec = pl.BlockSpec((row_tile, D), lambda r, i: (r, 0))
    side_spec = pl.BlockSpec((1, tile), lambda r, i: (0, i)) if forward else over
    out_shape = [jax.ShapeDtypeStruct((rows, D), out_type)]
    out_shape += [jax.ShapeDtypeStruct((rows_all, 2 * hidden), BF16)] * inner_count
    out_specs = [source_spec] + [over] * inner_count
    if not forward:
        out_shape.append(jax.ShapeDtypeStruct((rows // row_tile, 1, 2 * hidden), F32))
        out_specs.append(pl.BlockSpec((1, 1, tile), lambda r, i: (r, 0, i)))
    outs = pl.pallas_call(
        kernel,
        grid=(rows // row_tile, 2 * tiles),
        out_shape=out_shape,
        in_specs=[source_spec, own, part, own, part, side_spec]
        + [pl.BlockSpec(memory_space=pl.ANY)] * given,
        out_specs=out_specs,
        scratch_shapes=[pltpu.VMEM((row_tile, D), F32)],
        input_output_aliases={6 + i: 1 + i for i in range(given)},
        compiler_params=pltpu.CompilerParams(vmem_limit_bytes=40 << 20),
        cost_estimate=pl.CostEstimate(
            flops=8 * rows * D * hidden,
            bytes_accessed=8 * D * hidden,
            transcendentals=2 * rows * hidden if forward else 0,
        ),
        name="feed_forward" if forward else "feed_backward",
    )(source, *first, *second, side, *(filled or ()))
    return outs


def join(blocks):
    return blocks[0] if len(blocks) == 1 else jnp.concatenate(blocks, 0)


def body(
    tokens,
    cotangent,
    deal_slot,
    back_slot,
    lengths,
    time_step,
    time_table,
    w_qkv,
    b_qv,
    w_out,
    out_bias,
    ln_gain,
    ln_shift,
    w_ff1,
    b_ff1,
    w_ff2,
):
    wires = Wires(lax.axis_size("dp"), lax.axis_size("tensor"))
    rows_dev = tokens.shape[0]
    group_rows = rows_dev * wires.tensor_size
    tensor_index = lax.axis_index("tensor")
    layer_total = w_qkv.shape[0]
    inner = w_qkv.shape[3] // 2
    hidden = w_ff1.shape[2] // 2
    both = (True, False)

    time_piece = lax.dynamic_index_in_dim(time_table, time_step[0], 0, keepdims=False)
    own_rows = owner_swap(jnp.take(tokens, back_slot, axis=0))
    attn_cuts = ((0, 3 * inner), (3 * inner, 4 * inner))
    feed_cuts = ((0, hidden), (hidden, 2 * hidden))
    beside = Beside(3.0)
    tasks = []
    for layer in range(layer_total):
        attn_shards, feed_shards = [], []
        for mine in both:
            qkv = wires.half(w_qkv[layer], 2, mine)
            attn_shards.append(
                jnp.concatenate(
                    [qkv[0], qkv[1], qkv[2], wires.half(w_out[layer], 0, mine).T], axis=1
                )
            )
            feed_shards.append(
                jnp.concatenate(
                    [wires.half(w_ff1[layer], 1, mine), wires.half(w_ff2[layer], 0, mine).T], axis=1
                )
            )
        extra = time_piece if layer == 0 else None
        tasks.append(
            (
                Task(wires.gather_halves(attn_shards, attn_cuts, extra), 1.0),
                Task(wires.gather_halves(feed_shards, feed_cuts), 2.0),
            )
        )
    first_attn, time_row = beside.lead(*tasks[0])
    for task in [tasks[0][1]] + [task for pair in tasks[1:] for task in pair]:
        beside.add(task)


    def upstream_steps():
        picked = yield jnp.take(cotangent, back_slot, axis=0)
        arrived = yield owner_swap(picked)
        return arrived

    upstream = beside.add(Task(upstream_steps(), 1.0))
    seq_ends = jnp.cumsum(lengths[0])
    positions = jnp.arange(group_rows, dtype=jnp.int32)
    if wires.tensor_size == 2:
        positions = (positions + tensor_index * rows_dev) % group_rows
    segment = jnp.sum((positions[:, None] >= seq_ends[None, :]).astype(jnp.int32), axis=1)

    def relative(vector):
        return jnp.concatenate([wires.half(vector, 0, mine) for mine in both])

    weights = []
    stream = own_rows.astype(F32) + time_row.astype(F32)
    saved = []
    for layer in range(layer_total):
        input_blocks = wires.rows_in(stream.astype(BF16), beside if layer else None)
        qkv_w, out_w = first_attn if layer == 0 else tasks[layer][0].finish()
        attention = []
        for half, mine in enumerate(both):
            bias_q = wires.half(b_qv[layer, 0], 0, mine)
            bias_v = wires.half(b_qv[layer, 1], 0, mine)
            bias = jnp.concatenate([bias_q, jnp.zeros_like(bias_q), bias_v])
            attention.append(attend_forward(input_blocks, qkv_w[half], bias, segment))

        def attended_term(block):
            rows = input_blocks[0].shape[0]
            return sum(
                times_transposed(part[1][block * rows : (block + 1) * rows], out_w[half])
                for half, part in enumerate(attention)
            )

        middle = stream + wires.rows_out(attended_term, beside) + out_bias[layer, 0]
        normed = layer_norm(middle, ln_gain[layer, 0], ln_shift[layer, 0])
        normed_blocks = wires.rows_in(normed.astype(BF16), beside)
        first_w, second_w = tasks[layer][1].finish()
        weights.append((qkv_w, out_w, first_w, second_w))
        bias = relative(b_ff1[layer])[None]
        feed_sums, filled = [], None
        for block, rows in enumerate(normed_blocks):
            out_type = F32 if block == 0 else BF16
            total, *filled = feed(
                rows, first_w, second_w, bias, block, group_rows, filled, out_type, True
            )
            feed_sums.append(total)
        second_sum = normed + wires.rows_out(lambda i: feed_sums[i], beside) + out_bias[layer, 1]
        saved.append((input_blocks, attention, middle, normed_blocks, filled, second_sum))
        stream = layer_norm(second_sum, ln_gain[layer, 1], ln_shift[layer, 1])

    def returned_steps(rows):
        rows = yield rows
        rows = yield owner_swap(rows)
        return rows

    returned_out = beside.add(Task(returned_steps(stream.astype(BF16)), 1.0))
    gradient = upstream.finish().astype(F32)
    gradient_tasks = [None] * layer_total
    vector_grads = [None] * layer_total
    for layer in reversed(range(layer_total)):
        qkv_w, out_w, first_w, second_w = weights[layer]
        input_blocks, attention, middle, normed_blocks, (act, slope), second_sum = saved[layer]
        _, pull_second = jax.vjp(layer_norm, second_sum, ln_gain[layer, 1], ln_shift[layer, 1])
        grad_second, gain_second, shift_second = pull_second(gradient)
        branch_blocks = wires.rows_in(grad_second.astype(BF16), beside)
        feed_sums, hidden_sums, filled = [], [], None
        for block, rows in enumerate(branch_blocks):
            out_type = F32 if block == 0 else BF16
            total, grad_pre, sums = feed(
                rows, second_w, first_w, slope, block, group_rows, filled, out_type, False
            )
            filled = (grad_pre,)
            feed_sums.append(total)
            hidden_sums.append(sums)
        hidden_sums = sum(jnp.sum(sums, axis=(0, 1)) for sums in hidden_sums)
        width = act.shape[1] // 2
        feed_task = beside.add(
            Task(
                wires.reduce_halves(
                    [
                        lambda half, n=join(normed_blocks), g=grad_pre: contract_rows(
                            n, g[:, half * width : (half + 1) * width]
                        ),
                        lambda half, n=join(branch_blocks), g=act: contract_rows(
                            n, g[:, half * width : (half + 1) * width]
                        ),
                    ]
                ),
                2.0,
            )
        )
        grad_normed = grad_second + wires.rows_out(lambda i: feed_sums[i], beside)
        _, pull_first = jax.vjp(layer_norm, middle, ln_gain[layer, 0], ln_shift[layer, 0])
        grad_middle, gain_first, shift_first = pull_first(grad_normed)
        attend_blocks = wires.rows_in(grad_middle.astype(BF16), beside)
        grad_wide, qkv_sums = [], []
        for half in (0, 1):
            qkv, mixture, log_total = attention[half]
            wide, sums = attend_backward(
                attend_blocks, out_w[half], qkv, mixture, log_total, segment
            )
            grad_wide.append(wide)
            qkv_sums.append(sums.reshape(3, inner))

        def proj_term(block):
            rows = input_blocks[0].shape[0]
            return sum(
                times_transposed(grad_wide[half][block * rows : (block + 1) * rows], qkv_w[half])
                for half in (0, 1)
            )

        attn_task = beside.add(
            Task(
                wires.reduce_halves(
                    [
                        lambda half, n=join(input_blocks), g=grad_wide: contract_rows(n, g[half]),
                        lambda half, n=join(attend_blocks), g=attention: contract_rows(n, g[half][1]),
                    ]
                ),
                1.0,
            )
        )
        gradient = grad_middle + wires.rows_out(proj_term, beside)
        gradient_tasks[layer] = (attn_task, feed_task)
        vector_grads[layer] = (
            wires.ordered(qkv_sums[0][::2], qkv_sums[1][::2], 1),
            wires.ordered(hidden_sums[:width], hidden_sums[width:], 0),
            jnp.stack([jnp.sum(grad_middle, axis=0), jnp.sum(grad_second, axis=0)]),
            jnp.stack([gain_first, gain_second]),
            jnp.stack([shift_first, shift_second]),
        )
    returned_grad = owner_swap(gradient.astype(BF16))
    grad_tokens = jnp.take(returned_grad, deal_slot, axis=0)
    encoded = jnp.take(returned_out.finish(), deal_slot, axis=0)
    matrix_grads = []
    for attn_task, feed_task in gradient_tasks:
        first_pair, second_pair = feed_task.finish()
        qkv_pair, out_pair = attn_task.finish()
        rows = qkv_pair[0].shape[0]
        matrix_grads.append((
            wires.ordered(
                *(part.reshape(rows, 3, inner).transpose(1, 0, 2) for part in qkv_pair), 2
            ),
            wires.ordered(out_pair[0].T, out_pair[1].T, 0),
            wires.ordered(first_pair[0], first_pair[1], 1),
            wires.ordered(second_pair[0].T, second_pair[1].T, 0),
        ))
    time_grad = jnp.sum(gradient, axis=0)
    local = [jnp.stack([part[i] for part in vector_grads]) for i in range(5)]
    flat = jnp.concatenate([part.reshape(-1) for part in local[:2] + [time_grad] + local[2:]])
    flat = wires.butterfly(flat, "dp", wires.dp_size)
    border = local[0].size + local[1].size
    shared = wires.butterfly(flat[border:], "tensor", wires.tensor_size)
    grad_b_qv = flat[: local[0].size].reshape(local[0].shape)
    grad_b_ff1 = flat[local[0].size : border].reshape(local[1].shape)
    time_grad = shared[:D]
    rest = shared[D:].reshape(3, layer_total, 2, D)
    return (
        encoded,
        grad_tokens,
        time_grad,
        jnp.stack([part[0] for part in matrix_grads]),
        grad_b_qv,
        jnp.stack([part[1] for part in matrix_grads]),
        rest[0],
        rest[1],
        rest[2],
        jnp.stack([part[2] for part in matrix_grads]),
        grad_b_ff1,
        jnp.stack([part[3] for part in matrix_grads]),
    )


def solution(mesh):
    return jax.shard_map(
        body,
        mesh=mesh,
        in_specs=(
            P(("dp", "tensor"), None),
            P(("dp", "tensor"), None),
            P(("dp", "tensor")),
            P(("dp", "tensor")),
            P("dp", None),
            P(),
            P(None, "dp"),
            P(None, None, "dp", "tensor"),
            P(None, None, "tensor"),
            P(None, "tensor", "dp"),
            P(),
            P(),
            P(),
            P(None, "dp", "tensor"),
            P(None, "tensor"),
            P(None, "tensor", "dp"),
        ),
        out_specs=(
            P(("dp", "tensor"), None),
            P(("dp", "tensor"), None),
            P(),
            P(None, None, "dp", "tensor"),
            P(None, None, "tensor"),
            P(None, "tensor", "dp"),
            P(),
            P(),
            P(),
            P(None, "dp", "tensor"),
            P(None, "tensor"),
            P(None, "tensor", "dp"),
        ),
        check_vma=False,
    )
```

time: 709 us -> 700 us (0.987)
  matrix products: 196 us -> 64.9 us
  waiting for transfers between devices: 140 us -> 246 us
  Pallas kernels: 0 us -> 102 us
  local copies, waits for them, and re-layouts: 156 us -> 88.9 us
  between operations: 26.1 us -> 10 us
  other arithmetic: 53.2 us -> 37.5 us
  starting transfers between devices: 128 us -> 140 us
    dot_general x48 -> x0, matrix products: 103 us -> none  [the longest x24 77.6 us: dot(): return jnp.dot(left, right, preferred_element_type=F32)]
    ppermute x56, waiting for transfers between devices: 60.7 us -> 164 us  [hop(): return lax.ppermute(array, 'dp', self.ring)]
    pallas_call x0 -> x20, Pallas kernels: none -> 102 us  [the longest x8 44.6 us: feed(): pl.pallas_call(kernel, grid=(rows // row_tile, 2 * tiles), out_shape=out_...]
    dynamic_update_slice x58 -> x0, local copies, waits for them, and re-layouts: 71.5 us -> none  [the longest x50 71.3 us: gather_halves(): lax.dynamic_update_slice(whole, piece[:chip_rows, a:b], (chip * chip_rows...]
    dot_general x32 -> x16, matrix products: 55.1 us -> 23.7 us  [times_transposed(): lax.dot_general(left, right, (((1,), (1,)), ((), ())), preferred_element_...]
    unnamed x500 -> x475, local copies, waits for them, and re-layouts: 23.4 us -> 46.7 us
    ppermute x56, starting transfers between devices: 75.3 us -> 90.6 us  [hop(): return lax.ppermute(array, 'dp', self.ring)]
    ppermute x16, waiting for transfers between devices: 63.4 us -> 50.5 us  [across(): return lax.ppermute(array, 'tensor', [(0, 1), (1, 0)])]
  transfers between devices with their start and end apart: 106 -> 106, of which waited for: 36 -> 47; matrix products, arithmetic and copies ran while one was open for 53% -> 18% of each run, Pallas kernels for 0% -> 10%
where the time goes in v2:
time: 700 us; the launch traced here: 688 us
  waiting for transfers between devices  246 us (35%)
  starting transfers between devices  140 us (20%)
  Pallas kernels  102 us (15%)
  local copies, waits for them, and re-layouts  88.9 us (13%)
  matrix products  64.9 us (9%)
  other arithmetic  37.5 us (5%)
  between operations  10 us (1%)
    ppermute x56, waiting for transfers between devices, hop(): return lax.ppermute(array, 'dp', self.ring)  164 us
    ppermute x56, starting transfers between devices, hop(): return lax.ppermute(array, 'dp', self.ring)  90.6 us
    ppermute x16, waiting for transfers between devices, across(): return lax.ppermute(array, 'tensor', [(0, 1), (1, 0)])  50.5 us
    unnamed x475, local copies, waits for them, and re-layouts  46.7 us
    pallas_call x8, Pallas kernels, feed(): pl.pallas_call(kernel, grid=(rows // row_tile, 2 * tiles), out_shape=out_...  44.6 us
    dot_general x16, matrix products, contract_rows(): lax.dot_general(left, right, (((0,), (0,)), ((), ())), preferred_element_...  41.2 us
    pallas_call x4, Pallas kernels, attend_backward(): pl.pallas_call(kernel, out_shape=[jax.ShapeDtypeStruct((rows, 3 * inner),...  29.1 us
    dot_general x16, matrix products, times_transposed(): lax.dot_general(left, right, (((1,), (1,)), ((), ())), preferred_element_...  23.7 us
  transfers between devices with their start and end apart: 106, of which 47 were waited for; matrix products, arithmetic and copies ran while one was open for 18% of the time, Pallas kernels for 10%

profile of v2, /device:TPU:0, one launch (start us, length us, event | category | flops | bytes accessed | tf_op | source)
XLA Modules:
  0.0 688.5 jit_solution(17307516193749717552)
XLA Ops:
  55.9 7.6 %collective-permute-done.10.refs_6_ = bf16[136,1024]{1,0:T(8,128)(2,1)S(1)} collective-permute-done((bf16[136,1024]{1,0:T(8,128)(2,1)S(1)}, bf16[136,1024]{1,0:T(8,128)(2,1)S(1)}, u32[]{:S(2)}, u32[]{:S(2)}) %collective-permute-start.10) | collective-permute-done | bytes 278560 | tf_op jit(solution)/shard_map/ppermute | solution.py:58
  121.3 7.8 %collective-permute-done.20.refs_1_ = bf16[128,1024]{1,0:T(8,128)(2,1)S(1)} collective-permute-done((bf16[128,1024]{1,0:T(8,128)(2,1)S(1)}, bf16[128,1024]{1,0:T(8,128)(2,1)S(1)}, u32[]{:S(2)}, u32[]{:S(2)}) %collective-permute-start.20) | collective-permute-done | bytes 262176 | tf_op jit(solution)/shard_map/ppermute | solution.py:58
  134.9 8.2 %collective-permute-done.22.refs_2_ = bf16[128,1024]{1,0:T(8,128)(2,1)S(1)} collective-permute-done((bf16[128,1024]{1,0:T(8,128)(2,1)S(1)}, bf16[128,1024]{1,0:T(8,128)(2,1)S(1)}, u32[]{:S(2)}, u32[]{:S(2)}) %collective-permute-start.22) | collective-permute-done | bytes 262176 | tf_op jit(solution)/shard_map/ppermute | solution.py:58
  147.6 8.8 %collective-permute-done.25.refs_3_ = bf16[128,1024]{1,0:T(8,128)(2,1)S(1)} collective-permute-done((bf16[128,1024]{1,0:T(8,128)(2,1)S(1)}, bf16[128,1024]{1,0:T(8,128)(2,1)S(1)}, u32[]{:S(2)}, u32[]{:S(2)}) %collective-permute-start.25) | collective-permute-done | bytes 262176 | tf_op jit(solution)/shard_map/ppermute | solution.py:58
  158.4 6.7 collective-permute-done.29
  167.4 6.6 feed_forward.4
  174.1 6.6 feed_forward.5
  182.7 10.9 %collective-permute-done.31.refs_5_ = bf16[128,1024]{1,0:T(8,128)(2,1)S(1)} collective-permute-done((bf16[128,1024]{1,0:T(8,128)(2,1)S(1)}, bf16[128,1024]{1,0:T(8,128)(2,1)S(1)}, u32[]{:S(2)}, u32[]{:S(2)}) %collective-permute-start.31) | collective-permute-done | bytes 262176 | tf_op jit(solution)/shard_map/ppermute | solution.py:58
  209.9 9.9 %collective-permute-done.36.refs_7_ = bf16[128,1024]{1,0:T(8,128)(2,1)S(1)} collective-permute-done((bf16[128,1024]{1,0:T(8,128)(2,1)S(1)}, bf16[128,1024]{1,0:T(8,128)(2,1)S(1)}, u32[]{:S(2)}, u32[]{:S(2)}) %collective-permute-start.36) | collective-permute-done | bytes 262176 | tf_op jit(solution)/shard_map/ppermute | solution.py:58
  252.1 9.7 %collective-permute-done.41 = bf16[256,1024]{1,0:T(8,128)(2,1)} collective-permute-done((bf16[256,1024]{1,0:T(8,128)(2,1)}, bf16[256,1024]{1,0:T(8,128)(2,1)}, u32[]{:S(2)}, u32[]{:S(2)}) %collective-permute-start.41) | collective-permute-done | bytes 524320 | tf_op jit(solution)/shard_map/ppermute | solution.py:64
  270.0 6.5 collective-permute-done.43.refs_6_
  279.9 11.2 %collective-permute-done.44.x_ref = bf16[256,1024]{1,0:T(8,128)(2,1)S(1)} collective-permute-done((bf16[256,1024]{1,0:T(8,128)(2,1)S(1)}, bf16[256,1024]{1,0:T(8,128)(2,1)S(1)}, u32[]{:S(2)}, u32[]{:S(2)}) %collective-permute-start.44) | collective-permute-done | bytes 524320 | tf_op jit(solution)/shard_map/ppermute | solution.py:64
  300.4 6.6 feed_forward.6
  307.0 6.6 feed_forward.7
  314.5 13.2 %collective-permute-done.48 = bf16[256,1024]{1,0:T(8,128)(2,1)S(1)} collective-permute-done((bf16[256,1024]{1,0:T(8,128)(2,1)S(1)}, bf16[256,1024]{1,0:T(8,128)(2,1)S(1)}, u32[]{:S(2)}, u32[]{:S(2)}) %collective-permute-start.48) | collective-permute-done | bytes 524320 | tf_op jit(solution)/shard_map/ppermute | solution.py:64
  420.0 7.9 %collective-permute-done.55.refs_1_ = bf16[256,1024]{1,0:T(8,128)(2,1)S(1)} collective-permute-done((bf16[256,1024]{1,0:T(8,128)(2,1)S(1)}, bf16[256,1024]{1,0:T(8,128)(2,1)S(1)}, u32[]{:S(2)}, u32[]{:S(2)}) %collective-permute-start.55) | collective-permute-done | bytes 524320 | tf_op jit(solution)/shard_map/ppermute | solution.py:64
  428.7 7.3 %attend_backward.5 = (bf16[512,768]{1,0:T(8,128)(2,1)}, f32[1,768]{1,0:T(1,128)}) custom-call(bf16[256,1024]{1,0:T(8,128)(2,1)} %copy-done.101, bf16[256,1024]{1,0:T(8,128)(2,1)} %copy-done.147, bf16[1024,256]{1,0:T(8,128)(2,1)} %collective-permute-done.39.refs_2_, bf16[512,768]{1,0:T(8,128)(2,1)} %get-tuple-element.238.refs_3_, ...), custom_call_target="tpu_custom_call" | custom-call | flops 939524096 | bytes 1572864 | tf_op jit(solution)/shard_map/attend_backward/pallas_call | solution.py:370
  444.2 7.4 %attend_backward.4 = (bf16[512,768]{1,0:T(8,128)(2,1)}, f32[1,768]{1,0:T(1,128)}) custom-call(bf16[256,1024]{1,0:T(8,128)(2,1)} %copy-done.101, bf16[256,1024]{1,0:T(8,128)(2,1)} %copy-done.147, bf16[1024,256]{1,0:T(8,128)(2,1)} %copy-done.44, bf16[512,768]{1,0:T(8,128)(2,1)} %get-tuple-element.235.refs_3_, bf16[512,256]{1,0:T(8,128)(2,1)} %get-tuple-element.197.refs_4_, ...), custom_call_target="tpu_custom_call" | custom-call | flops 939524096 | bytes 1572864 | tf_op jit(solution)/shard_map/attend_backward/pallas_call | solution.py:370
  476.0 6.8 collective-permute-done.64
  534.3 8.0 %collective-permute-done.72 = bf16[128,1024]{1,0:T(8,128)(2,1)S(1)} collective-permute-done((bf16[128,1024]{1,0:T(8,128)(2,1)S(1)}, bf16[128,1024]{1,0:T(8,128)(2,1)S(1)}, u32[]{:S(2)}, u32[]{:S(2)}) %collective-permute-start.72) | collective-permute-done | bytes 262176 | tf_op jit(solution)/shard_map/ppermute | solution.py:58
  562.2 7.0 %collective-permute-done.77 = bf16[128,1024]{1,0:T(8,128)(2,1)S(1)} collective-permute-done((bf16[128,1024]{1,0:T(8,128)(2,1)S(1)}, bf16[128,1024]{1,0:T(8,128)(2,1)S(1)}, u32[]{:S(2)}, u32[]{:S(2)}) %collective-permute-start.77) | collective-permute-done | bytes 262176 | tf_op jit(solution)/shard_map/ppermute | solution.py:58
  571.7 7.2 %attend_backward.7 = (bf16[512,768]{1,0:T(8,128)(2,1)}, f32[1,768]{1,0:T(1,128)}) custom-call(bf16[256,1024]{1,0:T(8,128)(2,1)} %copy-done.100, bf16[256,1024]{1,0:T(8,128)(2,1)} %copy-done.145, bf16[1024,256]{1,0:T(8,128)(2,1)} %copy-done.97, bf16[512,768]{1,0:T(8,128)(2,1)} %get-tuple-element.274.refs_3_, bf16[512,256]{1,0:T(8,128)(2,1)} %get-tuple-element.165.refs_4_, ...), custom_call_target="tpu_custom_call" | custom-call | flops 939524096 | bytes 1572864 | tf_op jit(solution)/shard_map/attend_backward/pallas_call | solution.py:370
  584.6 7.2 %attend_backward.6 = (bf16[512,768]{1,0:T(8,128)(2,1)}, f32[1,768]{1,0:T(1,128)}) custom-call(bf16[256,1024]{1,0:T(8,128)(2,1)} %copy-done.100, bf16[256,1024]{1,0:T(8,128)(2,1)} %copy-done.145, bf16[1024,256]{1,0:T(8,128)(2,1)} %copy-done.43, bf16[512,768]{1,0:T(8,128)(2,1)} %get-tuple-element.271.refs_3_, bf16[512,256]{1,0:T(8,128)(2,1)} %get-tuple-element.163.refs_4_, ...), custom_call_target="tpu_custom_call" | custom-call | flops 939524096 | bytes 1572864 | tf_op jit(solution)/shard_map/attend_backward/pallas_call | solution.py:370
  627.0 10.3 %collective-permute-done.87 = f32[19456]{0:T(1024)S(1)} collective-permute-done((f32[19456]{0:T(1024)S(1)}, f32[19456]{0:T(1024)S(1)}, u32[]{:S(2)}, u32[]{:S(2)}) %collective-permute-start.87) | collective-permute-done | bytes 77856 | tf_op jit(solution)/shard_map/ppermute | solution.py:138
  (934 shorter events, 482.2 us)
Async XLA Ops:
  31.8 19.3 %collective-permute-start.9 = (bf16[128,2048]{1,0:T(8,128)(2,1)S(1)}, bf16[128,2048]{1,0:T(8,128)(2,1)S(1)}, u32[]{:S(2)}, u32[]{:S(2)}) collective-permute-start(bf16[128,2048]{1,0:T(8,128)(2,1)S(1)} %collective-permute-done.6.refs_1_), channel_id=1, source_target_pairs={{0,8},{2,6},{4,0},{6,14},{8,16},{10,2},{12,4},{14,22},{16,24},{18,... | collective-permute-start | bytes 1572872 | tf_op jit(solution)/shard_map/ppermute | solution.py:58
  46.1 38.0 %all-to-all-start = ((bf16[16,16,1024]{2,1,0:T(8,128)(2,1)}), bf16[16,16,1024]{2,1,0:T(8,128)(2,1)}, u32[]{:S(2)}, u32[]{:S(2)}) async-start(bf16[16,16,1024]{2,1,0:T(8,128)(2,1)} %bitcast.273), calls=%async_computation | async-start | bytes 1048576 | tf_op jit(solution)/shard_map/all_to_all | solution.py:247
  53.7 16.3 %collective-permute-start.12 = (bf16[128,2048]{1,0:T(8,128)(2,1)S(1)}, bf16[128,2048]{1,0:T(8,128)(2,1)S(1)}, u32[]{:S(2)}, u32[]{:S(2)}) collective-permute-start(bf16[128,2048]{1,0:T(8,128)(2,1)S(1)} %collective-permute-done.9.refs_2_), channel_id=1, source_target_pairs={{0,8},{2,6},{4,0},{6,14},{8,16},{10,2},{12,4},{14,22},{16,24},{18,... | collective-permute-start | bytes 1572872 | tf_op jit(solution)/shard_map/ppermute | solution.py:58
  55.9 34.0 %collective-permute-start.17 = (bf16[64,1024]{1,0:T(8,128)(2,1)}, bf16[64,1024]{1,0:T(8,128)(2,1)}, u32[]{:S(2)}, u32[]{:S(2)}) collective-permute-start(bf16[64,1024]{1,0:T(8,128)(2,1)} %pad_maximum_fusion.14), channel_id=1, source_target_pairs={{0,2},{2,0},{4,6},{6,4},{8,10},{10,8},{12,14},{14,12},{16,18},{18,... | collective-permute-start | bytes 393224 | tf_op jit(solution)/shard_map/ppermute | solution.py:61
  80.7 25.4 %collective-permute-start.14 = (bf16[1024,768]{1,0:T(8,128)(2,1)S(1)}, bf16[1024,768]{1,0:T(8,128)(2,1)}, u32[]{:S(2)}, u32[]{:S(2)}) collective-permute-start(bf16[1024,768]{1,0:T(8,128)(2,1)S(1)} %get-tuple-element.162.refs_2_), channel_id=1, source_target_pairs={{0,2},{2,0},{4,6},{6,4},{8,10},{10,8},{12,14},{14,12},{16,18},{18,... | collective-permute-start | bytes 4718600 | tf_op jit(solution)/shard_map/ppermute | solution.py:61
  89.1 22.8 %collective-permute-start.15 = (bf16[1024,256]{1,0:T(8,128)(2,1)S(1)}, bf16[1024,256]{1,0:T(8,128)(2,1)S(1)}, u32[]{:S(2)}, u32[]{:S(2)}) collective-permute-start(bf16[1024,256]{1,0:T(8,128)(2,1)S(1)} %get-tuple-element.164.refs_2_), channel_id=1, source_target_pairs={{0,2},{2,0},{4,6},{6,4},{8,10},{10,8},{12,14},{14,12},{16,18},{18,... | collective-permute-start | bytes 1572872 | tf_op jit(solution)/shard_map/ppermute | solution.py:61
  90.9 22.8 %collective-permute-start.16 = (bf16[128,2048]{1,0:T(8,128)(2,1)S(1)}, bf16[128,2048]{1,0:T(8,128)(2,1)S(1)}, u32[]{:S(2)}, u32[]{:S(2)}) collective-permute-start(bf16[128,2048]{1,0:T(8,128)(2,1)S(1)} %collective-permute-done.12.refs_3_), channel_id=1, source_target_pairs={{0,8},{2,6},{4,0},{6,14},{8,16},{10,2},{12,4},{14,22},{16,24},{18,... | collective-permute-start | bytes 1572872 | tf_op jit(solution)/shard_map/ppermute | solution.py:58
  113.7 15.4 %collective-permute-start.18 = (bf16[256,1024]{1,0:T(8,128)(2,1)S(1)}, bf16[256,1024]{1,0:T(8,128)(2,1)S(1)}, u32[]{:S(2)}, u32[]{:S(2)}) collective-permute-start(bf16[256,1024]{1,0:T(8,128)(2,1)S(1)} %fusion.14), channel_id=1, source_target_pairs={{0,1},{1,0},{2,3},{3,2},{4,5},{5,4},{6,7},{7,6},{8,9},{9,8},{10,11... | collective-permute-start | bytes 1572872 | tf_op jit(solution)/shard_map/ppermute | solution.py:64
  165.3 15.5 %collective-permute-start.28 = (bf16[128,1024]{1,0:T(8,128)(2,1)S(1)}, bf16[128,1024]{1,0:T(8,128)(2,1)S(1)}, u32[]{:S(2)}, u32[]{:S(2)}) collective-permute-start(bf16[128,1024]{1,0:T(8,128)(2,1)S(1)} %collective-permute-done.25.refs_3_), channel_id=1, source_target_pairs={{0,8},{2,6},{4,0},{6,14},{8,16},{10,2},{12,4},{14,22},{16,24},{18,... | collective-permute-start | bytes 786440 | tf_op jit(solution)/shard_map/ppermute | solution.py:58
  221.7 17.8 %collective-permute-start.39 = (bf16[1024,256]{1,0:T(8,128)(2,1)S(1)}, bf16[1024,256]{1,0:T(8,128)(2,1)}, u32[]{:S(2)}, u32[]{:S(2)}) collective-permute-start(bf16[1024,256]{1,0:T(8,128)(2,1)S(1)} %get-tuple-element.198.refs_2_), channel_id=1, source_target_pairs={{0,2},{2,0},{4,6},{6,4},{8,10},{10,8},{12,14},{14,12},{16,18},{18,... | collective-permute-start | bytes 1572872 | tf_op jit(solution)/shard_map/ppermute | solution.py:61
  223.5 18.3 %collective-permute-start.40 = (bf16[128,2048]{1,0:T(8,128)(2,1)S(1)}, bf16[128,2048]{1,0:T(8,128)(2,1)S(1)}, u32[]{:S(2)}, u32[]{:S(2)}) collective-permute-start(bf16[128,2048]{1,0:T(8,128)(2,1)S(1)} %collective-permute-done.37.refs_3_), channel_id=1, source_target_pairs={{0,8},{2,6},{4,0},{6,14},{8,16},{10,2},{12,4},{14,22},{16,24},{18,... | collective-permute-start | bytes 1572872 | tf_op jit(solution)/shard_map/ppermute | solution.py:58
  242.6 19.8 %all-to-all-start.1 = ((bf16[16,16,1024]{2,1,0:T(8,128)(2,1)}), bf16[16,16,1024]{2,1,0:T(8,128)(2,1)}, u32[]{:S(2)}, u32[]{:S(2)}) async-start(bf16[16,16,1024]{2,1,0:T(8,128)(2,1)} %bitcast.271), calls=%async_computation.1 | async-start | bytes 1048576 | tf_op jit(solution)/shard_map/all_to_all | solution.py:247
  335.4 23.3 %all-to-all-start.2 = ((bf16[16,16,1024]{2,1,0:T(8,128)(2,1)}), bf16[16,16,1024]{2,1,0:T(8,128)(2,1)}, u32[]{:S(2)}, u32[]{:S(2)}) async-start(bf16[16,16,1024]{2,1,0:T(8,128)(2,1)} %bitcast.274), calls=%async_computation.2 | async-start | bytes 1048576 | tf_op jit(solution)/shard_map/all_to_all | solution.py:247
  340.4 17.5 %collective-permute-start.49 = (bf16[256,1024]{1,0:T(8,128)(2,1)}, bf16[256,1024]{1,0:T(8,128)(2,1)S(1)}, u32[]{:S(2)}, u32[]{:S(2)}) collective-permute-start(bf16[256,1024]{1,0:T(8,128)(2,1)} %get-tuple-element.217.x_ref), channel_id=1, source_target_pairs={{0,1},{1,0},{2,3},{3,2},{4,5},{5,4},{6,7},{7,6},{8,9},{9,8},{10,11... | collective-permute-start | bytes 1572872 | tf_op jit(solution)/shard_map/ppermute | solution.py:64
  503.4 16.6 %collective-permute-start.69 = (bf16[1024,1024]{1,0:T(8,128)(2,1)}, bf16[1024,1024]{1,0:T(8,128)(2,1)}, u32[]{:S(2)}, u32[]{:S(2)}) collective-permute-start(bf16[1024,1024]{1,0:T(8,128)(2,1)} %convolution_convert_fusion.1), channel_id=1, source_target_pairs={{0,2},{2,0},{4,6},{6,4},{8,10},{10,8},{12,14},{14,12},{16,18},{18,... | collective-permute-start | bytes 6291464 | tf_op jit(solution)/shard_map/ppermute | solution.py:61
  516.3 17.1 %collective-permute-start.101 = (bf16[64,2048]{1,0:T(8,128)(2,1)S(1)}, bf16[64,2048]{1,0:T(8,128)(2,1)S(1)}, u32[]{:S(2)}, u32[]{:S(2)}) collective-permute-start(bf16[64,2048]{1,0:T(8,128)(2,1)S(1)} %dynamic-slice_convert_fusion), channel_id=1, source_target_pairs={{0,2},{2,0},{4,6},{6,4},{8,10},{10,8},{12,14},{14,12},{16,18},{18,... | collective-permute-start | bytes 786440 | tf_op jit(solution)/shard_map/ppermute | solution.py:61
  520.0 22.3 %collective-permute-start.71 = (bf16[256,1024]{1,0:T(8,128)(2,1)S(1)}, bf16[256,1024]{1,0:T(8,128)(2,1)S(1)}, u32[]{:S(2)}, u32[]{:S(2)}) collective-permute-start(bf16[256,1024]{1,0:T(8,128)(2,1)S(1)} %get-tuple-element.260), channel_id=1, source_target_pairs={{0,1},{1,0},{2,3},{3,2},{4,5},{5,4},{6,7},{7,6},{8,9},{9,8},{10,11... | collective-permute-start | bytes 1572872 | tf_op jit(solution)/shard_map/ppermute | solution.py:64
  570.3 29.3 %collective-permute-start.79 = (bf16[128,2048]{1,0:T(8,128)(2,1)}, bf16[128,2048]{1,0:T(8,128)(2,1)}, u32[]{:S(2)}, u32[]{:S(2)}) collective-permute-start(bf16[128,2048]{1,0:T(8,128)(2,1)} %add_convert_fusion.9), channel_id=1, source_target_pairs={{0,8},{2,6},{4,0},{6,14},{8,16},{10,2},{12,4},{14,22},{16,24},{18,... | collective-permute-start | bytes 1572872 | tf_op jit(solution)/shard_map/ppermute | solution.py:58
  582.7 16.9 %collective-permute-start.80 = (bf16[1024,768]{1,0:T(8,128)(2,1)}, bf16[1024,768]{1,0:T(8,128)(2,1)}, u32[]{:S(2)}, u32[]{:S(2)}) collective-permute-start(bf16[1024,768]{1,0:T(8,128)(2,1)} %convolution_convert_fusion.4), channel_id=1, source_target_pairs={{0,2},{2,0},{4,6},{6,4},{8,10},{10,8},{12,14},{14,12},{16,18},{18,... | collective-permute-start | bytes 4718600 | tf_op jit(solution)/shard_map/ppermute | solution.py:61
  584.1 15.5 %collective-permute-start.81 = (bf16[1024,256]{1,0:T(8,128)(2,1)}, bf16[1024,256]{1,0:T(8,128)(2,1)}, u32[]{:S(2)}, u32[]{:S(2)}) collective-permute-start(bf16[1024,256]{1,0:T(8,128)(2,1)} %convolution_convert_fusion.6), channel_id=1, source_target_pairs={{0,2},{2,0},{4,6},{6,4},{8,10},{10,8},{12,14},{14,12},{16,18},{18,... | collective-permute-start | bytes 1572872 | tf_op jit(solution)/shard_map/ppermute | solution.py:61
  595.9 22.8 %collective-permute-start.97 = (bf16[64,1024]{1,0:T(8,128)(2,1)S(1)}, bf16[64,1024]{1,0:T(8,128)(2,1)S(1)}, u32[]{:S(2)}, u32[]{:S(2)}) collective-permute-start(bf16[64,1024]{1,0:T(8,128)(2,1)S(1)} %dynamic-slice_convert_fusion.2), channel_id=1, source_target_pairs={{0,2},{2,0},{4,6},{6,4},{8,10},{10,8},{12,14},{14,12},{16,18},{18,... | collective-permute-start | bytes 393224 | tf_op jit(solution)/shard_map/ppermute | solution.py:61
  599.6 16.7 %collective-permute-start.82 = (bf16[256,1024]{1,0:T(8,128)(2,1)S(1)}, bf16[256,1024]{1,0:T(8,128)(2,1)S(1)}, u32[]{:S(2)}, u32[]{:S(2)}) collective-permute-start(bf16[256,1024]{1,0:T(8,128)(2,1)S(1)} %fusion.11), channel_id=1, source_target_pairs={{0,1},{1,0},{2,3},{3,2},{4,5},{5,4},{6,7},{7,6},{8,9},{9,8},{10,11... | collective-permute-start | bytes 1572872 | tf_op jit(solution)/shard_map/ppermute | solution.py:64
  620.7 40.9 %all-to-all-start.3 = ((bf16[16,16,1024]{2,1,0:T(8,128)(2,1)}), bf16[16,16,1024]{2,1,0:T(8,128)(2,1)S(1)}, u32[]{:S(2)}, u32[]{:S(2)}) async-start(bf16[16,16,1024]{2,1,0:T(8,128)(2,1)} %bitcast.272), calls=%async_computation.3 | async-start | bytes 1048576 | tf_op jit(solution)/shard_map/all_to_all | solution.py:247
  626.8 20.8 %collective-permute-start.90 = (bf16[128,1024]{1,0:T(8,128)(2,1)S(1)}, bf16[128,1024]{1,0:T(8,128)(2,1)S(1)}, u32[]{:S(2)}, u32[]{:S(2)}) collective-permute-start(bf16[128,1024]{1,0:T(8,128)(2,1)S(1)} %add_convert_fusion.28), channel_id=1, source_target_pairs={{0,8},{2,6},{4,0},{6,14},{8,16},{10,2},{12,4},{14,22},{16,24},{18,... | collective-permute-start | bytes 786440 | tf_op jit(solution)/shard_map/ppermute | solution.py:58
  (310 other events, 3077.9 us)

commit v3 on v2

v3 whole, which is shorter than its diff:
```python
import math

import jax
import jax.numpy as jnp
import numpy as np
from jax import lax
from jax.experimental import pallas as pl
from jax.experimental.pallas import tpu as pltpu
from jax.sharding import PartitionSpec as P

D = 1024
HEADS = 16
FF = 4096
HEAD = D // HEADS
F32 = jnp.float32
BF16 = jnp.bfloat16


def layer_norm(summed, scaling, offset_vec):
    centre = jnp.mean(summed, axis=-1, keepdims=True)
    spread = summed - centre
    variance = jnp.mean(spread * spread, axis=-1, keepdims=True)
    return spread * lax.rsqrt(variance + 1e-05) * scaling + offset_vec


def dot(left, right):
    return jnp.dot(left, right, preferred_element_type=F32)


def contract_rows(left, right):
    return lax.dot_general(left, right, (((0,), (0,)), ((), ())), preferred_element_type=F32)


def times_transposed(left, right):
    return lax.dot_general(left, right, (((1,), (1,)), ((), ())), preferred_element_type=F32)


class Wires:
    def __init__(self, dp_size, tensor_size):
        self.dp_size, self.tensor_size = dp_size, tensor_size
        chips = dp_size // 2
        self.chips = chips
        order = list(range(0, chips, 2)) + list(range(chips - 1, 0, -2))
        place = {chip: spot for spot, chip in enumerate(order)}
        ring, sources = [], np.zeros((dp_size, chips), np.int32)
        for device in range(dp_size):
            chip, core = divmod(device, 2)
            way = 1 if core == 0 else -1
            ring.append((device, 2 * order[(place[chip] + way) % chips] + core))
            sources[device] = [order[(place[chip] - way * s) % chips] for s in range(chips)]
        self.ring = ring
        self.cores = [list(range(core, dp_size, 2)) for core in (0, 1)]
        self.swap = [(d, d ^ 1) for d in range(dp_size)]
        dp_index = lax.axis_index("dp")
        self.core = dp_index % 2
        self.source = lax.dynamic_index_in_dim(jnp.asarray(sources), dp_index, 0, keepdims=False)

    def hop(self, array):
        return lax.ppermute(array, "dp", self.ring)

    def partner(self, array):
        return lax.ppermute(array, "dp", self.swap)

    def across(self, array):
        return lax.ppermute(array, "tensor", [(0, 1), (1, 0)])

    def half(self, array, axis, mine):
        width = array.shape[axis] // 2
        index = self.core if mine else 1 - self.core
        return lax.dynamic_slice_in_dim(array, index * width, width, axis)

    def ordered(self, mine, other, axis):
        return jnp.where(
            self.core == 0,
            jnp.concatenate([mine, other], axis),
            jnp.concatenate([other, mine], axis),
        )

    def chip_piece(self, shard):
        mine, other = shard
        return self.ordered(mine, self.partner(other), 0)

    def gather_ring(self, piece, extra=None):
        chip_rows = piece.shape[0]
        if extra is not None:
            tail = jnp.zeros((8, piece.shape[1]), piece.dtype)
            pair = self.ordered(extra, self.partner(extra), 0)
            tail = lax.dynamic_update_slice(tail, pair[None, :], (0, 0))
            piece = jnp.concatenate([piece, tail], 0)
        piece = yield piece
        pieces = [piece]
        for _ in range(1, self.chips):
            piece = yield self.hop(piece)
            pieces.append(piece)
        whole, vector = place_pieces(self.source, pieces, chip_rows)
        halves = (whole, self.partner(whole))
        return halves if extra is None else (halves, vector[:, 0, :chip_rows].reshape(-1))

    def gather_queue(self, piece):
        whole = lax.all_gather(piece, "dp", axis=0, tiled=True, axis_index_groups=self.cores)
        return whole, self.partner(whole)

    def own_half(self, terms, came):
        return [(term + part.astype(F32)).astype(BF16) for term, part in zip(terms, came)]

    def reduce_ring(self, sums):
        chip_rows = sums[0].shape[0] // self.chips

        def portion(step):
            start = self.source[(step + 1) % self.chips] * chip_rows
            return jnp.concatenate(
                [lax.dynamic_slice_in_dim(part, start, chip_rows, 0) for part in sums], 1
            )

        total = portion(0)
        for step in range(1, self.chips):
            arrived = yield self.hop(total.astype(BF16))
            total = arrived.astype(F32) + portion(step).astype(F32)
        return self.share_rows(total)

    def reduce_queue(self, sums):
        total = lax.psum_scatter(
            jnp.concatenate(sums, 1),
            "dp",
            scatter_dimension=0,
            tiled=True,
            axis_index_groups=self.cores,
        )
        return self.share_rows(total.astype(F32))

    def share_rows(self, total):
        mine = self.half(total, 0, True)
        other = self.partner(self.half(total, 0, False).astype(BF16)).astype(F32)
        return mine, other

    def rows_in(self, local_rows):
        if self.tensor_size == 2:
            return [local_rows, self.across(local_rows)]
        return [lax.all_gather(local_rows, "tensor", axis=0, tiled=True)]

    def rows_out(self, sums):
        if self.tensor_size == 2:
            return sums[0] + self.across(sums[1]).astype(F32)
        return lax.psum_scatter(sums[0], "tensor", scatter_dimension=0, tiled=True).astype(F32)

    def butterfly(self, array, border):
        for axis, size in (("dp", self.dp_size), ("tensor", self.tensor_size)):
            if axis == "tensor":
                array, kept = array[border:], array
            bit = 1
            while bit < size:
                pairs = [(i, i ^ bit) for i in range(size)]
                array = array + (yield lax.ppermute(array, axis, pairs))
                bit *= 2
        return kept, array


def owner_swap(rows):
    return lax.all_to_all(rows, "dp", split_axis=0, concat_axis=0, tiled=True)


class Task:
    def __init__(self, steps):
        self.steps, self.done, self.result = steps, False, None
        self.advance(None, first=True)

    def advance(self, arrived, first=False):
        try:
            self.pending = next(self.steps) if first else self.steps.send(arrived)
        except StopIteration as stop:
            self.done, self.result = True, stop.value

    def finish(self):
        while not self.done:
            self.advance(self.pending)
        return self.result


def tick(value, *tasks):
    tasks = [task for task in tasks if task is not None and not task.done]
    if not tasks:
        return value
    value, arrived = lax.optimization_barrier((value, [task.pending for task in tasks]))
    for task, part in zip(tasks, arrived):
        task.advance(part)
    return value


def tie(*values):
    return lax.optimization_barrier(values)


def place_pieces(source, pieces, chip_rows):
    count, width = len(pieces), pieces[0].shape[1]
    spare = pieces[0].shape[0] - chip_rows

    def kernel(source_ref, *refs):
        ins, outs, sems = refs[:count], refs[count:-1], refs[-1]
        copies = []
        for i, piece in enumerate(ins):
            rows = pl.ds(pl.multiple_of(source_ref[i] * chip_rows, chip_rows), chip_rows)
            copies.append(
                pltpu.make_async_copy(piece.at[0:chip_rows], outs[0].at[rows], sems.at[i, 0])
            )
            if spare:
                copies.append(
                    pltpu.make_async_copy(
                        piece.at[chip_rows : chip_rows + spare, 0:128],
                        outs[1].at[source_ref[i]],
                        sems.at[i, 1],
                    )
                )
        for copy in copies:
            copy.start()
        for copy in copies:
            copy.wait()

    shapes = [jax.ShapeDtypeStruct((count * chip_rows, width), BF16)]
    if spare:
        shapes.append(jax.ShapeDtypeStruct((count, spare, 128), BF16))
    outs = pl.pallas_call(
        kernel,
        out_shape=shapes,
        in_specs=[pl.BlockSpec(memory_space=pltpu.SMEM)]
        + [pl.BlockSpec(memory_space=pl.ANY)] * count,
        out_specs=[pl.BlockSpec(memory_space=pltpu.VMEM)] * len(shapes),
        scratch_shapes=[pltpu.SemaphoreType.DMA((count, 2))],
        compiler_params=pltpu.CompilerParams(vmem_limit_bytes=16 << 20),
        cost_estimate=pl.CostEstimate(
            flops=0, bytes_accessed=4 * count * pieces[0].size, transcendentals=0
        ),
        name="place_pieces",
    )(source, *pieces)
    return outs[0], (outs[1] if spare else None)


def erf(x):
    x = jnp.clip(x, -3.7439211627767994, 3.7439211627767994)
    s = x * x
    top = jnp.full_like(s, 0.00022905065861350646)
    for c in (0.0034082910107109506, 0.050955695062380861, 0.18520832239976145, 1.128379143519084):
        top = top * s + c
    low = jnp.full_like(s, -1.1791602954361697e-7)
    for c in (
        0.000023547966471313185,
        0.0010179625278914885,
        0.014070470171167667,
        0.11098505178285362,
        0.49746925110067538,
        1.0,
    ):
        low = low * s + c
    return x * top / low


def whole_spec(shape):
    return pl.BlockSpec(shape, lambda *_: (0,) * len(shape))


def attend_forward(blocks, weight, bias, segment, earlier=None):
    rows = sum(block.shape[0] for block in blocks)
    inner = weight.shape[1] // 4
    heads = inner // HEAD
    step = min(512, rows)
    scale = 1.0 / math.sqrt(HEAD)
    extra = 0 if earlier is None else 2

    def kernel(*refs):
        xs, refs = refs[: len(blocks)], refs[len(blocks) :]
        w_ref, bias_ref, col_ref, row_ref = refs[:4]
        before, refs = refs[4 : 4 + extra], refs[4 + extra :]
        qkv_ref, out_ref, log_ref = refs[:3]
        start = 0
        for x in xs:
            size = x.shape[0]
            projected = dot(x[...], w_ref[:, : 3 * inner]) + bias_ref[...]
            qkv_ref[start : start + size, :] = projected.astype(BF16)
            start += size
        for first in range(0, rows, step):
            part = slice(first, first + step)
            far = jnp.where(col_ref[...] == row_ref[:, part], 0.0, -1e30)
            mixed = []
            for h in range(heads):
                lanes = [slice(i * inner + h * HEAD, i * inner + (h + 1) * HEAD) for i in range(3)]
                scores = times_transposed(qkv_ref[:, lanes[1]], qkv_ref[part, lanes[0]])
                scores = scores * scale + far
                highest = jnp.max(scores, axis=0, keepdims=True)
                powers = jnp.exp(scores - highest)
                summed = jnp.sum(powers, axis=0, keepdims=True)
                mixture = contract_rows(qkv_ref[:, lanes[2]], powers.astype(BF16))
                mixed.append(mixture * (1.0 / summed))
                log_ref[h : h + 1, part] = highest + jnp.log(summed)
            out_ref[part, :] = jnp.concatenate(mixed, 0).T.astype(BF16)
        start = 0
        for sum_ref in refs[3:]:
            part = slice(start, start + sum_ref.shape[0])
            start += sum_ref.shape[0]
            total = times_transposed(before[0][part, :], before[1][:, 3 * inner :])
            total += times_transposed(out_ref[part, :], w_ref[:, 3 * inner :])
            sum_ref[...] = total.astype(sum_ref.dtype)

    shapes = [
        jax.ShapeDtypeStruct((rows, 3 * inner), BF16),
        jax.ShapeDtypeStruct((rows, inner), BF16),
        jax.ShapeDtypeStruct((heads, rows), F32),
    ]
    if earlier is not None:
        shapes += sum_shapes(blocks)
    outs = pl.pallas_call(
        kernel,
        out_shape=shapes,
        compiler_params=pltpu.CompilerParams(vmem_limit_bytes=56 << 20),
        cost_estimate=pl.CostEstimate(
            flops=2 * rows * (D * 3 * inner + 2 * rows * inner) + extra * rows * D * 2 * inner,
            bytes_accessed=2 * (rows + 4 * inner) * D,
            transcendentals=heads * rows**2,
        ),
        name="attend_forward",
    )(*blocks, weight, bias[None], segment[:, None], segment[None], *(earlier or ()))
    return tuple(outs[:3]), list(outs[3:])


def sum_shapes(blocks):
    kinds = (F32, BF16) if len(blocks) == 2 else (BF16,)
    return [jax.ShapeDtypeStruct(block.shape, kind) for block, kind in zip(blocks, kinds)]


def attend_backward(blocks, weight, qkv, mixture, log_total, segment, earlier=None):
    rows = sum(block.shape[0] for block in blocks)
    inner = weight.shape[1] // 4
    extra = 0 if earlier is None else 2
    heads = inner // HEAD
    step = min(512, rows)
    scale = 1.0 / math.sqrt(HEAD)

    def kernel(*refs):
        xs = refs[: len(blocks)]
        (w_ref, qkv_ref, mix_ref, log_ref, col_ref, row_ref) = refs[len(blocks) : len(blocks) + 6]
        refs = refs[len(blocks) + 6 :]
        before, refs = refs[:extra], refs[extra:]
        grad_ref, sum_ref, dout_ref = refs[0], refs[1], refs[-1]
        start = 0
        for x in xs:
            size = x.shape[0]
            dout_ref[start : start + size, :] = dot(x[...], w_ref[:, 3 * inner :]).astype(BF16)
            start += size
        ones = jnp.ones((8, HEAD), F32)
        keys = [jnp.zeros((rows, HEAD), F32)] * heads
        values = [jnp.zeros((rows, HEAD), F32)] * heads
        for first in range(0, rows, step):
            part = slice(first, first + step)
            far = jnp.where(col_ref[...] == row_ref[:, part], 0.0, -1e30)
            queries = []
            for h in range(heads):
                lanes = [slice(i * inner + h * HEAD, i * inner + (h + 1) * HEAD) for i in range(3)]
                query, key = qkv_ref[part, lanes[0]], qkv_ref[:, lanes[1]]
                dout = dout_ref[part, lanes[0]]
                scores = times_transposed(key, query) * scale + far
                weights = jnp.exp(scores - log_ref[h : h + 1, part])
                product = dout.astype(F32) * mix_ref[part, lanes[0]].astype(F32)
                centre = lax.dot_general(
                    ones,
                    product,
                    (((1,), (1,)), ((), ())),
                    precision=lax.Precision.HIGHEST,
                    preferred_element_type=F32,
                )[0:1]
                grad_weights = times_transposed(qkv_ref[:, lanes[2]], dout)
                grad_scores = (weights * (grad_weights - centre)).astype(BF16)
                queries.append(contract_rows(key, grad_scores))
                keys[h] = keys[h] + dot(grad_scores, query)
                values[h] = values[h] + dot(weights.astype(BF16), dout)
            grad_ref[part, 0:inner] = (jnp.concatenate(queries, 0).T * scale).astype(BF16)
        for h in range(heads):
            grad_ref[:, inner + h * HEAD : inner + (h + 1) * HEAD] = (keys[h] * scale).astype(BF16)
            grad_ref[:, 2 * inner + h * HEAD : 2 * inner + (h + 1) * HEAD] = values[h].astype(BF16)
        sum_ref[...] = jnp.sum(grad_ref[...].astype(F32), axis=0, keepdims=True)
        start = 0
        for out_ref in refs[2:-1]:
            part = slice(start, start + out_ref.shape[0])
            start += out_ref.shape[0]
            total = times_transposed(before[0][part, :], before[1][:, : 3 * inner])
            total += times_transposed(grad_ref[part, :], w_ref[:, : 3 * inner])
            out_ref[...] = total.astype(out_ref.dtype)

    flops = 2 * rows * (D * inner + 5 * rows * inner) + extra * rows * D * 6 * inner
    shapes = [
        jax.ShapeDtypeStruct((rows, 3 * inner), BF16),
        jax.ShapeDtypeStruct((1, 3 * inner), F32),
    ]
    if earlier is not None:
        shapes += sum_shapes(blocks)
    outs = pl.pallas_call(
        kernel,
        out_shape=shapes,
        scratch_shapes=[pltpu.VMEM((rows, inner), BF16)],
        compiler_params=pltpu.CompilerParams(vmem_limit_bytes=56 << 20),
        cost_estimate=pl.CostEstimate(
            flops=flops, bytes_accessed=2 * (rows + inner) * D, transcendentals=heads * rows**2
        ),
        name="attend_backward",
    )(*blocks, weight, qkv, mixture, log_total, segment[:, None], segment[None], *(earlier or ()))
    return outs[0], outs[1], list(outs[2:])


def feed(source, weights, side, block, rows_all, filled, out_type, forward):
    rows = source.shape[0]
    hidden = weights[0].shape[1] // 2
    tile = min(512, hidden)
    tiles = hidden // tile
    row_tile = min(256, rows)
    inner_count = 2 if forward else 1
    given = 0 if filled is None else inner_count

    def kernel(x_ref, a_own, a_part, b_own, b_part, side_ref, *refs):
        refs = refs[given:]
        out_ref, inner_refs, refs = refs[0], refs[1 : 1 + inner_count], refs[1 + inner_count :]
        total_ref = refs[-1]
        index = pl.program_id(1)

        def run(a_ref, b_ref):
            pre = dot(x_ref[...], a_ref[...])
            if forward:
                pre = pre + side_ref[...]
                cdf = 0.5 + 0.5 * erf(pre * 0.7071067811865476)
                bell = jnp.exp(-0.5 * pre * pre) * 0.3989422804014327
                kept = (pre * cdf).astype(BF16)
                inner_refs[0][...] = kept
                inner_refs[1][...] = (cdf + pre * bell).astype(BF16)
            else:
                kept = (pre * side_ref[...].astype(F32)).astype(BF16)
                inner_refs[0][...] = kept
                refs[0][...] = jnp.sum(kept.astype(F32), axis=0, keepdims=True)[None]
            term = times_transposed(kept, b_ref[...])

            @pl.when(index == 0)
            def _():
                total_ref[...] = term

            @pl.when(index > 0)
            def _():
                total_ref[...] += term

        @pl.when(index < tiles)
        def _():
            run(a_own, b_own)

        @pl.when(index >= tiles)
        def _():
            run(a_part, b_part)

        @pl.when(index == 2 * tiles - 1)
        def _():
            out_ref[...] = total_ref[...].astype(out_type)

    shift = block * (rows // row_tile)
    shifts = (0, tiles) if forward else (tiles, 0)
    owns = [
        pl.BlockSpec((D, tile), lambda r, i, k=k: (0, jnp.minimum(i, tiles - 1) + k)) for k in shifts
    ]
    parts = [
        pl.BlockSpec((D, tile), lambda r, i, k=k: (0, jnp.maximum(i - tiles, 0) + k)) for k in shifts
    ]
    over = pl.BlockSpec((row_tile, tile), lambda r, i: (r + shift, i))
    source_spec = pl.BlockSpec((row_tile, D), lambda r, i: (r, 0))
    side_spec = pl.BlockSpec((1, tile), lambda r, i: (0, i)) if forward else over
    out_shape = [jax.ShapeDtypeStruct((rows, D), out_type)]
    out_shape += [jax.ShapeDtypeStruct((rows_all, 2 * hidden), BF16)] * inner_count
    out_specs = [source_spec] + [over] * inner_count
    if not forward:
        out_shape.append(jax.ShapeDtypeStruct((rows // row_tile, 1, 2 * hidden), F32))
        out_specs.append(pl.BlockSpec((1, 1, tile), lambda r, i: (r, 0, i)))
    outs = pl.pallas_call(
        kernel,
        grid=(rows // row_tile, 2 * tiles),
        out_shape=out_shape,
        in_specs=[source_spec, owns[0], parts[0], owns[1], parts[1], side_spec]
        + [pl.BlockSpec(memory_space=pl.ANY)] * given,
        out_specs=out_specs,
        scratch_shapes=[pltpu.VMEM((row_tile, D), F32)],
        input_output_aliases={6 + i: 1 + i for i in range(given)},
        compiler_params=pltpu.CompilerParams(vmem_limit_bytes=60 << 20),
        cost_estimate=pl.CostEstimate(
            flops=8 * rows * D * hidden,
            bytes_accessed=8 * D * hidden,
            transcendentals=2 * rows * hidden if forward else 0,
        ),
        name="feed_forward" if forward else "feed_backward",
    )(source, *weights, *weights, side, *(filled or ()))
    return outs


def join(blocks):
    return blocks[0] if len(blocks) == 1 else jnp.concatenate(blocks, 0)


def body(
    tokens,
    cotangent,
    deal_slot,
    back_slot,
    lengths,
    time_step,
    time_table,
    w_qkv,
    b_qv,
    w_out,
    out_bias,
    ln_gain,
    ln_shift,
    w_ff1,
    b_ff1,
    w_ff2,
):
    wires = Wires(lax.axis_size("dp"), lax.axis_size("tensor"))
    rows_dev = tokens.shape[0]
    group_rows = rows_dev * wires.tensor_size
    tensor_index = lax.axis_index("tensor")
    layer_total = w_qkv.shape[0]
    inner = w_qkv.shape[3] // 2
    hidden = w_ff1.shape[2] // 2
    both = (True, False)

    own_tokens = owner_swap(jnp.take(tokens, back_slot, axis=0))
    time_piece = lax.dynamic_index_in_dim(time_table, time_step[0], 0, keepdims=False)
    pieces = []
    for layer in range(layer_total):
        attn_shard, feed_shard = [], []
        for mine in both:
            qkv = wires.half(w_qkv[layer], 2, mine)
            out = wires.half(w_out[layer], 0, mine).T
            attn_shard.append(jnp.concatenate([qkv[0], qkv[1], qkv[2], out], axis=1))
            first = wires.half(w_ff1[layer], 1, mine)
            second = wires.half(w_ff2[layer], 0, mine).T
            feed_shard.append(jnp.concatenate([first, second], axis=1))
        pieces.append((wires.chip_piece(attn_shard), wires.chip_piece(feed_shard)))
    attn_ring = Task(wires.gather_ring(pieces[0][0], time_piece))
    feed_ring = Task(wires.gather_ring(pieces[0][1]))
    step = 0
    while not attn_ring.done:
        if step == 3:
            own_tokens = tick(own_tokens, attn_ring, feed_ring)
            token_blocks = wires.rows_in(own_tokens)
        else:
            tick((), attn_ring, feed_ring if step % 2 else None)
        step += 1
    attn_w, time_row = attn_ring.result
    time_row, *queued = tie(time_row, *[part for pair in pieces[1:] for part in pair])
    weights = [[attn_w, None]]
    for i in range(0, len(queued), 2):
        weights.append([wires.gather_queue(queued[i]), wires.gather_queue(queued[i + 1])])
    time_row = time_row.astype(F32)

    seq_ends = jnp.cumsum(lengths[0])
    positions = jnp.arange(group_rows, dtype=jnp.int32)
    if wires.tensor_size == 2:
        positions = (positions + tensor_index * rows_dev) % group_rows
    segment = jnp.sum((positions[:, None] >= seq_ends[None, :]).astype(jnp.int32), axis=1)

    stream = own_tokens.astype(F32) + time_row
    saved = []
    for layer in range(layer_total):
        if layer == 0:
            input_blocks = [(rows.astype(F32) + time_row).astype(BF16) for rows in token_blocks]
        else:
            input_blocks = wires.rows_in(stream.astype(BF16))
        beside = feed_ring if layer == 0 else None
        attn_w = weights[layer][0]
        biases = []
        for mine in both:
            bias_q, bias_v = [wires.half(b_qv[layer, i], 0, mine) for i in (0, 1)]
            biases.append(jnp.concatenate([bias_q, jnp.zeros_like(bias_q), bias_v]))
        (qkv, mixture, log_total), _ = attend_forward(input_blocks, attn_w[0], biases[0], segment)
        mixture = tick(mixture, beside)
        attention = [(qkv, mixture, log_total)]
        part, sums = attend_forward(
            input_blocks, attn_w[1], biases[1], segment, (mixture, attn_w[0])
        )
        attention.append(part)
        sums[-1] = tick(sums[-1], beside)
        middle = stream + wires.rows_out(sums) + out_bias[layer, 0]
        normed = layer_norm(middle, ln_gain[layer, 0], ln_shift[layer, 0])
        normed_blocks = wires.rows_in(tick(normed.astype(BF16), beside))
        if layer == 0:
            weights[0][1] = feed_ring.finish()
        feed_w = weights[layer][1]
        bias = jnp.concatenate([wires.half(b_ff1[layer], 0, mine) for mine in both])[None]
        sums, filled = [], None
        for block, rows in enumerate(normed_blocks):
            kind = F32 if block == 0 and wires.tensor_size == 2 else BF16
            total, *filled = feed(rows, feed_w, bias, block, group_rows, filled, kind, True)
            sums.append(total)
        second_sum = normed + wires.rows_out(sums) + out_bias[layer, 1]
        saved.append((input_blocks, attention, middle, normed_blocks, filled, second_sum))
        stream = layer_norm(second_sum, ln_gain[layer, 1], ln_shift[layer, 1])
        if layer == 0:
            stream, cotangent = tie(stream, cotangent)
            upstream = owner_swap(jnp.take(cotangent, back_slot, axis=0))

    encoded_own = stream.astype(BF16)
    gradient = upstream.astype(F32)
    reduced = [None] * layer_total
    vector_grads = [None] * layer_total
    for layer in reversed(range(layer_total)):
        attn_w, feed_w = weights[layer]
        input_blocks, attention, middle, normed_blocks, (act, slope), second_sum = saved[layer]
        _, pull_second = jax.vjp(layer_norm, second_sum, ln_gain[layer, 1], ln_shift[layer, 1])
        grad_second, gain_second, shift_second = pull_second(gradient)
        branch_blocks = wires.rows_in(grad_second.astype(BF16))
        sums, hidden_sums, filled = [], [], None
        for block, rows in enumerate(branch_blocks):
            kind = F32 if block == 0 and wires.tensor_size == 2 else BF16
            total, grad_pre, more = feed(rows, feed_w, slope, block, group_rows, filled, kind, False)
            filled = (grad_pre,)
            sums.append(total)
            hidden_sums.append(more)
        hidden_sums = sum(jnp.sum(part, axis=(0, 1)) for part in hidden_sums)
        if layer == layer_total - 1:
            sums[-1], encoded_own = tie(sums[-1], encoded_own)
            returned_out = owner_swap(encoded_own)
        normed_all, branch_all = join(normed_blocks), join(branch_blocks)

        def feed_terms(half):
            columns = slice(half * hidden, (half + 1) * hidden)
            return [
                contract_rows(normed_all, grad_pre[:, columns]),
                contract_rows(branch_all, act[:, columns]),
            ]

        came = [wires.partner(term.astype(BF16)) for term in feed_terms(1)]
        grad_normed = grad_second + wires.rows_out(sums)
        grad_normed, came = tie(grad_normed, came)
        _, pull_first = jax.vjp(layer_norm, middle, ln_gain[layer, 0], ln_shift[layer, 0])
        grad_middle, gain_first, shift_first = pull_first(grad_normed)
        attend_blocks = wires.rows_in(grad_middle.astype(BF16))
        feed_sums = wires.own_half(feed_terms(0), came)
        attend_blocks[-1], feed_sums = tie(attend_blocks[-1], feed_sums)
        feed_task = None
        if layer == 0:
            feed_task = Task(wires.reduce_ring(feed_sums))
        else:
            feed_total = wires.reduce_queue(feed_sums)
        input_all, attend_all = join(input_blocks), join(attend_blocks)

        def attn_terms(half, wide):
            return [
                contract_rows(input_all, wide),
                contract_rows(attend_all, attention[half][1]),
            ]

        wide, part_sums, _ = attend_backward(attend_blocks, attn_w[1], *attention[1], segment)
        sends = [term.astype(BF16) for term in attn_terms(1, wide)]
        wide = tick(wide, feed_task)
        if layer == 0:
            wide, sends = tie(wide, sends)
        came = [wires.partner(term) for term in sends]
        own_wide, own_sums, sums = attend_backward(
            attend_blocks, attn_w[0], *attention[0], segment, (wide, attn_w[1])
        )
        sums[-1] = tick(sums[-1], feed_task)
        gradient = grad_middle + wires.rows_out(sums)
        attn_sums = wires.own_half(attn_terms(0, own_wide), came)
        if layer == 0:
            attn_task = Task(wires.reduce_ring(attn_sums))
        else:
            gradient, attn_sums = tie(gradient, attn_sums)
            reduced[layer] = (wires.reduce_queue(attn_sums), feed_total)
        qkv_sums = [part.reshape(3, inner)[::2] for part in (own_sums, part_sums)]
        vector_grads[layer] = (
            wires.ordered(qkv_sums[0], qkv_sums[1], 1),
            wires.ordered(hidden_sums[:hidden], hidden_sums[hidden:], 0),
            jnp.stack([jnp.sum(grad_middle, axis=0), jnp.sum(grad_second, axis=0)]),
            jnp.stack([gain_first, gain_second]),
            jnp.stack([shift_first, shift_second]),
        )

    returned_grad = owner_swap(gradient.astype(BF16))
    time_grad = jnp.sum(gradient, axis=0)
    local = [jnp.stack([part[i] for part in vector_grads]) for i in range(5)]
    flat = jnp.concatenate([part.reshape(-1) for part in local[:2] + [time_grad] + local[2:]])
    border = local[0].size + local[1].size
    vector_task = Task(wires.butterfly(flat, border))
    while not (attn_task.done and feed_task.done and vector_task.done):
        tick((), attn_task, feed_task, vector_task)
    reduced[0] = (attn_task.result, feed_task.result)
    flat, shared = vector_task.result
    grad_tokens = jnp.take(returned_grad, deal_slot, axis=0)
    encoded = jnp.take(returned_out, deal_slot, axis=0)
    matrix_grads = []
    for attn_pair, feed_pair in reduced:
        rows = attn_pair[0].shape[0]
        matrix_grads.append(
            (
                wires.ordered(
                    *(
                        part[:, : 3 * inner].reshape(rows, 3, inner).transpose(1, 0, 2)
                        for part in attn_pair
                    ),
                    2,
                ),
                wires.ordered(*(part[:, 3 * inner :].T for part in attn_pair), 0),
                wires.ordered(*(part[:, :hidden] for part in feed_pair), 1),
                wires.ordered(*(part[:, hidden:].T for part in feed_pair), 0),
            )
        )
    grad_b_qv = flat[: local[0].size].reshape(local[0].shape)
    grad_b_ff1 = flat[local[0].size : border].reshape(local[1].shape)
    time_grad = shared[:D]
    rest = shared[D:].reshape(3, layer_total, 2, D)
    return (
        encoded,
        grad_tokens,
        time_grad,
        jnp.stack([part[0] for part in matrix_grads]),
        grad_b_qv,
        jnp.stack([part[1] for part in matrix_grads]),
        rest[0],
        rest[1],
        rest[2],
        jnp.stack([part[2] for part in matrix_grads]),
        grad_b_ff1,
        jnp.stack([part[3] for part in matrix_grads]),
    )


def solution(mesh):
    return jax.shard_map(
        body,
        mesh=mesh,
        in_specs=(
            P(("dp", "tensor"), None),
            P(("dp", "tensor"), None),
            P(("dp", "tensor")),
            P(("dp", "tensor")),
            P("dp", None),
            P(),
            P(None, "dp"),
            P(None, None, "dp", "tensor"),
            P(None, None, "tensor"),
            P(None, "tensor", "dp"),
            P(),
            P(),
            P(),
            P(None, "dp", "tensor"),
            P(None, "tensor"),
            P(None, "tensor", "dp"),
        ),
        out_specs=(
            P(("dp", "tensor"), None),
            P(("dp", "tensor"), None),
            P(),
            P(None, None, "dp", "tensor"),
            P(None, None, "tensor"),
            P(None, "tensor", "dp"),
            P(),
            P(),
            P(),
            P(None, "dp", "tensor"),
            P(None, "tensor"),
            P(None, "tensor", "dp"),
        ),
        check_vma=False,
    )
```

time: 700 us -> 679 us (0.970)
  starting transfers between devices: 140 us -> 95.8 us
  local copies, waits for them, and re-layouts: 88.9 us -> 46.6 us
  Pallas kernels: 102 us -> 138 us
  other arithmetic: 37.5 us -> 71.6 us
  matrix products: 64.9 us -> 43.1 us
  between operations: 10 us -> 22.3 us
    ppermute x56 -> x28, waiting for transfers between devices: 164 us -> 83.6 us  [hop(): return lax.ppermute(array, 'dp', self.ring)]
    ppermute x16, waiting for transfers between devices: 50.5 us -> 96 us  [across(): return lax.ppermute(array, 'tensor', [(0, 1), (1, 0)])]
    ppermute x56 -> x28, starting transfers between devices: 90.6 us -> 51.9 us  [hop(): return lax.ppermute(array, 'dp', self.ring)]
    unnamed x475 -> x227, local copies, waits for them, and re-layouts: 46.7 us -> 16.6 us
    pallas_call x8, Pallas kernels: 44.6 us -> 71.5 us  [feed(): pl.pallas_call(kernel, grid=(rows // row_tile, 2 * tiles), out_shape=out_...]
    all_gather x0 -> x2, waiting for transfers between devices: none -> 24.4 us  [gather_queue(): lax.all_gather(piece, 'dp', axis=0, tiled=True, axis_index_groups=self.co...]
    dot_general x16 -> x0, matrix products: 23.7 us -> none  [times_transposed(): lax.dot_general(left, right, (((1,), (1,)), ((), ())), preferred_element_...]
    all_to_all x4, waiting for transfers between devices: 0.01 us -> 13.8 us  [owner_swap(): return lax.all_to_all(rows, 'dp', split_axis=0, concat_axis=0, tiled=True)]
  transfers between devices with their start and end apart: 106 -> 78, of which waited for: 47 -> 42; matrix products, arithmetic and copies ran while one was open for 18% -> 18% of each run, Pallas kernels for 10% -> 17%
where the time goes in v3:
time: 679 us; the launch traced here: 668 us
  waiting for transfers between devices  251 us (37%)
  Pallas kernels  138 us (20%)
  starting transfers between devices  95.8 us (14%)
  other arithmetic  71.6 us (11%)
  local copies, waits for them, and re-layouts  46.6 us (7%)
  matrix products  43.1 us (6%)
  between operations  22.3 us (3%)
    ppermute x16, waiting for transfers between devices, across(): return lax.ppermute(array, 'tensor', [(0, 1), (1, 0)])  96 us
    ppermute x28, waiting for transfers between devices, hop(): return lax.ppermute(array, 'dp', self.ring)  83.6 us
    pallas_call x8, Pallas kernels, feed(): pl.pallas_call(kernel, grid=(rows // row_tile, 2 * tiles), out_shape=out_...  71.5 us
    ppermute x28, starting transfers between devices, hop(): return lax.ppermute(array, 'dp', self.ring)  51.9 us
    dot_general x16, matrix products, contract_rows(): lax.dot_general(left, right, (((0,), (0,)), ((), ())), preferred_element_...  43.1 us
    pallas_call x4, Pallas kernels, attend_backward(): pl.pallas_call(kernel, out_shape=shapes, scratch_shapes=[pltpu.VMEM((rows...  36.6 us
    pallas_call x4, Pallas kernels, attend_forward(): pl.pallas_call(kernel, out_shape=shapes, compiler_params=pltpu.CompilerPa...  27.2 us
    ppermute x5, waiting for transfers between devices, butterfly(): array = array + (yield lax.ppermute(array, axis, pairs))  24.4 us
  transfers between devices with their start and end apart: 78, of which 42 were waited for; matrix products, arithmetic and copies ran while one was open for 18% of the time, Pallas kernels for 17%

profile of v3, /device:TPU:0, one launch (start us, length us, event | category | flops | bytes accessed | tf_op | source)
XLA Modules:
  0.0 668.2 jit_solution(15899444030375341768)
XLA Ops:
  90.0 10.7 %collective-permute-done.15 = bf16[256,1024]{1,0:T(8,128)(2,1)S(1)} collective-permute-done((bf16[256,1024]{1,0:T(8,128)(2,1)}, bf16[256,1024]{1,0:T(8,128)(2,1)S(1)}, u32[]{:S(2)}, u32[]{:S(2)}) %collective-permute-start.15) | collective-permute-done | bytes 524320 | tf_op jit(solution)/shard_map/ppermute | solution.py:65
  110.3 7.7 %attend_forward.5 = (bf16[512,768]{1,0:T(8,128)(2,1)}, bf16[512,256]{1,0:T(8,128)(2,1)}, f32[4,512]{1,0:T(4,128)}, f32[256,1024]{1,0:T(8,128)}, bf16[256,1024]{1,0:T(8,128)(2,1)}) custom-call(bf16[256,1024]{1,0:T(8,128)(2,1)} %get-tuple-element.404.refs_0_, bf16[256,1024]{1,0:T(8,128)(2,1)} %get-tuple-element.403.refs_1_, ...), custom_call_target="tpu_custom_call" | custom-call | flops 1610612736 | bytes 3145728 | tf_op jit(solution)/shard_map/attend_forward/pallas_call | solution.py:309
  126.1 7.8 %collective-permute-start.20 = (bf16[128,2048]{1,0:T(8,128)(2,1)S(1)}, bf16[128,2048]{1,0:T(8,128)(2,1)S(1)}, u32[]{:S(2)}, u32[]{:S(2)}) collective-permute-start(bf16[128,2048]{1,0:T(8,128)(2,1)S(1)} %collective-permute-done.18.refs_5_), channel_id=1, source_target_pairs={{0,8},{2,6},{4,0},{6,14},{8,16},{10,2},{12,4},{14,22},{16,24},{18,... | collective-permute-start | bytes 1572872 | tf_op jit(solution)/shard_map/ppermute | solution.py:59
  143.9 17.0 %collective-permute-done.21.refs_7_ = bf16[128,2048]{1,0:T(8,128)(2,1)S(1)} collective-permute-done((bf16[128,2048]{1,0:T(8,128)(2,1)S(1)}, bf16[128,2048]{1,0:T(8,128)(2,1)S(1)}, u32[]{:S(2)}, u32[]{:S(2)}) %collective-permute-start.21) | collective-permute-done | bytes 524320 | tf_op jit(solution)/shard_map/ppermute | solution.py:59
  173.1 9.8 %feed_forward.4 = (f32[256,1024]{1,0:T(8,128)}, bf16[512,2048]{1,0:T(8,128)(2,1)}, bf16[512,2048]{1,0:T(8,128)(2,1)}) custom-call(bf16[256,1024]{1,0:T(8,128)(2,1)} %copy-done.15, bf16[1024,2048]{1,0:T(8,128)(2,1)} %copy-done.2, bf16[1024,2048]{1,0:T(8,128)(2,1)} %copy-done.4, bf16[1024,2048]{1,0:T(8,128)(2,1)} %copy-done.2, bf16[1024,2048]{1,0:T(8,128)(2,1)} %copy-done.4, ...), custom_call_target="tpu_custom_call" | custom-call | flops 2147483648 | bytes 8388608 | tf_op jit(solution)/shard_map/feed_forward/pallas_call | solution.py:473
  183.7 9.7 %feed_forward.5 = (bf16[256,1024]{1,0:T(8,128)(2,1)}, bf16[512,2048]{1,0:T(8,128)(2,1)}, bf16[512,2048]{1,0:T(8,128)(2,1)}) custom-call(bf16[256,1024]{1,0:T(8,128)(2,1)} %copy-done.20, bf16[1024,2048]{1,0:T(8,128)(2,1)} %copy-done.2, bf16[1024,2048]{1,0:T(8,128)(2,1)} %copy-done.4, ...), custom_call_target="tpu_custom_call", output_to_operand_aliasing={{1}: (6, {}), {2}: (7, {})} | custom-call | flops 2147483648 | bytes 8388608 | tf_op jit(solution)/shard_map/feed_forward/pallas_call | solution.py:473
  193.7 24.4 %all-gather.5.cloned.1.call-done.a_own.b_own = bf16[1024,2048]{1,0:T(8,128)(2,1)} async-done(((bf16[128,2048]{1,0:T(8,128)(2,1)}), bf16[1024,2048]{1,0:T(8,128)(2,1)}) %all-gather.5.cloned.1.call-update) | async-done | bytes 4194320 | tf_op jit(solution)/shard_map/all_gather | solution.py:100
  222.3 11.7 %collective-permute-done.25.refs_1_ = bf16[256,1024]{1,0:T(8,128)(2,1)S(1)} collective-permute-done((bf16[256,1024]{1,0:T(8,128)(2,1)S(1)}, bf16[256,1024]{1,0:T(8,128)(2,1)S(1)}, u32[]{:S(2)}, u32[]{:S(2)}) %collective-permute-start.25) | collective-permute-done | bytes 524320 | tf_op jit(solution)/shard_map/ppermute | solution.py:65
  240.7 7.7 %attend_forward.7 = (bf16[512,768]{1,0:T(8,128)(2,1)}, bf16[512,256]{1,0:T(8,128)(2,1)}, f32[4,512]{1,0:T(4,128)}, f32[256,1024]{1,0:T(8,128)}, bf16[256,1024]{1,0:T(8,128)(2,1)}) custom-call(bf16[256,1024]{1,0:T(8,128)(2,1)} %copy-done.47, bf16[256,1024]{1,0:T(8,128)(2,1)} %copy-done.99, bf16[1024,1024]{1,0:T(8,128)(2,1)} %collective-permute-done.26.refs_2_.refs_9_, ...), custom_call_target="tpu_custom_call" | custom-call | flops 1610612736 | bytes 3145728 | tf_op jit(solution)/shard_map/attend_forward/pallas_call | solution.py:309
  249.9 12.3 %collective-permute-done.27 = bf16[256,1024]{1,0:T(8,128)(2,1)S(1)} collective-permute-done((bf16[256,1024]{1,0:T(8,128)(2,1)}, bf16[256,1024]{1,0:T(8,128)(2,1)S(1)}, u32[]{:S(2)}, u32[]{:S(2)}) %collective-permute-start.27) | collective-permute-done | bytes 524320 | tf_op jit(solution)/shard_map/ppermute | solution.py:65
  266.3 9.7 %feed_forward.6 = (f32[256,1024]{1,0:T(8,128)}, bf16[512,2048]{1,0:T(8,128)(2,1)}, bf16[512,2048]{1,0:T(8,128)(2,1)}) custom-call(bf16[256,1024]{1,0:T(8,128)(2,1)} %copy-done.21, bf16[1024,2048]{1,0:T(8,128)(2,1)} %all-gather.5.cloned.1.call-done.a_own.b_own, bf16[1024,2048]{1,0:T(8,128)(2,1)} %collective-permute-done.28.a_part.b_part, ...), custom_call_target="tpu_custom_call" | custom-call | flops 2147483648 | bytes 8388608 | tf_op jit(solution)/shard_map/feed_forward/pallas_call | solution.py:473
  277.7 9.7 %feed_forward.7 = (bf16[256,1024]{1,0:T(8,128)(2,1)}, bf16[512,2048]{1,0:T(8,128)(2,1)}, bf16[512,2048]{1,0:T(8,128)(2,1)}) custom-call(bf16[256,1024]{1,0:T(8,128)(2,1)} %copy-done.50, bf16[1024,2048]{1,0:T(8,128)(2,1)} %all-gather.5.cloned.1.call-done.a_own.b_own, ...), custom_call_target="tpu_custom_call", output_to_operand_aliasing={{1}: (6, {}), {2}: (7, {})} | custom-call | flops 2147483648 | bytes 8388608 | tf_op jit(solution)/shard_map/feed_forward/pallas_call | solution.py:473
  314.8 8.1 %feed_backward.4 = (f32[256,1024]{1,0:T(8,128)}, bf16[512,2048]{1,0:T(8,128)(2,1)}, f32[1,1,2048]{2,1,0:T(1,128)}) custom-call(bf16[256,1024]{1,0:T(8,128)(2,1)} %get-tuple-element.323.x_ref, bf16[1024,2048]{1,0:T(8,128)(2,1)} %all-gather.5.cloned.1.call-done.a_own.b_own, bf16[1024,2048]{1,0:T(8,128)(2,1)} %collective-permute-done.28.a_part.b_part, ...), custom_call_target="tpu_custom_call" | custom-call | flops 2147483648 | bytes 8388608 | tf_op jit(solution)/shard_map/feed_backward/pallas_call | solution.py:473
  328.5 8.1 %feed_backward.5 = (bf16[256,1024]{1,0:T(8,128)(2,1)}, bf16[512,2048]{1,0:T(8,128)(2,1)}, f32[1,1,2048]{2,1,0:T(1,128)}) custom-call(bf16[256,1024]{1,0:T(8,128)(2,1)} %collective-permute-done.31.x_ref, bf16[1024,2048]{1,0:T(8,128)(2,1)} %all-gather.5.cloned.1.call-done.a_own.b_own, ...), custom_call_target="tpu_custom_call", output_to_operand_aliasing={{1}: (6, {})} | custom-call | flops 2147483648 | bytes 8388608 | tf_op jit(solution)/shard_map/feed_backward/pallas_call | solution.py:473
  343.4 13.4 %collective-permute-done.32 = bf16[256,1024]{1,0:T(8,128)(2,1)S(1)} collective-permute-done((bf16[256,1024]{1,0:T(8,128)(2,1)S(1)}, bf16[256,1024]{1,0:T(8,128)(2,1)S(1)}, u32[]{:S(2)}, u32[]{:S(2)}) %collective-permute-start.32) | collective-permute-done | bytes 524320 | tf_op jit(solution)/shard_map/ppermute | solution.py:65
  373.0 7.8 %attend_backward.4 = (bf16[512,768]{1,0:T(8,128)(2,1)}, f32[1,768]{1,0:T(1,128)}) custom-call(bf16[256,1024]{1,0:T(8,128)(2,1)} %copy-done.28, bf16[256,1024]{1,0:T(8,128)(2,1)} %copy-done.59, bf16[1024,1024]{1,0:T(8,128)(2,1)} %collective-permute-done.26.refs_2_.refs_9_, bf16[512,768]{1,0:T(8,128)(2,1)} %get-tuple-element.176.refs_3_, ...), custom_call_target="tpu_custom_call" | custom-call | flops 939524096 | bytes 1572864 | tf_op jit(solution)/shard_map/attend_backward/pallas_call | solution.py:393
  386.1 10.7 %attend_backward.5 = (bf16[512,768]{1,0:T(8,128)(2,1)}, f32[1,768]{1,0:T(1,128)}, f32[256,1024]{1,0:T(8,128)}, bf16[256,1024]{1,0:T(8,128)(2,1)}) custom-call(bf16[256,1024]{1,0:T(8,128)(2,1)} %copy-done.28, bf16[256,1024]{1,0:T(8,128)(2,1)} %copy-done.59, bf16[1024,1024]{1,0:T(8,128)(2,1)} %all-gather.3.cloned.1.call-done.refs_2_.refs_7_, ...), custom_call_target="tpu_custom_call" | custom-call | flops 2550136832 | bytes 1572864 | tf_op jit(solution)/shard_map/attend_backward/pallas_call | solution.py:393
  428.4 8.4 %feed_backward.6 = (f32[256,1024]{1,0:T(8,128)}, bf16[512,2048]{1,0:T(8,128)(2,1)}, f32[1,1,2048]{2,1,0:T(1,128)}) custom-call(bf16[256,1024]{1,0:T(8,128)(2,1)} %copy-done.23, bf16[1024,2048]{1,0:T(8,128)(2,1)} %copy-done.2, bf16[1024,2048]{1,0:T(8,128)(2,1)} %copy-done.4, bf16[1024,2048]{1,0:T(8,128)(2,1)} %copy-done.2, bf16[1024,2048]{1,0:T(8,128)(2,1)} %copy-done.4, ...), custom_call_target="tpu_custom_call" | custom-call | flops 2147483648 | bytes 8388608 | tf_op jit(solution)/shard_map/feed_backward/pallas_call | solution.py:473
  437.6 8.0 %feed_backward.7 = (bf16[256,1024]{1,0:T(8,128)(2,1)}, bf16[512,2048]{1,0:T(8,128)(2,1)}, f32[1,1,2048]{2,1,0:T(1,128)}) custom-call(bf16[256,1024]{1,0:T(8,128)(2,1)} %copy-done.61, bf16[1024,2048]{1,0:T(8,128)(2,1)} %copy-done.2, bf16[1024,2048]{1,0:T(8,128)(2,1)} %copy-done.4, bf16[1024,2048]{1,0:T(8,128)(2,1)} %copy-done.2, ...), custom_call_target="tpu_custom_call", output_to_operand_aliasing={{1}: (6, {})} | custom-call | flops 2147483648 | bytes 8388608 | tf_op jit(solution)/shard_map/feed_backward/pallas_call | solution.py:473
  459.9 12.8 %collective-permute-done.40 = bf16[256,1024]{1,0:T(8,128)(2,1)S(1)} collective-permute-done((bf16[256,1024]{1,0:T(8,128)(2,1)}, bf16[256,1024]{1,0:T(8,128)(2,1)S(1)}, u32[]{:S(2)}, u32[]{:S(2)}) %collective-permute-start.40) | collective-permute-done | bytes 524320 | tf_op jit(solution)/shard_map/ppermute | solution.py:65
  493.2 7.8 %attend_backward.6 = (bf16[512,768]{1,0:T(8,128)(2,1)}, f32[1,768]{1,0:T(1,128)}) custom-call(bf16[256,1024]{1,0:T(8,128)(2,1)} %copy-done.25, bf16[256,1024]{1,0:T(8,128)(2,1)} %copy-done.58, bf16[1024,1024]{1,0:T(8,128)(2,1)} %collective-permute-done.16.refs_2_.refs_9_, bf16[512,768]{1,0:T(8,128)(2,1)} %get-tuple-element.196.refs_3_, ...), custom_call_target="tpu_custom_call" | custom-call | flops 939524096 | bytes 1572864 | tf_op jit(solution)/shard_map/attend_backward/pallas_call | solution.py:393
  510.5 10.3 %attend_backward.7 = (bf16[512,768]{1,0:T(8,128)(2,1)}, f32[1,768]{1,0:T(1,128)}, f32[256,1024]{1,0:T(8,128)}, bf16[256,1024]{1,0:T(8,128)(2,1)}) custom-call(bf16[256,1024]{1,0:T(8,128)(2,1)} %copy-done.25, bf16[256,1024]{1,0:T(8,128)(2,1)} %copy-done.58, bf16[1024,1024]{1,0:T(8,128)(2,1)} %copy-done.3, bf16[512,768]{1,0:T(8,128)(2,1)} %get-tuple-element.194.refs_3_, ...), custom_call_target="tpu_custom_call" | custom-call | flops 2550136832 | bytes 1572864 | tf_op jit(solution)/shard_map/attend_backward/pallas_call | solution.py:393
  587.1 8.4 %all-to-all-done.3 = bf16[16,16,1024]{2,1,0:T(8,128)(2,1)S(1)} async-done(((bf16[16,16,1024]{2,1,0:T(8,128)(2,1)}), bf16[16,16,1024]{2,1,0:T(8,128)(2,1)S(1)}, u32[]{:S(2)}, u32[]{:S(2)}) %all-to-all-start.3) | async-done | bytes 524320 | tf_op jit(solution)/shard_map/all_to_all | solution.py:159
  596.7 10.1 %collective-permute-done.57 = f32[19456]{0:T(1024)} collective-permute-done((f32[19456]{0:T(1024)S(1)}, f32[19456]{0:T(1024)}, u32[]{:S(2)}, u32[]{:S(2)}) %collective-permute-start.57) | collective-permute-done | bytes 77856 | tf_op jit(solution)/shard_map/ppermute | solution.py:153
  (610 shorter events, 393.9 us)
Async XLA Ops:
  12.9 37.2 %all-to-all-start = ((bf16[16,16,1024]{2,1,0:T(8,128)(2,1)}), bf16[16,16,1024]{2,1,0:T(8,128)(2,1)}, u32[]{:S(2)}, u32[]{:S(2)}) async-start(bf16[16,16,1024]{2,1,0:T(8,128)(2,1)} %bitcast), calls=%async_computation | async-start | bytes 1048576 | tf_op jit(solution)/shard_map/all_to_all | solution.py:159
  20.4 173.0 %all-gather.3.cloned.1.call-start = ((), (), s32[]{:S(2)}) async-start(), calls=%async_computation.6 | async-start | bytes 2359296 | tf_op jit(solution)/shard_map/all_gather | solution.py:100
  85.8 132.4 %all-gather.5.cloned.1.call-start = ((), (), s32[]{:S(2)}) async-start(), calls=%async_computation.7 | async-start | bytes 4718592 | tf_op jit(solution)/shard_map/all_gather | solution.py:100
  85.8 24.4 %collective-permute-start.16 = (bf16[1024,1024]{1,0:T(8,128)(2,1)}, bf16[1024,1024]{1,0:T(8,128)(2,1)}, u32[]{:S(2)}, u32[]{:S(2)}) collective-permute-start(bf16[1024,1024]{1,0:T(8,128)(2,1)} %copy-done.3), channel_id=1, source_target_pairs={{0,2},{2,0},{4,6},{6,4},{8,10},{10,8},{12,14},{14,12},{16,18},{18,... | collective-permute-start | bytes 6291464 | tf_op jit(solution)/shard_map/ppermute | solution.py:62
  87.8 21.1 %collective-permute-start.17 = (bf16[128,2048]{1,0:T(8,128)(2,1)S(1)}, bf16[128,2048]{1,0:T(8,128)(2,1)S(1)}, u32[]{:S(2)}, u32[]{:S(2)}) collective-permute-start(bf16[128,2048]{1,0:T(8,128)(2,1)S(1)} %collective-permute-done.12.refs_3_), channel_id=1, source_target_pairs={{0,8},{2,6},{4,0},{6,14},{8,16},{10,2},{12,4},{14,22},{16,24},{18,... | collective-permute-start | bytes 1572872 | tf_op jit(solution)/shard_map/ppermute | solution.py:59
  163.9 19.0 %collective-permute-start.23 = (bf16[256,1024]{1,0:T(8,128)(2,1)S(1)}, bf16[256,1024]{1,0:T(8,128)(2,1)S(1)}, u32[]{:S(2)}, u32[]{:S(2)}) collective-permute-start(bf16[256,1024]{1,0:T(8,128)(2,1)S(1)} %fusion.15.x_ref), channel_id=1, source_target_pairs={{0,1},{1,0},{2,3},{3,2},{4,5},{5,4},{6,7},{7,6},{8,9},{9,8},{10,11... | collective-permute-start | bytes 1572872 | tf_op jit(solution)/shard_map/ppermute | solution.py:65
  193.4 24.7 %collective-permute-start.24 = (bf16[256,1024]{1,0:T(8,128)(2,1)}, bf16[256,1024]{1,0:T(8,128)(2,1)S(1)}, u32[]{:S(2)}, u32[]{:S(2)}) collective-permute-start(bf16[256,1024]{1,0:T(8,128)(2,1)} %get-tuple-element.150), channel_id=1, source_target_pairs={{0,1},{1,0},{2,3},{3,2},{4,5},{5,4},{6,7},{7,6},{8,9},{9,8},{10,11... | collective-permute-start | bytes 1572872 | tf_op jit(solution)/shard_map/ppermute | solution.py:65
  193.5 47.2 %collective-permute-start.26 = (bf16[1024,1024]{1,0:T(8,128)(2,1)}, bf16[1024,1024]{1,0:T(8,128)(2,1)}, u32[]{:S(2)}, u32[]{:S(2)}) collective-permute-start(bf16[1024,1024]{1,0:T(8,128)(2,1)} %all-gather.3.cloned.1.call-done.refs_2_.refs_7_), channel_id=1, source_target_pairs={{0,2},{2,0},{4,6},{6,4},{8,10},{10,8},{12,14},{14,12},{16,18},{18,... | collective-permute-start | bytes 6291464 | tf_op jit(solution)/shard_map/ppermute | solution.py:62
  218.1 48.2 %collective-permute-start.28 = (bf16[1024,2048]{1,0:T(8,128)(2,1)}, bf16[1024,2048]{1,0:T(8,128)(2,1)}, u32[]{:S(2)}, u32[]{:S(2)}) collective-permute-start(bf16[1024,2048]{1,0:T(8,128)(2,1)} %all-gather.5.cloned.1.call-done.a_own.b_own), channel_id=1, source_target_pairs={{0,2},{2,0},{4,6},{6,4},{8,10},{10,8},{12,14},{14,12},{16,18},{18,... | collective-permute-start | bytes 12582920 | tf_op jit(solution)/shard_map/ppermute | solution.py:62
  294.8 268.5 %reduce-scatter.3.cloned.1.call-start = ((), (), s32[]{:S(2)}) async-start(), calls=%async_computation.8 | async-start | bytes 2359296 | tf_op jit(solution)/shard_map/reduce_scatter | solution.py:122
  384.3 28.9 %collective-permute-start.37 = (bf16[1024,768]{1,0:T(8,128)(2,1)}, bf16[1024,768]{1,0:T(8,128)(2,1)}, u32[]{:S(2)}, u32[]{:S(2)}) collective-permute-start(bf16[1024,768]{1,0:T(8,128)(2,1)} %convolution_convert_fusion.5), channel_id=1, source_target_pairs={{0,2},{2,0},{4,6},{6,4},{8,10},{10,8},{12,14},{14,12},{16,18},{18,... | collective-permute-start | bytes 4718600 | tf_op jit(solution)/shard_map/ppermute | solution.py:62
  423.9 138.1 %all-to-all-start.2 = ((bf16[16,16,1024]{2,1,0:T(8,128)(2,1)}), bf16[16,16,1024]{2,1,0:T(8,128)(2,1)S(1)}, u32[]{:S(2)}, u32[]{:S(2)}) async-start(bf16[16,16,1024]{2,1,0:T(8,128)(2,1)} %bitcast.70), calls=%async_computation.2 | async-start | bytes 1048576 | tf_op jit(solution)/shard_map/all_to_all | solution.py:159
  428.3 189.4 %reduce-scatter.5.cloned.1.call-start = ((), (), s32[]{:S(2)}) async-start(), calls=%async_computation.9 | async-start | bytes 4718592 | tf_op jit(solution)/shard_map/reduce_scatter | solution.py:122
  450.0 24.2 %collective-permute-start.41 = (bf16[1024,1024]{1,0:T(8,128)(2,1)}, bf16[1024,1024]{1,0:T(8,128)(2,1)}, u32[]{:S(2)}, u32[]{:S(2)}) collective-permute-start(bf16[1024,1024]{1,0:T(8,128)(2,1)} %convolution_convert_fusion.1), channel_id=1, source_target_pairs={{0,2},{2,0},{4,6},{6,4},{8,10},{10,8},{12,14},{14,12},{16,18},{18,... | collective-permute-start | bytes 6291464 | tf_op jit(solution)/shard_map/ppermute | solution.py:62
  453.0 21.1 %collective-permute-start.42 = (bf16[1024,1024]{1,0:T(8,128)(2,1)}, bf16[1024,1024]{1,0:T(8,128)(2,1)}, u32[]{:S(2)}, u32[]{:S(2)}) collective-permute-start(bf16[1024,1024]{1,0:T(8,128)(2,1)} %convolution_convert_fusion), channel_id=1, source_target_pairs={{0,2},{2,0},{4,6},{6,4},{8,10},{10,8},{12,14},{14,12},{16,18},{18,... | collective-permute-start | bytes 6291464 | tf_op jit(solution)/shard_map/ppermute | solution.py:62
  508.5 19.9 %collective-permute-start.45 = (bf16[128,2048]{1,0:T(8,128)(2,1)}, bf16[128,2048]{1,0:T(8,128)(2,1)}, u32[]{:S(2)}, u32[]{:S(2)}) collective-permute-start(bf16[128,2048]{1,0:T(8,128)(2,1)} %add_convert_fusion.11), channel_id=1, source_target_pairs={{0,8},{2,6},{4,0},{6,14},{8,16},{10,2},{12,4},{14,22},{16,24},{18,... | collective-permute-start | bytes 1572872 | tf_op jit(solution)/shard_map/ppermute | solution.py:59
  510.0 25.4 %collective-permute-start.48 = (bf16[1024,256]{1,0:T(8,128)(2,1)}, bf16[1024,256]{1,0:T(8,128)(2,1)}, u32[]{:S(2)}, u32[]{:S(2)}) collective-permute-start(bf16[1024,256]{1,0:T(8,128)(2,1)} %convolution_convert_fusion.6), channel_id=1, source_target_pairs={{0,2},{2,0},{4,6},{6,4},{8,10},{10,8},{12,14},{14,12},{16,18},{18,... | collective-permute-start | bytes 1572872 | tf_op jit(solution)/shard_map/ppermute | solution.py:62
  510.0 32.0 %collective-permute-start.47 = (bf16[1024,768]{1,0:T(8,128)(2,1)}, bf16[1024,768]{1,0:T(8,128)(2,1)}, u32[]{:S(2)}, u32[]{:S(2)}) collective-permute-start(bf16[1024,768]{1,0:T(8,128)(2,1)} %convolution_convert_fusion.4), channel_id=1, source_target_pairs={{0,2},{2,0},{4,6},{6,4},{8,10},{10,8},{12,14},{14,12},{16,18},{18,... | collective-permute-start | bytes 4718600 | tf_op jit(solution)/shard_map/ppermute | solution.py:62
  531.2 21.4 %collective-permute-start.50 = (bf16[128,2048]{1,0:T(8,128)(2,1)S(1)}, bf16[128,2048]{1,0:T(8,128)(2,1)S(1)}, u32[]{:S(2)}, u32[]{:S(2)}) collective-permute-start(bf16[128,2048]{1,0:T(8,128)(2,1)S(1)} %add_convert_fusion.10), channel_id=1, source_target_pairs={{0,8},{2,6},{4,0},{6,14},{8,16},{10,2},{12,4},{14,22},{16,24},{18,... | collective-permute-start | bytes 1572872 | tf_op jit(solution)/shard_map/ppermute | solution.py:59
  565.0 20.3 %collective-permute-start.67 = (bf16[64,1024]{1,0:T(8,128)(2,1)}, bf16[64,1024]{1,0:T(8,128)(2,1)S(1)}, u32[]{:S(2)}, u32[]{:S(2)}) collective-permute-start(bf16[64,1024]{1,0:T(8,128)(2,1)} %dynamic-slice_convert_fusion.2), channel_id=1, source_target_pairs={{0,2},{2,0},{4,6},{6,4},{8,10},{10,8},{12,14},{14,12},{16,18},{18,... | collective-permute-start | bytes 393224 | tf_op jit(solution)/shard_map/ppermute | solution.py:62
  568.8 26.7 %all-to-all-start.3 = ((bf16[16,16,1024]{2,1,0:T(8,128)(2,1)}), bf16[16,16,1024]{2,1,0:T(8,128)(2,1)S(1)}, u32[]{:S(2)}, u32[]{:S(2)}) async-start(bf16[16,16,1024]{2,1,0:T(8,128)(2,1)} %bitcast.74), calls=%async_computation.3 | async-start | bytes 1048576 | tf_op jit(solution)/shard_map/all_to_all | solution.py:159
  581.9 24.9 %collective-permute-start.56 = (bf16[128,2048]{1,0:T(8,128)(2,1)}, bf16[128,2048]{1,0:T(8,128)(2,1)}, u32[]{:S(2)}, u32[]{:S(2)}) collective-permute-start(bf16[128,2048]{1,0:T(8,128)(2,1)} %add_convert_fusion.8), channel_id=1, source_target_pairs={{0,8},{2,6},{4,0},{6,14},{8,16},{10,2},{12,4},{14,22},{16,24},{18,... | collective-permute-start | bytes 1572872 | tf_op jit(solution)/shard_map/ppermute | solution.py:59
  583.7 23.1 %collective-permute-start.55 = (bf16[128,1024]{1,0:T(8,128)(2,1)}, bf16[128,1024]{1,0:T(8,128)(2,1)}, u32[]{:S(2)}, u32[]{:S(2)}) collective-permute-start(bf16[128,1024]{1,0:T(8,128)(2,1)} %add_convert_fusion.22), channel_id=1, source_target_pairs={{0,8},{2,6},{4,0},{6,14},{8,16},{10,2},{12,4},{14,22},{16,24},{18,... | collective-permute-start | bytes 786440 | tf_op jit(solution)/shard_map/ppermute | solution.py:59
  586.3 20.5 %collective-permute-start.57 = (f32[19456]{0:T(1024)S(1)}, f32[19456]{0:T(1024)}, u32[]{:S(2)}, u32[]{:S(2)}) collective-permute-start(f32[19456]{0:T(1024)S(1)} %add.513), channel_id=1, source_target_pairs={{0,8},{2,10},{4,12},{6,14},{8,0},{10,2},{12,4},{14,6},{16,24},{18,... | collective-permute-start | bytes 233480 | tf_op jit(solution)/shard_map/ppermute | solution.py:153
  (161 other events, 1486.8 us)
Sparse Core Ops, SparseCore 0:
  85.9 50.6 all-gather.2
  138.7 79.3 all-gather.4
  417.4 73.9 reduce-scatter.2
  494.9 109.3 reduce-scatter.4

commit v4 on v3

--- a/solution.py
+++ b/solution.py
@@ -42,21 +42,24 @@
         self.chips = chips
         order = list(range(0, chips, 2)) + list(range(chips - 1, 0, -2))
         place = {chip: spot for spot, chip in enumerate(order)}
-        ring, sources = [], np.zeros((dp_size, chips), np.int32)
+        self.rounds = chips // 2
+        ahead, spots = [], np.zeros((dp_size, chips), np.int32)
         for device in range(dp_size):
             chip, core = divmod(device, 2)
             way = 1 if core == 0 else -1
-            ring.append((device, 2 * order[(place[chip] + way) % chips] + core))
-            sources[device] = [order[(place[chip] - way * s) % chips] for s in range(chips)]
-        self.ring = ring
-        self.cores = [list(range(core, dp_size, 2)) for core in (0, 1)]
+            ahead.append((device, 2 * order[(place[chip] + way) % chips] + core))
+            spots[device] = [order[(place[chip] + way * s) % chips] for s in range(chips)]
+        self.ahead = ahead
+        self.back = [(there, here) for here, there in ahead]
         self.swap = [(d, d ^ 1) for d in range(dp_size)]
         dp_index = lax.axis_index("dp")
         self.core = dp_index % 2
-        self.source = lax.dynamic_index_in_dim(jnp.asarray(sources), dp_index, 0, keepdims=False)
-
-    def hop(self, array):
-        return lax.ppermute(array, "dp", self.ring)
+        self.spot = lax.dynamic_index_in_dim(jnp.asarray(spots), dp_index, 0, keepdims=False)
+
+    def round(self, forth, back):
+        if back is None:
+            return [lax.ppermute(forth, "dp", self.ahead)]
+        return [lax.ppermute(forth, "dp", self.ahead), lax.ppermute(back, "dp", self.back)]
 
     def partner(self, array):
         return lax.ppermute(array, "dp", self.swap)
@@ -88,45 +91,43 @@
             tail = lax.dynamic_update_slice(tail, pair[None, :], (0, 0))
             piece = jnp.concatenate([piece, tail], 0)
         piece = yield piece
-        pieces = [piece]
-        for _ in range(1, self.chips):
-            piece = yield self.hop(piece)
-            pieces.append(piece)
-        whole, vector = place_pieces(self.source, pieces, chip_rows)
+        forth, back = [piece], [piece]
+        for step in range(1, self.rounds + 1):
+            both_ways = step < self.chips - self.rounds
+            came = yield self.round(forth[-1], back[-1] if both_ways else None)
+            forth.append(came[0])
+            back += came[1:]
+        blocks = [0] + [self.chips - s for s in range(1, len(forth))] + list(range(1, len(back)))
+        whole, vector = place_pieces(self.spot[np.array(blocks)], forth + back[1:], chip_rows)
         halves = (whole, self.partner(whole))
         return halves if extra is None else (halves, vector[:, 0, :chip_rows].reshape(-1))
 
-    def gather_queue(self, piece):
-        whole = lax.all_gather(piece, "dp", axis=0, tiled=True, axis_index_groups=self.cores)
-        return whole, self.partner(whole)
-
     def own_half(self, terms, came):
         return [(term + part.astype(F32)).astype(BF16) for term, part in zip(terms, came)]
 
     def reduce_ring(self, sums):
         chip_rows = sums[0].shape[0] // self.chips
 
-        def portion(step):
-            start = self.source[(step + 1) % self.chips] * chip_rows
+        def portion(ahead):
+            start = self.spot[ahead % self.chips] * chip_rows
             return jnp.concatenate(
                 [lax.dynamic_slice_in_dim(part, start, chip_rows, 0) for part in sums], 1
             )
 
-        total = portion(0)
-        for step in range(1, self.chips):
-            arrived = yield self.hop(total.astype(BF16))
-            total = arrived.astype(F32) + portion(step).astype(F32)
-        return self.share_rows(total)
-
-    def reduce_queue(self, sums):
-        total = lax.psum_scatter(
-            jnp.concatenate(sums, 1),
-            "dp",
-            scatter_dimension=0,
-            tiled=True,
-            axis_index_groups=self.cores,
-        )
-        return self.share_rows(total.astype(F32))
+        forth, back = portion(self.rounds), portion(1 + self.rounds)
+        for step in range(1, self.rounds + 1):
+            both_ways = step < self.chips - self.rounds
+            came = yield self.round(forth, back if both_ways else None)
+            if step < self.rounds:
+                forth = (came[0].astype(F32) + portion(self.rounds - step).astype(F32)).astype(BF16)
+            else:
+                forth = came[0]
+            if both_ways:
+                back = came[1]
+                if step + 1 < self.chips - self.rounds:
+                    more = portion(1 + self.rounds + step)
+                    back = (back.astype(F32) + more.astype(F32)).astype(BF16)
+        return self.share_rows(portion(0).astype(F32) + forth.astype(F32) + back.astype(F32))
 
     def share_rows(self, total):
         mine = self.half(total, 0, True)
@@ -521,10 +522,10 @@
     hidden = w_ff1.shape[2] // 2
     both = (True, False)
 
-    own_tokens = owner_swap(jnp.take(tokens, back_slot, axis=0))
     time_piece = lax.dynamic_index_in_dim(time_table, time_step[0], 0, keepdims=False)
-    pieces = []
-    for layer in range(layer_total):
+
+    def rings(layer, arrays, extra):
+        w_qkv, w_out, w_ff1, w_ff2 = arrays
         attn_shard, feed_shard = [], []
         for mine in both:
             qkv = wires.half(w_qkv[layer], 2, mine)
@@ -533,22 +534,30 @@
             first = wires.half(w_ff1[layer], 1, mine)
             second = wires.half(w_ff2[layer], 0, mine).T
             feed_shard.append(jnp.concatenate([first, second], axis=1))
-        pieces.append((wires.chip_piece(attn_shard), wires.chip_piece(feed_shard)))
-    attn_ring = Task(wires.gather_ring(pieces[0][0], time_piece))
-    feed_ring = Task(wires.gather_ring(pieces[0][1]))
+        return (
+            Task(wires.gather_ring(wires.chip_piece(attn_shard), extra)),
+            Task(wires.gather_ring(wires.chip_piece(feed_shard))),
+        )
+
+    arrays = (w_qkv, w_out, w_ff1, w_ff2)
+    attn_rings, feed_rings = [None] * (layer_total + 1), [None] * (layer_total + 1)
+    attn_rings[0], feed_rings[0] = rings(0, arrays, time_piece)
     step = 0
-    while not attn_ring.done:
-        if step == 3:
-            own_tokens = tick(own_tokens, attn_ring, feed_ring)
+    while not attn_rings[0].done:
+        beside = (attn_rings[0], feed_rings[0] if step % 2 else None)
+        if step == 0:
+            tokens, back_slot = tick((tokens, back_slot), *beside)
+            own_tokens = owner_swap(jnp.take(tokens, back_slot, axis=0))
+        elif step == 2:
+            own_tokens = tick(own_tokens, *beside)
             token_blocks = wires.rows_in(own_tokens)
         else:
-            tick((), attn_ring, feed_ring if step % 2 else None)
+            tick((), *beside)
         step += 1
-    attn_w, time_row = attn_ring.result
-    time_row, *queued = tie(time_row, *[part for pair in pieces[1:] for part in pair])
-    weights = [[attn_w, None]]
-    for i in range(0, len(queued), 2):
-        weights.append([wires.gather_queue(queued[i]), wires.gather_queue(queued[i + 1])])
+    attn_w, time_row = attn_rings[0].result
+    time_row, *arrays = tie(time_row, *arrays)
+    for layer in range(1, layer_total):
+        attn_rings[layer], feed_rings[layer] = rings(layer, arrays, None)
     time_row = time_row.astype(F32)
 
     seq_ends = jnp.cumsum(lengths[0])
@@ -558,38 +567,43 @@
     segment = jnp.sum((positions[:, None] >= seq_ends[None, :]).astype(jnp.int32), axis=1)
 
     stream = own_tokens.astype(F32) + time_row
-    saved = []
+    weights, saved = [], []
     for layer in range(layer_total):
         if layer == 0:
             input_blocks = [(rows.astype(F32) + time_row).astype(BF16) for rows in token_blocks]
         else:
-            input_blocks = wires.rows_in(stream.astype(BF16))
-        beside = feed_ring if layer == 0 else None
-        attn_w = weights[layer][0]
+            now = (attn_rings[layer], feed_rings[layer])
+            input_blocks = wires.rows_in(tick(stream.astype(BF16), *now))
+            input_blocks[-1] = tick(input_blocks[-1], *now)
+            attn_w = attn_rings[layer].finish()
+        ahead = (attn_rings[layer + 1], feed_rings[layer + 1])
         biases = []
         for mine in both:
             bias_q, bias_v = [wires.half(b_qv[layer, i], 0, mine) for i in (0, 1)]
             biases.append(jnp.concatenate([bias_q, jnp.zeros_like(bias_q), bias_v]))
         (qkv, mixture, log_total), _ = attend_forward(input_blocks, attn_w[0], biases[0], segment)
-        mixture = tick(mixture, beside)
+        if layer == 0:
+            mixture = tick(mixture, feed_rings[0])
         attention = [(qkv, mixture, log_total)]
         part, sums = attend_forward(
             input_blocks, attn_w[1], biases[1], segment, (mixture, attn_w[0])
         )
         attention.append(part)
-        sums[-1] = tick(sums[-1], beside)
+        sums[-1] = tick(sums[-1], feed_rings[layer])
         middle = stream + wires.rows_out(sums) + out_bias[layer, 0]
         normed = layer_norm(middle, ln_gain[layer, 0], ln_shift[layer, 0])
-        normed_blocks = wires.rows_in(tick(normed.astype(BF16), beside))
-        if layer == 0:
-            weights[0][1] = feed_ring.finish()
-        feed_w = weights[layer][1]
+        normed_low = tick(normed.astype(BF16), feed_rings[layer], ahead[0])
+        normed_blocks = wires.rows_in(normed_low)
+        normed_blocks[-1] = tick(normed_blocks[-1], ahead[0])
+        feed_w = feed_rings[layer].finish()
+        weights.append((attn_w, feed_w))
         bias = jnp.concatenate([wires.half(b_ff1[layer], 0, mine) for mine in both])[None]
         sums, filled = [], None
         for block, rows in enumerate(normed_blocks):
             kind = F32 if block == 0 and wires.tensor_size == 2 else BF16
             total, *filled = feed(rows, feed_w, bias, block, group_rows, filled, kind, True)
             sums.append(total)
+        sums[-1] = tick(sums[-1], *ahead)
         second_sum = normed + wires.rows_out(sums) + out_bias[layer, 1]
         saved.append((input_blocks, attention, middle, normed_blocks, filled, second_sum))
         stream = layer_norm(second_sum, ln_gain[layer, 1], ln_shift[layer, 1])
@@ -599,14 +613,21 @@
 
     encoded_own = stream.astype(BF16)
     gradient = upstream.astype(F32)
-    reduced = [None] * layer_total
+    feed_tasks, attn_tasks = [None] * (layer_total + 1), [None] * (layer_total + 1)
+    attn_sums = None
     vector_grads = [None] * layer_total
     for layer in reversed(range(layer_total)):
         attn_w, feed_w = weights[layer]
         input_blocks, attention, middle, normed_blocks, (act, slope), second_sum = saved[layer]
         _, pull_second = jax.vjp(layer_norm, second_sum, ln_gain[layer, 1], ln_shift[layer, 1])
         grad_second, gain_second, shift_second = pull_second(gradient)
-        branch_blocks = wires.rows_in(grad_second.astype(BF16))
+        later = (feed_tasks[layer + 1], attn_tasks[layer + 1])
+        branch_blocks = wires.rows_in(tick(grad_second.astype(BF16), later[0]))
+        if attn_sums is not None:
+            branch_blocks[-1], attn_sums = tie(branch_blocks[-1], attn_sums)
+            branch_blocks[-1] = tick(branch_blocks[-1], later[0])
+            attn_tasks[layer + 1] = Task(wires.reduce_ring(attn_sums))
+            later = (later[0], attn_tasks[layer + 1])
         sums, hidden_sums, filled = [], [], None
         for block, rows in enumerate(branch_blocks):
             kind = F32 if block == 0 and wires.tensor_size == 2 else BF16
@@ -618,6 +639,7 @@
         if layer == layer_total - 1:
             sums[-1], encoded_own = tie(sums[-1], encoded_own)
             returned_out = owner_swap(encoded_own)
+        sums[-1] = tick(sums[-1], *later)
         normed_all, branch_all = join(normed_blocks), join(branch_blocks)
 
         def feed_terms(half):
@@ -632,14 +654,11 @@
         grad_normed, came = tie(grad_normed, came)
         _, pull_first = jax.vjp(layer_norm, middle, ln_gain[layer, 0], ln_shift[layer, 0])
         grad_middle, gain_first, shift_first = pull_first(grad_normed)
-        attend_blocks = wires.rows_in(grad_middle.astype(BF16))
+        attend_blocks = wires.rows_in(tick(grad_middle.astype(BF16), later[1]))
         feed_sums = wires.own_half(feed_terms(0), came)
         attend_blocks[-1], feed_sums = tie(attend_blocks[-1], feed_sums)
-        feed_task = None
-        if layer == 0:
-            feed_task = Task(wires.reduce_ring(feed_sums))
-        else:
-            feed_total = wires.reduce_queue(feed_sums)
+        attend_blocks[-1] = tick(attend_blocks[-1], later[1])
+        feed_tasks[layer] = Task(wires.reduce_ring(feed_sums))
         input_all, attend_all = join(input_blocks), join(attend_blocks)
 
         def attn_terms(half, wide):
@@ -650,21 +669,15 @@
 
         wide, part_sums, _ = attend_backward(attend_blocks, attn_w[1], *attention[1], segment)
         sends = [term.astype(BF16) for term in attn_terms(1, wide)]
-        wide = tick(wide, feed_task)
         if layer == 0:
             wide, sends = tie(wide, sends)
         came = [wires.partner(term) for term in sends]
         own_wide, own_sums, sums = attend_backward(
             attend_blocks, attn_w[0], *attention[0], segment, (wide, attn_w[1])
         )
-        sums[-1] = tick(sums[-1], feed_task)
+        sums[-1] = tick(sums[-1], feed_tasks[layer], later[1])
         gradient = grad_middle + wires.rows_out(sums)
         attn_sums = wires.own_half(attn_terms(0, own_wide), came)
-        if layer == 0:
-            attn_task = Task(wires.reduce_ring(attn_sums))
-        else:
-            gradient, attn_sums = tie(gradient, attn_sums)
-            reduced[layer] = (wires.reduce_queue(attn_sums), feed_total)
         qkv_sums = [part.reshape(3, inner)[::2] for part in (own_sums, part_sums)]
         vector_grads[layer] = (
             wires.ordered(qkv_sums[0], qkv_sums[1], 1),
@@ -674,15 +687,19 @@
             jnp.stack([shift_first, shift_second]),
         )
 
+    attn_tasks[0] = Task(wires.reduce_ring(attn_sums))
     returned_grad = owner_swap(gradient.astype(BF16))
     time_grad = jnp.sum(gradient, axis=0)
     local = [jnp.stack([part[i] for part in vector_grads]) for i in range(5)]
     flat = jnp.concatenate([part.reshape(-1) for part in local[:2] + [time_grad] + local[2:]])
     border = local[0].size + local[1].size
     vector_task = Task(wires.butterfly(flat, border))
-    while not (attn_task.done and feed_task.done and vector_task.done):
-        tick((), attn_task, feed_task, vector_task)
-    reduced[0] = (attn_task.result, feed_task.result)
+    final = (attn_tasks[0], feed_tasks[0], vector_task)
+    while not all(task.done for task in final):
+        tick((), *final)
+    reduced = [
+        (attn_tasks[layer].finish(), feed_tasks[layer].finish()) for layer in range(layer_total)
+    ]
     flat, shared = vector_task.result
     grad_tokens = jnp.take(returned_grad, deal_slot, axis=0)
     encoded = jnp.take(returned_out, deal_slot, axis=0)

time: 679 us -> 625 us (0.920)
  waiting for transfers between devices: 251 us -> 186 us
  starting transfers between devices: 95.8 us -> 113 us
  between operations: 22.3 us -> 9.57 us
    all_gather x2 -> x0, waiting for transfers between devices: 24.4 us -> none  [gather_queue(): lax.all_gather(piece, 'dp', axis=0, tiled=True, axis_index_groups=self.co...]
    ppermute x28 -> x56, waiting for transfers between devices: 83.6 us -> 65 us  [the longest x24 38.5 us: round(): lax.ppermute(forth, 'dp', self.ahead)]
    ppermute x28 -> x56, starting transfers between devices: 51.9 us -> 69 us  [the longest x24 27.8 us: round(): lax.ppermute(forth, 'dp', self.ahead)]
    ppermute x16, waiting for transfers between devices: 96 us -> 81.4 us  [across(): return lax.ppermute(array, 'tensor', [(0, 1), (1, 0)])]
    concatenate x6 -> x4, other arithmetic: 7.85 us -> 0.06 us  [the longest x2 0.04 us: rings(): feed_shard.append(jnp.concatenate([first, second], axis=1))]
    convert_element_type x18 -> x24, other arithmetic: 18.2 us -> 24.5 us  [the longest x12 13.7 us: reduce_ring(): (came[0].astype(F32) + portion(self.rounds - step).astype(F32)).astype(BF16)]
    unnamed x227 -> x311, local copies, waits for them, and re-layouts: 16.6 us -> 20.4 us
  transfers between devices with their start and end apart: 78 -> 102, of which waited for: 42 -> 38; matrix products, arithmetic and copies ran while one was open for 18% -> 20% of each run, Pallas kernels for 17% -> 18%
where the time goes in v4:
time: 625 us; the launch traced here: 614 us
  waiting for transfers between devices  186 us (30%)
  Pallas kernels  140 us (22%)
  starting transfers between devices  113 us (18%)
  other arithmetic  75.4 us (12%)
  local copies, waits for them, and re-layouts  51.4 us (8%)
  matrix products  38.5 us (6%)
  between operations  9.57 us (2%)
    ppermute x16, waiting for transfers between devices, across(): return lax.ppermute(array, 'tensor', [(0, 1), (1, 0)])  81.4 us
    pallas_call x8, Pallas kernels, feed(): pl.pallas_call(kernel, grid=(rows // row_tile, 2 * tiles), out_shape=out_...  71 us
    ppermute x24, waiting for transfers between devices, round(): lax.ppermute(forth, 'dp', self.ahead)  38.5 us
    dot_general x16, matrix products, contract_rows(): lax.dot_general(left, right, (((0,), (0,)), ((), ())), preferred_element_...  38.5 us
    pallas_call x4, Pallas kernels, attend_backward(): pl.pallas_call(kernel, out_shape=shapes, scratch_shapes=[pltpu.VMEM((rows...  36.1 us
    ppermute x24, starting transfers between devices, round(): lax.ppermute(forth, 'dp', self.ahead)  27.8 us
    pallas_call x4, Pallas kernels, attend_forward(): pl.pallas_call(kernel, out_shape=shapes, compiler_params=pltpu.CompilerPa...  27.3 us
    ppermute x24, starting transfers between devices, round(): lax.ppermute(back, 'dp', self.back)  25 us
  transfers between devices with their start and end apart: 102, of which 38 were waited for; matrix products, arithmetic and copies ran while one was open for 20% of the time, Pallas kernels for 18%

profile of v4, /device:TPU:0, one launch (start us, length us, event | category | flops | bytes accessed | tf_op | source)
XLA Modules:
  0.0 614.4 jit_solution(830201734442709421)
XLA Ops:
  8.0 7.1 %all-to-all-start = ((bf16[16,16,1024]{2,1,0:T(8,128)(2,1)}), bf16[16,16,1024]{2,1,0:T(8,128)(2,1)}, u32[]{:S(2)}, u32[]{:S(2)}) async-start(bf16[16,16,1024]{2,1,0:T(8,128)(2,1)} %bitcast.13), calls=%async_computation | async-start | bytes 1048576 | tf_op jit(solution)/shard_map/all_to_all | solution.py:160
  17.7 12.8 %collective-permute-done.2.refs_1_ = bf16[136,1024]{1,0:T(8,128)(2,1)S(1)} collective-permute-done((bf16[136,1024]{1,0:T(8,128)(2,1)S(1)}, bf16[136,1024]{1,0:T(8,128)(2,1)S(1)}, u32[]{:S(2)}, u32[]{:S(2)}) %collective-permute-start.2) | collective-permute-done | bytes 278560 | tf_op jit(solution)/shard_map/ppermute | solution.py:62
  77.3 8.8 %collective-permute-done.12 = bf16[256,1024]{1,0:T(8,128)(2,1)} collective-permute-done((bf16[256,1024]{1,0:T(8,128)(2,1)}, bf16[256,1024]{1,0:T(8,128)(2,1)}, u32[]{:S(2)}, u32[]{:S(2)}) %collective-permute-start.12) | collective-permute-done | bytes 524320 | tf_op jit(solution)/shard_map/ppermute | solution.py:68
  98.5 7.7 %attend_forward.5 = (bf16[512,768]{1,0:T(8,128)(2,1)}, bf16[512,256]{1,0:T(8,128)(2,1)}, f32[4,512]{1,0:T(4,128)}, f32[256,1024]{1,0:T(8,128)}, bf16[256,1024]{1,0:T(8,128)(2,1)}) custom-call(bf16[256,1024]{1,0:T(8,128)(2,1)} %get-tuple-element.529.refs_0_, bf16[256,1024]{1,0:T(8,128)(2,1)} %get-tuple-element.528.refs_1_, ...), custom_call_target="tpu_custom_call" | custom-call | flops 1610612736 | bytes 3145728 | tf_op jit(solution)/shard_map/attend_forward/pallas_call | solution.py:310
  113.4 9.8 %collective-permute-done.18 = bf16[256,1024]{1,0:T(8,128)(2,1)S(1)} collective-permute-done((bf16[256,1024]{1,0:T(8,128)(2,1)}, bf16[256,1024]{1,0:T(8,128)(2,1)S(1)}, u32[]{:S(2)}, u32[]{:S(2)}) %collective-permute-start.18) | collective-permute-done | bytes 524320 | tf_op jit(solution)/shard_map/ppermute | solution.py:68
  147.1 9.7 %feed_forward.4 = (f32[256,1024]{1,0:T(8,128)}, bf16[512,2048]{1,0:T(8,128)(2,1)}, bf16[512,2048]{1,0:T(8,128)(2,1)}) custom-call(bf16[256,1024]{1,0:T(8,128)(2,1)} %copy-done.17, bf16[1024,2048]{1,0:T(8,128)(2,1)} %copy-done.2, bf16[1024,2048]{1,0:T(8,128)(2,1)} %copy-done.5, bf16[1024,2048]{1,0:T(8,128)(2,1)} %copy-done.2, bf16[1024,2048]{1,0:T(8,128)(2,1)} %copy-done.5, ...), custom_call_target="tpu_custom_call" | custom-call | flops 2147483648 | bytes 8388608 | tf_op jit(solution)/shard_map/feed_forward/pallas_call | solution.py:474
  156.8 9.6 %feed_forward.5 = (bf16[256,1024]{1,0:T(8,128)(2,1)}, bf16[512,2048]{1,0:T(8,128)(2,1)}, bf16[512,2048]{1,0:T(8,128)(2,1)}) custom-call(bf16[256,1024]{1,0:T(8,128)(2,1)} %copy-done.27, bf16[1024,2048]{1,0:T(8,128)(2,1)} %copy-done.2, bf16[1024,2048]{1,0:T(8,128)(2,1)} %copy-done.5, ...), custom_call_target="tpu_custom_call", output_to_operand_aliasing={{1}: (6, {}), {2}: (7, {})} | custom-call | flops 2147483648 | bytes 8388608 | tf_op jit(solution)/shard_map/feed_forward/pallas_call | solution.py:474
  172.1 7.4 %collective-permute-done.28 = bf16[256,1024]{1,0:T(8,128)(2,1)S(1)} collective-permute-done((bf16[256,1024]{1,0:T(8,128)(2,1)}, bf16[256,1024]{1,0:T(8,128)(2,1)S(1)}, u32[]{:S(2)}, u32[]{:S(2)}) %collective-permute-start.28) | collective-permute-done | bytes 524320 | tf_op jit(solution)/shard_map/ppermute | solution.py:68
  190.5 13.2 %collective-permute-done.34.refs_4_ = bf16[128,1024]{1,0:T(8,128)(2,1)S(1)} collective-permute-done((bf16[128,1024]{1,0:T(8,128)(2,1)S(1)}, bf16[128,1024]{1,0:T(8,128)(2,1)S(1)}, u32[]{:S(2)}, u32[]{:S(2)}) %collective-permute-start.34) | collective-permute-done | bytes 262176 | tf_op jit(solution)/shard_map/ppermute | solution.py:61
  214.2 7.8 %attend_forward.7 = (bf16[512,768]{1,0:T(8,128)(2,1)}, bf16[512,256]{1,0:T(8,128)(2,1)}, f32[4,512]{1,0:T(4,128)}, f32[256,1024]{1,0:T(8,128)}, bf16[256,1024]{1,0:T(8,128)(2,1)}) custom-call(bf16[256,1024]{1,0:T(8,128)(2,1)} %copy-done.29, bf16[256,1024]{1,0:T(8,128)(2,1)} %copy-done.69, bf16[1024,1024]{1,0:T(8,128)(2,1)} %collective-permute-done.37.refs_2_.refs_9_, ...), custom_call_target="tpu_custom_call" | custom-call | flops 1610612736 | bytes 3145728 | tf_op jit(solution)/shard_map/attend_forward/pallas_call | solution.py:310
  225.7 10.2 %collective-permute-done.40 = bf16[256,1024]{1,0:T(8,128)(2,1)S(1)} collective-permute-done((bf16[256,1024]{1,0:T(8,128)(2,1)}, bf16[256,1024]{1,0:T(8,128)(2,1)S(1)}, u32[]{:S(2)}, u32[]{:S(2)}) %collective-permute-start.40) | collective-permute-done | bytes 524320 | tf_op jit(solution)/shard_map/ppermute | solution.py:68
  250.1 9.8 %feed_forward.6 = (f32[256,1024]{1,0:T(8,128)}, bf16[512,2048]{1,0:T(8,128)(2,1)}, bf16[512,2048]{1,0:T(8,128)(2,1)}) custom-call(bf16[256,1024]{1,0:T(8,128)(2,1)} %copy-done.19, bf16[1024,2048]{1,0:T(8,128)(2,1)} %copy-done.3, bf16[1024,2048]{1,0:T(8,128)(2,1)} %copy-done.6, bf16[1024,2048]{1,0:T(8,128)(2,1)} %copy-done.3, bf16[1024,2048]{1,0:T(8,128)(2,1)} %copy-done.6, ...), custom_call_target="tpu_custom_call" | custom-call | flops 2147483648 | bytes 8388608 | tf_op jit(solution)/shard_map/feed_forward/pallas_call | solution.py:474
  260.7 9.6 %feed_forward.7 = (bf16[256,1024]{1,0:T(8,128)(2,1)}, bf16[512,2048]{1,0:T(8,128)(2,1)}, bf16[512,2048]{1,0:T(8,128)(2,1)}) custom-call(bf16[256,1024]{1,0:T(8,128)(2,1)} %copy-done.31, bf16[1024,2048]{1,0:T(8,128)(2,1)} %copy-done.3, bf16[1024,2048]{1,0:T(8,128)(2,1)} %copy-done.6, ...), custom_call_target="tpu_custom_call", output_to_operand_aliasing={{1}: (6, {}), {2}: (7, {})} | custom-call | flops 2147483648 | bytes 8388608 | tf_op jit(solution)/shard_map/feed_forward/pallas_call | solution.py:474
  303.9 8.1 %feed_backward.4 = (f32[256,1024]{1,0:T(8,128)}, bf16[512,2048]{1,0:T(8,128)(2,1)}, f32[1,1,2048]{2,1,0:T(1,128)}) custom-call(bf16[256,1024]{1,0:T(8,128)(2,1)} %copy-done.33, bf16[1024,2048]{1,0:T(8,128)(2,1)} %copy-done.3, bf16[1024,2048]{1,0:T(8,128)(2,1)} %copy-done.6, bf16[1024,2048]{1,0:T(8,128)(2,1)} %copy-done.3, bf16[1024,2048]{1,0:T(8,128)(2,1)} %copy-done.6, ...), custom_call_target="tpu_custom_call" | custom-call | flops 2147483648 | bytes 8388608 | tf_op jit(solution)/shard_map/feed_backward/pallas_call | solution.py:474
  312.0 8.0 %feed_backward.5 = (bf16[256,1024]{1,0:T(8,128)(2,1)}, bf16[512,2048]{1,0:T(8,128)(2,1)}, f32[1,1,2048]{2,1,0:T(1,128)}) custom-call(bf16[256,1024]{1,0:T(8,128)(2,1)} %collective-permute-done.45.x_ref, bf16[1024,2048]{1,0:T(8,128)(2,1)} %copy-done.3, bf16[1024,2048]{1,0:T(8,128)(2,1)} %copy-done.6, ...), custom_call_target="tpu_custom_call", output_to_operand_aliasing={{1}: (6, {})} | custom-call | flops 2147483648 | bytes 8388608 | tf_op jit(solution)/shard_map/feed_backward/pallas_call | solution.py:474
  336.5 8.0 %collective-permute-done.46 = bf16[256,1024]{1,0:T(8,128)(2,1)S(1)} collective-permute-done((bf16[256,1024]{1,0:T(8,128)(2,1)S(1)}, bf16[256,1024]{1,0:T(8,128)(2,1)S(1)}, u32[]{:S(2)}, u32[]{:S(2)}) %collective-permute-start.46) | collective-permute-done | bytes 524320 | tf_op jit(solution)/shard_map/ppermute | solution.py:68
  373.9 7.8 %attend_backward.4 = (bf16[512,768]{1,0:T(8,128)(2,1)}, f32[1,768]{1,0:T(1,128)}) custom-call(bf16[256,1024]{1,0:T(8,128)(2,1)} %copy-done.38, bf16[256,1024]{1,0:T(8,128)(2,1)} %copy-done.76, bf16[1024,1024]{1,0:T(8,128)(2,1)} %collective-permute-done.37.refs_2_.refs_9_, bf16[512,768]{1,0:T(8,128)(2,1)} %get-tuple-element.256.refs_3_, ...), custom_call_target="tpu_custom_call" | custom-call | flops 939524096 | bytes 1572864 | tf_op jit(solution)/shard_map/attend_backward/pallas_call | solution.py:394
  387.0 10.3 %attend_backward.5 = (bf16[512,768]{1,0:T(8,128)(2,1)}, f32[1,768]{1,0:T(1,128)}, f32[256,1024]{1,0:T(8,128)}, bf16[256,1024]{1,0:T(8,128)(2,1)}) custom-call(bf16[256,1024]{1,0:T(8,128)(2,1)} %copy-done.38, bf16[256,1024]{1,0:T(8,128)(2,1)} %copy-done.76, bf16[1024,1024]{1,0:T(8,128)(2,1)} %copy-done.4, bf16[512,768]{1,0:T(8,128)(2,1)} %get-tuple-element.254.refs_3_, ...), custom_call_target="tpu_custom_call" | custom-call | flops 2550136832 | bytes 1572864 | tf_op jit(solution)/shard_map/attend_backward/pallas_call | solution.py:394
  420.8 8.1 %feed_backward.6 = (f32[256,1024]{1,0:T(8,128)}, bf16[512,2048]{1,0:T(8,128)(2,1)}, f32[1,1,2048]{2,1,0:T(1,128)}) custom-call(bf16[256,1024]{1,0:T(8,128)(2,1)} %copy-done.21, bf16[1024,2048]{1,0:T(8,128)(2,1)} %copy-done.2, bf16[1024,2048]{1,0:T(8,128)(2,1)} %copy-done.5, bf16[1024,2048]{1,0:T(8,128)(2,1)} %copy-done.2, bf16[1024,2048]{1,0:T(8,128)(2,1)} %copy-done.5, ...), custom_call_target="tpu_custom_call" | custom-call | flops 2147483648 | bytes 8388608 | tf_op jit(solution)/shard_map/feed_backward/pallas_call | solution.py:474
  441.6 7.9 %feed_backward.7 = (bf16[256,1024]{1,0:T(8,128)(2,1)}, bf16[512,2048]{1,0:T(8,128)(2,1)}, f32[1,1,2048]{2,1,0:T(1,128)}) custom-call(bf16[256,1024]{1,0:T(8,128)(2,1)} %copy-done.43, bf16[1024,2048]{1,0:T(8,128)(2,1)} %copy-done.2, bf16[1024,2048]{1,0:T(8,128)(2,1)} %copy-done.5, bf16[1024,2048]{1,0:T(8,128)(2,1)} %copy-done.2, ...), custom_call_target="tpu_custom_call", output_to_operand_aliasing={{1}: (6, {})} | custom-call | flops 2147483648 | bytes 8388608 | tf_op jit(solution)/shard_map/feed_backward/pallas_call | solution.py:474
  462.3 6.9 %collective-permute-done.63 = bf16[256,1024]{1,0:T(8,128)(2,1)S(1)} collective-permute-done((bf16[256,1024]{1,0:T(8,128)(2,1)S(1)}, bf16[256,1024]{1,0:T(8,128)(2,1)S(1)}, u32[]{:S(2)}, u32[]{:S(2)}) %collective-permute-start.63) | collective-permute-done | bytes 524320 | tf_op jit(solution)/shard_map/ppermute | solution.py:68
  484.5 7.8 %attend_backward.6 = (bf16[512,768]{1,0:T(8,128)(2,1)}, f32[1,768]{1,0:T(1,128)}) custom-call(bf16[256,1024]{1,0:T(8,128)(2,1)} %copy-done.22, bf16[256,1024]{1,0:T(8,128)(2,1)} %copy-done.36, bf16[1024,1024]{1,0:T(8,128)(2,1)} %collective-permute-done.13.refs_2_.refs_9_, bf16[512,768]{1,0:T(8,128)(2,1)} %get-tuple-element.295.refs_3_, ...), custom_call_target="tpu_custom_call" | custom-call | flops 939524096 | bytes 1572864 | tf_op jit(solution)/shard_map/attend_backward/pallas_call | solution.py:394
  506.2 10.2 %attend_backward.7 = (bf16[512,768]{1,0:T(8,128)(2,1)}, f32[1,768]{1,0:T(1,128)}, f32[256,1024]{1,0:T(8,128)}, bf16[256,1024]{1,0:T(8,128)(2,1)}) custom-call(bf16[256,1024]{1,0:T(8,128)(2,1)} %copy-done.22, bf16[256,1024]{1,0:T(8,128)(2,1)} %copy-done.36, bf16[1024,1024]{1,0:T(8,128)(2,1)} %get-tuple-element.189.refs_2_.refs_7_, ...), custom_call_target="tpu_custom_call" | custom-call | flops 2550136832 | bytes 1572864 | tf_op jit(solution)/shard_map/attend_backward/pallas_call | solution.py:394
  565.8 7.4 %collective-permute-done.86 = f32[19456]{0:T(1024)} collective-permute-done((f32[19456]{0:T(1024)}, f32[19456]{0:T(1024)}, u32[]{:S(2)}, u32[]{:S(2)}) %collective-permute-start.86) | collective-permute-done | bytes 77856 | tf_op jit(solution)/shard_map/ppermute | solution.py:154
  (773 shorter events, 390.5 us)
Async XLA Ops:
  8.0 38.5 %all-to-all-start = ((bf16[16,16,1024]{2,1,0:T(8,128)(2,1)}), bf16[16,16,1024]{2,1,0:T(8,128)(2,1)}, u32[]{:S(2)}, u32[]{:S(2)}) async-start(bf16[16,16,1024]{2,1,0:T(8,128)(2,1)} %bitcast.13), calls=%async_computation | async-start | bytes 1048576 | tf_op jit(solution)/shard_map/all_to_all | solution.py:160
  38.9 18.7 %collective-permute-start.10 = (bf16[128,2048]{1,0:T(8,128)(2,1)S(1)}, bf16[128,2048]{1,0:T(8,128)(2,1)S(1)}, u32[]{:S(2)}, u32[]{:S(2)}) collective-permute-start(bf16[128,2048]{1,0:T(8,128)(2,1)S(1)} %maximum_select_fusion.refs_0_), channel_id=1, source_target_pairs={{8,0},{6,2},{0,4},{14,6},{16,8},{2,10},{4,12},{22,14},{24,16},{10,... | collective-permute-start | bytes 1572872 | tf_op jit(solution)/shard_map/ppermute | solution.py:62
  70.5 28.0 %collective-permute-start.13 = (bf16[1024,1024]{1,0:T(8,128)(2,1)}, bf16[1024,1024]{1,0:T(8,128)(2,1)}, u32[]{:S(2)}, u32[]{:S(2)}) collective-permute-start(bf16[1024,1024]{1,0:T(8,128)(2,1)} %get-tuple-element.189.refs_2_.refs_7_), channel_id=1, source_target_pairs={{0,2},{2,0},{4,6},{6,4},{8,10},{10,8},{12,14},{14,12},{16,18},{18,... | collective-permute-start | bytes 6291464 | tf_op jit(solution)/shard_map/ppermute | solution.py:65
  73.1 21.4 %collective-permute-start.14 = (bf16[128,2048]{1,0:T(8,128)(2,1)S(1)}, bf16[128,2048]{1,0:T(8,128)(2,1)S(1)}, u32[]{:S(2)}, u32[]{:S(2)}) collective-permute-start(bf16[128,2048]{1,0:T(8,128)(2,1)S(1)} %collective-permute-done.9.refs_1_), channel_id=1, source_target_pairs={{0,8},{2,6},{4,0},{6,14},{8,16},{10,2},{12,4},{14,22},{16,24},{18,... | collective-permute-start | bytes 1572872 | tf_op jit(solution)/shard_map/ppermute | solution.py:62
  74.8 19.7 %collective-permute-start.15 = (bf16[128,2048]{1,0:T(8,128)(2,1)S(1)}, bf16[128,2048]{1,0:T(8,128)(2,1)S(1)}, u32[]{:S(2)}, u32[]{:S(2)}) collective-permute-start(bf16[128,2048]{1,0:T(8,128)(2,1)S(1)} %collective-permute-done.10.refs_5_), channel_id=1, source_target_pairs={{8,0},{6,2},{0,4},{14,6},{16,8},{2,10},{4,12},{22,14},{24,16},{10,... | collective-permute-start | bytes 1572872 | tf_op jit(solution)/shard_map/ppermute | solution.py:62
  143.1 23.4 %collective-permute-start.25 = (bf16[128,1024]{1,0:T(8,128)(2,1)S(1)}, bf16[128,1024]{1,0:T(8,128)(2,1)S(1)}, u32[]{:S(2)}, u32[]{:S(2)}) collective-permute-start(bf16[128,1024]{1,0:T(8,128)(2,1)S(1)} %collective-permute-done.23.refs_1_), channel_id=1, source_target_pairs={{0,8},{2,6},{4,0},{6,14},{8,16},{10,2},{12,4},{14,22},{16,24},{18,... | collective-permute-start | bytes 786440 | tf_op jit(solution)/shard_map/ppermute | solution.py:62
  143.3 23.1 %collective-permute-start.26 = (bf16[128,1024]{1,0:T(8,128)(2,1)S(1)}, bf16[128,1024]{1,0:T(8,128)(2,1)S(1)}, u32[]{:S(2)}, u32[]{:S(2)}) collective-permute-start(bf16[128,1024]{1,0:T(8,128)(2,1)S(1)} %collective-permute-done.24.refs_5_), channel_id=1, source_target_pairs={{8,0},{6,2},{0,4},{14,6},{16,8},{2,10},{4,12},{22,14},{24,16},{10,... | collective-permute-start | bytes 786440 | tf_op jit(solution)/shard_map/ppermute | solution.py:62
  168.1 19.5 %collective-permute-start.31 = (bf16[128,2048]{1,0:T(8,128)(2,1)S(1)}, bf16[128,2048]{1,0:T(8,128)(2,1)S(1)}, u32[]{:S(2)}, u32[]{:S(2)}) collective-permute-start(bf16[128,2048]{1,0:T(8,128)(2,1)S(1)} %maximum_select_fusion.1.refs_0_), channel_id=1, source_target_pairs={{0,8},{2,6},{4,0},{6,14},{8,16},{10,2},{12,4},{14,22},{16,24},{18,... | collective-permute-start | bytes 1572872 | tf_op jit(solution)/shard_map/ppermute | solution.py:62
  168.3 19.3 %collective-permute-start.32 = (bf16[128,2048]{1,0:T(8,128)(2,1)S(1)}, bf16[128,2048]{1,0:T(8,128)(2,1)S(1)}, u32[]{:S(2)}, u32[]{:S(2)}) collective-permute-start(bf16[128,2048]{1,0:T(8,128)(2,1)S(1)} %maximum_select_fusion.1.refs_0_), channel_id=1, source_target_pairs={{8,0},{6,2},{0,4},{14,6},{16,8},{2,10},{4,12},{22,14},{24,16},{10,... | collective-permute-start | bytes 1572872 | tf_op jit(solution)/shard_map/ppermute | solution.py:62
  240.9 18.9 %collective-permute-start.43 = (bf16[256,1024]{1,0:T(8,128)(2,1)S(1)}, bf16[256,1024]{1,0:T(8,128)(2,1)S(1)}, u32[]{:S(2)}, u32[]{:S(2)}) collective-permute-start(bf16[256,1024]{1,0:T(8,128)(2,1)S(1)} %fusion.15.x_ref), channel_id=1, source_target_pairs={{0,1},{1,0},{2,3},{3,2},{4,5},{5,4},{6,7},{7,6},{8,9},{9,8},{10,11... | collective-permute-start | bytes 1572872 | tf_op jit(solution)/shard_map/ppermute | solution.py:68
  324.0 27.5 %collective-permute-start.47 = (bf16[1024,1024]{1,0:T(8,128)(2,1)}, bf16[1024,1024]{1,0:T(8,128)(2,1)}, u32[]{:S(2)}, u32[]{:S(2)}) collective-permute-start(bf16[1024,1024]{1,0:T(8,128)(2,1)} %convolution_convert_fusion.3), channel_id=1, source_target_pairs={{0,2},{2,0},{4,6},{6,4},{8,10},{10,8},{12,14},{14,12},{16,18},{18,... | collective-permute-start | bytes 6291464 | tf_op jit(solution)/shard_map/ppermute | solution.py:65
  327.8 23.7 %collective-permute-start.48 = (bf16[1024,1024]{1,0:T(8,128)(2,1)}, bf16[1024,1024]{1,0:T(8,128)(2,1)}, u32[]{:S(2)}, u32[]{:S(2)}) collective-permute-start(bf16[1024,1024]{1,0:T(8,128)(2,1)} %convolution_convert_fusion.2), channel_id=1, source_target_pairs={{0,2},{2,0},{4,6},{6,4},{8,10},{10,8},{12,14},{14,12},{16,18},{18,... | collective-permute-start | bytes 6291464 | tf_op jit(solution)/shard_map/ppermute | solution.py:65
  331.8 18.5 %all-to-all-start.2 = ((bf16[16,16,1024]{2,1,0:T(8,128)(2,1)}), bf16[16,16,1024]{2,1,0:T(8,128)(2,1)S(1)}, u32[]{:S(2)}, u32[]{:S(2)}) async-start(bf16[16,16,1024]{2,1,0:T(8,128)(2,1)} %bitcast.70), calls=%async_computation.2 | async-start | bytes 1048576 | tf_op jit(solution)/shard_map/all_to_all | solution.py:160
  370.8 27.9 %collective-permute-start.50 = (bf16[128,2048]{1,0:T(8,128)(2,1)}, bf16[128,2048]{1,0:T(8,128)(2,1)}, u32[]{:S(2)}, u32[]{:S(2)}) collective-permute-start(bf16[128,2048]{1,0:T(8,128)(2,1)} %pad_maximum_fusion.14), channel_id=1, source_target_pairs={{0,8},{2,6},{4,0},{6,14},{8,16},{10,2},{12,4},{14,22},{16,24},{18,... | collective-permute-start | bytes 1572872 | tf_op jit(solution)/shard_map/ppermute | solution.py:62
  373.4 25.3 %collective-permute-start.51 = (bf16[128,2048]{1,0:T(8,128)(2,1)}, bf16[128,2048]{1,0:T(8,128)(2,1)}, u32[]{:S(2)}, u32[]{:S(2)}) collective-permute-start(bf16[128,2048]{1,0:T(8,128)(2,1)} %pad_maximum_fusion.15), channel_id=1, source_target_pairs={{8,0},{6,2},{0,4},{14,6},{16,8},{2,10},{4,12},{22,14},{24,16},{10,... | collective-permute-start | bytes 1572872 | tf_op jit(solution)/shard_map/ppermute | solution.py:62
  385.1 43.8 %collective-permute-start.56 = (bf16[1024,768]{1,0:T(8,128)(2,1)}, bf16[1024,768]{1,0:T(8,128)(2,1)}, u32[]{:S(2)}, u32[]{:S(2)}) collective-permute-start(bf16[1024,768]{1,0:T(8,128)(2,1)} %convolution_convert_fusion.5), channel_id=1, source_target_pairs={{0,2},{2,0},{4,6},{6,4},{8,10},{10,8},{12,14},{14,12},{16,18},{18,... | collective-permute-start | bytes 4718600 | tf_op jit(solution)/shard_map/ppermute | solution.py:65
  434.4 20.8 %collective-permute-start.60 = (bf16[128,2048]{1,0:T(8,128)(2,1)}, bf16[128,2048]{1,0:T(8,128)(2,1)}, u32[]{:S(2)}, u32[]{:S(2)}) collective-permute-start(bf16[128,2048]{1,0:T(8,128)(2,1)} %add_convert_fusion.11), channel_id=1, source_target_pairs={{0,8},{2,6},{4,0},{6,14},{8,16},{10,2},{12,4},{14,22},{16,24},{18,... | collective-permute-start | bytes 1572872 | tf_op jit(solution)/shard_map/ppermute | solution.py:61
  522.3 24.4 %collective-permute-start.79 = (bf16[128,2048]{1,0:T(8,128)(2,1)}, bf16[128,2048]{1,0:T(8,128)(2,1)}, u32[]{:S(2)}, u32[]{:S(2)}) collective-permute-start(bf16[128,2048]{1,0:T(8,128)(2,1)} %add_convert_fusion.10), channel_id=1, source_target_pairs={{0,8},{2,6},{4,0},{6,14},{8,16},{10,2},{12,4},{14,22},{16,24},{18,... | collective-permute-start | bytes 1572872 | tf_op jit(solution)/shard_map/ppermute | solution.py:62
  525.2 21.9 %collective-permute-start.80 = (bf16[128,2048]{1,0:T(8,128)(2,1)}, bf16[128,2048]{1,0:T(8,128)(2,1)}, u32[]{:S(2)}, u32[]{:S(2)}) collective-permute-start(bf16[128,2048]{1,0:T(8,128)(2,1)} %add_convert_fusion.9), channel_id=1, source_target_pairs={{8,0},{6,2},{0,4},{14,6},{16,8},{2,10},{4,12},{22,14},{24,16},{10,... | collective-permute-start | bytes 1572872 | tf_op jit(solution)/shard_map/ppermute | solution.py:62
  543.1 21.3 %all-to-all-start.3 = ((bf16[16,16,1024]{2,1,0:T(8,128)(2,1)}), bf16[16,16,1024]{2,1,0:T(8,128)(2,1)S(1)}, u32[]{:S(2)}, u32[]{:S(2)}) async-start(bf16[16,16,1024]{2,1,0:T(8,128)(2,1)} %bitcast.79), calls=%async_computation.3 | async-start | bytes 1048576 | tf_op jit(solution)/shard_map/all_to_all | solution.py:160
  549.1 24.1 %collective-permute-start.82 = (bf16[128,1024]{1,0:T(8,128)(2,1)}, bf16[128,1024]{1,0:T(8,128)(2,1)}, u32[]{:S(2)}, u32[]{:S(2)}) collective-permute-start(bf16[128,1024]{1,0:T(8,128)(2,1)} %add_convert_fusion.27), channel_id=1, source_target_pairs={{0,8},{2,6},{4,0},{6,14},{8,16},{10,2},{12,4},{14,22},{16,24},{18,... | collective-permute-start | bytes 786440 | tf_op jit(solution)/shard_map/ppermute | solution.py:62
  552.6 22.5 %collective-permute-start.84 = (bf16[128,2048]{1,0:T(8,128)(2,1)}, bf16[128,2048]{1,0:T(8,128)(2,1)}, u32[]{:S(2)}, u32[]{:S(2)}) collective-permute-start(bf16[128,2048]{1,0:T(8,128)(2,1)} %add_convert_fusion.8), channel_id=1, source_target_pairs={{0,8},{2,6},{4,0},{6,14},{8,16},{10,2},{12,4},{14,22},{16,24},{18,... | collective-permute-start | bytes 1572872 | tf_op jit(solution)/shard_map/ppermute | solution.py:62
  556.1 19.0 %collective-permute-start.85 = (bf16[128,2048]{1,0:T(8,128)(2,1)}, bf16[128,2048]{1,0:T(8,128)(2,1)}, u32[]{:S(2)}, u32[]{:S(2)}) collective-permute-start(bf16[128,2048]{1,0:T(8,128)(2,1)} %add_convert_fusion.7), channel_id=1, source_target_pairs={{8,0},{6,2},{0,4},{14,6},{16,8},{2,10},{4,12},{22,14},{24,16},{10,... | collective-permute-start | bytes 1572872 | tf_op jit(solution)/shard_map/ppermute | solution.py:62
  576.4 18.4 %collective-permute-start.89 = (bf16[128,2048]{1,0:T(8,128)(2,1)S(1)}, bf16[128,2048]{1,0:T(8,128)(2,1)S(1)}, u32[]{:S(2)}, u32[]{:S(2)}) collective-permute-start(bf16[128,2048]{1,0:T(8,128)(2,1)S(1)} %add_convert_fusion.6), channel_id=1, source_target_pairs={{0,8},{2,6},{4,0},{6,14},{8,16},{10,2},{12,4},{14,22},{16,24},{18,... | collective-permute-start | bytes 1572872 | tf_op jit(solution)/shard_map/ppermute | solution.py:61
  (233 other events, 2040.1 us)

commit v5 on v4

--- a/solution.py
+++ b/solution.py
@@ -98,35 +98,28 @@
             forth.append(came[0])
             back += came[1:]
         blocks = [0] + [self.chips - s for s in range(1, len(forth))] + list(range(1, len(back)))
-        whole, vector = place_pieces(self.spot[np.array(blocks)], forth + back[1:], chip_rows)
+        whole, vector = place_pieces(self.spot, blocks, forth + back[1:], chip_rows)
         halves = (whole, self.partner(whole))
         return halves if extra is None else (halves, vector[:, 0, :chip_rows].reshape(-1))
 
-    def own_half(self, terms, came):
-        return [(term + part.astype(F32)).astype(BF16) for term, part in zip(terms, came)]
-
     def reduce_ring(self, sums):
-        chip_rows = sums[0].shape[0] // self.chips
+        chip_rows = sums.shape[0] // self.chips
 
         def portion(ahead):
             start = self.spot[ahead % self.chips] * chip_rows
-            return jnp.concatenate(
-                [lax.dynamic_slice_in_dim(part, start, chip_rows, 0) for part in sums], 1
-            )
+            return lax.dynamic_slice_in_dim(sums, start, chip_rows, 0)
 
         forth, back = portion(self.rounds), portion(1 + self.rounds)
         for step in range(1, self.rounds + 1):
             both_ways = step < self.chips - self.rounds
             came = yield self.round(forth, back if both_ways else None)
-            if step < self.rounds:
-                forth = (came[0].astype(F32) + portion(self.rounds - step).astype(F32)).astype(BF16)
-            else:
-                forth = came[0]
+            places = [self.rounds - step] if step < self.rounds else []
+            if step + 1 < self.chips - self.rounds:
+                places.append(1 + self.rounds + step)
+            added = add_portions(self.spot, places, came, sums) if places else []
+            forth = added[0] if step < self.rounds else came[0]
             if both_ways:
-                back = came[1]
-                if step + 1 < self.chips - self.rounds:
-                    more = portion(1 + self.rounds + step)
-                    back = (back.astype(F32) + more.astype(F32)).astype(BF16)
+                back = added[1] if len(places) == 2 else came[1]
         return self.share_rows(portion(0).astype(F32) + forth.astype(F32) + back.astype(F32))
 
     def share_rows(self, total):
@@ -191,15 +184,16 @@
     return lax.optimization_barrier(values)
 
 
-def place_pieces(source, pieces, chip_rows):
+def place_pieces(spot, places, pieces, chip_rows):
     count, width = len(pieces), pieces[0].shape[1]
     spare = pieces[0].shape[0] - chip_rows
 
-    def kernel(source_ref, *refs):
+    def kernel(spot_ref, *refs):
         ins, outs, sems = refs[:count], refs[count:-1], refs[-1]
         copies = []
         for i, piece in enumerate(ins):
-            rows = pl.ds(pl.multiple_of(source_ref[i] * chip_rows, chip_rows), chip_rows)
+            chip = spot_ref[places[i]]
+            rows = pl.ds(pl.multiple_of(chip * chip_rows, chip_rows), chip_rows)
             copies.append(
                 pltpu.make_async_copy(piece.at[0:chip_rows], outs[0].at[rows], sems.at[i, 0])
             )
@@ -207,7 +201,7 @@
                 copies.append(
                     pltpu.make_async_copy(
                         piece.at[chip_rows : chip_rows + spare, 0:128],
-                        outs[1].at[source_ref[i]],
+                        outs[1].at[chip],
                         sems.at[i, 1],
                     )
                 )
@@ -231,31 +225,8 @@
             flops=0, bytes_accessed=4 * count * pieces[0].size, transcendentals=0
         ),
         name="place_pieces",
-    )(source, *pieces)
+    )(spot, *pieces)
     return outs[0], (outs[1] if spare else None)
-
-
-def erf(x):
-    x = jnp.clip(x, -3.7439211627767994, 3.7439211627767994)
-    s = x * x
-    top = jnp.full_like(s, 0.00022905065861350646)
-    for c in (0.0034082910107109506, 0.050955695062380861, 0.18520832239976145, 1.128379143519084):
-        top = top * s + c
-    low = jnp.full_like(s, -1.1791602954361697e-7)
-    for c in (
-        0.000023547966471313185,
-        0.0010179625278914885,
-        0.014070470171167667,
-        0.11098505178285362,
-        0.49746925110067538,
-        1.0,
-    ):
-        low = low * s + c
-    return x * top / low
-
-
-def whole_spec(shape):
-    return pl.BlockSpec(shape, lambda *_: (0,) * len(shape))
 
 
 def attend_forward(blocks, weight, bias, segment, earlier=None):
@@ -310,12 +281,8 @@
     outs = pl.pallas_call(
         kernel,
         out_shape=shapes,
-        compiler_params=pltpu.CompilerParams(vmem_limit_bytes=56 << 20),
-        cost_estimate=pl.CostEstimate(
-            flops=2 * rows * (D * 3 * inner + 2 * rows * inner) + extra * rows * D * 2 * inner,
-            bytes_accessed=2 * (rows + 4 * inner) * D,
-            transcendentals=heads * rows**2,
-        ),
+        compiler_params=pltpu.CompilerParams(vmem_limit_bytes=32 << 20),
+        cost_estimate=pl.CostEstimate(flops=1000, bytes_accessed=1000, transcendentals=0),
         name="attend_forward",
     )(*blocks, weight, bias[None], segment[:, None], segment[None], *(earlier or ()))
     return tuple(outs[:3]), list(outs[3:])
@@ -384,7 +351,6 @@
             total += times_transposed(grad_ref[part, :], w_ref[:, : 3 * inner])
             out_ref[...] = total.astype(out_ref.dtype)
 
-    flops = 2 * rows * (D * inner + 5 * rows * inner) + extra * rows * D * 6 * inner
     shapes = [
         jax.ShapeDtypeStruct((rows, 3 * inner), BF16),
         jax.ShapeDtypeStruct((1, 3 * inner), F32),
@@ -395,100 +361,188 @@
         kernel,
         out_shape=shapes,
         scratch_shapes=[pltpu.VMEM((rows, inner), BF16)],
-        compiler_params=pltpu.CompilerParams(vmem_limit_bytes=56 << 20),
-        cost_estimate=pl.CostEstimate(
-            flops=flops, bytes_accessed=2 * (rows + inner) * D, transcendentals=heads * rows**2
-        ),
+        compiler_params=pltpu.CompilerParams(vmem_limit_bytes=32 << 20),
+        cost_estimate=pl.CostEstimate(flops=1000, bytes_accessed=1000, transcendentals=0),
         name="attend_backward",
     )(*blocks, weight, qkv, mixture, log_total, segment[:, None], segment[None], *(earlier or ()))
     return outs[0], outs[1], list(outs[2:])
 
 
-def feed(source, weights, side, block, rows_all, filled, out_type, forward):
-    rows = source.shape[0]
+def normal_parts(x):
+    bell = jnp.exp(-0.5 * x * x)
+    t = 1.0 / (1.0 + 0.23164189 * jnp.abs(x))
+    tail = 0.5307027145
+    for c in (-0.7265760135, 0.7107068705, -0.142248368, 0.127414796):
+        tail = tail * t + c
+    tail = tail * t * bell
+    return jnp.where(x >= 0.0, 1.0 - tail, tail), bell * 0.3989422804014327
+
+
+def feed(blocks, weights, side, forward):
+    rows = sum(block.shape[0] for block in blocks)
     hidden = weights[0].shape[1] // 2
     tile = min(512, hidden)
     tiles = hidden // tile
-    row_tile = min(256, rows)
-    inner_count = 2 if forward else 1
-    given = 0 if filled is None else inner_count
-
-    def kernel(x_ref, a_own, a_part, b_own, b_part, side_ref, *refs):
-        refs = refs[given:]
-        out_ref, inner_refs, refs = refs[0], refs[1 : 1 + inner_count], refs[1 + inner_count :]
-        total_ref = refs[-1]
-        index = pl.program_id(1)
-
-        def run(a_ref, b_ref):
-            pre = dot(x_ref[...], a_ref[...])
+    into, onto = (0, hidden) if forward else (hidden, 0)
+
+    def kernel(*refs):
+        xs, refs = refs[: len(blocks)], refs[len(blocks) :]
+        *halves, side_ref = refs[:3]
+        outs, (kept_ref, more_ref, pre_ref) = refs[3:-3], refs[-3:]
+
+        def project(half, index):
+            start, slot = 0, lax.rem(index, 2)
+            first = index * tile + into
+            if not isinstance(index, int):
+                first = pl.multiple_of(first, tile)
+            for x in xs:
+                part = pl.ds(start, x.shape[0])
+                pre_ref[slot, part, :] = dot(x[...], halves[half][:, pl.ds(first, tile)])
+                start += x.shape[0]
+
+        def activate(half, index):
+            first = index * tile + half * hidden
+            if not isinstance(index, int):
+                first = pl.multiple_of(first, tile)
+            columns = pl.ds(first, tile)
+            pre = pre_ref[lax.rem(index, 2)]
             if forward:
-                pre = pre + side_ref[...]
-                cdf = 0.5 + 0.5 * erf(pre * 0.7071067811865476)
-                bell = jnp.exp(-0.5 * pre * pre) * 0.3989422804014327
-                kept = (pre * cdf).astype(BF16)
-                inner_refs[0][...] = kept
-                inner_refs[1][...] = (cdf + pre * bell).astype(BF16)
+                pre = pre + side_ref[:, columns]
+                cdf, bell = normal_parts(pre)
+                kept_ref[:, columns] = (pre * cdf).astype(BF16)
+                more_ref[:, columns] = (cdf + pre * bell).astype(BF16)
             else:
-                kept = (pre * side_ref[...].astype(F32)).astype(BF16)
-                inner_refs[0][...] = kept
-                refs[0][...] = jnp.sum(kept.astype(F32), axis=0, keepdims=True)[None]
-            term = times_transposed(kept, b_ref[...])
-
-            @pl.when(index == 0)
-            def _():
-                total_ref[...] = term
-
-            @pl.when(index > 0)
-            def _():
-                total_ref[...] += term
-
-        @pl.when(index < tiles)
-        def _():
-            run(a_own, b_own)
-
-        @pl.when(index >= tiles)
-        def _():
-            run(a_part, b_part)
-
-        @pl.when(index == 2 * tiles - 1)
-        def _():
-            out_ref[...] = total_ref[...].astype(out_type)
-
-    shift = block * (rows // row_tile)
-    shifts = (0, tiles) if forward else (tiles, 0)
-    owns = [
-        pl.BlockSpec((D, tile), lambda r, i, k=k: (0, jnp.minimum(i, tiles - 1) + k)) for k in shifts
-    ]
-    parts = [
-        pl.BlockSpec((D, tile), lambda r, i, k=k: (0, jnp.maximum(i - tiles, 0) + k)) for k in shifts
-    ]
-    over = pl.BlockSpec((row_tile, tile), lambda r, i: (r + shift, i))
-    source_spec = pl.BlockSpec((row_tile, D), lambda r, i: (r, 0))
-    side_spec = pl.BlockSpec((1, tile), lambda r, i: (0, i)) if forward else over
-    out_shape = [jax.ShapeDtypeStruct((rows, D), out_type)]
-    out_shape += [jax.ShapeDtypeStruct((rows_all, 2 * hidden), BF16)] * inner_count
-    out_specs = [source_spec] + [over] * inner_count
-    if not forward:
-        out_shape.append(jax.ShapeDtypeStruct((rows // row_tile, 1, 2 * hidden), F32))
-        out_specs.append(pl.BlockSpec((1, 1, tile), lambda r, i: (r, 0, i)))
+                kept = (pre * side_ref[:, columns].astype(F32)).astype(BF16)
+                kept_ref[:, columns] = kept
+                more_ref[:, columns] = jnp.sum(kept.astype(F32), axis=0, keepdims=True)
+
+        for half in (0, 1):
+            project(half, 0)
+
+            def step(index, _, half=half):
+                project(half, index)
+                activate(half, index - 1)
+                return 0
+
+            lax.fori_loop(1, tiles, step, 0)
+            activate(half, tiles - 1)
+        start = 0
+        for out in outs:
+            part = slice(start, start + out.shape[0])
+            start += out.shape[0]
+            total = times_transposed(kept_ref[part, 0:hidden], halves[0][:, onto : onto + hidden])
+            total += times_transposed(kept_ref[part, hidden:], halves[1][:, onto : onto + hidden])
+            out[...] = total.astype(out.dtype)
+
+    wide = jax.ShapeDtypeStruct((rows, 2 * hidden), BF16)
     outs = pl.pallas_call(
         kernel,
-        grid=(rows // row_tile, 2 * tiles),
-        out_shape=out_shape,
-        in_specs=[source_spec, owns[0], parts[0], owns[1], parts[1], side_spec]
-        + [pl.BlockSpec(memory_space=pl.ANY)] * given,
-        out_specs=out_specs,
-        scratch_shapes=[pltpu.VMEM((row_tile, D), F32)],
-        input_output_aliases={6 + i: 1 + i for i in range(given)},
-        compiler_params=pltpu.CompilerParams(vmem_limit_bytes=60 << 20),
-        cost_estimate=pl.CostEstimate(
-            flops=8 * rows * D * hidden,
-            bytes_accessed=8 * D * hidden,
-            transcendentals=2 * rows * hidden if forward else 0,
+        out_shape=sum_shapes(blocks)
+        + [wide, wide if forward else jax.ShapeDtypeStruct((1, 2 * hidden), F32)],
+        scratch_shapes=[pltpu.VMEM((2, rows, tile), F32)],
+        compiler_params=pltpu.CompilerParams(vmem_limit_bytes=32 << 20),
+        cost_estimate=pl.CostEstimate(flops=1000, bytes_accessed=1000, transcendentals=0),
+        name="feed_forward" if forward else "feed_backward",
+    )(*blocks, *weights, side)
+    return list(outs[:-2]), outs[-2], outs[-1]
+
+
+def weight_gradients(pairs, half, came=None):
+    widths = [width for _, _, width in pairs]
+    tile = math.gcd(256, *widths)
+    if tile % 128:
+        terms = [
+            contract_rows(join(blocks), _columns(right, half, width))
+            for blocks, right, width in pairs
+        ]
+        total = jnp.concatenate(terms, 1)
+        return (total if came is None else total + came.astype(F32)).astype(BF16)
+    counts = [width // tile for width in widths]
+    edge = counts[0]
+    blocks_flat = [block for blocks, _, _ in pairs for block in blocks]
+    per = len(pairs[0][0])
+    rows = sum(block.shape[0] for block in pairs[0][0])
+
+    def kernel(*refs):
+        lefts, refs = refs[: 2 * per], refs[2 * per :]
+        rights, refs = refs[:2], refs[2:]
+        came_ref = refs[0] if came is not None else None
+        out_ref, turned = refs[-2:]
+        index = pl.program_id(0)
+
+        @pl.when(index == 0)
+        def _():
+            for pair in (0, 1):
+                start = 0
+                for left in lefts[pair * per : (pair + 1) * per]:
+                    turned[pair, :, start : start + left.shape[0]] = left[...].T
+                    start += left.shape[0]
+
+        def run(pair):
+            total = dot(turned[pair], rights[pair][...])
+            if came_ref is not None:
+                total += came_ref[...].astype(F32)
+            out_ref[...] = total.astype(BF16)
+
+        @pl.when(index < edge)
+        def _():
+            run(0)
+
+        @pl.when(index >= edge)
+        def _():
+            run(1)
+
+    shifts = [
+        half * counts[i] if pairs[i][1].shape[1] > widths[i] else 0 for i in (0, 1)
+    ]
+    last = counts[1] - 1
+    specs = [pl.BlockSpec(block.shape, lambda i: (0, 0)) for block in blocks_flat]
+    specs += [
+        pl.BlockSpec((rows, tile), lambda i: (0, jnp.minimum(i, edge - 1) + shifts[0])),
+        pl.BlockSpec((rows, tile), lambda i: (0, jnp.clip(i - edge, 0, last) + shifts[1])),
+    ]
+    over = pl.BlockSpec((D, tile), lambda i: (0, i))
+    return pl.pallas_call(
+        kernel,
+        grid=(sum(counts),),
+        out_shape=jax.ShapeDtypeStruct((D, sum(widths)), BF16),
+        in_specs=specs + ([over] if came is not None else []),
+        out_specs=over,
+        scratch_shapes=[pltpu.VMEM((2, D, rows), BF16)],
+        compiler_params=pltpu.CompilerParams(vmem_limit_bytes=24 << 20),
+        cost_estimate=pl.CostEstimate(flops=1000, bytes_accessed=1000, transcendentals=0),
+        name="weight_gradients",
+    )(*blocks_flat, pairs[0][1], pairs[1][1], *(() if came is None else (came,)))
+
+
+def _columns(right, half, width):
+    return right[:, half * width : (half + 1) * width] if right.shape[1] > width else right
+
+
+def add_portions(spot, places, came, sums):
+    count = len(places)
+    came, shape = came[:count], came[0].shape
+
+    def kernel(spots_ref, *refs):
+        ins, parts, outs = refs[:count], refs[count : 2 * count], refs[2 * count :]
+        for value, part, out in zip(ins, parts, outs):
+            out[...] = (value[...].astype(F32) + part[...].astype(F32)).astype(BF16)
+
+    whole = pl.BlockSpec(shape, lambda i, spots_ref: (0, 0))
+    return pl.pallas_call(
+        kernel,
+        grid_spec=pltpu.PrefetchScalarGridSpec(
+            num_scalar_prefetch=1,
+            grid=(1,),
+            in_specs=[whole] * count
+            + [pl.BlockSpec(shape, lambda i, s, k=k: (s[k], 0)) for k in places],
+            out_specs=[whole] * count,
         ),
-        name="feed_forward" if forward else "feed_backward",
-    )(source, *weights, *weights, side, *(filled or ()))
-    return outs
+        out_shape=[jax.ShapeDtypeStruct(shape, BF16)] * count,
+        compiler_params=pltpu.CompilerParams(vmem_limit_bytes=16 << 20),
+        cost_estimate=pl.CostEstimate(flops=1000, bytes_accessed=1000, transcendentals=0),
+        name="add_portions",
+    )(spot, *came, *([sums] * count))
 
 
 def join(blocks):
@@ -545,12 +599,14 @@
     step = 0
     while not attn_rings[0].done:
         beside = (attn_rings[0], feed_rings[0] if step % 2 else None)
-        if step == 0:
+        if step == 1:
             tokens, back_slot = tick((tokens, back_slot), *beside)
             own_tokens = owner_swap(jnp.take(tokens, back_slot, axis=0))
         elif step == 2:
             own_tokens = tick(own_tokens, *beside)
             token_blocks = wires.rows_in(own_tokens)
+        elif step == 4:
+            token_blocks[-1] = tick(token_blocks[-1], *beside)
         else:
             tick((), *beside)
         step += 1
@@ -598,11 +654,7 @@
         feed_w = feed_rings[layer].finish()
         weights.append((attn_w, feed_w))
         bias = jnp.concatenate([wires.half(b_ff1[layer], 0, mine) for mine in both])[None]
-        sums, filled = [], None
-        for block, rows in enumerate(normed_blocks):
-            kind = F32 if block == 0 and wires.tensor_size == 2 else BF16
-            total, *filled = feed(rows, feed_w, bias, block, group_rows, filled, kind, True)
-            sums.append(total)
+        sums, *filled = feed(normed_blocks, feed_w, bias, True)
         sums[-1] = tick(sums[-1], *ahead)
         second_sum = normed + wires.rows_out(sums) + out_bias[layer, 1]
         saved.append((input_blocks, attention, middle, normed_blocks, filled, second_sum))
@@ -628,56 +680,43 @@
             branch_blocks[-1] = tick(branch_blocks[-1], later[0])
             attn_tasks[layer + 1] = Task(wires.reduce_ring(attn_sums))
             later = (later[0], attn_tasks[layer + 1])
-        sums, hidden_sums, filled = [], [], None
-        for block, rows in enumerate(branch_blocks):
-            kind = F32 if block == 0 and wires.tensor_size == 2 else BF16
-            total, grad_pre, more = feed(rows, feed_w, slope, block, group_rows, filled, kind, False)
-            filled = (grad_pre,)
-            sums.append(total)
-            hidden_sums.append(more)
-        hidden_sums = sum(jnp.sum(part, axis=(0, 1)) for part in hidden_sums)
+        sums, grad_pre, hidden_sums = feed(branch_blocks, feed_w, slope, False)
+        hidden_sums = hidden_sums[0]
         if layer == layer_total - 1:
             sums[-1], encoded_own = tie(sums[-1], encoded_own)
             returned_out = owner_swap(encoded_own)
         sums[-1] = tick(sums[-1], *later)
-        normed_all, branch_all = join(normed_blocks), join(branch_blocks)
-
-        def feed_terms(half):
-            columns = slice(half * hidden, (half + 1) * hidden)
-            return [
-                contract_rows(normed_all, grad_pre[:, columns]),
-                contract_rows(branch_all, act[:, columns]),
-            ]
-
-        came = [wires.partner(term.astype(BF16)) for term in feed_terms(1)]
+        pairs = [(normed_blocks, grad_pre, hidden), (branch_blocks, act, hidden)]
+        came = wires.partner(weight_gradients(pairs, 1))
         grad_normed = grad_second + wires.rows_out(sums)
         grad_normed, came = tie(grad_normed, came)
         _, pull_first = jax.vjp(layer_norm, middle, ln_gain[layer, 0], ln_shift[layer, 0])
         grad_middle, gain_first, shift_first = pull_first(grad_normed)
         attend_blocks = wires.rows_in(tick(grad_middle.astype(BF16), later[1]))
-        feed_sums = wires.own_half(feed_terms(0), came)
+        feed_sums = weight_gradients(pairs, 0, came)
         attend_blocks[-1], feed_sums = tie(attend_blocks[-1], feed_sums)
         attend_blocks[-1] = tick(attend_blocks[-1], later[1])
         feed_tasks[layer] = Task(wires.reduce_ring(feed_sums))
-        input_all, attend_all = join(input_blocks), join(attend_blocks)
-
-        def attn_terms(half, wide):
-            return [
-                contract_rows(input_all, wide),
-                contract_rows(attend_all, attention[half][1]),
-            ]
+
+        def attn_pairs(half, wide):
+            return [(input_blocks, wide, 3 * inner), (attend_blocks, attention[half][1], inner)]
 
         wide, part_sums, _ = attend_backward(attend_blocks, attn_w[1], *attention[1], segment)
-        sends = [term.astype(BF16) for term in attn_terms(1, wide)]
+        send = weight_gradients(attn_pairs(1, wide), 1)
         if layer == 0:
-            wide, sends = tie(wide, sends)
-        came = [wires.partner(term) for term in sends]
+            wide, send = tie(wide, send)
+        came = wires.partner(send)
         own_wide, own_sums, sums = attend_backward(
             attend_blocks, attn_w[0], *attention[0], segment, (wide, attn_w[1])
         )
         sums[-1] = tick(sums[-1], feed_tasks[layer], later[1])
+        if layer == 0:
+            attn_sums = weight_gradients(attn_pairs(0, own_wide), 0, came)
+            sums[-1], attn_sums = tie(sums[-1], attn_sums)
+            attn_tasks[0] = Task(wires.reduce_ring(attn_sums))
         gradient = grad_middle + wires.rows_out(sums)
-        attn_sums = wires.own_half(attn_terms(0, own_wide), came)
+        if layer:
+            attn_sums = weight_gradients(attn_pairs(0, own_wide), 0, came)
         qkv_sums = [part.reshape(3, inner)[::2] for part in (own_sums, part_sums)]
         vector_grads[layer] = (
             wires.ordered(qkv_sums[0], qkv_sums[1], 1),
@@ -687,7 +726,6 @@
             jnp.stack([shift_first, shift_second]),
         )
 
-    attn_tasks[0] = Task(wires.reduce_ring(attn_sums))
     returned_grad = owner_swap(gradient.astype(BF16))
     time_grad = jnp.sum(gradient, axis=0)
     local = [jnp.stack([part[i] for part in vector_grads]) for i in range(5)]

time: 625 us -> 617 us (0.987)
  waiting for transfers between devices: 186 us -> 226 us
  matrix products: 38.5 us -> 0 us
  other arithmetic: 75.4 us -> 40.4 us
  local copies, waits for them, and re-layouts: 51.4 us -> 84.6 us
  Pallas kernels: 140 us -> 132 us
    dot_general x16 -> x0, matrix products: 38.5 us -> none  [contract_rows(): lax.dot_general(left, right, (((0,), (0,)), ((), ())), preferred_element_...]
    unnamed x311 -> x338, local copies, waits for them, and re-layouts: 20.4 us -> 56.3 us
    convert_element_type x20 -> x0, other arithmetic: 23.8 us -> none  [the longest x12 13.7 us: reduce_ring(): (came[0].astype(F32) + portion(self.rounds - step).astype(F32)).astype(BF16)]
    ppermute x24, waiting for transfers between devices: 9.56 us -> 29.8 us  [round(): lax.ppermute(back, 'dp', self.back)]
    ppermute x16, waiting for transfers between devices: 81.4 us -> 99.5 us  [across(): return lax.ppermute(array, 'tensor', [(0, 1), (1, 0)])]
    ppermute x24, waiting for transfers between devices: 38.5 us -> 56 us  [round(): lax.ppermute(forth, 'dp', self.ahead)]
    pallas_call x8 -> x24, Pallas kernels: 71 us -> 82.5 us  [the longest x8 42.9 us: weight_gradients(): pl.pallas_call(kernel, grid=(sum(counts),), out_shape=jax.ShapeDtypeStruc...]
    pallas_call x4, Pallas kernels: 27.3 us -> 15.9 us  [attend_forward(): pl.pallas_call(kernel, out_shape=shapes, compiler_params=pltpu.CompilerPa...]
  transfers between devices with their start and end apart: 102 -> 98, of which waited for: 38 -> 42; matrix products, arithmetic and copies ran while one was open for 20% -> 9% of each run, Pallas kernels for 18% -> 14%
where the time goes in v5:
time: 617 us; the launch traced here: 606 us
  waiting for transfers between devices  226 us (37%)
  Pallas kernels  132 us (21%)
  starting transfers between devices  116 us (19%)
  local copies, waits for them, and re-layouts  84.6 us (14%)
  other arithmetic  40.4 us (7%)
  between operations  6.54 us (1%)
    ppermute x16, waiting for transfers between devices, across(): return lax.ppermute(array, 'tensor', [(0, 1), (1, 0)])  99.5 us
    unnamed x338, local copies, waits for them, and re-layouts  56.3 us
    ppermute x24, waiting for transfers between devices, round(): lax.ppermute(forth, 'dp', self.ahead)  56 us
    pallas_call x8, Pallas kernels, weight_gradients(): pl.pallas_call(kernel, grid=(sum(counts),), out_shape=jax.ShapeDtypeStruc...  42.9 us
    ppermute x24, starting transfers between devices, round(): lax.ppermute(forth, 'dp', self.ahead)  33.8 us
    ppermute x24, waiting for transfers between devices, round(): lax.ppermute(back, 'dp', self.back)  29.8 us
    pallas_call x4, Pallas kernels, attend_backward(): pl.pallas_call(kernel, out_shape=shapes, scratch_shapes=[pltpu.VMEM((rows...  29.3 us
    pallas_call x4, Pallas kernels, feed(): pl.pallas_call(kernel, out_shape=sum_shapes(blocks) + [wide, wide if forw...  24.9 us
  transfers between devices with their start and end apart: 98, of which 42 were waited for; matrix products, arithmetic and copies ran while one was open for 9% of the time, Pallas kernels for 14%

profile of v5, /device:TPU:0, one launch (start us, length us, event | category | flops | bytes accessed | tf_op | source)
XLA Modules:
  0.0 605.8 jit_solution(7467266955355545545)
XLA Ops:
  8.7 6.3 %collective-permute-done.3.refs_5_ = bf16[136,1024]{1,0:T(8,128)(2,1)S(1)} collective-permute-done((bf16[136,1024]{1,0:T(8,128)(2,1)S(1)}, bf16[136,1024]{1,0:T(8,128)(2,1)S(1)}, u32[]{:S(2)}, u32[]{:S(2)}) %collective-permute-start.3) | collective-permute-done | bytes 278560 | tf_op jit(solution)/shard_map/ppermute | solution.py:62
  17.8 6.4 %all-to-all-start = ((bf16[16,16,1024]{2,1,0:T(8,128)(2,1)}), bf16[16,16,1024]{2,1,0:T(8,128)(2,1)}, u32[]{:S(2)}, u32[]{:S(2)}) async-start(bf16[16,16,1024]{2,1,0:T(8,128)(2,1)} %bitcast.19), calls=%async_computation | async-start | bytes 1048576 | tf_op jit(solution)/shard_map/all_to_all | solution.py:153
  28.3 11.5 %collective-permute-done.5.refs_2_ = bf16[136,1024]{1,0:T(8,128)(2,1)S(1)} collective-permute-done((bf16[136,1024]{1,0:T(8,128)(2,1)S(1)}, bf16[136,1024]{1,0:T(8,128)(2,1)S(1)}, u32[]{:S(2)}, u32[]{:S(2)}) %collective-permute-start.5) | collective-permute-done | bytes 278560 | tf_op jit(solution)/shard_map/ppermute | solution.py:62
  99.6 7.1 %collective-permute-done.16.refs_3_ = bf16[128,2048]{1,0:T(8,128)(2,1)S(1)} collective-permute-done((bf16[128,2048]{1,0:T(8,128)(2,1)}, bf16[128,2048]{1,0:T(8,128)(2,1)S(1)}, u32[]{:S(2)}, u32[]{:S(2)}) %collective-permute-start.16) | collective-permute-done | bytes 524320 | tf_op jit(solution)/shard_map/ppermute | solution.py:62
  110.6 10.0 %collective-permute-done.18 = bf16[256,1024]{1,0:T(8,128)(2,1)S(1)} collective-permute-done((bf16[256,1024]{1,0:T(8,128)(2,1)S(1)}, bf16[256,1024]{1,0:T(8,128)(2,1)S(1)}, u32[]{:S(2)}, u32[]{:S(2)}) %collective-permute-start.18) | collective-permute-done | bytes 524320 | tf_op jit(solution)/shard_map/ppermute | solution.py:68
  135.2 7.0 %collective-permute-done.21.refs_1_ = bf16[256,1024]{1,0:T(8,128)(2,1)S(1)} collective-permute-done((bf16[256,1024]{1,0:T(8,128)(2,1)S(1)}, bf16[256,1024]{1,0:T(8,128)(2,1)S(1)}, u32[]{:S(2)}, u32[]{:S(2)}) %collective-permute-start.21) | collective-permute-done | bytes 524320 | tf_op jit(solution)/shard_map/ppermute | solution.py:68
  144.4 6.9 %feed_forward.2 = (f32[256,1024]{1,0:T(8,128)S(1)}, bf16[256,1024]{1,0:T(8,128)(2,1)S(1)}, bf16[512,2048]{1,0:T(8,128)(2,1)S(1)}, bf16[512,2048]{1,0:T(8,128)(2,1)S(1)}) custom-call(bf16[256,1024]{1,0:T(8,128)(2,1)S(1)} %fusion.5.refs_0_, bf16[256,1024]{1,0:T(8,128)(2,1)S(1)} %collective-permute-done.21.refs_1_, bf16[1024,2048]{1,0:T(8,128)(2,1)S(1)} %place_pieces.5.refs_2_, ...), custom_call_target="tpu_custom_call" | custom-call | flops 1000 | bytes 1000 | tf_op jit(solution)/shard_map/feed_forward/pallas_call | solution.py:438
  157.0 6.3 %collective-permute-done.28 = bf16[256,1024]{1,0:T(8,128)(2,1)S(1)} collective-permute-done((bf16[256,1024]{1,0:T(8,128)(2,1)S(1)}, bf16[256,1024]{1,0:T(8,128)(2,1)S(1)}, u32[]{:S(2)}, u32[]{:S(2)}) %collective-permute-start.28) | collective-permute-done | bytes 524320 | tf_op jit(solution)/shard_map/ppermute | solution.py:68
  174.0 12.1 %collective-permute-done.34.refs_4_ = bf16[128,1024]{1,0:T(8,128)(2,1)S(1)} collective-permute-done((bf16[128,1024]{1,0:T(8,128)(2,1)S(1)}, bf16[128,1024]{1,0:T(8,128)(2,1)S(1)}, u32[]{:S(2)}, u32[]{:S(2)}) %collective-permute-start.34) | collective-permute-done | bytes 262176 | tf_op jit(solution)/shard_map/ppermute | solution.py:61
  202.4 13.2 %collective-permute-done.40 = bf16[256,1024]{1,0:T(8,128)(2,1)S(1)} collective-permute-done((bf16[256,1024]{1,0:T(8,128)(2,1)S(1)}, bf16[256,1024]{1,0:T(8,128)(2,1)S(1)}, u32[]{:S(2)}, u32[]{:S(2)}) %collective-permute-start.40) | collective-permute-done | bytes 524320 | tf_op jit(solution)/shard_map/ppermute | solution.py:68
  218.5 13.7 %collective-permute-done.42.refs_1_ = bf16[256,1024]{1,0:T(8,128)(2,1)S(1)} collective-permute-done((bf16[256,1024]{1,0:T(8,128)(2,1)S(1)}, bf16[256,1024]{1,0:T(8,128)(2,1)S(1)}, u32[]{:S(2)}, u32[]{:S(2)}) %collective-permute-start.42) | collective-permute-done | bytes 524320 | tf_op jit(solution)/shard_map/ppermute | solution.py:68
  232.3 7.7 %feed_forward.3 = (f32[256,1024]{1,0:T(8,128)S(1)}, bf16[256,1024]{1,0:T(8,128)(2,1)}, bf16[512,2048]{1,0:T(8,128)(2,1)S(1)}, bf16[512,2048]{1,0:T(8,128)(2,1)S(1)}) custom-call(bf16[256,1024]{1,0:T(8,128)(2,1)S(1)} %fusion.6.refs_0_, bf16[256,1024]{1,0:T(8,128)(2,1)S(1)} %collective-permute-done.42.refs_1_, bf16[1024,2048]{1,0:T(8,128)(2,1)S(1)} %place_pieces.7.refs_2_, ...), custom_call_target="tpu_custom_call" | custom-call | flops 1000 | bytes 1000 | tf_op jit(solution)/shard_map/feed_forward/pallas_call | solution.py:438
  260.8 7.7 %all-to-all-done.1 = bf16[16,16,1024]{2,1,0:T(8,128)(2,1)} async-done(((bf16[16,16,1024]{2,1,0:T(8,128)(2,1)}), bf16[16,16,1024]{2,1,0:T(8,128)(2,1)}, u32[]{:S(2)}, u32[]{:S(2)}) %all-to-all-start.1) | async-done | bytes 524320 | tf_op jit(solution)/shard_map/all_to_all | solution.py:153
  274.9 12.4 %collective-permute-done.45.refs_1_.refs_3_ = bf16[256,1024]{1,0:T(8,128)(2,1)S(1)} collective-permute-done((bf16[256,1024]{1,0:T(8,128)(2,1)S(1)}, bf16[256,1024]{1,0:T(8,128)(2,1)S(1)}, u32[]{:S(2)}, u32[]{:S(2)}) %collective-permute-start.45) | collective-permute-done | bytes 524320 | tf_op jit(solution)/shard_map/ppermute | solution.py:68
  301.3 12.8 %collective-permute-done.46 = bf16[256,1024]{1,0:T(8,128)(2,1)S(1)} collective-permute-done((bf16[256,1024]{1,0:T(8,128)(2,1)S(1)}, bf16[256,1024]{1,0:T(8,128)(2,1)S(1)}, u32[]{:S(2)}, u32[]{:S(2)}) %collective-permute-start.46) | collective-permute-done | bytes 524320 | tf_op jit(solution)/shard_map/ppermute | solution.py:68
  340.0 5.9 attend_backward.4
  345.9 7.5 %attend_backward.5 = (bf16[512,768]{1,0:T(8,128)(2,1)S(1)}, f32[1,768]{1,0:T(1,128)S(1)}, f32[256,1024]{1,0:T(8,128)S(1)}, bf16[256,1024]{1,0:T(8,128)(2,1)S(1)}) custom-call(bf16[256,1024]{1,0:T(8,128)(2,1)} %get-tuple-element.416.refs_0_.refs_2_, bf16[256,1024]{1,0:T(8,128)(2,1)} %collective-permute-done.48.refs_1_.refs_3_, ...), custom_call_target="tpu_custom_call" | custom-call | flops 1000 | bytes 1000 | tf_op jit(solution)/shard_map/attend_backward/pallas_call | solution.py:360
  396.8 6.5 %weight_gradients.12 = bf16[1024,2048]{1,0:T(8,128)(2,1)} custom-call(bf16[256,1024]{1,0:T(8,128)(2,1)S(1)} %copy-done.44, bf16[256,1024]{1,0:T(8,128)(2,1)S(1)} %copy-done.54, bf16[256,1024]{1,0:T(8,128)(2,1)S(1)} %get-tuple-element.268.refs_0_.refs_2_, bf16[256,1024]{1,0:T(8,128)(2,1)S(1)} %collective-permute-done.54.refs_1_.refs_3_, ...), custom_call_target="tpu_custom_call" | custom-call | flops 1000 | bytes 1000 | tf_op jit(solution)/shard_map/weight_gradients/pallas_call | solution.py:505
  407.1 7.2 %collective-permute-done.60.refs_1_ = bf16[128,1024]{1,0:T(8,128)(2,1)S(1)} collective-permute-done((bf16[128,1024]{1,0:T(8,128)(2,1)S(1)}, bf16[128,1024]{1,0:T(8,128)(2,1)S(1)}, u32[]{:S(2)}, u32[]{:S(2)}) %collective-permute-start.60) | collective-permute-done | bytes 262176 | tf_op jit(solution)/shard_map/ppermute | solution.py:62
  464.7 7.8 %weight_gradients.13.refs_2_.refs_3_.refs_1_ = bf16[1024,2048]{1,0:T(8,128)(2,1)S(1)} custom-call(bf16[256,1024]{1,0:T(8,128)(2,1)S(1)} %copy-done.45, bf16[256,1024]{1,0:T(8,128)(2,1)S(1)} %copy-done.55, bf16[256,1024]{1,0:T(8,128)(2,1)S(1)} %copy-done.40, bf16[256,1024]{1,0:T(8,128)(2,1)S(1)} %copy-done.50, bf16[512,2048]{1,0:T(8,128)(2,1)S(1)} %copy-done.31, ...), custom_call_target="tpu_custom_call" | custom-call | flops 1000 | bytes 1000 | tf_op jit(solution)/shard_map/weight_gradients/pallas_call | solution.py:505
  472.6 7.9 %attend_backward.6 = (bf16[512,768]{1,0:T(8,128)(2,1)S(1)}, f32[1,768]{1,0:T(1,128)S(1)}) custom-call(bf16[256,1024]{1,0:T(8,128)(2,1)S(1)} %copy-done.25, bf16[256,1024]{1,0:T(8,128)(2,1)} %collective-permute-done.65.refs_1_.refs_3_, bf16[1024,1024]{1,0:T(8,128)(2,1)} %collective-permute-done.13.refs_2_.refs_9_, bf16[512,768]{1,0:T(8,128)(2,1)S(1)} %copy-done.88, ...), custom_call_target="tpu_custom_call" | custom-call | flops 1000 | bytes 1000 | tf_op jit(solution)/shard_map/attend_backward/pallas_call | solution.py:360
  495.3 8.0 %attend_backward.7 = (bf16[512,768]{1,0:T(8,128)(2,1)S(1)}, f32[1,768]{1,0:T(1,128)S(1)}, f32[256,1024]{1,0:T(8,128)S(1)}, bf16[256,1024]{1,0:T(8,128)(2,1)S(1)}) custom-call(bf16[256,1024]{1,0:T(8,128)(2,1)S(1)} %copy-done.25, bf16[256,1024]{1,0:T(8,128)(2,1)} %collective-permute-done.65.refs_1_.refs_3_, bf16[1024,1024]{1,0:T(8,128)(2,1)S(1)} %copy-done.15, ...), custom_call_target="tpu_custom_call" | custom-call | flops 1000 | bytes 1000 | tf_op jit(solution)/shard_map/attend_backward/pallas_call | solution.py:360
  522.1 6.1 %collective-permute-done.72 = bf16[256,1024]{1,0:T(8,128)(2,1)S(1)} collective-permute-done((bf16[256,1024]{1,0:T(8,128)(2,1)S(1)}, bf16[256,1024]{1,0:T(8,128)(2,1)S(1)}, u32[]{:S(2)}, u32[]{:S(2)}) %collective-permute-start.72) | collective-permute-done | bytes 524320 | tf_op jit(solution)/shard_map/ppermute | solution.py:68
  553.0 12.9 %collective-permute-done.82 = f32[19456]{0:T(1024)S(1)} collective-permute-done((f32[19456]{0:T(1024)S(1)}, f32[19456]{0:T(1024)S(1)}, u32[]{:S(2)}, u32[]{:S(2)}) %collective-permute-start.82) | collective-permute-done | bytes 77856 | tf_op jit(solution)/shard_map/ppermute | solution.py:147
  (749 shorter events, 388.3 us)
Async XLA Ops:
  17.8 24.4 %all-to-all-start = ((bf16[16,16,1024]{2,1,0:T(8,128)(2,1)}), bf16[16,16,1024]{2,1,0:T(8,128)(2,1)}, u32[]{:S(2)}, u32[]{:S(2)}) async-start(bf16[16,16,1024]{2,1,0:T(8,128)(2,1)} %bitcast.19), calls=%async_computation | async-start | bytes 1048576 | tf_op jit(solution)/shard_map/all_to_all | solution.py:153
  26.3 27.1 %collective-permute-start.10 = (bf16[128,2048]{1,0:T(8,128)(2,1)S(1)}, bf16[128,2048]{1,0:T(8,128)(2,1)S(1)}, u32[]{:S(2)}, u32[]{:S(2)}) collective-permute-start(bf16[128,2048]{1,0:T(8,128)(2,1)S(1)} %maximum_select_fusion.refs_0_), channel_id=1, source_target_pairs={{8,0},{6,2},{0,4},{14,6},{16,8},{2,10},{4,12},{22,14},{24,16},{10,... | collective-permute-start | bytes 1572872 | tf_op jit(solution)/shard_map/ppermute | solution.py:62
  28.2 25.2 %collective-permute-start.9 = (bf16[128,2048]{1,0:T(8,128)(2,1)S(1)}, bf16[128,2048]{1,0:T(8,128)(2,1)S(1)}, u32[]{:S(2)}, u32[]{:S(2)}) collective-permute-start(bf16[128,2048]{1,0:T(8,128)(2,1)S(1)} %maximum_select_fusion.refs_0_), channel_id=1, source_target_pairs={{0,8},{2,6},{4,0},{6,14},{8,16},{10,2},{12,4},{14,22},{16,24},{18,... | collective-permute-start | bytes 1572872 | tf_op jit(solution)/shard_map/ppermute | solution.py:62
  76.3 17.8 %collective-permute-start.13 = (bf16[1024,1024]{1,0:T(8,128)(2,1)S(1)}, bf16[1024,1024]{1,0:T(8,128)(2,1)}, u32[]{:S(2)}, u32[]{:S(2)}) collective-permute-start(bf16[1024,1024]{1,0:T(8,128)(2,1)S(1)} %get-tuple-element.195.refs_2_.refs_7_), channel_id=1, source_target_pairs={{0,2},{2,0},{4,6},{6,4},{8,10},{10,8},{12,14},{14,12},{16,18},{18,... | collective-permute-start | bytes 6291464 | tf_op jit(solution)/shard_map/ppermute | solution.py:65
  125.8 18.6 %collective-permute-start.24 = (bf16[1024,2048]{1,0:T(8,128)(2,1)S(1)}, bf16[1024,2048]{1,0:T(8,128)(2,1)S(1)}, u32[]{:S(2)}, u32[]{:S(2)}) collective-permute-start(bf16[1024,2048]{1,0:T(8,128)(2,1)S(1)} %place_pieces.5.refs_2_), channel_id=1, source_target_pairs={{0,2},{2,0},{4,6},{6,4},{8,10},{10,8},{12,14},{14,12},{16,18},{18,... | collective-permute-start | bytes 12582920 | tf_op jit(solution)/shard_map/ppermute | solution.py:65
  126.0 18.3 %collective-permute-start.27 = (bf16[64,2048]{1,0:T(8,128)(2,1)S(1)}, bf16[64,2048]{1,0:T(8,128)(2,1)S(1)}, u32[]{:S(2)}, u32[]{:S(2)}) collective-permute-start(bf16[64,2048]{1,0:T(8,128)(2,1)S(1)} %pad_maximum_fusion.4), channel_id=1, source_target_pairs={{0,2},{2,0},{4,6},{6,4},{8,10},{10,8},{12,14},{14,12},{16,18},{18,... | collective-permute-start | bytes 786440 | tf_op jit(solution)/shard_map/ppermute | solution.py:65
  249.6 18.9 %all-to-all-start.1 = ((bf16[16,16,1024]{2,1,0:T(8,128)(2,1)}), bf16[16,16,1024]{2,1,0:T(8,128)(2,1)}, u32[]{:S(2)}, u32[]{:S(2)}) async-start(bf16[16,16,1024]{2,1,0:T(8,128)(2,1)} %bitcast.234), calls=%async_computation.1 | async-start | bytes 1048576 | tf_op jit(solution)/shard_map/all_to_all | solution.py:153
  318.2 18.6 %collective-permute-start.48 = (bf16[256,1024]{1,0:T(8,128)(2,1)}, bf16[256,1024]{1,0:T(8,128)(2,1)}, u32[]{:S(2)}, u32[]{:S(2)}) collective-permute-start(bf16[256,1024]{1,0:T(8,128)(2,1)} %get-tuple-element.416.refs_0_.refs_2_), channel_id=1, source_target_pairs={{0,1},{1,0},{2,3},{3,2},{4,5},{5,4},{6,7},{7,6},{8,9},{9,8},{10,11... | collective-permute-start | bytes 1572872 | tf_op jit(solution)/shard_map/ppermute | solution.py:68
  358.1 19.6 %collective-permute-start.55 = (bf16[1024,1024]{1,0:T(8,128)(2,1)S(1)}, bf16[1024,1024]{1,0:T(8,128)(2,1)S(1)}, u32[]{:S(2)}, u32[]{:S(2)}) collective-permute-start(bf16[1024,1024]{1,0:T(8,128)(2,1)S(1)} %weight_gradients.10), channel_id=1, source_target_pairs={{0,2},{2,0},{4,6},{6,4},{8,10},{10,8},{12,14},{14,12},{16,18},{18,... | collective-permute-start | bytes 6291464 | tf_op jit(solution)/shard_map/ppermute | solution.py:65
  403.2 31.5 %collective-permute-start.62 = (bf16[1024,2048]{1,0:T(8,128)(2,1)}, bf16[1024,2048]{1,0:T(8,128)(2,1)}, u32[]{:S(2)}, u32[]{:S(2)}) collective-permute-start(bf16[1024,2048]{1,0:T(8,128)(2,1)} %weight_gradients.12), channel_id=1, source_target_pairs={{0,2},{2,0},{4,6},{6,4},{8,10},{10,8},{12,14},{14,12},{16,18},{18,... | collective-permute-start | bytes 12582920 | tf_op jit(solution)/shard_map/ppermute | solution.py:65
  422.6 23.4 %all-to-all-start.2 = ((bf16[16,16,1024]{2,1,0:T(8,128)(2,1)}), bf16[16,16,1024]{2,1,0:T(8,128)(2,1)}, u32[]{:S(2)}, u32[]{:S(2)}) async-start(bf16[16,16,1024]{2,1,0:T(8,128)(2,1)} %bitcast.233), calls=%async_computation.2 | async-start | bytes 1048576 | tf_op jit(solution)/shard_map/all_to_all | solution.py:153
  444.6 27.9 %collective-permute-start.65 = (bf16[256,1024]{1,0:T(8,128)(2,1)S(1)}, bf16[256,1024]{1,0:T(8,128)(2,1)}, u32[]{:S(2)}, u32[]{:S(2)}) collective-permute-start(bf16[256,1024]{1,0:T(8,128)(2,1)S(1)} %add_convert_fusion.2.refs_0_.refs_2_), channel_id=1, source_target_pairs={{0,1},{1,0},{2,3},{3,2},{4,5},{5,4},{6,7},{7,6},{8,9},{9,8},{10,11... | collective-permute-start | bytes 1572872 | tf_op jit(solution)/shard_map/ppermute | solution.py:68
  452.8 19.7 %collective-permute-start.66 = (bf16[128,1024]{1,0:T(8,128)(2,1)}, bf16[128,1024]{1,0:T(8,128)(2,1)}, u32[]{:S(2)}, u32[]{:S(2)}) collective-permute-start(bf16[128,1024]{1,0:T(8,128)(2,1)} %get-tuple-element.294), channel_id=1, source_target_pairs={{0,8},{2,6},{4,0},{6,14},{8,16},{10,2},{12,4},{14,22},{16,24},{18,... | collective-permute-start | bytes 786440 | tf_op jit(solution)/shard_map/ppermute | solution.py:62
  485.2 20.9 %collective-permute-start.71 = (bf16[1024,1024]{1,0:T(8,128)(2,1)}, bf16[1024,1024]{1,0:T(8,128)(2,1)}, u32[]{:S(2)}, u32[]{:S(2)}) collective-permute-start(bf16[1024,1024]{1,0:T(8,128)(2,1)} %weight_gradients.14), channel_id=1, source_target_pairs={{0,2},{2,0},{4,6},{6,4},{8,10},{10,8},{12,14},{14,12},{16,18},{18,... | collective-permute-start | bytes 6291464 | tf_op jit(solution)/shard_map/ppermute | solution.py:65
  487.8 18.3 %collective-permute-start.69 = (bf16[128,2048]{1,0:T(8,128)(2,1)}, bf16[128,2048]{1,0:T(8,128)(2,1)}, u32[]{:S(2)}, u32[]{:S(2)}) collective-permute-start(bf16[128,2048]{1,0:T(8,128)(2,1)} %get-tuple-element.403), channel_id=1, source_target_pairs={{8,0},{6,2},{0,4},{14,6},{16,8},{2,10},{4,12},{22,14},{24,16},{10,... | collective-permute-start | bytes 1572872 | tf_op jit(solution)/shard_map/ppermute | solution.py:62
  490.8 39.7 %collective-permute-start.93 = (bf16[64,2048]{1,0:T(8,128)(2,1)}, bf16[64,2048]{1,0:T(8,128)(2,1)}, u32[]{:S(2)}, u32[]{:S(2)}) collective-permute-start(bf16[64,2048]{1,0:T(8,128)(2,1)} %dynamic-slice_convert_fusion), channel_id=1, source_target_pairs={{0,2},{2,0},{4,6},{6,4},{8,10},{10,8},{12,14},{14,12},{16,18},{18,... | collective-permute-start | bytes 786440 | tf_op jit(solution)/shard_map/ppermute | solution.py:65
  517.6 20.3 %collective-permute-start.75 = (bf16[128,2048]{1,0:T(8,128)(2,1)}, bf16[128,2048]{1,0:T(8,128)(2,1)S(1)}, u32[]{:S(2)}, u32[]{:S(2)}) collective-permute-start(bf16[128,2048]{1,0:T(8,128)(2,1)} %get-tuple-element.321), channel_id=1, source_target_pairs={{0,8},{2,6},{4,0},{6,14},{8,16},{10,2},{12,4},{14,22},{16,24},{18,... | collective-permute-start | bytes 1572872 | tf_op jit(solution)/shard_map/ppermute | solution.py:62
  518.8 19.1 %collective-permute-start.76 = (bf16[128,2048]{1,0:T(8,128)(2,1)}, bf16[128,2048]{1,0:T(8,128)(2,1)S(1)}, u32[]{:S(2)}, u32[]{:S(2)}) collective-permute-start(bf16[128,2048]{1,0:T(8,128)(2,1)} %get-tuple-element.322), channel_id=1, source_target_pairs={{8,0},{6,2},{0,4},{14,6},{16,8},{2,10},{4,12},{22,14},{24,16},{10,... | collective-permute-start | bytes 1572872 | tf_op jit(solution)/shard_map/ppermute | solution.py:62
  533.6 45.7 %all-to-all-start.3 = ((bf16[16,16,1024]{2,1,0:T(8,128)(2,1)}), bf16[16,16,1024]{2,1,0:T(8,128)(2,1)}, u32[]{:S(2)}, u32[]{:S(2)}) async-start(bf16[16,16,1024]{2,1,0:T(8,128)(2,1)} %bitcast.235), calls=%async_computation.3 | async-start | bytes 1048576 | tf_op jit(solution)/shard_map/all_to_all | solution.py:153
  541.6 25.3 %collective-permute-start.80 = (bf16[128,2048]{1,0:T(8,128)(2,1)S(1)}, bf16[128,2048]{1,0:T(8,128)(2,1)S(1)}, u32[]{:S(2)}, u32[]{:S(2)}) collective-permute-start(bf16[128,2048]{1,0:T(8,128)(2,1)S(1)} %get-tuple-element.330), channel_id=1, source_target_pairs={{0,8},{2,6},{4,0},{6,14},{8,16},{10,2},{12,4},{14,22},{16,24},{18,... | collective-permute-start | bytes 1572872 | tf_op jit(solution)/shard_map/ppermute | solution.py:62
  543.4 23.5 %collective-permute-start.81 = (bf16[128,2048]{1,0:T(8,128)(2,1)S(1)}, bf16[128,2048]{1,0:T(8,128)(2,1)}, u32[]{:S(2)}, u32[]{:S(2)}) collective-permute-start(bf16[128,2048]{1,0:T(8,128)(2,1)S(1)} %get-tuple-element.331), channel_id=1, source_target_pairs={{8,0},{6,2},{0,4},{14,6},{16,8},{2,10},{4,12},{22,14},{24,16},{10,... | collective-permute-start | bytes 1572872 | tf_op jit(solution)/shard_map/ppermute | solution.py:62
  546.4 20.5 %collective-permute-start.78 = (bf16[128,1024]{1,0:T(8,128)(2,1)S(1)}, bf16[128,1024]{1,0:T(8,128)(2,1)S(1)}, u32[]{:S(2)}, u32[]{:S(2)}) collective-permute-start(bf16[128,1024]{1,0:T(8,128)(2,1)S(1)} %get-tuple-element.326), channel_id=1, source_target_pairs={{0,8},{2,6},{4,0},{6,14},{8,16},{10,2},{12,4},{14,22},{16,24},{18,... | collective-permute-start | bytes 786440 | tf_op jit(solution)/shard_map/ppermute | solution.py:62
  548.2 18.7 %collective-permute-start.79 = (bf16[128,1024]{1,0:T(8,128)(2,1)S(1)}, bf16[128,1024]{1,0:T(8,128)(2,1)S(1)}, u32[]{:S(2)}, u32[]{:S(2)}) collective-permute-start(bf16[128,1024]{1,0:T(8,128)(2,1)S(1)} %get-tuple-element.327), channel_id=1, source_target_pairs={{8,0},{6,2},{0,4},{14,6},{16,8},{2,10},{4,12},{22,14},{24,16},{10,... | collective-permute-start | bytes 786440 | tf_op jit(solution)/shard_map/ppermute | solution.py:62
  567.7 18.4 %collective-permute-start.85 = (bf16[128,2048]{1,0:T(8,128)(2,1)S(1)}, bf16[128,2048]{1,0:T(8,128)(2,1)}, u32[]{:S(2)}, u32[]{:S(2)}) collective-permute-start(bf16[128,2048]{1,0:T(8,128)(2,1)S(1)} %add_portions.22), channel_id=1, source_target_pairs={{0,8},{2,6},{4,0},{6,14},{8,16},{10,2},{12,4},{14,22},{16,24},{18,... | collective-permute-start | bytes 1572872 | tf_op jit(solution)/shard_map/ppermute | solution.py:61
  (243 other events, 2245.0 us)

commit v6 on v5

--- a/solution.py
+++ b/solution.py
@@ -14,6 +14,7 @@
 HEAD = D // HEADS
 F32 = jnp.float32
 BF16 = jnp.bfloat16
+SMALL_COST = pl.CostEstimate(flops=1000, bytes_accessed=1000, transcendentals=0)
 
 
 def layer_norm(summed, scaling, offset_vec):
@@ -43,12 +44,13 @@
         order = list(range(0, chips, 2)) + list(range(chips - 1, 0, -2))
         place = {chip: spot for spot, chip in enumerate(order)}
         self.rounds = chips // 2
-        ahead, spots = [], np.zeros((dp_size, chips), np.int32)
+        ahead, spots = [], np.zeros((dp_size, chips + 1), np.int32)
         for device in range(dp_size):
             chip, core = divmod(device, 2)
             way = 1 if core == 0 else -1
             ahead.append((device, 2 * order[(place[chip] + way) % chips] + core))
-            spots[device] = [order[(place[chip] + way * s) % chips] for s in range(chips)]
+            spots[device, :chips] = [order[(place[chip] + way * s) % chips] for s in range(chips)]
+            spots[device, chips] = core
         self.ahead = ahead
         self.back = [(there, here) for here, there in ahead]
         self.swap = [(d, d ^ 1) for d in range(dp_size)]
@@ -103,13 +105,7 @@
         return halves if extra is None else (halves, vector[:, 0, :chip_rows].reshape(-1))
 
     def reduce_ring(self, sums):
-        chip_rows = sums.shape[0] // self.chips
-
-        def portion(ahead):
-            start = self.spot[ahead % self.chips] * chip_rows
-            return lax.dynamic_slice_in_dim(sums, start, chip_rows, 0)
-
-        forth, back = portion(self.rounds), portion(1 + self.rounds)
+        forth, back = add_portions(self.spot, [self.rounds, 1 + self.rounds], [], sums)
         for step in range(1, self.rounds + 1):
             both_ways = step < self.chips - self.rounds
             came = yield self.round(forth, back if both_ways else None)
@@ -120,12 +116,8 @@
             forth = added[0] if step < self.rounds else came[0]
             if both_ways:
                 back = added[1] if len(places) == 2 else came[1]
-        return self.share_rows(portion(0).astype(F32) + forth.astype(F32) + back.astype(F32))
-
-    def share_rows(self, total):
-        mine = self.half(total, 0, True)
-        other = self.partner(self.half(total, 0, False).astype(BF16)).astype(F32)
-        return mine, other
+        mine, other = last_portion(self.spot, [forth, back], sums)
+        return mine, self.partner(other)
 
     def rows_in(self, local_rows):
         if self.tensor_size == 2:
@@ -217,13 +209,11 @@
         kernel,
         out_shape=shapes,
         in_specs=[pl.BlockSpec(memory_space=pltpu.SMEM)]
-        + [pl.BlockSpec(memory_space=pl.ANY)] * count,
+        + [pl.BlockSpec(memory_space=pltpu.HBM)] * count,
         out_specs=[pl.BlockSpec(memory_space=pltpu.VMEM)] * len(shapes),
         scratch_shapes=[pltpu.SemaphoreType.DMA((count, 2))],
         compiler_params=pltpu.CompilerParams(vmem_limit_bytes=16 << 20),
-        cost_estimate=pl.CostEstimate(
-            flops=0, bytes_accessed=4 * count * pieces[0].size, transcendentals=0
-        ),
+        cost_estimate=SMALL_COST,
         name="place_pieces",
     )(spot, *pieces)
     return outs[0], (outs[1] if spare else None)
@@ -282,7 +272,7 @@
         kernel,
         out_shape=shapes,
         compiler_params=pltpu.CompilerParams(vmem_limit_bytes=32 << 20),
-        cost_estimate=pl.CostEstimate(flops=1000, bytes_accessed=1000, transcendentals=0),
+        cost_estimate=SMALL_COST,
         name="attend_forward",
     )(*blocks, weight, bias[None], segment[:, None], segment[None], *(earlier or ()))
     return tuple(outs[:3]), list(outs[3:])
@@ -362,7 +352,7 @@
         out_shape=shapes,
         scratch_shapes=[pltpu.VMEM((rows, inner), BF16)],
         compiler_params=pltpu.CompilerParams(vmem_limit_bytes=32 << 20),
-        cost_estimate=pl.CostEstimate(flops=1000, bytes_accessed=1000, transcendentals=0),
+        cost_estimate=SMALL_COST,
         name="attend_backward",
     )(*blocks, weight, qkv, mixture, log_total, segment[:, None], segment[None], *(earlier or ()))
     return outs[0], outs[1], list(outs[2:])
@@ -441,13 +431,13 @@
         + [wide, wide if forward else jax.ShapeDtypeStruct((1, 2 * hidden), F32)],
         scratch_shapes=[pltpu.VMEM((2, rows, tile), F32)],
         compiler_params=pltpu.CompilerParams(vmem_limit_bytes=32 << 20),
-        cost_estimate=pl.CostEstimate(flops=1000, bytes_accessed=1000, transcendentals=0),
+        cost_estimate=SMALL_COST,
         name="feed_forward" if forward else "feed_backward",
     )(*blocks, *weights, side)
     return list(outs[:-2]), outs[-2], outs[-1]
 
 
-def weight_gradients(pairs, half, came=None):
+def weight_gradients(pairs, half):
     widths = [width for _, _, width in pairs]
     tile = math.gcd(256, *widths)
     if tile % 128:
@@ -455,8 +445,7 @@
             contract_rows(join(blocks), _columns(right, half, width))
             for blocks, right, width in pairs
         ]
-        total = jnp.concatenate(terms, 1)
-        return (total if came is None else total + came.astype(F32)).astype(BF16)
+        return jnp.concatenate(terms, 1).astype(BF16)
     counts = [width // tile for width in widths]
     edge = counts[0]
     blocks_flat = [block for blocks, _, _ in pairs for block in blocks]
@@ -465,9 +454,7 @@
 
     def kernel(*refs):
         lefts, refs = refs[: 2 * per], refs[2 * per :]
-        rights, refs = refs[:2], refs[2:]
-        came_ref = refs[0] if came is not None else None
-        out_ref, turned = refs[-2:]
+        rights, (out_ref, turned) = refs[:2], refs[2:]
         index = pl.program_id(0)
 
         @pl.when(index == 0)
@@ -479,10 +466,7 @@
                     start += left.shape[0]
 
         def run(pair):
-            total = dot(turned[pair], rights[pair][...])
-            if came_ref is not None:
-                total += came_ref[...].astype(F32)
-            out_ref[...] = total.astype(BF16)
+            out_ref[...] = dot(turned[pair], rights[pair][...]).astype(BF16)
 
         @pl.when(index < edge)
         def _():
@@ -506,13 +490,13 @@
         kernel,
         grid=(sum(counts),),
         out_shape=jax.ShapeDtypeStruct((D, sum(widths)), BF16),
-        in_specs=specs + ([over] if came is not None else []),
+        in_specs=specs,
         out_specs=over,
         scratch_shapes=[pltpu.VMEM((2, D, rows), BF16)],
         compiler_params=pltpu.CompilerParams(vmem_limit_bytes=24 << 20),
-        cost_estimate=pl.CostEstimate(flops=1000, bytes_accessed=1000, transcendentals=0),
+        cost_estimate=SMALL_COST,
         name="weight_gradients",
-    )(*blocks_flat, pairs[0][1], pairs[1][1], *(() if came is None else (came,)))
+    )(*blocks_flat, pairs[0][1], pairs[1][1])
 
 
 def _columns(right, half, width):
@@ -520,29 +504,110 @@
 
 
 def add_portions(spot, places, came, sums):
-    count = len(places)
-    came, shape = came[:count], came[0].shape
-
-    def kernel(spots_ref, *refs):
-        ins, parts, outs = refs[:count], refs[count : 2 * count], refs[2 * count :]
-        for value, part, out in zip(ins, parts, outs):
-            out[...] = (value[...].astype(F32) + part[...].astype(F32)).astype(BF16)
-
-    whole = pl.BlockSpec(shape, lambda i, spots_ref: (0, 0))
+    count, given = len(places), min(len(came), len(places))
+    shape = (sums[0].shape[0] // (spot.shape[0] - 1), sums[0].shape[1])
+
+    def kernel(spot_ref, *refs):
+        ins, parts, outs = refs[:given], refs[given:-count], refs[-count:]
+        for i, out in enumerate(outs):
+            total = sum(part[...].astype(F32) for part in parts[i * len(sums) : (i + 1) * len(sums)])
+            if given:
+                total += ins[i][...].astype(F32)
+            out[...] = total.astype(BF16)
+
+    whole = pl.BlockSpec(shape, lambda i, s: (0, 0))
+    portions = [pl.BlockSpec(shape, lambda i, s, k=k: (s[k], 0)) for k in places for _ in sums]
     return pl.pallas_call(
         kernel,
         grid_spec=pltpu.PrefetchScalarGridSpec(
             num_scalar_prefetch=1,
             grid=(1,),
-            in_specs=[whole] * count
-            + [pl.BlockSpec(shape, lambda i, s, k=k: (s[k], 0)) for k in places],
+            in_specs=[whole] * given + portions,
             out_specs=[whole] * count,
         ),
         out_shape=[jax.ShapeDtypeStruct(shape, BF16)] * count,
-        compiler_params=pltpu.CompilerParams(vmem_limit_bytes=16 << 20),
-        cost_estimate=pl.CostEstimate(flops=1000, bytes_accessed=1000, transcendentals=0),
+        compiler_params=pltpu.CompilerParams(vmem_limit_bytes=24 << 20),
+        cost_estimate=SMALL_COST,
         name="add_portions",
-    )(spot, *came, *([sums] * count))
+    )(spot, *came[:given], *(list(sums) * count))
+
+
+def last_portion(spot, came, sums):
+    chips = spot.shape[0] - 1
+    shape = (sums[0].shape[0] // chips, sums[0].shape[1])
+    rows = shape[0] // 2
+
+    def kernel(spot_ref, *refs):
+        ins, (mine, other, total) = refs[:-3], refs[-3:]
+        total[...] = sum(part[...].astype(F32) for part in ins)
+        first = pl.multiple_of(spot_ref[chips] * rows, rows)
+        mine[...] = total[pl.ds(first, rows), :]
+        other[...] = total[pl.ds(rows - first, rows), :].astype(BF16)
+
+    whole = pl.BlockSpec(shape, lambda i, s: (0, 0))
+    half = pl.BlockSpec((rows, shape[1]), lambda i, s: (0, 0))
+    return pl.pallas_call(
+        kernel,
+        grid_spec=pltpu.PrefetchScalarGridSpec(
+            num_scalar_prefetch=1,
+            grid=(1,),
+            in_specs=[whole] * len(came) + [pl.BlockSpec(shape, lambda i, s: (s[0], 0))] * len(sums),
+            out_specs=[half] * 2,
+            scratch_shapes=[pltpu.VMEM(shape, F32)],
+        ),
+        out_shape=[
+            jax.ShapeDtypeStruct((rows, shape[1]), F32),
+            jax.ShapeDtypeStruct((rows, shape[1]), BF16),
+        ],
+        compiler_params=pltpu.CompilerParams(vmem_limit_bytes=24 << 20),
+        cost_estimate=SMALL_COST,
+        name="last_portion",
+    )(spot, *came, *sums)
+
+
+def matrix_outputs(spot, layer, layer_total, attn_pair, feed_pair, filled):
+    rows, inner, hidden = attn_pair[0].shape[0], attn_pair[0].shape[1] // 4, feed_pair[0].shape[1] // 2
+    chips = spot.shape[0] - 1
+    shapes = [
+        (layer_total, 3, rows, 2 * inner),
+        (layer_total, 2 * inner, rows),
+        (layer_total, rows, 2 * hidden),
+        (layer_total, 2 * hidden, rows),
+    ]
+    given = 0 if filled is None else 4
+
+    def kernel(spot_ref, *refs):
+        pairs, (qkv, out, first, second) = (refs[0:2], refs[2:4]), refs[4 + given :]
+        for index in (0, 1):
+            attn, feed = (pair[index][...].astype(F32) for pair in pairs)
+            core = spot_ref[chips] if index == 0 else 1 - spot_ref[chips]
+            heads = pl.ds(pl.multiple_of(core * inner, inner), inner)
+            units = pl.ds(pl.multiple_of(core * hidden, hidden), hidden)
+            for i in range(3):
+                qkv[0, i, :, heads] = attn[:, i * inner : (i + 1) * inner]
+            out[0, heads, :] = attn[:, 3 * inner :].T
+            first[0, :, units] = feed[:, :hidden]
+            second[0, units, :] = feed[:, hidden:].T
+
+    def over(shape):
+        return pl.BlockSpec((1,) + shape[1:], lambda i, s: (layer,) + (0,) * (len(shape) - 1))
+
+    ins = (*attn_pair, *feed_pair)
+    return pl.pallas_call(
+        kernel,
+        grid_spec=pltpu.PrefetchScalarGridSpec(
+            num_scalar_prefetch=1,
+            grid=(1,),
+            in_specs=[pl.BlockSpec(part.shape, lambda i, s: (0, 0)) for part in ins]
+            + [pl.BlockSpec(memory_space=pl.ANY)] * given,
+            out_specs=[over(shape) for shape in shapes],
+        ),
+        out_shape=[jax.ShapeDtypeStruct(shape, F32) for shape in shapes],
+        input_output_aliases={5 + i: i for i in range(given)},
+        compiler_params=pltpu.CompilerParams(vmem_limit_bytes=24 << 20),
+        cost_estimate=SMALL_COST,
+        name="matrix_outputs",
+    )(spot, *ins, *(filled or ()))
 
 
 def join(blocks):
@@ -627,6 +692,7 @@
     for layer in range(layer_total):
         if layer == 0:
             input_blocks = [(rows.astype(F32) + time_row).astype(BF16) for rows in token_blocks]
+            input_blocks[-1] = tick(input_blocks[-1], feed_rings[0])
         else:
             now = (attn_rings[layer], feed_rings[layer])
             input_blocks = wires.rows_in(tick(stream.astype(BF16), *now))
@@ -638,8 +704,6 @@
             bias_q, bias_v = [wires.half(b_qv[layer, i], 0, mine) for i in (0, 1)]
             biases.append(jnp.concatenate([bias_q, jnp.zeros_like(bias_q), bias_v]))
         (qkv, mixture, log_total), _ = attend_forward(input_blocks, attn_w[0], biases[0], segment)
-        if layer == 0:
-            mixture = tick(mixture, feed_rings[0])
         attention = [(qkv, mixture, log_total)]
         part, sums = attend_forward(
             input_blocks, attn_w[1], biases[1], segment, (mixture, attn_w[0])
@@ -649,19 +713,21 @@
         middle = stream + wires.rows_out(sums) + out_bias[layer, 0]
         normed = layer_norm(middle, ln_gain[layer, 0], ln_shift[layer, 0])
         normed_low = tick(normed.astype(BF16), feed_rings[layer], ahead[0])
+        if layer == layer_total - 1:
+            normed_low, upstream = tie(normed_low, upstream)
         normed_blocks = wires.rows_in(normed_low)
         normed_blocks[-1] = tick(normed_blocks[-1], ahead[0])
         feed_w = feed_rings[layer].finish()
         weights.append((attn_w, feed_w))
         bias = jnp.concatenate([wires.half(b_ff1[layer], 0, mine) for mine in both])[None]
         sums, *filled = feed(normed_blocks, feed_w, bias, True)
+        if layer == 0:
+            sums[-1], cotangent = tie(sums[-1], cotangent)
+            upstream = owner_swap(jnp.take(cotangent, back_slot, axis=0))
         sums[-1] = tick(sums[-1], *ahead)
         second_sum = normed + wires.rows_out(sums) + out_bias[layer, 1]
         saved.append((input_blocks, attention, middle, normed_blocks, filled, second_sum))
         stream = layer_norm(second_sum, ln_gain[layer, 1], ln_shift[layer, 1])
-        if layer == 0:
-            stream, cotangent = tie(stream, cotangent)
-            upstream = owner_swap(jnp.take(cotangent, back_slot, axis=0))
 
     encoded_own = stream.astype(BF16)
     gradient = upstream.astype(F32)
@@ -673,30 +739,32 @@
         input_blocks, attention, middle, normed_blocks, (act, slope), second_sum = saved[layer]
         _, pull_second = jax.vjp(layer_norm, second_sum, ln_gain[layer, 1], ln_shift[layer, 1])
         grad_second, gain_second, shift_second = pull_second(gradient)
-        later = (feed_tasks[layer + 1], attn_tasks[layer + 1])
-        branch_blocks = wires.rows_in(tick(grad_second.astype(BF16), later[0]))
+        later_feed, later_attn = feed_tasks[layer + 1], None
+        send = tick(grad_second.astype(BF16), later_feed)
+        if layer == layer_total - 1:
+            send, encoded_own = tie(send, encoded_own)
+            returned_out = owner_swap(encoded_own)
         if attn_sums is not None:
-            branch_blocks[-1], attn_sums = tie(branch_blocks[-1], attn_sums)
-            branch_blocks[-1] = tick(branch_blocks[-1], later[0])
-            attn_tasks[layer + 1] = Task(wires.reduce_ring(attn_sums))
-            later = (later[0], attn_tasks[layer + 1])
+            send, *attn_sums = tie(send, *attn_sums)
+            later_attn = attn_tasks[layer + 1] = Task(wires.reduce_ring(attn_sums))
+        branch_blocks = wires.rows_in(send)
+        branch_blocks[-1] = tick(branch_blocks[-1], later_feed, later_attn)
         sums, grad_pre, hidden_sums = feed(branch_blocks, feed_w, slope, False)
         hidden_sums = hidden_sums[0]
         if layer == layer_total - 1:
-            sums[-1], encoded_own = tie(sums[-1], encoded_own)
-            returned_out = owner_swap(encoded_own)
-        sums[-1] = tick(sums[-1], *later)
+            sums[-1], returned_out = tie(sums[-1], returned_out)
+        sums[-1] = tick(sums[-1], later_attn)
         pairs = [(normed_blocks, grad_pre, hidden), (branch_blocks, act, hidden)]
         came = wires.partner(weight_gradients(pairs, 1))
         grad_normed = grad_second + wires.rows_out(sums)
-        grad_normed, came = tie(grad_normed, came)
+        grad_normed = tick(grad_normed, later_attn)
         _, pull_first = jax.vjp(layer_norm, middle, ln_gain[layer, 0], ln_shift[layer, 0])
         grad_middle, gain_first, shift_first = pull_first(grad_normed)
-        attend_blocks = wires.rows_in(tick(grad_middle.astype(BF16), later[1]))
-        feed_sums = weight_gradients(pairs, 0, came)
-        attend_blocks[-1], feed_sums = tie(attend_blocks[-1], feed_sums)
-        attend_blocks[-1] = tick(attend_blocks[-1], later[1])
+        send, *feed_sums = tie(grad_middle.astype(BF16), weight_gradients(pairs, 0), came)
+        send = tick(send, later_attn)
         feed_tasks[layer] = Task(wires.reduce_ring(feed_sums))
+        attend_blocks = wires.rows_in(send)
+        attend_blocks[-1] = tick(attend_blocks[-1], feed_tasks[layer])
 
         def attn_pairs(half, wide):
             return [(input_blocks, wide, 3 * inner), (attend_blocks, attention[half][1], inner)]
@@ -709,14 +777,12 @@
         own_wide, own_sums, sums = attend_backward(
             attend_blocks, attn_w[0], *attention[0], segment, (wide, attn_w[1])
         )
-        sums[-1] = tick(sums[-1], feed_tasks[layer], later[1])
+        sums[-1] = tick(sums[-1], feed_tasks[layer])
+        attn_sums = [weight_gradients(attn_pairs(0, own_wide), 0), came]
         if layer == 0:
-            attn_sums = weight_gradients(attn_pairs(0, own_wide), 0, came)
-            sums[-1], attn_sums = tie(sums[-1], attn_sums)
+            sums[-1], *attn_sums = tie(sums[-1], *attn_sums)
             attn_tasks[0] = Task(wires.reduce_ring(attn_sums))
         gradient = grad_middle + wires.rows_out(sums)
-        if layer:
-            attn_sums = weight_gradients(attn_pairs(0, own_wide), 0, came)
         qkv_sums = [part.reshape(3, inner)[::2] for part in (own_sums, part_sums)]
         vector_grads[layer] = (
             wires.ordered(qkv_sums[0], qkv_sums[1], 1),
@@ -741,23 +807,27 @@
     flat, shared = vector_task.result
     grad_tokens = jnp.take(returned_grad, deal_slot, axis=0)
     encoded = jnp.take(returned_out, deal_slot, axis=0)
-    matrix_grads = []
-    for attn_pair, feed_pair in reduced:
-        rows = attn_pair[0].shape[0]
-        matrix_grads.append(
-            (
-                wires.ordered(
-                    *(
-                        part[:, : 3 * inner].reshape(rows, 3, inner).transpose(1, 0, 2)
-                        for part in attn_pair
-                    ),
-                    2,
-                ),
-                wires.ordered(*(part[:, 3 * inner :].T for part in attn_pair), 0),
-                wires.ordered(*(part[:, :hidden] for part in feed_pair), 1),
-                wires.ordered(*(part[:, hidden:].T for part in feed_pair), 0),
+    if inner % 128 == 0 and hidden % 128 == 0:
+        matrices = None
+        for layer in reversed(range(layer_total)):
+            matrices = matrix_outputs(wires.spot, layer, layer_total, *reduced[layer], matrices)
+    else:
+        parts = []
+        for attn_pair, feed_pair in reduced:
+            rows = attn_pair[0].shape[0]
+            qkv = [
+                part[:, : 3 * inner].reshape(rows, 3, inner).transpose(1, 0, 2).astype(F32)
+                for part in attn_pair
+            ]
+            parts.append(
+                (
+                    wires.ordered(*qkv, 2),
+                    wires.ordered(*(part[:, 3 * inner :].T.astype(F32) for part in attn_pair), 0),
+                    wires.ordered(*(part[:, :hidden].astype(F32) for part in feed_pair), 1),
+                    wires.ordered(*(part[:, hidden:].T.astype(F32) for part in feed_pair), 0),
+                )
             )
-        )
+        matrices = [jnp.stack([part[i] for part in parts]) for i in range(4)]
     grad_b_qv = flat[: local[0].size].reshape(local[0].shape)
     grad_b_ff1 = flat[local[0].size : border].reshape(local[1].shape)
     time_grad = shared[:D]
@@ -766,15 +836,15 @@
         encoded,
         grad_tokens,
         time_grad,
-        jnp.stack([part[0] for part in matrix_grads]),
+        matrices[0],
         grad_b_qv,
-        jnp.stack([part[1] for part in matrix_grads]),
+        matrices[1],
         rest[0],
         rest[1],
         rest[2],
-        jnp.stack([part[2] for part in matrix_grads]),
+        matrices[2],
         grad_b_ff1,
-        jnp.stack([part[3] for part in matrix_grads]),
+        matrices[3],
     )
 
 

time: 617 us -> 624 us (1.011)
  blocking collectives: 0 us -> 38.4 us
  other arithmetic: 40.4 us -> 19.2 us
  local copies, waits for them, and re-layouts: 84.6 us -> 65.8 us
  waiting for transfers between devices: 226 us -> 236 us
  Pallas kernels: 132 us -> 140 us
    ppermute x24, waiting for transfers between devices: 56 us -> 96.5 us  [round(): lax.ppermute(forth, 'dp', self.ahead)]
    all_to_all x0 -> x2, blocking collectives: none -> 38.4 us  [owner_swap(): return lax.all_to_all(rows, 'dp', split_axis=0, concat_axis=0, tiled=True)]
    ppermute x24, waiting for transfers between devices: 29.8 us -> 12 us  [round(): lax.ppermute(back, 'dp', self.back)]
    ppermute x16, waiting for transfers between devices: 99.5 us -> 88.7 us  [across(): return lax.ppermute(array, 'tensor', [(0, 1), (1, 0)])]
    pallas_call x8, Pallas kernels: 42.9 us -> 33 us  [weight_gradients(): pl.pallas_call(kernel, grid=(sum(counts),), out_shape=jax.ShapeDtypeStruc...]
    ppermute x8, waiting for transfers between devices: 16 us -> 25.1 us  [round(): return [lax.ppermute(forth, 'dp', self.ahead)]]
    pallas_call x0 -> x6, Pallas kernels: none -> 8.89 us  [the longest x4 5.34 us: last_portion(): pl.pallas_call(kernel, grid_spec=pltpu.PrefetchScalarGridSpec(num_scalar_...]
    all_to_all x4 -> x2, starting transfers between devices: 19.3 us -> 10.6 us  [owner_swap(): return lax.all_to_all(rows, 'dp', split_axis=0, concat_axis=0, tiled=True)]
  transfers between devices with their start and end apart: 98 -> 96, of which waited for: 42 -> 42; matrix products, arithmetic and copies ran while one was open for 9% -> 5% of each run, Pallas kernels for 14% -> 14%
where the time goes in v6:
time: 624 us; the launch traced here: 614 us
  waiting for transfers between devices  236 us (38%)
  Pallas kernels  140 us (22%)
  starting transfers between devices  110 us (18%)
  local copies, waits for them, and re-layouts  65.8 us (11%)
  blocking collectives  38.4 us (6%)
  other arithmetic  19.2 us (3%)
    ppermute x24, waiting for transfers between devices, round(): lax.ppermute(forth, 'dp', self.ahead)  96.5 us
    ppermute x16, waiting for transfers between devices, across(): return lax.ppermute(array, 'tensor', [(0, 1), (1, 0)])  88.7 us
    unnamed x295, local copies, waits for them, and re-layouts  47.6 us
    all_to_all x2, blocking collectives, owner_swap(): return lax.all_to_all(rows, 'dp', split_axis=0, concat_axis=0, tiled=True)  38.4 us
    ppermute x24, starting transfers between devices, round(): lax.ppermute(forth, 'dp', self.ahead)  38 us
    pallas_call x8, Pallas kernels, weight_gradients(): pl.pallas_call(kernel, grid=(sum(counts),), out_shape=jax.ShapeDtypeStruc...  33 us
    pallas_call x4, Pallas kernels, feed(): pl.pallas_call(kernel, out_shape=sum_shapes(blocks) + [wide, wide if forw...  30.7 us
    pallas_call x4, Pallas kernels, attend_backward(): pl.pallas_call(kernel, out_shape=shapes, scratch_shapes=[pltpu.VMEM((rows...  26.1 us
  transfers between devices with their start and end apart: 96, of which 42 were waited for; matrix products, arithmetic and copies ran while one was open for 5% of the time, Pallas kernels for 14%

profile of v6, /device:TPU:0, one launch (start us, length us, event | category | flops | bytes accessed | tf_op | source)
XLA Modules:
  0.0 613.9 jit_solution(5992923757266450842)
XLA Ops:
  27.9 11.5 %collective-permute-done.5.refs_2_ = bf16[136,1024]{1,0:T(8,128)(2,1)S(1)} collective-permute-done((bf16[136,1024]{1,0:T(8,128)(2,1)S(1)}, bf16[136,1024]{1,0:T(8,128)(2,1)S(1)}, u32[]{:S(2)}, u32[]{:S(2)}) %collective-permute-start.5) | collective-permute-done | bytes 278560 | tf_op jit(solution)/shard_map/ppermute | solution.py:64
  77.7 10.2 %collective-permute-done.13.refs_2_ = bf16[128,2048]{1,0:T(8,128)(2,1)} collective-permute-done((bf16[128,2048]{1,0:T(8,128)(2,1)}, bf16[128,2048]{1,0:T(8,128)(2,1)}, u32[]{:S(2)}, u32[]{:S(2)}) %collective-permute-start.13) | collective-permute-done | bytes 524320 | tf_op jit(solution)/shard_map/ppermute | solution.py:64
  107.4 10.0 %collective-permute-done.18 = bf16[256,1024]{1,0:T(8,128)(2,1)S(1)} collective-permute-done((bf16[256,1024]{1,0:T(8,128)(2,1)S(1)}, bf16[256,1024]{1,0:T(8,128)(2,1)S(1)}, u32[]{:S(2)}, u32[]{:S(2)}) %collective-permute-start.18) | collective-permute-done | bytes 524320 | tf_op jit(solution)/shard_map/ppermute | solution.py:70
  131.9 6.8 %collective-permute-done.21.refs_1_ = bf16[256,1024]{1,0:T(8,128)(2,1)S(1)} collective-permute-done((bf16[256,1024]{1,0:T(8,128)(2,1)S(1)}, bf16[256,1024]{1,0:T(8,128)(2,1)S(1)}, u32[]{:S(2)}, u32[]{:S(2)}) %collective-permute-start.21) | collective-permute-done | bytes 524320 | tf_op jit(solution)/shard_map/ppermute | solution.py:70
  140.9 7.0 %feed_forward.2 = (f32[256,1024]{1,0:T(8,128)S(1)}, bf16[256,1024]{1,0:T(8,128)(2,1)S(1)}, bf16[512,2048]{1,0:T(8,128)(2,1)S(1)}, bf16[512,2048]{1,0:T(8,128)(2,1)S(1)}) custom-call(bf16[256,1024]{1,0:T(8,128)(2,1)S(1)} %fusion.5.refs_0_, bf16[256,1024]{1,0:T(8,128)(2,1)S(1)} %collective-permute-done.21.refs_1_, bf16[1024,2048]{1,0:T(8,128)(2,1)S(1)} %place_pieces.5.refs_2_, ...), custom_call_target="tpu_custom_call" | custom-call | flops 1000 | bytes 1000 | tf_op jit(solution)/shard_map/feed_forward/pallas_call | solution.py:428
  160.9 6.9 %collective-permute-done.29.refs_3_ = bf16[128,1024]{1,0:T(8,128)(2,1)S(1)} collective-permute-done((bf16[128,1024]{1,0:T(8,128)(2,1)S(1)}, bf16[128,1024]{1,0:T(8,128)(2,1)S(1)}, u32[]{:S(2)}, u32[]{:S(2)}) %collective-permute-start.29) | collective-permute-done | bytes 262176 | tf_op jit(solution)/shard_map/ppermute | solution.py:64
  171.1 11.7 %collective-permute-done.34.refs_4_ = bf16[128,1024]{1,0:T(8,128)(2,1)S(1)} collective-permute-done((bf16[128,1024]{1,0:T(8,128)(2,1)S(1)}, bf16[128,1024]{1,0:T(8,128)(2,1)S(1)}, u32[]{:S(2)}, u32[]{:S(2)}) %collective-permute-start.34) | collective-permute-done | bytes 262176 | tf_op jit(solution)/shard_map/ppermute | solution.py:63
  201.7 10.8 %collective-permute-done.40 = bf16[256,1024]{1,0:T(8,128)(2,1)S(1)} collective-permute-done((bf16[256,1024]{1,0:T(8,128)(2,1)S(1)}, bf16[256,1024]{1,0:T(8,128)(2,1)S(1)}, u32[]{:S(2)}, u32[]{:S(2)}) %collective-permute-start.40) | collective-permute-done | bytes 524320 | tf_op jit(solution)/shard_map/ppermute | solution.py:70
  222.2 18.9 %all_to_all.48 = bf16[16,16,1024]{2,1,0:T(8,128)(2,1)S(1)} all-to-all(bf16[16,16,1024]{2,1,0:T(8,128)(2,1)S(1)} %bitcast.169), channel_id=1, replica_groups=mesh['dp'=16,'tensor'=2] {'dp'}, dimensions={0} | all-to-all | bytes 1048576 | tf_op jit(solution)/shard_map/all_to_all | solution.py:145
  242.6 12.3 %collective-permute-done.42.refs_1_ = bf16[256,1024]{1,0:T(8,128)(2,1)S(1)} collective-permute-done((bf16[256,1024]{1,0:T(8,128)(2,1)S(1)}, bf16[256,1024]{1,0:T(8,128)(2,1)S(1)}, u32[]{:S(2)}, u32[]{:S(2)}) %collective-permute-start.42) | collective-permute-done | bytes 524320 | tf_op jit(solution)/shard_map/ppermute | solution.py:70
  254.9 10.5 %feed_forward.3 = (f32[256,1024]{1,0:T(8,128)S(1)}, bf16[256,1024]{1,0:T(8,128)(2,1)S(1)}, bf16[512,2048]{1,0:T(8,128)(2,1)S(1)}, bf16[512,2048]{1,0:T(8,128)(2,1)S(1)}) custom-call(bf16[256,1024]{1,0:T(8,128)(2,1)S(1)} %copy-done.42, bf16[256,1024]{1,0:T(8,128)(2,1)S(1)} %collective-permute-done.42.refs_1_, bf16[1024,2048]{1,0:T(8,128)(2,1)} %place_pieces.7.refs_2_, ...), custom_call_target="tpu_custom_call" | custom-call | flops 1000 | bytes 1000 | tf_op jit(solution)/shard_map/feed_forward/pallas_call | solution.py:428
  267.0 11.5 %collective-permute-done.44 = bf16[256,1024]{1,0:T(8,128)(2,1)S(1)} collective-permute-done((bf16[256,1024]{1,0:T(8,128)(2,1)S(1)}, bf16[256,1024]{1,0:T(8,128)(2,1)S(1)}, u32[]{:S(2)}, u32[]{:S(2)}) %collective-permute-start.44) | collective-permute-done | bytes 524320 | tf_op jit(solution)/shard_map/ppermute | solution.py:70
  281.9 10.6 %collective-permute-done.45.refs_1_.refs_3_ = bf16[256,1024]{1,0:T(8,128)(2,1)S(1)} collective-permute-done((bf16[256,1024]{1,0:T(8,128)(2,1)S(1)}, bf16[256,1024]{1,0:T(8,128)(2,1)S(1)}, u32[]{:S(2)}, u32[]{:S(2)}) %collective-permute-start.45) | collective-permute-done | bytes 524320 | tf_op jit(solution)/shard_map/ppermute | solution.py:70
  292.5 8.4 %feed_backward.2 = (f32[256,1024]{1,0:T(8,128)S(1)}, bf16[256,1024]{1,0:T(8,128)(2,1)S(1)}, bf16[512,2048]{1,0:T(8,128)(2,1)S(1)}, f32[1,2048]{1,0:T(1,128)S(1)}) custom-call(bf16[256,1024]{1,0:T(8,128)(2,1)S(1)} %get-tuple-element.276.refs_0_.refs_2_, bf16[256,1024]{1,0:T(8,128)(2,1)S(1)} %collective-permute-done.45.refs_1_.refs_3_, ...), custom_call_target="tpu_custom_call" | custom-call | flops 1000 | bytes 1000 | tf_op jit(solution)/shard_map/feed_backward/pallas_call | solution.py:428
  306.2 19.5 %all_to_all.49 = bf16[16,16,1024]{2,1,0:T(8,128)(2,1)} all-to-all(bf16[16,16,1024]{2,1,0:T(8,128)(2,1)S(1)} %bitcast.168), channel_id=1, replica_groups=mesh['dp'=16,'tensor'=2] {'dp'}, dimensions={0} | all-to-all | bytes 1048576 | tf_op jit(solution)/shard_map/all_to_all | solution.py:145
  332.3 7.2 %collective-permute-done.46 = bf16[256,1024]{1,0:T(8,128)(2,1)S(1)} collective-permute-done((bf16[256,1024]{1,0:T(8,128)(2,1)S(1)}, bf16[256,1024]{1,0:T(8,128)(2,1)S(1)}, u32[]{:S(2)}, u32[]{:S(2)}) %collective-permute-start.46) | collective-permute-done | bytes 524320 | tf_op jit(solution)/shard_map/ppermute | solution.py:70
  345.2 11.1 %collective-permute-done.49.refs_0_ = bf16[128,2048]{1,0:T(8,128)(2,1)S(1)} collective-permute-done((bf16[128,2048]{1,0:T(8,128)(2,1)S(1)}, bf16[128,2048]{1,0:T(8,128)(2,1)S(1)}, u32[]{:S(2)}, u32[]{:S(2)}) %collective-permute-start.49) | collective-permute-done | bytes 524320 | tf_op jit(solution)/shard_map/ppermute | solution.py:64
  381.6 7.0 %collective-permute-done.53 = bf16[256,1024]{1,0:T(8,128)(2,1)S(1)} collective-permute-done((bf16[256,1024]{1,0:T(8,128)(2,1)S(1)}, bf16[256,1024]{1,0:T(8,128)(2,1)S(1)}, u32[]{:S(2)}, u32[]{:S(2)}) %collective-permute-start.53) | collective-permute-done | bytes 524320 | tf_op jit(solution)/shard_map/ppermute | solution.py:70
  399.6 7.5 %collective-permute-done.58.refs_0_ = bf16[128,2048]{1,0:T(8,128)(2,1)S(1)} collective-permute-done((bf16[128,2048]{1,0:T(8,128)(2,1)S(1)}, bf16[128,2048]{1,0:T(8,128)(2,1)S(1)}, u32[]{:S(2)}, u32[]{:S(2)}) %collective-permute-start.58) | collective-permute-done | bytes 524320 | tf_op jit(solution)/shard_map/ppermute | solution.py:63
  423.0 6.8 %collective-permute-done.61.refs_0_ = bf16[128,1024]{1,0:T(8,128)(2,1)S(1)} collective-permute-done((bf16[128,1024]{1,0:T(8,128)(2,1)S(1)}, bf16[128,1024]{1,0:T(8,128)(2,1)S(1)}, u32[]{:S(2)}, u32[]{:S(2)}) %collective-permute-start.61) | collective-permute-done | bytes 262176 | tf_op jit(solution)/shard_map/ppermute | solution.py:64
  456.4 9.5 %collective-permute-done.69.refs_0_ = bf16[128,2048]{1,0:T(8,128)(2,1)S(1)} collective-permute-done((bf16[128,2048]{1,0:T(8,128)(2,1)S(1)}, bf16[128,2048]{1,0:T(8,128)(2,1)S(1)}, u32[]{:S(2)}, u32[]{:S(2)}) %collective-permute-start.69) | collective-permute-done | bytes 524320 | tf_op jit(solution)/shard_map/ppermute | solution.py:64
  467.5 6.5 %attend_backward.6 = (bf16[512,768]{1,0:T(8,128)(2,1)S(1)}, f32[1,768]{1,0:T(1,128)S(1)}) custom-call(bf16[256,1024]{1,0:T(8,128)(2,1)S(1)} %add_convert_fusion.2.refs_0_.refs_2_, bf16[256,1024]{1,0:T(8,128)(2,1)S(1)} %collective-permute-done.68.refs_1_.refs_3_, bf16[1024,1024]{1,0:T(8,128)(2,1)} %collective-permute-done.15.refs_2_.refs_9_, ...), custom_call_target="tpu_custom_call" | custom-call | flops 1000 | bytes 1000 | tf_op jit(solution)/shard_map/attend_backward/pallas_call | solution.py:350
  488.9 8.7 %attend_backward.7 = (bf16[512,768]{1,0:T(8,128)(2,1)S(1)}, f32[1,768]{1,0:T(1,128)S(1)}, f32[256,1024]{1,0:T(8,128)S(1)}, bf16[256,1024]{1,0:T(8,128)(2,1)}) custom-call(bf16[256,1024]{1,0:T(8,128)(2,1)S(1)} %copy-done.33, bf16[256,1024]{1,0:T(8,128)(2,1)S(1)} %copy-done.39, bf16[1024,1024]{1,0:T(8,128)(2,1)S(1)} %copy-done.25, ...), custom_call_target="tpu_custom_call" | custom-call | flops 1000 | bytes 1000 | tf_op jit(solution)/shard_map/attend_backward/pallas_call | solution.py:350
  547.3 9.1 %collective-permute-done.83 = f32[19456]{0:T(1024)S(1)} collective-permute-done((f32[19456]{0:T(1024)S(1)}, f32[19456]{0:T(1024)S(1)}, u32[]{:S(2)}, u32[]{:S(2)}) %collective-permute-start.83) | collective-permute-done | bytes 77856 | tf_op jit(solution)/shard_map/ppermute | solution.py:139
  (666 shorter events, 369.9 us)
Async XLA Ops:
  17.4 24.3 %all-to-all-start = ((bf16[16,16,1024]{2,1,0:T(8,128)(2,1)}), bf16[16,16,1024]{2,1,0:T(8,128)(2,1)}, u32[]{:S(2)}, u32[]{:S(2)}) async-start(bf16[16,16,1024]{2,1,0:T(8,128)(2,1)} %bitcast.19), calls=%async_computation | async-start | bytes 1048576 | tf_op jit(solution)/shard_map/all_to_all | solution.py:145
  23.8 15.6 %collective-permute-start.5 = (bf16[136,1024]{1,0:T(8,128)(2,1)S(1)}, bf16[136,1024]{1,0:T(8,128)(2,1)S(1)}, u32[]{:S(2)}, u32[]{:S(2)}) collective-permute-start(bf16[136,1024]{1,0:T(8,128)(2,1)S(1)} %collective-permute-done.2.refs_1_), channel_id=1, source_target_pairs={{0,8},{2,6},{4,0},{6,14},{8,16},{10,2},{12,4},{14,22},{16,24},{18,... | collective-permute-start | bytes 835592 | tf_op jit(solution)/shard_map/ppermute | solution.py:64
  25.7 16.1 %collective-permute-start.6 = (bf16[136,1024]{1,0:T(8,128)(2,1)S(1)}, bf16[136,1024]{1,0:T(8,128)(2,1)S(1)}, u32[]{:S(2)}, u32[]{:S(2)}) collective-permute-start(bf16[136,1024]{1,0:T(8,128)(2,1)S(1)} %collective-permute-done.3.refs_5_), channel_id=1, source_target_pairs={{8,0},{6,2},{0,4},{14,6},{16,8},{2,10},{4,12},{22,14},{24,16},{10,... | collective-permute-start | bytes 835592 | tf_op jit(solution)/shard_map/ppermute | solution.py:64
  25.9 27.2 %collective-permute-start.10 = (bf16[128,2048]{1,0:T(8,128)(2,1)S(1)}, bf16[128,2048]{1,0:T(8,128)(2,1)}, u32[]{:S(2)}, u32[]{:S(2)}) collective-permute-start(bf16[128,2048]{1,0:T(8,128)(2,1)S(1)} %maximum_select_fusion.refs_0_), channel_id=1, source_target_pairs={{8,0},{6,2},{0,4},{14,6},{16,8},{2,10},{4,12},{22,14},{24,16},{10,... | collective-permute-start | bytes 1572872 | tf_op jit(solution)/shard_map/ppermute | solution.py:64
  27.7 25.4 %collective-permute-start.9 = (bf16[128,2048]{1,0:T(8,128)(2,1)S(1)}, bf16[128,2048]{1,0:T(8,128)(2,1)}, u32[]{:S(2)}, u32[]{:S(2)}) collective-permute-start(bf16[128,2048]{1,0:T(8,128)(2,1)S(1)} %maximum_select_fusion.refs_0_), channel_id=1, source_target_pairs={{0,8},{2,6},{4,0},{6,14},{8,16},{10,2},{12,4},{14,22},{16,24},{18,... | collective-permute-start | bytes 1572872 | tf_op jit(solution)/shard_map/ppermute | solution.py:64
  46.8 18.1 %collective-permute-start.11 = (bf16[256,1024]{1,0:T(8,128)(2,1)}, bf16[256,1024]{1,0:T(8,128)(2,1)S(1)}, u32[]{:S(2)}, u32[]{:S(2)}) collective-permute-start(bf16[256,1024]{1,0:T(8,128)(2,1)} %bitcast.20), channel_id=1, source_target_pairs={{0,1},{1,0},{2,3},{3,2},{4,5},{5,4},{6,7},{7,6},{8,9},{9,8},{10,11... | collective-permute-start | bytes 1572872 | tf_op jit(solution)/shard_map/ppermute | solution.py:70
  73.0 22.0 %collective-permute-start.15 = (bf16[1024,1024]{1,0:T(8,128)(2,1)S(1)}, bf16[1024,1024]{1,0:T(8,128)(2,1)}, u32[]{:S(2)}, u32[]{:S(2)}) collective-permute-start(bf16[1024,1024]{1,0:T(8,128)(2,1)S(1)} %get-tuple-element.228.refs_2_.refs_7_), channel_id=1, source_target_pairs={{0,2},{2,0},{4,6},{6,4},{8,10},{10,8},{12,14},{14,12},{16,18},{18,... | collective-permute-start | bytes 6291464 | tf_op jit(solution)/shard_map/ppermute | solution.py:67
  122.4 18.4 %collective-permute-start.24 = (bf16[1024,2048]{1,0:T(8,128)(2,1)S(1)}, bf16[1024,2048]{1,0:T(8,128)(2,1)S(1)}, u32[]{:S(2)}, u32[]{:S(2)}) collective-permute-start(bf16[1024,2048]{1,0:T(8,128)(2,1)S(1)} %place_pieces.5.refs_2_), channel_id=1, source_target_pairs={{0,2},{2,0},{4,6},{6,4},{8,10},{10,8},{12,14},{14,12},{16,18},{18,... | collective-permute-start | bytes 12582920 | tf_op jit(solution)/shard_map/ppermute | solution.py:67
  122.6 18.1 %collective-permute-start.27 = (bf16[64,2048]{1,0:T(8,128)(2,1)S(1)}, bf16[64,2048]{1,0:T(8,128)(2,1)S(1)}, u32[]{:S(2)}, u32[]{:S(2)}) collective-permute-start(bf16[64,2048]{1,0:T(8,128)(2,1)S(1)} %pad_maximum_fusion.1), channel_id=1, source_target_pairs={{0,2},{2,0},{4,6},{6,4},{8,10},{10,8},{12,14},{14,12},{16,18},{18,... | collective-permute-start | bytes 786440 | tf_op jit(solution)/shard_map/ppermute | solution.py:67
  149.5 18.4 %collective-permute-start.31 = (bf16[128,2048]{1,0:T(8,128)(2,1)S(1)}, bf16[128,2048]{1,0:T(8,128)(2,1)S(1)}, u32[]{:S(2)}, u32[]{:S(2)}) collective-permute-start(bf16[128,2048]{1,0:T(8,128)(2,1)S(1)} %maximum_select_fusion.1.refs_0_), channel_id=1, source_target_pairs={{0,8},{2,6},{4,0},{6,14},{8,16},{10,2},{12,4},{14,22},{16,24},{18,... | collective-permute-start | bytes 1572872 | tf_op jit(solution)/shard_map/ppermute | solution.py:64
  150.4 17.4 %collective-permute-start.32 = (bf16[128,2048]{1,0:T(8,128)(2,1)S(1)}, bf16[128,2048]{1,0:T(8,128)(2,1)S(1)}, u32[]{:S(2)}, u32[]{:S(2)}) collective-permute-start(bf16[128,2048]{1,0:T(8,128)(2,1)S(1)} %maximum_select_fusion.1.refs_0_), channel_id=1, source_target_pairs={{8,0},{6,2},{0,4},{14,6},{16,8},{2,10},{4,12},{22,14},{24,16},{10,... | collective-permute-start | bytes 1572872 | tf_op jit(solution)/shard_map/ppermute | solution.py:64
  151.5 16.4 %collective-permute-start.29 = (bf16[128,1024]{1,0:T(8,128)(2,1)S(1)}, bf16[128,1024]{1,0:T(8,128)(2,1)S(1)}, u32[]{:S(2)}, u32[]{:S(2)}) collective-permute-start(bf16[128,1024]{1,0:T(8,128)(2,1)S(1)} %collective-permute-done.25.refs_2_), channel_id=1, source_target_pairs={{0,8},{2,6},{4,0},{6,14},{8,16},{10,2},{12,4},{14,22},{16,24},{18,... | collective-permute-start | bytes 786440 | tf_op jit(solution)/shard_map/ppermute | solution.py:64
  152.5 15.4 %collective-permute-start.30 = (bf16[128,1024]{1,0:T(8,128)(2,1)S(1)}, bf16[128,1024]{1,0:T(8,128)(2,1)S(1)}, u32[]{:S(2)}, u32[]{:S(2)}) collective-permute-start(bf16[128,1024]{1,0:T(8,128)(2,1)S(1)} %collective-permute-done.26.refs_6_), channel_id=1, source_target_pairs={{8,0},{6,2},{0,4},{14,6},{16,8},{2,10},{4,12},{22,14},{24,16},{10,... | collective-permute-start | bytes 786440 | tf_op jit(solution)/shard_map/ppermute | solution.py:64
  217.4 37.5 %collective-permute-start.43 = (bf16[1024,2048]{1,0:T(8,128)(2,1)}, bf16[1024,2048]{1,0:T(8,128)(2,1)}, u32[]{:S(2)}, u32[]{:S(2)}) collective-permute-start(bf16[1024,2048]{1,0:T(8,128)(2,1)} %place_pieces.7.refs_2_), channel_id=1, source_target_pairs={{0,2},{2,0},{4,6},{6,4},{8,10},{10,8},{12,14},{14,12},{16,18},{18,... | collective-permute-start | bytes 12582920 | tf_op jit(solution)/shard_map/ppermute | solution.py:67
  306.1 34.7 %collective-permute-start.47 = (bf16[1024,2048]{1,0:T(8,128)(2,1)S(1)}, bf16[1024,2048]{1,0:T(8,128)(2,1)S(1)}, u32[]{:S(2)}, u32[]{:S(2)}) collective-permute-start(bf16[1024,2048]{1,0:T(8,128)(2,1)S(1)} %weight_gradients.9), channel_id=1, source_target_pairs={{0,2},{2,0},{4,6},{6,4},{8,10},{10,8},{12,14},{14,12},{16,18},{18,... | collective-permute-start | bytes 12582920 | tf_op jit(solution)/shard_map/ppermute | solution.py:67
  357.8 16.5 %collective-permute-start.51 = (bf16[128,2048]{1,0:T(8,128)(2,1)S(1)}, bf16[128,2048]{1,0:T(8,128)(2,1)S(1)}, u32[]{:S(2)}, u32[]{:S(2)}) collective-permute-start(bf16[128,2048]{1,0:T(8,128)(2,1)S(1)} %get-tuple-element.301), channel_id=1, source_target_pairs={{0,8},{2,6},{4,0},{6,14},{8,16},{10,2},{12,4},{14,22},{16,24},{18,... | collective-permute-start | bytes 1572872 | tf_op jit(solution)/shard_map/ppermute | solution.py:64
  367.8 28.4 %collective-permute-start.56 = (bf16[1024,1024]{1,0:T(8,128)(2,1)S(1)}, bf16[1024,1024]{1,0:T(8,128)(2,1)S(1)}, u32[]{:S(2)}, u32[]{:S(2)}) collective-permute-start(bf16[1024,1024]{1,0:T(8,128)(2,1)S(1)} %weight_gradients.11), channel_id=1, source_target_pairs={{0,2},{2,0},{4,6},{6,4},{8,10},{10,8},{12,14},{14,12},{16,18},{18,... | collective-permute-start | bytes 6291464 | tf_op jit(solution)/shard_map/ppermute | solution.py:67
  420.1 27.8 %collective-permute-start.66 = (bf16[1024,2048]{1,0:T(8,128)(2,1)S(1)}, bf16[1024,2048]{1,0:T(8,128)(2,1)S(1)}, u32[]{:S(2)}, u32[]{:S(2)}) collective-permute-start(bf16[1024,2048]{1,0:T(8,128)(2,1)S(1)} %weight_gradients.13), channel_id=1, source_target_pairs={{0,2},{2,0},{4,6},{6,4},{8,10},{10,8},{12,14},{14,12},{16,18},{18,... | collective-permute-start | bytes 12582920 | tf_op jit(solution)/shard_map/ppermute | solution.py:67
  477.7 25.6 %collective-permute-start.73 = (bf16[1024,1024]{1,0:T(8,128)(2,1)}, bf16[1024,1024]{1,0:T(8,128)(2,1)}, u32[]{:S(2)}, u32[]{:S(2)}) collective-permute-start(bf16[1024,1024]{1,0:T(8,128)(2,1)} %weight_gradients.14), channel_id=1, source_target_pairs={{0,2},{2,0},{4,6},{6,4},{8,10},{10,8},{12,14},{14,12},{16,18},{18,... | collective-permute-start | bytes 6291464 | tf_op jit(solution)/shard_map/ppermute | solution.py:67
  516.4 15.7 %collective-permute-start.75 = (bf16[128,1024]{1,0:T(8,128)(2,1)S(1)}, bf16[128,1024]{1,0:T(8,128)(2,1)S(1)}, u32[]{:S(2)}, u32[]{:S(2)}) collective-permute-start(bf16[128,1024]{1,0:T(8,128)(2,1)S(1)} %get-tuple-element.365), channel_id=1, source_target_pairs={{0,8},{2,6},{4,0},{6,14},{8,16},{10,2},{12,4},{14,22},{16,24},{18,... | collective-permute-start | bytes 786440 | tf_op jit(solution)/shard_map/ppermute | solution.py:64
  533.6 22.8 %collective-permute-start.82 = (bf16[128,2048]{1,0:T(8,128)(2,1)S(1)}, bf16[128,2048]{1,0:T(8,128)(2,1)S(1)}, u32[]{:S(2)}, u32[]{:S(2)}) collective-permute-start(bf16[128,2048]{1,0:T(8,128)(2,1)S(1)} %add_portions.29), channel_id=1, source_target_pairs={{0,8},{2,6},{4,0},{6,14},{8,16},{10,2},{12,4},{14,22},{16,24},{18,... | collective-permute-start | bytes 1572872 | tf_op jit(solution)/shard_map/ppermute | solution.py:63
  534.8 57.6 %all-to-all-start.3 = ((bf16[16,16,1024]{2,1,0:T(8,128)(2,1)}), bf16[16,16,1024]{2,1,0:T(8,128)(2,1)}, u32[]{:S(2)}, u32[]{:S(2)}) async-start(bf16[16,16,1024]{2,1,0:T(8,128)(2,1)} %bitcast.170), calls=%async_computation.3 | async-start | bytes 1048576 | tf_op jit(solution)/shard_map/all_to_all | solution.py:145
  572.8 23.1 %collective-permute-start.87 = (bf16[128,1024]{1,0:T(8,128)(2,1)}, bf16[128,1024]{1,0:T(8,128)(2,1)}, u32[]{:S(2)}, u32[]{:S(2)}) collective-permute-start(bf16[128,1024]{1,0:T(8,128)(2,1)} %add_portions.31), channel_id=1, source_target_pairs={{0,8},{2,6},{4,0},{6,14},{8,16},{10,2},{12,4},{14,22},{16,24},{18,... | collective-permute-start | bytes 786440 | tf_op jit(solution)/shard_map/ppermute | solution.py:63
  574.8 21.1 %collective-permute-start.88 = (f32[19456]{0:T(1024)S(1)}, f32[19456]{0:T(1024)S(1)}, u32[]{:S(2)}, u32[]{:S(2)}) collective-permute-start(f32[19456]{0:T(1024)S(1)} %add.340), channel_id=1, source_target_pairs={{0,16},{2,18},{4,20},{6,22},{8,24},{10,26},{12,28},{14,30},{16,0},... | collective-permute-start | bytes 233480 | tf_op jit(solution)/shard_map/ppermute | solution.py:139
  (219 other events, 2179.3 us)

commit v7 on v6

--- a/solution.py
+++ b/solution.py
@@ -213,7 +213,9 @@
         out_specs=[pl.BlockSpec(memory_space=pltpu.VMEM)] * len(shapes),
         scratch_shapes=[pltpu.SemaphoreType.DMA((count, 2))],
         compiler_params=pltpu.CompilerParams(vmem_limit_bytes=16 << 20),
-        cost_estimate=SMALL_COST,
+        cost_estimate=pl.CostEstimate(
+            flops=0, bytes_accessed=1 << 26, transcendentals=0
+        ),
         name="place_pieces",
     )(spot, *pieces)
     return outs[0], (outs[1] if spare else None)
@@ -713,8 +715,6 @@
         middle = stream + wires.rows_out(sums) + out_bias[layer, 0]
         normed = layer_norm(middle, ln_gain[layer, 0], ln_shift[layer, 0])
         normed_low = tick(normed.astype(BF16), feed_rings[layer], ahead[0])
-        if layer == layer_total - 1:
-            normed_low, upstream = tie(normed_low, upstream)
         normed_blocks = wires.rows_in(normed_low)
         normed_blocks[-1] = tick(normed_blocks[-1], ahead[0])
         feed_w = feed_rings[layer].finish()
@@ -751,9 +751,6 @@
         branch_blocks[-1] = tick(branch_blocks[-1], later_feed, later_attn)
         sums, grad_pre, hidden_sums = feed(branch_blocks, feed_w, slope, False)
         hidden_sums = hidden_sums[0]
-        if layer == layer_total - 1:
-            sums[-1], returned_out = tie(sums[-1], returned_out)
-        sums[-1] = tick(sums[-1], later_attn)
         pairs = [(normed_blocks, grad_pre, hidden), (branch_blocks, act, hidden)]
         came = wires.partner(weight_gradients(pairs, 1))
         grad_normed = grad_second + wires.rows_out(sums)
@@ -761,26 +758,22 @@
         _, pull_first = jax.vjp(layer_norm, middle, ln_gain[layer, 0], ln_shift[layer, 0])
         grad_middle, gain_first, shift_first = pull_first(grad_normed)
         send, *feed_sums = tie(grad_middle.astype(BF16), weight_gradients(pairs, 0), came)
-        send = tick(send, later_attn)
         feed_tasks[layer] = Task(wires.reduce_ring(feed_sums))
         attend_blocks = wires.rows_in(send)
-        attend_blocks[-1] = tick(attend_blocks[-1], feed_tasks[layer])
+        attend_blocks[-1] = tick(attend_blocks[-1], feed_tasks[layer], later_attn)
 
         def attn_pairs(half, wide):
             return [(input_blocks, wide, 3 * inner), (attend_blocks, attention[half][1], inner)]
 
         wide, part_sums, _ = attend_backward(attend_blocks, attn_w[1], *attention[1], segment)
         send = weight_gradients(attn_pairs(1, wide), 1)
-        if layer == 0:
-            wide, send = tie(wide, send)
         came = wires.partner(send)
         own_wide, own_sums, sums = attend_backward(
             attend_blocks, attn_w[0], *attention[0], segment, (wide, attn_w[1])
         )
-        sums[-1] = tick(sums[-1], feed_tasks[layer])
+        sums[-1] = tick(sums[-1], feed_tasks[layer], later_attn)
         attn_sums = [weight_gradients(attn_pairs(0, own_wide), 0), came]
         if layer == 0:
-            sums[-1], *attn_sums = tie(sums[-1], *attn_sums)
             attn_tasks[0] = Task(wires.reduce_ring(attn_sums))
         gradient = grad_middle + wires.rows_out(sums)
         qkv_sums = [part.reshape(3, inner)[::2] for part in (own_sums, part_sums)]
@@ -798,9 +791,7 @@
     flat = jnp.concatenate([part.reshape(-1) for part in local[:2] + [time_grad] + local[2:]])
     border = local[0].size + local[1].size
     vector_task = Task(wires.butterfly(flat, border))
-    final = (attn_tasks[0], feed_tasks[0], vector_task)
-    while not all(task.done for task in final):
-        tick((), *final)
+    vector_task.finish()
     reduced = [
         (attn_tasks[layer].finish(), feed_tasks[layer].finish()) for layer in range(layer_total)
     ]

time: 624 us -> 594 us (0.952)
  blocking collectives: 38.4 us -> 0 us
  Pallas kernels: 140 us -> 150 us
  waiting for transfers between devices: 236 us -> 226 us
  other arithmetic: 19.2 us -> 26.8 us
    all_to_all x2 -> x0, blocking collectives: 38.4 us -> none  [owner_swap(): return lax.all_to_all(rows, 'dp', split_axis=0, concat_axis=0, tiled=True)]
    ppermute x24, waiting for transfers between devices: 96.5 us -> 58.5 us  [round(): lax.ppermute(forth, 'dp', self.ahead)]
    ppermute x16, waiting for transfers between devices: 88.7 us -> 108 us  [across(): return lax.ppermute(array, 'tensor', [(0, 1), (1, 0)])]
    pallas_call x16, Pallas kernels: 17.7 us -> 27.9 us  [add_portions(): pl.pallas_call(kernel, grid_spec=pltpu.PrefetchScalarGridSpec(num_scalar_...]
    ppermute x24, waiting for transfers between devices: 12 us -> 21.2 us  [round(): lax.ppermute(back, 'dp', self.back)]
    all_to_all x2 -> x4, starting transfers between devices: 10.6 us -> 19.4 us  [owner_swap(): return lax.all_to_all(rows, 'dp', split_axis=0, concat_axis=0, tiled=True)]
    ppermute x24, starting transfers between devices: 17.8 us -> 26.6 us  [round(): lax.ppermute(back, 'dp', self.back)]
    all_to_all x2 -> x4, waiting for transfers between devices: 0.01 us -> 7.62 us  [owner_swap(): return lax.all_to_all(rows, 'dp', split_axis=0, concat_axis=0, tiled=True)]
  transfers between devices with their start and end apart: 96 -> 98, of which waited for: 42 -> 42; matrix products, arithmetic and copies ran while one was open for 5% -> 7% of each run, Pallas kernels for 14% -> 19%
where the time goes in v7:
time: 594 us; the launch traced here: 583 us
  waiting for transfers between devices  226 us (38%)
  Pallas kernels  150 us (25%)
  starting transfers between devices  112 us (19%)
  local copies, waits for them, and re-layouts  64.3 us (11%)
  other arithmetic  26.8 us (5%)
    ppermute x16, waiting for transfers between devices, across(): return lax.ppermute(array, 'tensor', [(0, 1), (1, 0)])  108 us
    ppermute x24, waiting for transfers between devices, round(): lax.ppermute(forth, 'dp', self.ahead)  58.5 us
    unnamed x291, local copies, waits for them, and re-layouts  44.2 us
    pallas_call x8, Pallas kernels, weight_gradients(): pl.pallas_call(kernel, grid=(sum(counts),), out_shape=jax.ShapeDtypeStruc...  36.1 us
    ppermute x24, starting transfers between devices, round(): lax.ppermute(forth, 'dp', self.ahead)  30.5 us
    pallas_call x16, Pallas kernels, add_portions(): pl.pallas_call(kernel, grid_spec=pltpu.PrefetchScalarGridSpec(num_scalar_...  27.9 us
    ppermute x24, starting transfers between devices, round(): lax.ppermute(back, 'dp', self.back)  26.6 us
    pallas_call x4, Pallas kernels, attend_backward(): pl.pallas_call(kernel, out_shape=shapes, scratch_shapes=[pltpu.VMEM((rows...  26.2 us
  transfers between devices with their start and end apart: 98, of which 42 were waited for; matrix products, arithmetic and copies ran while one was open for 7% of the time, Pallas kernels for 19%

profile of v7, /device:TPU:0, one launch (start us, length us, event | category | flops | bytes accessed | tf_op | source)
XLA Modules:
  0.0 583.0 jit_solution(1353619361456762479)
XLA Ops:
  8.7 6.3 %collective-permute-done.3.refs_5_ = bf16[136,1024]{1,0:T(8,128)(2,1)S(1)} collective-permute-done((bf16[136,1024]{1,0:T(8,128)(2,1)S(1)}, bf16[136,1024]{1,0:T(8,128)(2,1)S(1)}, u32[]{:S(2)}, u32[]{:S(2)}) %collective-permute-start.3) | collective-permute-done | bytes 278560 | tf_op jit(solution)/shard_map/ppermute | solution.py:64
  17.8 6.4 %all-to-all-start = ((bf16[16,16,1024]{2,1,0:T(8,128)(2,1)}), bf16[16,16,1024]{2,1,0:T(8,128)(2,1)}, u32[]{:S(2)}, u32[]{:S(2)}) async-start(bf16[16,16,1024]{2,1,0:T(8,128)(2,1)} %bitcast.19), calls=%async_computation | async-start | bytes 1048576 | tf_op jit(solution)/shard_map/all_to_all | solution.py:145
  28.3 11.5 %collective-permute-done.5.refs_2_ = bf16[136,1024]{1,0:T(8,128)(2,1)S(1)} collective-permute-done((bf16[136,1024]{1,0:T(8,128)(2,1)S(1)}, bf16[136,1024]{1,0:T(8,128)(2,1)S(1)}, u32[]{:S(2)}, u32[]{:S(2)}) %collective-permute-start.5) | collective-permute-done | bytes 278560 | tf_op jit(solution)/shard_map/ppermute | solution.py:64
  81.0 10.0 %collective-permute-done.13.refs_2_ = bf16[128,2048]{1,0:T(8,128)(2,1)} collective-permute-done((bf16[128,2048]{1,0:T(8,128)(2,1)}, bf16[128,2048]{1,0:T(8,128)(2,1)}, u32[]{:S(2)}, u32[]{:S(2)}) %collective-permute-start.13) | collective-permute-done | bytes 524320 | tf_op jit(solution)/shard_map/ppermute | solution.py:64
  110.6 10.0 %collective-permute-done.18 = bf16[256,1024]{1,0:T(8,128)(2,1)S(1)} collective-permute-done((bf16[256,1024]{1,0:T(8,128)(2,1)S(1)}, bf16[256,1024]{1,0:T(8,128)(2,1)S(1)}, u32[]{:S(2)}, u32[]{:S(2)}) %collective-permute-start.18) | collective-permute-done | bytes 524320 | tf_op jit(solution)/shard_map/ppermute | solution.py:70
  135.2 7.0 %collective-permute-done.21.refs_1_ = bf16[256,1024]{1,0:T(8,128)(2,1)S(1)} collective-permute-done((bf16[256,1024]{1,0:T(8,128)(2,1)S(1)}, bf16[256,1024]{1,0:T(8,128)(2,1)S(1)}, u32[]{:S(2)}, u32[]{:S(2)}) %collective-permute-start.21) | collective-permute-done | bytes 524320 | tf_op jit(solution)/shard_map/ppermute | solution.py:70
  144.4 6.9 %feed_forward.2 = (f32[256,1024]{1,0:T(8,128)S(1)}, bf16[256,1024]{1,0:T(8,128)(2,1)S(1)}, bf16[512,2048]{1,0:T(8,128)(2,1)S(1)}, bf16[512,2048]{1,0:T(8,128)(2,1)S(1)}) custom-call(bf16[256,1024]{1,0:T(8,128)(2,1)S(1)} %fusion.5.refs_0_, bf16[256,1024]{1,0:T(8,128)(2,1)S(1)} %collective-permute-done.21.refs_1_, bf16[1024,2048]{1,0:T(8,128)(2,1)S(1)} %place_pieces.5.refs_2_, ...), custom_call_target="tpu_custom_call" | custom-call | flops 1000 | bytes 1000 | tf_op jit(solution)/shard_map/feed_forward/pallas_call | solution.py:430
  157.0 6.3 %collective-permute-done.28 = bf16[256,1024]{1,0:T(8,128)(2,1)S(1)} collective-permute-done((bf16[256,1024]{1,0:T(8,128)(2,1)S(1)}, bf16[256,1024]{1,0:T(8,128)(2,1)S(1)}, u32[]{:S(2)}, u32[]{:S(2)}) %collective-permute-start.28) | collective-permute-done | bytes 524320 | tf_op jit(solution)/shard_map/ppermute | solution.py:70
  174.0 12.1 %collective-permute-done.34.refs_4_ = bf16[128,1024]{1,0:T(8,128)(2,1)S(1)} collective-permute-done((bf16[128,1024]{1,0:T(8,128)(2,1)S(1)}, bf16[128,1024]{1,0:T(8,128)(2,1)S(1)}, u32[]{:S(2)}, u32[]{:S(2)}) %collective-permute-start.34) | collective-permute-done | bytes 262176 | tf_op jit(solution)/shard_map/ppermute | solution.py:63
  202.4 13.2 %collective-permute-done.40 = bf16[256,1024]{1,0:T(8,128)(2,1)S(1)} collective-permute-done((bf16[256,1024]{1,0:T(8,128)(2,1)S(1)}, bf16[256,1024]{1,0:T(8,128)(2,1)S(1)}, u32[]{:S(2)}, u32[]{:S(2)}) %collective-permute-start.40) | collective-permute-done | bytes 524320 | tf_op jit(solution)/shard_map/ppermute | solution.py:70
  218.8 13.7 %collective-permute-done.42.refs_1_ = bf16[256,1024]{1,0:T(8,128)(2,1)S(1)} collective-permute-done((bf16[256,1024]{1,0:T(8,128)(2,1)S(1)}, bf16[256,1024]{1,0:T(8,128)(2,1)S(1)}, u32[]{:S(2)}, u32[]{:S(2)}) %collective-permute-start.42) | collective-permute-done | bytes 524320 | tf_op jit(solution)/shard_map/ppermute | solution.py:70
  232.5 7.7 %feed_forward.3 = (f32[256,1024]{1,0:T(8,128)S(1)}, bf16[256,1024]{1,0:T(8,128)(2,1)}, bf16[512,2048]{1,0:T(8,128)(2,1)S(1)}, bf16[512,2048]{1,0:T(8,128)(2,1)S(1)}) custom-call(bf16[256,1024]{1,0:T(8,128)(2,1)S(1)} %fusion.7.refs_0_, bf16[256,1024]{1,0:T(8,128)(2,1)S(1)} %collective-permute-done.42.refs_1_, bf16[1024,2048]{1,0:T(8,128)(2,1)S(1)} %place_pieces.7.refs_2_, ...), custom_call_target="tpu_custom_call" | custom-call | flops 1000 | bytes 1000 | tf_op jit(solution)/shard_map/feed_forward/pallas_call | solution.py:430
  261.2 7.6 %all-to-all-done.1 = bf16[16,16,1024]{2,1,0:T(8,128)(2,1)} async-done(((bf16[16,16,1024]{2,1,0:T(8,128)(2,1)}), bf16[16,16,1024]{2,1,0:T(8,128)(2,1)}, u32[]{:S(2)}, u32[]{:S(2)}) %all-to-all-start.1) | async-done | bytes 524320 | tf_op jit(solution)/shard_map/all_to_all | solution.py:145
  275.3 12.4 %collective-permute-done.45.refs_1_.refs_3_ = bf16[256,1024]{1,0:T(8,128)(2,1)S(1)} collective-permute-done((bf16[256,1024]{1,0:T(8,128)(2,1)S(1)}, bf16[256,1024]{1,0:T(8,128)(2,1)S(1)}, u32[]{:S(2)}, u32[]{:S(2)}) %collective-permute-start.45) | collective-permute-done | bytes 524320 | tf_op jit(solution)/shard_map/ppermute | solution.py:70
  306.6 7.6 %collective-permute-done.46 = bf16[256,1024]{1,0:T(8,128)(2,1)S(1)} collective-permute-done((bf16[256,1024]{1,0:T(8,128)(2,1)S(1)}, bf16[256,1024]{1,0:T(8,128)(2,1)S(1)}, u32[]{:S(2)}, u32[]{:S(2)}) %collective-permute-start.46) | collective-permute-done | bytes 524320 | tf_op jit(solution)/shard_map/ppermute | solution.py:70
  319.9 9.1 %collective-permute-done.48.refs_1_.refs_3_ = bf16[256,1024]{1,0:T(8,128)(2,1)S(1)} collective-permute-done((bf16[256,1024]{1,0:T(8,128)(2,1)S(1)}, bf16[256,1024]{1,0:T(8,128)(2,1)S(1)}, u32[]{:S(2)}, u32[]{:S(2)}) %collective-permute-start.48) | collective-permute-done | bytes 524320 | tf_op jit(solution)/shard_map/ppermute | solution.py:70
  343.0 6.2 %attend_backward.5 = (bf16[512,768]{1,0:T(8,128)(2,1)S(1)}, f32[1,768]{1,0:T(1,128)S(1)}, f32[256,1024]{1,0:T(8,128)S(1)}, bf16[256,1024]{1,0:T(8,128)(2,1)S(1)}) custom-call(bf16[256,1024]{1,0:T(8,128)(2,1)S(1)} %get-tuple-element.256.refs_0_.refs_2_, bf16[256,1024]{1,0:T(8,128)(2,1)S(1)} %collective-permute-done.48.refs_1_.refs_3_, ...), custom_call_target="tpu_custom_call" | custom-call | flops 1000 | bytes 1000 | tf_op jit(solution)/shard_map/attend_backward/pallas_call | solution.py:352
  355.6 8.0 %collective-permute-done.53 = bf16[256,1024]{1,0:T(8,128)(2,1)S(1)} collective-permute-done((bf16[256,1024]{1,0:T(8,128)(2,1)S(1)}, bf16[256,1024]{1,0:T(8,128)(2,1)S(1)}, u32[]{:S(2)}, u32[]{:S(2)}) %collective-permute-start.53) | collective-permute-done | bytes 524320 | tf_op jit(solution)/shard_map/ppermute | solution.py:70
  375.3 6.3 %collective-permute-done.58.refs_0_ = bf16[128,2048]{1,0:T(8,128)(2,1)S(1)} collective-permute-done((bf16[128,2048]{1,0:T(8,128)(2,1)S(1)}, bf16[128,2048]{1,0:T(8,128)(2,1)S(1)}, u32[]{:S(2)}, u32[]{:S(2)}) %collective-permute-start.58) | collective-permute-done | bytes 524320 | tf_op jit(solution)/shard_map/ppermute | solution.py:63
  392.4 6.5 %weight_gradients.13 = bf16[1024,2048]{1,0:T(8,128)(2,1)} custom-call(bf16[256,1024]{1,0:T(8,128)(2,1)S(1)} %copy-done.45, bf16[256,1024]{1,0:T(8,128)(2,1)S(1)} %copy-done.52, bf16[256,1024]{1,0:T(8,128)(2,1)S(1)} %get-tuple-element.281.refs_0_.refs_2_, bf16[256,1024]{1,0:T(8,128)(2,1)S(1)} %collective-permute-done.57.refs_1_.refs_3_, ...), custom_call_target="tpu_custom_call" | custom-call | flops 1000 | bytes 1000 | tf_op jit(solution)/shard_map/weight_gradients/pallas_call | solution.py:491
  437.5 8.2 %collective-permute-done.65.refs_1_.refs_3_ = bf16[256,1024]{1,0:T(8,128)(2,1)} collective-permute-done((bf16[256,1024]{1,0:T(8,128)(2,1)S(1)}, bf16[256,1024]{1,0:T(8,128)(2,1)}, u32[]{:S(2)}, u32[]{:S(2)}) %collective-permute-start.65) | collective-permute-done | bytes 524320 | tf_op jit(solution)/shard_map/ppermute | solution.py:70
  457.1 6.5 %attend_backward.6 = (bf16[512,768]{1,0:T(8,128)(2,1)S(1)}, f32[1,768]{1,0:T(1,128)S(1)}) custom-call(bf16[256,1024]{1,0:T(8,128)(2,1)S(1)} %copy-done.32, bf16[256,1024]{1,0:T(8,128)(2,1)} %collective-permute-done.65.refs_1_.refs_3_, bf16[1024,1024]{1,0:T(8,128)(2,1)} %collective-permute-done.15.refs_2_.refs_9_, bf16[512,768]{1,0:T(8,128)(2,1)S(1)} %copy-done.79, ...), custom_call_target="tpu_custom_call" | custom-call | flops 1000 | bytes 1000 | tf_op jit(solution)/shard_map/attend_backward/pallas_call | solution.py:352
  471.2 8.8 %attend_backward.7 = (bf16[512,768]{1,0:T(8,128)(2,1)S(1)}, f32[1,768]{1,0:T(1,128)S(1)}, f32[256,1024]{1,0:T(8,128)S(1)}, bf16[256,1024]{1,0:T(8,128)(2,1)}) custom-call(bf16[256,1024]{1,0:T(8,128)(2,1)S(1)} %copy-done.32, bf16[256,1024]{1,0:T(8,128)(2,1)} %collective-permute-done.65.refs_1_.refs_3_, bf16[1024,1024]{1,0:T(8,128)(2,1)S(1)} %copy-done.22, ...), custom_call_target="tpu_custom_call" | custom-call | flops 1000 | bytes 1000 | tf_op jit(solution)/shard_map/attend_backward/pallas_call | solution.py:352
  485.7 9.2 %collective-permute-done.73 = bf16[256,1024]{1,0:T(8,128)(2,1)} collective-permute-done((bf16[256,1024]{1,0:T(8,128)(2,1)}, bf16[256,1024]{1,0:T(8,128)(2,1)}, u32[]{:S(2)}, u32[]{:S(2)}) %collective-permute-start.73) | collective-permute-done | bytes 524320 | tf_op jit(solution)/shard_map/ppermute | solution.py:70
  (666 shorter events, 371.2 us)
Async XLA Ops:
  17.8 24.4 %all-to-all-start = ((bf16[16,16,1024]{2,1,0:T(8,128)(2,1)}), bf16[16,16,1024]{2,1,0:T(8,128)(2,1)}, u32[]{:S(2)}, u32[]{:S(2)}) async-start(bf16[16,16,1024]{2,1,0:T(8,128)(2,1)} %bitcast.19), calls=%async_computation | async-start | bytes 1048576 | tf_op jit(solution)/shard_map/all_to_all | solution.py:145
  26.3 27.1 %collective-permute-start.10 = (bf16[128,2048]{1,0:T(8,128)(2,1)S(1)}, bf16[128,2048]{1,0:T(8,128)(2,1)S(1)}, u32[]{:S(2)}, u32[]{:S(2)}) collective-permute-start(bf16[128,2048]{1,0:T(8,128)(2,1)S(1)} %maximum_select_fusion.refs_0_), channel_id=1, source_target_pairs={{8,0},{6,2},{0,4},{14,6},{16,8},{2,10},{4,12},{22,14},{24,16},{10,... | collective-permute-start | bytes 1572872 | tf_op jit(solution)/shard_map/ppermute | solution.py:64
  28.2 25.2 %collective-permute-start.9 = (bf16[128,2048]{1,0:T(8,128)(2,1)S(1)}, bf16[128,2048]{1,0:T(8,128)(2,1)S(1)}, u32[]{:S(2)}, u32[]{:S(2)}) collective-permute-start(bf16[128,2048]{1,0:T(8,128)(2,1)S(1)} %maximum_select_fusion.refs_0_), channel_id=1, source_target_pairs={{0,8},{2,6},{4,0},{6,14},{8,16},{10,2},{12,4},{14,22},{16,24},{18,... | collective-permute-start | bytes 1572872 | tf_op jit(solution)/shard_map/ppermute | solution.py:64
  47.9 17.4 %collective-permute-start.11 = (bf16[256,1024]{1,0:T(8,128)(2,1)}, bf16[256,1024]{1,0:T(8,128)(2,1)}, u32[]{:S(2)}, u32[]{:S(2)}) collective-permute-start(bf16[256,1024]{1,0:T(8,128)(2,1)} %bitcast.20), channel_id=1, source_target_pairs={{0,1},{1,0},{2,3},{3,2},{4,5},{5,4},{6,7},{7,6},{8,9},{9,8},{10,11... | collective-permute-start | bytes 1572872 | tf_op jit(solution)/shard_map/ppermute | solution.py:70
  76.3 22.9 %collective-permute-start.15 = (bf16[1024,1024]{1,0:T(8,128)(2,1)S(1)}, bf16[1024,1024]{1,0:T(8,128)(2,1)}, u32[]{:S(2)}, u32[]{:S(2)}) collective-permute-start(bf16[1024,1024]{1,0:T(8,128)(2,1)S(1)} %get-tuple-element.203.refs_2_.refs_7_), channel_id=1, source_target_pairs={{0,2},{2,0},{4,6},{6,4},{8,10},{10,8},{12,14},{14,12},{16,18},{18,... | collective-permute-start | bytes 6291464 | tf_op jit(solution)/shard_map/ppermute | solution.py:67
  125.8 18.6 %collective-permute-start.24 = (bf16[1024,2048]{1,0:T(8,128)(2,1)S(1)}, bf16[1024,2048]{1,0:T(8,128)(2,1)S(1)}, u32[]{:S(2)}, u32[]{:S(2)}) collective-permute-start(bf16[1024,2048]{1,0:T(8,128)(2,1)S(1)} %place_pieces.5.refs_2_), channel_id=1, source_target_pairs={{0,2},{2,0},{4,6},{6,4},{8,10},{10,8},{12,14},{14,12},{16,18},{18,... | collective-permute-start | bytes 12582920 | tf_op jit(solution)/shard_map/ppermute | solution.py:67
  126.0 18.3 %collective-permute-start.27 = (bf16[64,2048]{1,0:T(8,128)(2,1)S(1)}, bf16[64,2048]{1,0:T(8,128)(2,1)S(1)}, u32[]{:S(2)}, u32[]{:S(2)}) collective-permute-start(bf16[64,2048]{1,0:T(8,128)(2,1)S(1)} %pad_maximum_fusion.1), channel_id=1, source_target_pairs={{0,2},{2,0},{4,6},{6,4},{8,10},{10,8},{12,14},{14,12},{16,18},{18,... | collective-permute-start | bytes 786440 | tf_op jit(solution)/shard_map/ppermute | solution.py:67
  153.0 17.7 %collective-permute-start.32 = (bf16[128,2048]{1,0:T(8,128)(2,1)S(1)}, bf16[128,2048]{1,0:T(8,128)(2,1)S(1)}, u32[]{:S(2)}, u32[]{:S(2)}) collective-permute-start(bf16[128,2048]{1,0:T(8,128)(2,1)S(1)} %maximum_select_fusion.1.refs_0_), channel_id=1, source_target_pairs={{8,0},{6,2},{0,4},{14,6},{16,8},{2,10},{4,12},{22,14},{24,16},{10,... | collective-permute-start | bytes 1572872 | tf_op jit(solution)/shard_map/ppermute | solution.py:64
  249.9 18.9 %all-to-all-start.1 = ((bf16[16,16,1024]{2,1,0:T(8,128)(2,1)}), bf16[16,16,1024]{2,1,0:T(8,128)(2,1)}, u32[]{:S(2)}, u32[]{:S(2)}) async-start(bf16[16,16,1024]{2,1,0:T(8,128)(2,1)} %bitcast.179), calls=%async_computation.1 | async-start | bytes 1048576 | tf_op jit(solution)/shard_map/all_to_all | solution.py:145
  342.9 28.0 %collective-permute-start.56 = (bf16[1024,1024]{1,0:T(8,128)(2,1)S(1)}, bf16[1024,1024]{1,0:T(8,128)(2,1)S(1)}, u32[]{:S(2)}, u32[]{:S(2)}) collective-permute-start(bf16[1024,1024]{1,0:T(8,128)(2,1)S(1)} %weight_gradients.11), channel_id=1, source_target_pairs={{0,2},{2,0},{4,6},{6,4},{8,10},{10,8},{12,14},{14,12},{16,18},{18,... | collective-permute-start | bytes 6291464 | tf_op jit(solution)/shard_map/ppermute | solution.py:67
  398.9 33.1 %collective-permute-start.64 = (bf16[1024,2048]{1,0:T(8,128)(2,1)}, bf16[1024,2048]{1,0:T(8,128)(2,1)}, u32[]{:S(2)}, u32[]{:S(2)}) collective-permute-start(bf16[1024,2048]{1,0:T(8,128)(2,1)} %weight_gradients.13), channel_id=1, source_target_pairs={{0,2},{2,0},{4,6},{6,4},{8,10},{10,8},{12,14},{14,12},{16,18},{18,... | collective-permute-start | bytes 12582920 | tf_op jit(solution)/shard_map/ppermute | solution.py:67
  398.9 21.3 %collective-permute-start.61 = (bf16[256,1024]{1,0:T(8,128)(2,1)}, bf16[256,1024]{1,0:T(8,128)(2,1)}, u32[]{:S(2)}, u32[]{:S(2)}) collective-permute-start(bf16[256,1024]{1,0:T(8,128)(2,1)} %get-tuple-element.290), channel_id=1, source_target_pairs={{0,1},{1,0},{2,3},{3,2},{4,5},{5,4},{6,7},{7,6},{8,9},{9,8},{10,11... | collective-permute-start | bytes 1572872 | tf_op jit(solution)/shard_map/ppermute | solution.py:70
  401.5 129.9 %all-to-all-start.2 = ((bf16[16,16,1024]{2,1,0:T(8,128)(2,1)}), bf16[16,16,1024]{2,1,0:T(8,128)(2,1)}, u32[]{:S(2)}, u32[]{:S(2)}) async-start(bf16[16,16,1024]{2,1,0:T(8,128)(2,1)} %bitcast.178), calls=%async_computation.2 | async-start | bytes 1048576 | tf_op jit(solution)/shard_map/all_to_all | solution.py:145
  455.0 25.0 %collective-permute-start.70 = (bf16[128,2048]{1,0:T(8,128)(2,1)S(1)}, bf16[128,2048]{1,0:T(8,128)(2,1)S(1)}, u32[]{:S(2)}, u32[]{:S(2)}) collective-permute-start(bf16[128,2048]{1,0:T(8,128)(2,1)S(1)} %get-tuple-element.318), channel_id=1, source_target_pairs={{0,8},{2,6},{4,0},{6,14},{8,16},{10,2},{12,4},{14,22},{16,24},{18,... | collective-permute-start | bytes 1572872 | tf_op jit(solution)/shard_map/ppermute | solution.py:64
  455.5 24.6 %collective-permute-start.71 = (bf16[128,2048]{1,0:T(8,128)(2,1)S(1)}, bf16[128,2048]{1,0:T(8,128)(2,1)S(1)}, u32[]{:S(2)}, u32[]{:S(2)}) collective-permute-start(bf16[128,2048]{1,0:T(8,128)(2,1)S(1)} %get-tuple-element.319), channel_id=1, source_target_pairs={{8,0},{6,2},{0,4},{14,6},{16,8},{2,10},{4,12},{22,14},{24,16},{10,... | collective-permute-start | bytes 1572872 | tf_op jit(solution)/shard_map/ppermute | solution.py:64
  468.5 29.2 %collective-permute-start.79 = (bf16[1024,1024]{1,0:T(8,128)(2,1)}, bf16[1024,1024]{1,0:T(8,128)(2,1)}, u32[]{:S(2)}, u32[]{:S(2)}) collective-permute-start(bf16[1024,1024]{1,0:T(8,128)(2,1)} %weight_gradients.15), channel_id=1, source_target_pairs={{0,2},{2,0},{4,6},{6,4},{8,10},{10,8},{12,14},{14,12},{16,18},{18,... | collective-permute-start | bytes 6291464 | tf_op jit(solution)/shard_map/ppermute | solution.py:67
  515.7 32.0 %collective-permute-start.88 = (bf16[128,2048]{1,0:T(8,128)(2,1)}, bf16[128,2048]{1,0:T(8,128)(2,1)}, u32[]{:S(2)}, u32[]{:S(2)}) collective-permute-start(bf16[128,2048]{1,0:T(8,128)(2,1)} %get-tuple-element.339), channel_id=1, source_target_pairs={{0,8},{2,6},{4,0},{6,14},{8,16},{10,2},{12,4},{14,22},{16,24},{18,... | collective-permute-start | bytes 1572872 | tf_op jit(solution)/shard_map/ppermute | solution.py:64
  519.3 22.3 %collective-permute-start.93 = (bf16[64,2048]{1,0:T(8,128)(2,1)}, bf16[64,2048]{1,0:T(8,128)(2,1)}, u32[]{:S(2)}, u32[]{:S(2)}) collective-permute-start(bf16[64,2048]{1,0:T(8,128)(2,1)} %get-tuple-element.350), channel_id=1, source_target_pairs={{0,2},{2,0},{4,6},{6,4},{8,10},{10,8},{12,14},{14,12},{16,18},{18,... | collective-permute-start | bytes 786440 | tf_op jit(solution)/shard_map/ppermute | solution.py:67
  525.7 17.9 %collective-permute-start.92 = (bf16[64,1024]{1,0:T(8,128)(2,1)}, bf16[64,1024]{1,0:T(8,128)(2,1)S(1)}, u32[]{:S(2)}, u32[]{:S(2)}) collective-permute-start(bf16[64,1024]{1,0:T(8,128)(2,1)} %get-tuple-element.346), channel_id=1, source_target_pairs={{0,2},{2,0},{4,6},{6,4},{8,10},{10,8},{12,14},{14,12},{16,18},{18,... | collective-permute-start | bytes 393224 | tf_op jit(solution)/shard_map/ppermute | solution.py:67
  529.5 26.4 %collective-permute-start.84 = (bf16[128,1024]{1,0:T(8,128)(2,1)}, bf16[128,1024]{1,0:T(8,128)(2,1)}, u32[]{:S(2)}, u32[]{:S(2)}) collective-permute-start(bf16[128,1024]{1,0:T(8,128)(2,1)} %get-tuple-element.333), channel_id=1, source_target_pairs={{0,8},{2,6},{4,0},{6,14},{8,16},{10,2},{12,4},{14,22},{16,24},{18,... | collective-permute-start | bytes 786440 | tf_op jit(solution)/shard_map/ppermute | solution.py:64
  531.4 38.9 %all-to-all-start.3 = ((bf16[16,16,1024]{2,1,0:T(8,128)(2,1)}), bf16[16,16,1024]{2,1,0:T(8,128)(2,1)}, u32[]{:S(2)}, u32[]{:S(2)}) async-start(bf16[16,16,1024]{2,1,0:T(8,128)(2,1)} %bitcast.180), calls=%async_computation.3 | async-start | bytes 1048576 | tf_op jit(solution)/shard_map/all_to_all | solution.py:145
  536.4 22.0 %collective-permute-start.78 = (f32[13312]{0:T(1024)}, f32[13312]{0:T(1024)}, u32[]{:S(2)}, u32[]{:S(2)}) collective-permute-start(f32[13312]{0:T(1024)} %slice.293), channel_id=1, source_target_pairs={{0,1},{1,0},{2,3},{3,2},{4,5},{5,4},{6,7},{7,6},{8,9},{9,8},{10,11... | collective-permute-start | bytes 159752 | tf_op jit(solution)/shard_map/ppermute | solution.py:139
  541.5 20.2 %collective-permute-start.90 = (bf16[128,2048]{1,0:T(8,128)(2,1)}, bf16[128,2048]{1,0:T(8,128)(2,1)}, u32[]{:S(2)}, u32[]{:S(2)}) collective-permute-start(bf16[128,2048]{1,0:T(8,128)(2,1)} %get-tuple-element.340), channel_id=1, source_target_pairs={{8,0},{6,2},{0,4},{14,6},{16,8},{2,10},{4,12},{22,14},{24,16},{10,... | collective-permute-start | bytes 1572872 | tf_op jit(solution)/shard_map/ppermute | solution.py:64
  554.1 19.7 %collective-permute-start.86 = (bf16[128,1024]{1,0:T(8,128)(2,1)}, bf16[128,1024]{1,0:T(8,128)(2,1)}, u32[]{:S(2)}, u32[]{:S(2)}) collective-permute-start(bf16[128,1024]{1,0:T(8,128)(2,1)} %get-tuple-element.334), channel_id=1, source_target_pairs={{8,0},{6,2},{0,4},{14,6},{16,8},{2,10},{4,12},{22,14},{24,16},{10,... | collective-permute-start | bytes 786440 | tf_op jit(solution)/shard_map/ppermute | solution.py:64
  (220 other events, 2205.8 us)

commit v8 on v7

--- a/solution.py
+++ b/solution.py
@@ -99,13 +99,19 @@
             came = yield self.round(forth[-1], back[-1] if both_ways else None)
             forth.append(came[0])
             back += came[1:]
-        blocks = [0] + [self.chips - s for s in range(1, len(forth))] + list(range(1, len(back)))
-        whole, vector = place_pieces(self.spot, blocks, forth + back[1:], chip_rows)
+            if step == self.rounds - 1:
+                places = [0] + [-s % self.chips for s in range(1, len(forth))] + list(range(1, len(back)))
+                outs = place_pieces(self.spot, places, forth + back[1:], chip_rows, None)
+        outs = place_pieces(self.spot, [-self.rounds % self.chips], forth[-1:], chip_rows, outs)
+        whole, vector = outs[0], outs[-1]
         halves = (whole, self.partner(whole))
         return halves if extra is None else (halves, vector[:, 0, :chip_rows].reshape(-1))
 
-    def reduce_ring(self, sums):
-        forth, back = add_portions(self.spot, [self.rounds, 1 + self.rounds], [], sums)
+    def first_portions(self, sums):
+        return add_portions(self.spot, [self.rounds, 1 + self.rounds], [], sums)
+
+    def reduce_ring(self, sums, first=None):
+        forth, back = first or self.first_portions(sums)
         for step in range(1, self.rounds + 1):
             both_ways = step < self.chips - self.rounds
             came = yield self.round(forth, back if both_ways else None)
@@ -141,6 +147,10 @@
         return kept, array
 
 
+def pick(rows, index):
+    return rows.at[index].get(mode="promise_in_bounds")
+
+
 def owner_swap(rows):
     return lax.all_to_all(rows, "dp", split_axis=0, concat_axis=0, tiled=True)
 
@@ -176,12 +186,14 @@
     return lax.optimization_barrier(values)
 
 
-def place_pieces(spot, places, pieces, chip_rows):
+def place_pieces(spot, places, pieces, chip_rows, filled):
     count, width = len(pieces), pieces[0].shape[1]
+    chips = spot.shape[0] - 1
     spare = pieces[0].shape[0] - chip_rows
+    given = 0 if filled is None else len(filled)
 
     def kernel(spot_ref, *refs):
-        ins, outs, sems = refs[:count], refs[count:-1], refs[-1]
+        ins, outs, sems = refs[:count], refs[count + given : -1], refs[-1]
         copies = []
         for i, piece in enumerate(ins):
             chip = spot_ref[places[i]]
@@ -202,23 +214,23 @@
         for copy in copies:
             copy.wait()
 
-    shapes = [jax.ShapeDtypeStruct((count * chip_rows, width), BF16)]
+    shapes = [jax.ShapeDtypeStruct((chips * chip_rows, width), BF16)]
     if spare:
-        shapes.append(jax.ShapeDtypeStruct((count, spare, 128), BF16))
-    outs = pl.pallas_call(
+        shapes.append(jax.ShapeDtypeStruct((chips, spare, 128), BF16))
+    return pl.pallas_call(
         kernel,
         out_shape=shapes,
         in_specs=[pl.BlockSpec(memory_space=pltpu.SMEM)]
-        + [pl.BlockSpec(memory_space=pltpu.HBM)] * count,
-        out_specs=[pl.BlockSpec(memory_space=pltpu.VMEM)] * len(shapes),
+        + [pl.BlockSpec(memory_space=pl.ANY)] * (count + given),
+        out_specs=[pl.BlockSpec(memory_space=pl.ANY)] * len(shapes),
         scratch_shapes=[pltpu.SemaphoreType.DMA((count, 2))],
+        input_output_aliases={1 + count + i: i for i in range(given)},
         compiler_params=pltpu.CompilerParams(vmem_limit_bytes=16 << 20),
         cost_estimate=pl.CostEstimate(
             flops=0, bytes_accessed=1 << 26, transcendentals=0
         ),
         name="place_pieces",
-    )(spot, *pieces)
-    return outs[0], (outs[1] if spare else None)
+    )(spot, *pieces, *(filled or ()))
 
 
 def attend_forward(blocks, weight, bias, segment, earlier=None):
@@ -572,9 +584,9 @@
     chips = spot.shape[0] - 1
     shapes = [
         (layer_total, 3, rows, 2 * inner),
-        (layer_total, 2 * inner, rows),
+        (layer_total, rows, 2 * inner),
         (layer_total, rows, 2 * hidden),
-        (layer_total, 2 * hidden, rows),
+        (layer_total, rows, 2 * hidden),
     ]
     given = 0 if filled is None else 4
 
@@ -587,9 +599,9 @@
             units = pl.ds(pl.multiple_of(core * hidden, hidden), hidden)
             for i in range(3):
                 qkv[0, i, :, heads] = attn[:, i * inner : (i + 1) * inner]
-            out[0, heads, :] = attn[:, 3 * inner :].T
+            out[0, :, heads] = attn[:, 3 * inner :]
             first[0, :, units] = feed[:, :hidden]
-            second[0, units, :] = feed[:, hidden:].T
+            second[0, :, units] = feed[:, hidden:]
 
     def over(shape):
         return pl.BlockSpec((1,) + shape[1:], lambda i, s: (layer,) + (0,) * (len(shape) - 1))
@@ -663,24 +675,27 @@
     arrays = (w_qkv, w_out, w_ff1, w_ff2)
     attn_rings, feed_rings = [None] * (layer_total + 1), [None] * (layer_total + 1)
     attn_rings[0], feed_rings[0] = rings(0, arrays, time_piece)
+    for layer in range(1, layer_total):
+        attn_rings[layer], feed_rings[layer] = rings(layer, arrays, None)
+    later = attn_rings[1:-1] + feed_rings[1:-1]
     step = 0
     while not attn_rings[0].done:
-        beside = (attn_rings[0], feed_rings[0] if step % 2 else None)
+        beside = (attn_rings[0], feed_rings[0] if step % 2 or step == 4 else None)
         if step == 1:
             tokens, back_slot = tick((tokens, back_slot), *beside)
-            own_tokens = owner_swap(jnp.take(tokens, back_slot, axis=0))
+            own_tokens = owner_swap(pick(tokens, back_slot))
         elif step == 2:
             own_tokens = tick(own_tokens, *beside)
             token_blocks = wires.rows_in(own_tokens)
         elif step == 4:
             token_blocks[-1] = tick(token_blocks[-1], *beside)
+            token_blocks[-1], *pieces = tie(token_blocks[-1], *(task.pending for task in later))
+            for task, piece in zip(later, pieces):
+                task.pending = piece
         else:
             tick((), *beside)
         step += 1
     attn_w, time_row = attn_rings[0].result
-    time_row, *arrays = tie(time_row, *arrays)
-    for layer in range(1, layer_total):
-        attn_rings[layer], feed_rings[layer] = rings(layer, arrays, None)
     time_row = time_row.astype(F32)
 
     seq_ends = jnp.cumsum(lengths[0])
@@ -694,11 +709,9 @@
     for layer in range(layer_total):
         if layer == 0:
             input_blocks = [(rows.astype(F32) + time_row).astype(BF16) for rows in token_blocks]
-            input_blocks[-1] = tick(input_blocks[-1], feed_rings[0])
         else:
-            now = (attn_rings[layer], feed_rings[layer])
-            input_blocks = wires.rows_in(tick(stream.astype(BF16), *now))
-            input_blocks[-1] = tick(input_blocks[-1], *now)
+            input_blocks = wires.rows_in(stream.astype(BF16))
+            input_blocks[-1] = tick(input_blocks[-1], feed_rings[layer])
             attn_w = attn_rings[layer].finish()
         ahead = (attn_rings[layer + 1], feed_rings[layer + 1])
         biases = []
@@ -711,28 +724,31 @@
             input_blocks, attn_w[1], biases[1], segment, (mixture, attn_w[0])
         )
         attention.append(part)
-        sums[-1] = tick(sums[-1], feed_rings[layer])
-        middle = stream + wires.rows_out(sums) + out_bias[layer, 0]
+        sums[-1] = tick(sums[-1], feed_rings[layer], ahead[0])
+        attended = tick(wires.rows_out(sums), feed_rings[layer], *ahead)
+        middle = stream + attended + out_bias[layer, 0]
         normed = layer_norm(middle, ln_gain[layer, 0], ln_shift[layer, 0])
-        normed_low = tick(normed.astype(BF16), feed_rings[layer], ahead[0])
+        normed_low = normed.astype(BF16)
         normed_blocks = wires.rows_in(normed_low)
-        normed_blocks[-1] = tick(normed_blocks[-1], ahead[0])
+        normed_blocks[-1] = tick(normed_blocks[-1], *ahead)
         feed_w = feed_rings[layer].finish()
         weights.append((attn_w, feed_w))
         bias = jnp.concatenate([wires.half(b_ff1[layer], 0, mine) for mine in both])[None]
         sums, *filled = feed(normed_blocks, feed_w, bias, True)
         if layer == 0:
             sums[-1], cotangent = tie(sums[-1], cotangent)
-            upstream = owner_swap(jnp.take(cotangent, back_slot, axis=0))
-        sums[-1] = tick(sums[-1], *ahead)
-        second_sum = normed + wires.rows_out(sums) + out_bias[layer, 1]
+            upstream = owner_swap(pick(cotangent, back_slot))
+        sums[-1] = tick(sums[-1], ahead[0])
+        arrived = tick(wires.rows_out(sums), *ahead)
+        second_sum = normed + arrived + out_bias[layer, 1]
         saved.append((input_blocks, attention, middle, normed_blocks, filled, second_sum))
         stream = layer_norm(second_sum, ln_gain[layer, 1], ln_shift[layer, 1])
 
     encoded_own = stream.astype(BF16)
     gradient = upstream.astype(F32)
     feed_tasks, attn_tasks = [None] * (layer_total + 1), [None] * (layer_total + 1)
-    attn_sums = None
+    attn_sums, reduced, matrices = None, [None] * layer_total, None
+    direct = inner % 128 == 0 and hidden % 128 == 0
     vector_grads = [None] * layer_total
     for layer in reversed(range(layer_total)):
         attn_w, feed_w = weights[layer]
@@ -774,8 +790,19 @@
         sums[-1] = tick(sums[-1], feed_tasks[layer], later_attn)
         attn_sums = [weight_gradients(attn_pairs(0, own_wide), 0), came]
         if layer == 0:
-            attn_tasks[0] = Task(wires.reduce_ring(attn_sums))
-        gradient = grad_middle + wires.rows_out(sums)
+            first_portions = wires.first_portions(attn_sums)
+        arrived = wires.rows_out(sums)
+        if layer + 1 < layer_total:
+            reduced[layer + 1] = (later_attn.finish(), later_feed.finish())
+            if direct:
+                matrices = matrix_outputs(
+                    wires.spot, layer + 1, layer_total, *reduced[layer + 1], matrices
+                )
+                arrived, matrices = tie(arrived, matrices)
+        if layer == 0:
+            arrived, encoded = tie(arrived, pick(returned_out, deal_slot))
+            attn_tasks[0] = Task(wires.reduce_ring(attn_sums, first_portions))
+        gradient = grad_middle + arrived
         qkv_sums = [part.reshape(3, inner)[::2] for part in (own_sums, part_sums)]
         vector_grads[layer] = (
             wires.ordered(qkv_sums[0], qkv_sums[1], 1),
@@ -792,16 +819,12 @@
     border = local[0].size + local[1].size
     vector_task = Task(wires.butterfly(flat, border))
     vector_task.finish()
-    reduced = [
-        (attn_tasks[layer].finish(), feed_tasks[layer].finish()) for layer in range(layer_total)
-    ]
+    reduced[0] = (attn_tasks[0].finish(), feed_tasks[0].finish())
     flat, shared = vector_task.result
-    grad_tokens = jnp.take(returned_grad, deal_slot, axis=0)
-    encoded = jnp.take(returned_out, deal_slot, axis=0)
-    if inner % 128 == 0 and hidden % 128 == 0:
-        matrices = None
-        for layer in reversed(range(layer_total)):
-            matrices = matrix_outputs(wires.spot, layer, layer_total, *reduced[layer], matrices)
+    grad_tokens = pick(returned_grad, deal_slot)
+    if direct:
+        matrices = matrix_outputs(wires.spot, 0, layer_total, *reduced[0], matrices)
+        matrices = [part.transpose(0, 2, 1) if i % 2 else part for i, part in enumerate(matrices)]
     else:
         parts = []
         for attn_pair, feed_pair in reduced:

time: 594 us -> 579 us (0.975)
  waiting for transfers between devices: 226 us -> 207 us
    ppermute x24, waiting for transfers between devices: 21.2 us -> 35.1 us  [round(): lax.ppermute(back, 'dp', self.back)]
    ppermute x8, waiting for transfers between devices: 24.2 us -> 11.4 us  [round(): return [lax.ppermute(forth, 'dp', self.ahead)]]
    ppermute x24, waiting for transfers between devices: 58.5 us -> 45.6 us  [round(): lax.ppermute(forth, 'dp', self.ahead)]
    ppermute x16, waiting for transfers between devices: 108 us -> 98.8 us  [across(): return lax.ppermute(array, 'tensor', [(0, 1), (1, 0)])]
    unnamed x291 -> x287, local copies, waits for them, and re-layouts: 44.2 us -> 40.3 us
  transfers between devices with their start and end apart: 98 -> 98, of which waited for: 42 -> 41; matrix products, arithmetic and copies ran while one was open for 7% -> 8% of each run, Pallas kernels for 19% -> 20%
where the time goes in v8:
time: 579 us; the launch traced here: 569 us
  waiting for transfers between devices  207 us (36%)
  Pallas kernels  152 us (26%)
  starting transfers between devices  117 us (20%)
  local copies, waits for them, and re-layouts  62.4 us (11%)
  other arithmetic  26.6 us (5%)
    ppermute x16, waiting for transfers between devices, across(): return lax.ppermute(array, 'tensor', [(0, 1), (1, 0)])  98.8 us
    ppermute x24, waiting for transfers between devices, round(): lax.ppermute(forth, 'dp', self.ahead)  45.6 us
    unnamed x287, local copies, waits for them, and re-layouts  40.3 us
    pallas_call x8, Pallas kernels, weight_gradients(): pl.pallas_call(kernel, grid=(sum(counts),), out_shape=jax.ShapeDtypeStruc...  36.3 us
    ppermute x24, waiting for transfers between devices, round(): lax.ppermute(back, 'dp', self.back)  35.1 us
    ppermute x24, starting transfers between devices, round(): lax.ppermute(forth, 'dp', self.ahead)  32.5 us
    pallas_call x16, Pallas kernels, add_portions(): pl.pallas_call(kernel, grid_spec=pltpu.PrefetchScalarGridSpec(num_scalar_...  27.2 us
    pallas_call x4, Pallas kernels, attend_backward(): pl.pallas_call(kernel, out_shape=shapes, scratch_shapes=[pltpu.VMEM((rows...  26.5 us
  transfers between devices with their start and end apart: 98, of which 41 were waited for; matrix products, arithmetic and copies ran while one was open for 8% of the time, Pallas kernels for 20%

profile of v8, /device:TPU:0, one launch (start us, length us, event | category | flops | bytes accessed | tf_op | source)
XLA Modules:
  0.0 569.2 jit_solution(10059504117834617547)
XLA Ops:
  8.9 6.3 %collective-permute-done.3.refs_4_ = bf16[136,1024]{1,0:T(8,128)(2,1)S(1)} collective-permute-done((bf16[136,1024]{1,0:T(8,128)(2,1)S(1)}, bf16[136,1024]{1,0:T(8,128)(2,1)S(1)}, u32[]{:S(2)}, u32[]{:S(2)}) %collective-permute-start.3) | collective-permute-done | bytes 278560 | tf_op jit(solution)/shard_map/ppermute | solution.py:64
  17.8 6.4 %all-to-all-start = ((bf16[16,16,1024]{2,1,0:T(8,128)(2,1)}), bf16[16,16,1024]{2,1,0:T(8,128)(2,1)}, u32[]{:S(2)}, u32[]{:S(2)}) async-start(bf16[16,16,1024]{2,1,0:T(8,128)(2,1)} %bitcast.19), calls=%async_computation | async-start | bytes 1048576 | tf_op jit(solution)/shard_map/all_to_all | solution.py:155
  28.3 11.5 %collective-permute-done.5.refs_2_ = bf16[136,1024]{1,0:T(8,128)(2,1)S(1)} collective-permute-done((bf16[136,1024]{1,0:T(8,128)(2,1)S(1)}, bf16[136,1024]{1,0:T(8,128)(2,1)S(1)}, u32[]{:S(2)}, u32[]{:S(2)}) %collective-permute-start.5) | collective-permute-done | bytes 278560 | tf_op jit(solution)/shard_map/ppermute | solution.py:64
  91.2 5.6 attend_forward.5
  104.2 7.0 %collective-permute-done.20 = bf16[256,1024]{1,0:T(8,128)(2,1)S(1)} collective-permute-done((bf16[256,1024]{1,0:T(8,128)(2,1)S(1)}, bf16[256,1024]{1,0:T(8,128)(2,1)S(1)}, u32[]{:S(2)}, u32[]{:S(2)}) %collective-permute-start.20) | collective-permute-done | bytes 524320 | tf_op jit(solution)/shard_map/ppermute | solution.py:70
  123.2 12.5 %collective-permute-done.26.refs_5_ = bf16[128,1024]{1,0:T(8,128)(2,1)S(1)} collective-permute-done((bf16[128,1024]{1,0:T(8,128)(2,1)S(1)}, bf16[128,1024]{1,0:T(8,128)(2,1)S(1)}, u32[]{:S(2)}, u32[]{:S(2)}) %collective-permute-start.26) | collective-permute-done | bytes 262176 | tf_op jit(solution)/shard_map/ppermute | solution.py:64
  138.0 7.1 %feed_forward.2 = (f32[256,1024]{1,0:T(8,128)S(1)}, bf16[256,1024]{1,0:T(8,128)(2,1)S(1)}, bf16[512,2048]{1,0:T(8,128)(2,1)S(1)}, bf16[512,2048]{1,0:T(8,128)(2,1)S(1)}) custom-call(bf16[256,1024]{1,0:T(8,128)(2,1)S(1)} %fusion.5.refs_0_, bf16[256,1024]{1,0:T(8,128)(2,1)S(1)} %collective-permute-done.24.refs_1_, ...), custom_call_target="tpu_custom_call" | custom-call | flops 1000 | bytes 1000 | tf_op jit(solution)/shard_map/feed_forward/pallas_call | solution.py:442
  150.1 8.1 %collective-permute-done.32 = bf16[256,1024]{1,0:T(8,128)(2,1)S(1)} collective-permute-done((bf16[256,1024]{1,0:T(8,128)(2,1)S(1)}, bf16[256,1024]{1,0:T(8,128)(2,1)S(1)}, u32[]{:S(2)}, u32[]{:S(2)}) %collective-permute-start.32) | collective-permute-done | bytes 524320 | tf_op jit(solution)/shard_map/ppermute | solution.py:70
  167.2 10.8 %collective-permute-done.36.refs_1_ = bf16[256,1024]{1,0:T(8,128)(2,1)S(1)} collective-permute-done((bf16[256,1024]{1,0:T(8,128)(2,1)S(1)}, bf16[256,1024]{1,0:T(8,128)(2,1)S(1)}, u32[]{:S(2)}, u32[]{:S(2)}) %collective-permute-start.36) | collective-permute-done | bytes 524320 | tf_op jit(solution)/shard_map/ppermute | solution.py:70
  193.5 13.7 %collective-permute-done.41 = bf16[256,1024]{1,0:T(8,128)(2,1)S(1)} collective-permute-done((bf16[256,1024]{1,0:T(8,128)(2,1)S(1)}, bf16[256,1024]{1,0:T(8,128)(2,1)S(1)}, u32[]{:S(2)}, u32[]{:S(2)}) %collective-permute-start.41) | collective-permute-done | bytes 524320 | tf_op jit(solution)/shard_map/ppermute | solution.py:70
  208.9 12.9 %collective-permute-done.42.refs_1_ = bf16[256,1024]{1,0:T(8,128)(2,1)S(1)} collective-permute-done((bf16[256,1024]{1,0:T(8,128)(2,1)S(1)}, bf16[256,1024]{1,0:T(8,128)(2,1)S(1)}, u32[]{:S(2)}, u32[]{:S(2)}) %collective-permute-start.42) | collective-permute-done | bytes 524320 | tf_op jit(solution)/shard_map/ppermute | solution.py:70
  221.9 7.8 %feed_forward.3 = (f32[256,1024]{1,0:T(8,128)S(1)}, bf16[256,1024]{1,0:T(8,128)(2,1)}, bf16[512,2048]{1,0:T(8,128)(2,1)S(1)}, bf16[512,2048]{1,0:T(8,128)(2,1)S(1)}) custom-call(bf16[256,1024]{1,0:T(8,128)(2,1)S(1)} %fusion.7.refs_0_, bf16[256,1024]{1,0:T(8,128)(2,1)S(1)} %collective-permute-done.42.refs_1_, bf16[1024,2048]{1,0:T(8,128)(2,1)S(1)} %place_pieces.15.refs_2_, ...), custom_call_target="tpu_custom_call" | custom-call | flops 1000 | bytes 1000 | tf_op jit(solution)/shard_map/feed_forward/pallas_call | solution.py:442
  249.8 6.6 %all-to-all-done.1 = bf16[16,16,1024]{2,1,0:T(8,128)(2,1)} async-done(((bf16[16,16,1024]{2,1,0:T(8,128)(2,1)}), bf16[16,16,1024]{2,1,0:T(8,128)(2,1)}, u32[]{:S(2)}, u32[]{:S(2)}) %all-to-all-start.1) | async-done | bytes 524320 | tf_op jit(solution)/shard_map/all_to_all | solution.py:155
  262.9 12.4 %collective-permute-done.45.refs_1_.refs_3_ = bf16[256,1024]{1,0:T(8,128)(2,1)S(1)} collective-permute-done((bf16[256,1024]{1,0:T(8,128)(2,1)S(1)}, bf16[256,1024]{1,0:T(8,128)(2,1)S(1)}, u32[]{:S(2)}, u32[]{:S(2)}) %collective-permute-start.45) | collective-permute-done | bytes 524320 | tf_op jit(solution)/shard_map/ppermute | solution.py:70
  294.2 7.6 %collective-permute-done.46 = bf16[256,1024]{1,0:T(8,128)(2,1)S(1)} collective-permute-done((bf16[256,1024]{1,0:T(8,128)(2,1)S(1)}, bf16[256,1024]{1,0:T(8,128)(2,1)S(1)}, u32[]{:S(2)}, u32[]{:S(2)}) %collective-permute-start.46) | collective-permute-done | bytes 524320 | tf_op jit(solution)/shard_map/ppermute | solution.py:70
  307.5 9.1 %collective-permute-done.48.refs_1_.refs_3_ = bf16[256,1024]{1,0:T(8,128)(2,1)S(1)} collective-permute-done((bf16[256,1024]{1,0:T(8,128)(2,1)S(1)}, bf16[256,1024]{1,0:T(8,128)(2,1)S(1)}, u32[]{:S(2)}, u32[]{:S(2)}) %collective-permute-start.48) | collective-permute-done | bytes 524320 | tf_op jit(solution)/shard_map/ppermute | solution.py:70
  330.6 6.3 %attend_backward.5 = (bf16[512,768]{1,0:T(8,128)(2,1)S(1)}, f32[1,768]{1,0:T(1,128)S(1)}, f32[256,1024]{1,0:T(8,128)S(1)}, bf16[256,1024]{1,0:T(8,128)(2,1)S(1)}) custom-call(bf16[256,1024]{1,0:T(8,128)(2,1)S(1)} %get-tuple-element.257.refs_0_.refs_2_, bf16[256,1024]{1,0:T(8,128)(2,1)S(1)} %collective-permute-done.48.refs_1_.refs_3_, ...), custom_call_target="tpu_custom_call" | custom-call | flops 1000 | bytes 1000 | tf_op jit(solution)/shard_map/attend_backward/pallas_call | solution.py:364
  343.2 8.0 %collective-permute-done.53 = bf16[256,1024]{1,0:T(8,128)(2,1)S(1)} collective-permute-done((bf16[256,1024]{1,0:T(8,128)(2,1)S(1)}, bf16[256,1024]{1,0:T(8,128)(2,1)S(1)}, u32[]{:S(2)}, u32[]{:S(2)}) %collective-permute-start.53) | collective-permute-done | bytes 524320 | tf_op jit(solution)/shard_map/ppermute | solution.py:70
  363.0 6.2 %collective-permute-done.58.refs_0_ = bf16[128,2048]{1,0:T(8,128)(2,1)S(1)} collective-permute-done((bf16[128,2048]{1,0:T(8,128)(2,1)S(1)}, bf16[128,2048]{1,0:T(8,128)(2,1)S(1)}, u32[]{:S(2)}, u32[]{:S(2)}) %collective-permute-start.58) | collective-permute-done | bytes 524320 | tf_op jit(solution)/shard_map/ppermute | solution.py:63
  373.5 5.5 feed_backward.3
  380.1 6.5 %weight_gradients.13 = bf16[1024,2048]{1,0:T(8,128)(2,1)} custom-call(bf16[256,1024]{1,0:T(8,128)(2,1)S(1)} %copy-done.42, bf16[256,1024]{1,0:T(8,128)(2,1)S(1)} %copy-done.49, bf16[256,1024]{1,0:T(8,128)(2,1)S(1)} %get-tuple-element.282.refs_0_.refs_2_, bf16[256,1024]{1,0:T(8,128)(2,1)S(1)} %collective-permute-done.57.refs_1_.refs_3_, ...), custom_call_target="tpu_custom_call" | custom-call | flops 1000 | bytes 1000 | tf_op jit(solution)/shard_map/weight_gradients/pallas_call | solution.py:503
  444.5 6.6 %attend_backward.6 = (bf16[512,768]{1,0:T(8,128)(2,1)S(1)}, f32[1,768]{1,0:T(1,128)S(1)}) custom-call(bf16[256,1024]{1,0:T(8,128)(2,1)S(1)} %copy-done.30, bf16[256,1024]{1,0:T(8,128)(2,1)} %collective-permute-done.65.refs_1_.refs_3_, bf16[1024,1024]{1,0:T(8,128)(2,1)} %collective-permute-done.17.refs_2_.refs_9_, bf16[512,768]{1,0:T(8,128)(2,1)S(1)} %copy-done.80, ...), custom_call_target="tpu_custom_call" | custom-call | flops 1000 | bytes 1000 | tf_op jit(solution)/shard_map/attend_backward/pallas_call | solution.py:364
  463.3 9.0 %attend_backward.7 = (bf16[512,768]{1,0:T(8,128)(2,1)S(1)}, f32[1,768]{1,0:T(1,128)S(1)}, f32[256,1024]{1,0:T(8,128)S(1)}, bf16[256,1024]{1,0:T(8,128)(2,1)}) custom-call(bf16[256,1024]{1,0:T(8,128)(2,1)S(1)} %copy-done.30, bf16[256,1024]{1,0:T(8,128)(2,1)} %collective-permute-done.65.refs_1_.refs_3_, bf16[1024,1024]{1,0:T(8,128)(2,1)S(1)} %copy-done.20, ...), custom_call_target="tpu_custom_call" | custom-call | flops 1000 | bytes 1000 | tf_op jit(solution)/shard_map/attend_backward/pallas_call | solution.py:364
  503.5 6.4 %collective-permute-done.82.refs_0_ = bf16[128,1024]{1,0:T(8,128)(2,1)S(1)} collective-permute-done((bf16[128,1024]{1,0:T(8,128)(2,1)S(1)}, bf16[128,1024]{1,0:T(8,128)(2,1)S(1)}, u32[]{:S(2)}, u32[]{:S(2)}) %collective-permute-start.82) | collective-permute-done | bytes 262176 | tf_op jit(solution)/shard_map/ppermute | solution.py:64
  (652 shorter events, 365.3 us)
Async XLA Ops:
  17.8 24.4 %all-to-all-start = ((bf16[16,16,1024]{2,1,0:T(8,128)(2,1)}), bf16[16,16,1024]{2,1,0:T(8,128)(2,1)}, u32[]{:S(2)}, u32[]{:S(2)}) async-start(bf16[16,16,1024]{2,1,0:T(8,128)(2,1)} %bitcast.19), calls=%async_computation | async-start | bytes 1048576 | tf_op jit(solution)/shard_map/all_to_all | solution.py:155
  26.3 27.1 %collective-permute-start.11 = (bf16[128,2048]{1,0:T(8,128)(2,1)S(1)}, bf16[128,2048]{1,0:T(8,128)(2,1)S(1)}, u32[]{:S(2)}, u32[]{:S(2)}) collective-permute-start(bf16[128,2048]{1,0:T(8,128)(2,1)S(1)} %maximum_select_fusion.refs_0_), channel_id=1, source_target_pairs={{8,0},{6,2},{0,4},{14,6},{16,8},{2,10},{4,12},{22,14},{24,16},{10,... | collective-permute-start | bytes 1572872 | tf_op jit(solution)/shard_map/ppermute | solution.py:64
  28.2 25.2 %collective-permute-start.10 = (bf16[128,2048]{1,0:T(8,128)(2,1)S(1)}, bf16[128,2048]{1,0:T(8,128)(2,1)}, u32[]{:S(2)}, u32[]{:S(2)}) collective-permute-start(bf16[128,2048]{1,0:T(8,128)(2,1)S(1)} %maximum_select_fusion.refs_0_), channel_id=1, source_target_pairs={{0,8},{2,6},{4,0},{6,14},{8,16},{10,2},{12,4},{14,22},{16,24},{18,... | collective-permute-start | bytes 1572872 | tf_op jit(solution)/shard_map/ppermute | solution.py:64
  46.5 28.6 %collective-permute-start.7 = (bf16[256,1024]{1,0:T(8,128)(2,1)}, bf16[256,1024]{1,0:T(8,128)(2,1)}, u32[]{:S(2)}, u32[]{:S(2)}) collective-permute-start(bf16[256,1024]{1,0:T(8,128)(2,1)} %bitcast.20), channel_id=1, source_target_pairs={{0,1},{1,0},{2,3},{3,2},{4,5},{5,4},{6,7},{7,6},{8,9},{9,8},{10,11... | collective-permute-start | bytes 1572872 | tf_op jit(solution)/shard_map/ppermute | solution.py:70
  58.9 18.4 %collective-permute-start.13 = (bf16[128,2048]{1,0:T(8,128)(2,1)}, bf16[128,2048]{1,0:T(8,128)(2,1)}, u32[]{:S(2)}, u32[]{:S(2)}) collective-permute-start(bf16[128,2048]{1,0:T(8,128)(2,1)} %collective-permute-done.10.refs_1_), channel_id=1, source_target_pairs={{0,8},{2,6},{4,0},{6,14},{8,16},{10,2},{12,4},{14,22},{16,24},{18,... | collective-permute-start | bytes 1572872 | tf_op jit(solution)/shard_map/ppermute | solution.py:64
  114.5 23.4 %collective-permute-start.29 = (bf16[1024,2048]{1,0:T(8,128)(2,1)S(1)}, bf16[1024,2048]{1,0:T(8,128)(2,1)S(1)}, u32[]{:S(2)}, u32[]{:S(2)}) collective-permute-start(bf16[1024,2048]{1,0:T(8,128)(2,1)S(1)} %place_pieces.11.refs_2_), channel_id=1, source_target_pairs={{0,2},{2,0},{4,6},{6,4},{8,10},{10,8},{12,14},{14,12},{16,18},{18,... | collective-permute-start | bytes 12582920 | tf_op jit(solution)/shard_map/ppermute | solution.py:67
  117.8 17.9 %collective-permute-start.24 = (bf16[256,1024]{1,0:T(8,128)(2,1)S(1)}, bf16[256,1024]{1,0:T(8,128)(2,1)S(1)}, u32[]{:S(2)}, u32[]{:S(2)}) collective-permute-start(bf16[256,1024]{1,0:T(8,128)(2,1)S(1)} %fusion.5.refs_0_), channel_id=1, source_target_pairs={{0,1},{1,0},{2,3},{3,2},{4,5},{5,4},{6,7},{7,6},{8,9},{9,8},{10,11... | collective-permute-start | bytes 1572872 | tf_op jit(solution)/shard_map/ppermute | solution.py:70
  162.6 23.9 %collective-permute-start.39 = (bf16[1024,1024]{1,0:T(8,128)(2,1)S(1)}, bf16[1024,1024]{1,0:T(8,128)(2,1)S(1)}, u32[]{:S(2)}, u32[]{:S(2)}) collective-permute-start(bf16[1024,1024]{1,0:T(8,128)(2,1)S(1)} %place_pieces.13.refs_2_.refs_7_), channel_id=1, source_target_pairs={{0,2},{2,0},{4,6},{6,4},{8,10},{10,8},{12,14},{14,12},{16,18},{18,... | collective-permute-start | bytes 6291464 | tf_op jit(solution)/shard_map/ppermute | solution.py:67
  192.8 29.0 %collective-permute-start.43 = (bf16[1024,2048]{1,0:T(8,128)(2,1)S(1)}, bf16[1024,2048]{1,0:T(8,128)(2,1)S(1)}, u32[]{:S(2)}, u32[]{:S(2)}) collective-permute-start(bf16[1024,2048]{1,0:T(8,128)(2,1)S(1)} %place_pieces.15.refs_2_), channel_id=1, source_target_pairs={{0,2},{2,0},{4,6},{6,4},{8,10},{10,8},{12,14},{14,12},{16,18},{18,... | collective-permute-start | bytes 12582920 | tf_op jit(solution)/shard_map/ppermute | solution.py:67
  237.5 18.9 %all-to-all-start.1 = ((bf16[16,16,1024]{2,1,0:T(8,128)(2,1)}), bf16[16,16,1024]{2,1,0:T(8,128)(2,1)}, u32[]{:S(2)}, u32[]{:S(2)}) async-start(bf16[16,16,1024]{2,1,0:T(8,128)(2,1)} %bitcast.182), calls=%async_computation.1 | async-start | bytes 1048576 | tf_op jit(solution)/shard_map/all_to_all | solution.py:155
  330.5 28.1 %collective-permute-start.56 = (bf16[1024,1024]{1,0:T(8,128)(2,1)S(1)}, bf16[1024,1024]{1,0:T(8,128)(2,1)S(1)}, u32[]{:S(2)}, u32[]{:S(2)}) collective-permute-start(bf16[1024,1024]{1,0:T(8,128)(2,1)S(1)} %weight_gradients.11), channel_id=1, source_target_pairs={{0,2},{2,0},{4,6},{6,4},{8,10},{10,8},{12,14},{14,12},{16,18},{18,... | collective-permute-start | bytes 6291464 | tf_op jit(solution)/shard_map/ppermute | solution.py:67
  386.5 32.3 %collective-permute-start.64 = (bf16[1024,2048]{1,0:T(8,128)(2,1)}, bf16[1024,2048]{1,0:T(8,128)(2,1)}, u32[]{:S(2)}, u32[]{:S(2)}) collective-permute-start(bf16[1024,2048]{1,0:T(8,128)(2,1)} %weight_gradients.13), channel_id=1, source_target_pairs={{0,2},{2,0},{4,6},{6,4},{8,10},{10,8},{12,14},{14,12},{16,18},{18,... | collective-permute-start | bytes 12582920 | tf_op jit(solution)/shard_map/ppermute | solution.py:67
  386.6 21.3 %collective-permute-start.61 = (bf16[256,1024]{1,0:T(8,128)(2,1)}, bf16[256,1024]{1,0:T(8,128)(2,1)}, u32[]{:S(2)}, u32[]{:S(2)}) collective-permute-start(bf16[256,1024]{1,0:T(8,128)(2,1)} %get-tuple-element.291), channel_id=1, source_target_pairs={{0,1},{1,0},{2,3},{3,2},{4,5},{5,4},{6,7},{7,6},{8,9},{9,8},{10,11... | collective-permute-start | bytes 1572872 | tf_op jit(solution)/shard_map/ppermute | solution.py:70
  389.2 35.2 %all-to-all-start.2 = ((bf16[16,16,1024]{2,1,0:T(8,128)(2,1)}), bf16[16,16,1024]{2,1,0:T(8,128)(2,1)}, u32[]{:S(2)}, u32[]{:S(2)}) async-start(bf16[16,16,1024]{2,1,0:T(8,128)(2,1)} %bitcast.180), calls=%async_computation.2 | async-start | bytes 1048576 | tf_op jit(solution)/shard_map/all_to_all | solution.py:155
  442.1 30.2 %collective-permute-start.70 = (bf16[128,2048]{1,0:T(8,128)(2,1)S(1)}, bf16[128,2048]{1,0:T(8,128)(2,1)S(1)}, u32[]{:S(2)}, u32[]{:S(2)}) collective-permute-start(bf16[128,2048]{1,0:T(8,128)(2,1)S(1)} %get-tuple-element.319), channel_id=1, source_target_pairs={{0,8},{2,6},{4,0},{6,14},{8,16},{10,2},{12,4},{14,22},{16,24},{18,... | collective-permute-start | bytes 1572872 | tf_op jit(solution)/shard_map/ppermute | solution.py:64
  443.4 28.9 %collective-permute-start.71 = (bf16[128,2048]{1,0:T(8,128)(2,1)S(1)}, bf16[128,2048]{1,0:T(8,128)(2,1)S(1)}, u32[]{:S(2)}, u32[]{:S(2)}) collective-permute-start(bf16[128,2048]{1,0:T(8,128)(2,1)S(1)} %get-tuple-element.320), channel_id=1, source_target_pairs={{8,0},{6,2},{0,4},{14,6},{16,8},{2,10},{4,12},{22,14},{24,16},{10,... | collective-permute-start | bytes 1572872 | tf_op jit(solution)/shard_map/ppermute | solution.py:64
  456.1 42.4 %collective-permute-start.81 = (bf16[1024,1024]{1,0:T(8,128)(2,1)}, bf16[1024,1024]{1,0:T(8,128)(2,1)}, u32[]{:S(2)}, u32[]{:S(2)}) collective-permute-start(bf16[1024,1024]{1,0:T(8,128)(2,1)} %weight_gradients.15), channel_id=1, source_target_pairs={{0,2},{2,0},{4,6},{6,4},{8,10},{10,8},{12,14},{14,12},{16,18},{18,... | collective-permute-start | bytes 6291464 | tf_op jit(solution)/shard_map/ppermute | solution.py:67
  459.3 29.4 %collective-permute-start.75 = (bf16[64,2048]{1,0:T(8,128)(2,1)}, bf16[64,2048]{1,0:T(8,128)(2,1)}, u32[]{:S(2)}, u32[]{:S(2)}) collective-permute-start(bf16[64,2048]{1,0:T(8,128)(2,1)} %get-tuple-element.330), channel_id=1, source_target_pairs={{0,2},{2,0},{4,6},{6,4},{8,10},{10,8},{12,14},{14,12},{16,18},{18,... | collective-permute-start | bytes 786440 | tf_op jit(solution)/shard_map/ppermute | solution.py:67
  472.3 23.8 %collective-permute-start.73 = (bf16[256,1024]{1,0:T(8,128)(2,1)}, bf16[256,1024]{1,0:T(8,128)(2,1)}, u32[]{:S(2)}, u32[]{:S(2)}) collective-permute-start(bf16[256,1024]{1,0:T(8,128)(2,1)} %get-tuple-element.322), channel_id=1, source_target_pairs={{0,1},{1,0},{2,3},{3,2},{4,5},{5,4},{6,7},{7,6},{8,9},{9,8},{10,11... | collective-permute-start | bytes 1572872 | tf_op jit(solution)/shard_map/ppermute | solution.py:70
  488.7 55.5 %collective-permute-start.92 = (bf16[128,2048]{1,0:T(8,128)(2,1)}, bf16[128,2048]{1,0:T(8,128)(2,1)S(1)}, u32[]{:S(2)}, u32[]{:S(2)}) collective-permute-start(bf16[128,2048]{1,0:T(8,128)(2,1)} %get-tuple-element.357), channel_id=1, source_target_pairs={{8,0},{6,2},{0,4},{14,6},{16,8},{2,10},{4,12},{22,14},{24,16},{10,... | collective-permute-start | bytes 1572872 | tf_op jit(solution)/shard_map/ppermute | solution.py:64
  494.9 49.3 %collective-permute-start.91 = (bf16[128,2048]{1,0:T(8,128)(2,1)}, bf16[128,2048]{1,0:T(8,128)(2,1)}, u32[]{:S(2)}, u32[]{:S(2)}) collective-permute-start(bf16[128,2048]{1,0:T(8,128)(2,1)} %add_portions.31), channel_id=1, source_target_pairs={{0,8},{2,6},{4,0},{6,14},{8,16},{10,2},{12,4},{14,22},{16,24},{18,... | collective-permute-start | bytes 1572872 | tf_op jit(solution)/shard_map/ppermute | solution.py:63
  515.5 47.8 %all-to-all-start.3 = ((bf16[16,16,1024]{2,1,0:T(8,128)(2,1)}), bf16[16,16,1024]{2,1,0:T(8,128)(2,1)}, u32[]{:S(2)}, u32[]{:S(2)}) async-start(bf16[16,16,1024]{2,1,0:T(8,128)(2,1)} %bitcast.181), calls=%async_computation.3 | async-start | bytes 1048576 | tf_op jit(solution)/shard_map/all_to_all | solution.py:155
  526.0 25.6 %collective-permute-start.86 = (bf16[128,1024]{1,0:T(8,128)(2,1)}, bf16[128,1024]{1,0:T(8,128)(2,1)}, u32[]{:S(2)}, u32[]{:S(2)}) collective-permute-start(bf16[128,1024]{1,0:T(8,128)(2,1)} %get-tuple-element.350), channel_id=1, source_target_pairs={{0,8},{2,6},{4,0},{6,14},{8,16},{10,2},{12,4},{14,22},{16,24},{18,... | collective-permute-start | bytes 786440 | tf_op jit(solution)/shard_map/ppermute | solution.py:64
  549.3 17.7 %collective-permute-start.93 = (bf16[64,2048]{1,0:T(8,128)(2,1)}, bf16[64,2048]{1,0:T(8,128)(2,1)S(1)}, u32[]{:S(2)}, u32[]{:S(2)}) collective-permute-start(bf16[64,2048]{1,0:T(8,128)(2,1)} %get-tuple-element.359), channel_id=1, source_target_pairs={{0,2},{2,0},{4,6},{6,4},{8,10},{10,8},{12,14},{14,12},{16,18},{18,... | collective-permute-start | bytes 786440 | tf_op jit(solution)/shard_map/ppermute | solution.py:67
  (212 other events, 2003.8 us)

commit v9 on v8

--- a/solution.py
+++ b/solution.py
@@ -680,11 +680,11 @@
     later = attn_rings[1:-1] + feed_rings[1:-1]
     step = 0
     while not attn_rings[0].done:
-        beside = (attn_rings[0], feed_rings[0] if step % 2 or step == 4 else None)
+        beside = (attn_rings[0], feed_rings[0] if step >= 3 else None)
         if step == 1:
             tokens, back_slot = tick((tokens, back_slot), *beside)
             own_tokens = owner_swap(pick(tokens, back_slot))
-        elif step == 2:
+        elif step == 3:
             own_tokens = tick(own_tokens, *beside)
             token_blocks = wires.rows_in(own_tokens)
         elif step == 4:
@@ -711,7 +711,7 @@
             input_blocks = [(rows.astype(F32) + time_row).astype(BF16) for rows in token_blocks]
         else:
             input_blocks = wires.rows_in(stream.astype(BF16))
-            input_blocks[-1] = tick(input_blocks[-1], feed_rings[layer])
+            input_blocks[-1] = tick(input_blocks[-1], attn_rings[layer], feed_rings[layer])
             attn_w = attn_rings[layer].finish()
         ahead = (attn_rings[layer + 1], feed_rings[layer + 1])
         biases = []
@@ -724,11 +724,12 @@
             input_blocks, attn_w[1], biases[1], segment, (mixture, attn_w[0])
         )
         attention.append(part)
-        sums[-1] = tick(sums[-1], feed_rings[layer], ahead[0])
-        attended = tick(wires.rows_out(sums), feed_rings[layer], *ahead)
+        sums[-1] = tick(sums[-1], feed_rings[layer])
+        attended = tick(wires.rows_out(sums), feed_rings[layer], ahead[0])
         middle = stream + attended + out_bias[layer, 0]
         normed = layer_norm(middle, ln_gain[layer, 0], ln_shift[layer, 0])
         normed_low = normed.astype(BF16)
+        tick(normed_low, feed_rings[layer])
         normed_blocks = wires.rows_in(normed_low)
         normed_blocks[-1] = tick(normed_blocks[-1], *ahead)
         feed_w = feed_rings[layer].finish()
@@ -770,7 +771,6 @@
         pairs = [(normed_blocks, grad_pre, hidden), (branch_blocks, act, hidden)]
         came = wires.partner(weight_gradients(pairs, 1))
         grad_normed = grad_second + wires.rows_out(sums)
-        grad_normed = tick(grad_normed, later_attn)
         _, pull_first = jax.vjp(layer_norm, middle, ln_gain[layer, 0], ln_shift[layer, 0])
         grad_middle, gain_first, shift_first = pull_first(grad_normed)
         send, *feed_sums = tie(grad_middle.astype(BF16), weight_gradients(pairs, 0), came)

time: 579 us -> 574 us (level)
    ppermute x8, waiting for transfers between devices: 11.4 us -> 29.2 us  [round(): return [lax.ppermute(forth, 'dp', self.ahead)]]
    ppermute x24, waiting for transfers between devices: 35.1 us -> 21 us  [round(): lax.ppermute(back, 'dp', self.back)]
    unnamed x287 -> x291, local copies, waits for them, and re-layouts: 40.3 us -> 33.4 us
  transfers between devices with their start and end apart: 98 -> 98, of which waited for: 41 -> 43; matrix products, arithmetic and copies ran while one was open for 8% -> 8% of each run, Pallas kernels for 20% -> 20%
where the time goes in v9:
time: 574 us; the launch traced here: 564 us
  waiting for transfers between devices  212 us (37%)
  Pallas kernels  152 us (26%)
  starting transfers between devices  112 us (20%)
  local copies, waits for them, and re-layouts  57.5 us (10%)
  other arithmetic  27.2 us (5%)
    ppermute x16, waiting for transfers between devices, across(): return lax.ppermute(array, 'tensor', [(0, 1), (1, 0)])  97.5 us
    ppermute x24, waiting for transfers between devices, round(): lax.ppermute(forth, 'dp', self.ahead)  48.4 us
    pallas_call x8, Pallas kernels, weight_gradients(): pl.pallas_call(kernel, grid=(sum(counts),), out_shape=jax.ShapeDtypeStruc...  36.3 us
    unnamed x291, local copies, waits for them, and re-layouts  33.4 us
    ppermute x24, starting transfers between devices, round(): lax.ppermute(forth, 'dp', self.ahead)  30.5 us
    ppermute x8, waiting for transfers between devices, round(): return [lax.ppermute(forth, 'dp', self.ahead)]  29.2 us
    pallas_call x16, Pallas kernels, add_portions(): pl.pallas_call(kernel, grid_spec=pltpu.PrefetchScalarGridSpec(num_scalar_...  27.9 us
    pallas_call x4, Pallas kernels, attend_backward(): pl.pallas_call(kernel, out_shape=shapes, scratch_shapes=[pltpu.VMEM((rows...  26.3 us
  transfers between devices with their start and end apart: 98, of which 43 were waited for; matrix products, arithmetic and copies ran while one was open for 8% of the time, Pallas kernels for 20%

profile of v9, /device:TPU:0, one launch (start us, length us, event | category | flops | bytes accessed | tf_op | source)
XLA Modules:
  0.0 564.2 jit_solution(11310995380433173626)
XLA Ops:
  9.1 6.3 %collective-permute-done.3.refs_4_ = bf16[136,1024]{1,0:T(8,128)(2,1)S(1)} collective-permute-done((bf16[136,1024]{1,0:T(8,128)(2,1)S(1)}, bf16[136,1024]{1,0:T(8,128)(2,1)S(1)}, u32[]{:S(2)}, u32[]{:S(2)}) %collective-permute-start.3) | collective-permute-done | bytes 278560 | tf_op jit(solution)/shard_map/ppermute | solution.py:64
  18.0 6.4 %all-to-all-start = ((bf16[16,16,1024]{2,1,0:T(8,128)(2,1)}), bf16[16,16,1024]{2,1,0:T(8,128)(2,1)}, u32[]{:S(2)}, u32[]{:S(2)}) async-start(bf16[16,16,1024]{2,1,0:T(8,128)(2,1)} %bitcast.13), calls=%async_computation | async-start | bytes 1048576 | tf_op jit(solution)/shard_map/all_to_all | solution.py:155
  26.8 13.1 %collective-permute-done.4.refs_2_ = bf16[136,1024]{1,0:T(8,128)(2,1)S(1)} collective-permute-done((bf16[136,1024]{1,0:T(8,128)(2,1)S(1)}, bf16[136,1024]{1,0:T(8,128)(2,1)S(1)}, u32[]{:S(2)}, u32[]{:S(2)}) %collective-permute-start.4) | collective-permute-done | bytes 278560 | tf_op jit(solution)/shard_map/ppermute | solution.py:64
  80.3 5.8 %attend_forward.5 = (bf16[512,768]{1,0:T(8,128)(2,1)S(1)}, bf16[512,256]{1,0:T(8,128)(2,1)S(1)}, f32[4,512]{1,0:T(4,128)S(1)}, f32[256,1024]{1,0:T(8,128)S(1)}, bf16[256,1024]{1,0:T(8,128)(2,1)S(1)}) custom-call(bf16[256,1024]{1,0:T(8,128)(2,1)S(1)} %get-tuple-element.468.refs_0_, bf16[256,1024]{1,0:T(8,128)(2,1)S(1)} %get-tuple-element.467.refs_1_, ...), custom_call_target="tpu_custom_call" | custom-call | flops 1000 | bytes 1000 | tf_op jit(solution)/shard_map/attend_forward/pallas_call | solution.py:285
  91.3 10.5 %collective-permute-done.18 = bf16[256,1024]{1,0:T(8,128)(2,1)S(1)} collective-permute-done((bf16[256,1024]{1,0:T(8,128)(2,1)S(1)}, bf16[256,1024]{1,0:T(8,128)(2,1)S(1)}, u32[]{:S(2)}, u32[]{:S(2)}) %collective-permute-start.18) | collective-permute-done | bytes 524320 | tf_op jit(solution)/shard_map/ppermute | solution.py:70
  117.6 6.9 %collective-permute-done.23.refs_4_ = bf16[128,1024]{1,0:T(8,128)(2,1)S(1)} collective-permute-done((bf16[128,1024]{1,0:T(8,128)(2,1)S(1)}, bf16[128,1024]{1,0:T(8,128)(2,1)S(1)}, u32[]{:S(2)}, u32[]{:S(2)}) %collective-permute-start.23) | collective-permute-done | bytes 262176 | tf_op jit(solution)/shard_map/ppermute | solution.py:64
  131.5 6.9 %feed_forward.2 = (f32[256,1024]{1,0:T(8,128)S(1)}, bf16[256,1024]{1,0:T(8,128)(2,1)S(1)}, bf16[512,2048]{1,0:T(8,128)(2,1)S(1)}, bf16[512,2048]{1,0:T(8,128)(2,1)S(1)}) custom-call(bf16[256,1024]{1,0:T(8,128)(2,1)S(1)} %fusion.5.refs_0_, bf16[256,1024]{1,0:T(8,128)(2,1)S(1)} %collective-permute-done.21.refs_1_, ...), custom_call_target="tpu_custom_call" | custom-call | flops 1000 | bytes 1000 | tf_op jit(solution)/shard_map/feed_forward/pallas_call | solution.py:442
  143.1 9.1 %collective-permute-done.28 = bf16[256,1024]{1,0:T(8,128)(2,1)S(1)} collective-permute-done((bf16[256,1024]{1,0:T(8,128)(2,1)S(1)}, bf16[256,1024]{1,0:T(8,128)(2,1)S(1)}, u32[]{:S(2)}, u32[]{:S(2)}) %collective-permute-start.28) | collective-permute-done | bytes 524320 | tf_op jit(solution)/shard_map/ppermute | solution.py:70
  165.2 11.9 %collective-permute-done.34.refs_0_ = bf16[128,1024]{1,0:T(8,128)(2,1)S(1)} collective-permute-done((bf16[128,1024]{1,0:T(8,128)(2,1)S(1)}, bf16[128,1024]{1,0:T(8,128)(2,1)S(1)}, u32[]{:S(2)}, u32[]{:S(2)}) %collective-permute-start.34) | collective-permute-done | bytes 262176 | tf_op jit(solution)/shard_map/ppermute | solution.py:63
  194.8 11.6 %collective-permute-done.40 = bf16[256,1024]{1,0:T(8,128)(2,1)S(1)} collective-permute-done((bf16[256,1024]{1,0:T(8,128)(2,1)S(1)}, bf16[256,1024]{1,0:T(8,128)(2,1)S(1)}, u32[]{:S(2)}, u32[]{:S(2)}) %collective-permute-start.40) | collective-permute-done | bytes 524320 | tf_op jit(solution)/shard_map/ppermute | solution.py:70
  208.9 13.8 %collective-permute-done.42.refs_1_ = bf16[256,1024]{1,0:T(8,128)(2,1)S(1)} collective-permute-done((bf16[256,1024]{1,0:T(8,128)(2,1)S(1)}, bf16[256,1024]{1,0:T(8,128)(2,1)S(1)}, u32[]{:S(2)}, u32[]{:S(2)}) %collective-permute-start.42) | collective-permute-done | bytes 524320 | tf_op jit(solution)/shard_map/ppermute | solution.py:70
  222.6 7.8 %feed_forward.3 = (f32[256,1024]{1,0:T(8,128)S(1)}, bf16[256,1024]{1,0:T(8,128)(2,1)}, bf16[512,2048]{1,0:T(8,128)(2,1)S(1)}, bf16[512,2048]{1,0:T(8,128)(2,1)S(1)}) custom-call(bf16[256,1024]{1,0:T(8,128)(2,1)S(1)} %fusion.7.refs_0_, bf16[256,1024]{1,0:T(8,128)(2,1)S(1)} %collective-permute-done.42.refs_1_, bf16[1024,2048]{1,0:T(8,128)(2,1)S(1)} %place_pieces.15.refs_2_, ...), custom_call_target="tpu_custom_call" | custom-call | flops 1000 | bytes 1000 | tf_op jit(solution)/shard_map/feed_forward/pallas_call | solution.py:442
  263.5 12.4 %collective-permute-done.45.refs_1_.refs_3_ = bf16[256,1024]{1,0:T(8,128)(2,1)S(1)} collective-permute-done((bf16[256,1024]{1,0:T(8,128)(2,1)S(1)}, bf16[256,1024]{1,0:T(8,128)(2,1)S(1)}, u32[]{:S(2)}, u32[]{:S(2)}) %collective-permute-start.45) | collective-permute-done | bytes 524320 | tf_op jit(solution)/shard_map/ppermute | solution.py:70
  294.8 7.6 %collective-permute-done.46 = bf16[256,1024]{1,0:T(8,128)(2,1)S(1)} collective-permute-done((bf16[256,1024]{1,0:T(8,128)(2,1)S(1)}, bf16[256,1024]{1,0:T(8,128)(2,1)S(1)}, u32[]{:S(2)}, u32[]{:S(2)}) %collective-permute-start.46) | collective-permute-done | bytes 524320 | tf_op jit(solution)/shard_map/ppermute | solution.py:70
  308.1 9.1 %collective-permute-done.48.refs_1_.refs_3_ = bf16[256,1024]{1,0:T(8,128)(2,1)S(1)} collective-permute-done((bf16[256,1024]{1,0:T(8,128)(2,1)S(1)}, bf16[256,1024]{1,0:T(8,128)(2,1)S(1)}, u32[]{:S(2)}, u32[]{:S(2)}) %collective-permute-start.48) | collective-permute-done | bytes 524320 | tf_op jit(solution)/shard_map/ppermute | solution.py:70
  331.1 6.3 %attend_backward.5 = (bf16[512,768]{1,0:T(8,128)(2,1)S(1)}, f32[1,768]{1,0:T(1,128)S(1)}, f32[256,1024]{1,0:T(8,128)S(1)}, bf16[256,1024]{1,0:T(8,128)(2,1)S(1)}) custom-call(bf16[256,1024]{1,0:T(8,128)(2,1)S(1)} %get-tuple-element.257.refs_0_.refs_2_, bf16[256,1024]{1,0:T(8,128)(2,1)S(1)} %collective-permute-done.48.refs_1_.refs_3_, ...), custom_call_target="tpu_custom_call" | custom-call | flops 1000 | bytes 1000 | tf_op jit(solution)/shard_map/attend_backward/pallas_call | solution.py:364
  343.8 8.0 %collective-permute-done.53 = bf16[256,1024]{1,0:T(8,128)(2,1)S(1)} collective-permute-done((bf16[256,1024]{1,0:T(8,128)(2,1)S(1)}, bf16[256,1024]{1,0:T(8,128)(2,1)S(1)}, u32[]{:S(2)}, u32[]{:S(2)}) %collective-permute-start.53) | collective-permute-done | bytes 524320 | tf_op jit(solution)/shard_map/ppermute | solution.py:70
  363.5 6.3 %collective-permute-done.58.refs_0_ = bf16[128,2048]{1,0:T(8,128)(2,1)S(1)} collective-permute-done((bf16[128,2048]{1,0:T(8,128)(2,1)S(1)}, bf16[128,2048]{1,0:T(8,128)(2,1)S(1)}, u32[]{:S(2)}, u32[]{:S(2)}) %collective-permute-start.58) | collective-permute-done | bytes 524320 | tf_op jit(solution)/shard_map/ppermute | solution.py:63
  374.1 5.5 feed_backward.3
  380.6 6.5 %weight_gradients.13 = bf16[1024,2048]{1,0:T(8,128)(2,1)} custom-call(bf16[256,1024]{1,0:T(8,128)(2,1)S(1)} %copy-done.42, bf16[256,1024]{1,0:T(8,128)(2,1)S(1)} %copy-done.49, bf16[256,1024]{1,0:T(8,128)(2,1)S(1)} %get-tuple-element.282.refs_0_.refs_2_, bf16[256,1024]{1,0:T(8,128)(2,1)S(1)} %collective-permute-done.57.refs_1_.refs_3_, ...), custom_call_target="tpu_custom_call" | custom-call | flops 1000 | bytes 1000 | tf_op jit(solution)/shard_map/weight_gradients/pallas_call | solution.py:503
  437.3 6.6 %attend_backward.6 = (bf16[512,768]{1,0:T(8,128)(2,1)S(1)}, f32[1,768]{1,0:T(1,128)S(1)}) custom-call(bf16[256,1024]{1,0:T(8,128)(2,1)S(1)} %copy-done.30, bf16[256,1024]{1,0:T(8,128)(2,1)} %collective-permute-done.63.refs_1_.refs_3_, bf16[1024,1024]{1,0:T(8,128)(2,1)} %collective-permute-done.15.refs_2_.refs_9_, bf16[512,768]{1,0:T(8,128)(2,1)S(1)} %copy-done.80, ...), custom_call_target="tpu_custom_call" | custom-call | flops 1000 | bytes 1000 | tf_op jit(solution)/shard_map/attend_backward/pallas_call | solution.py:364
  455.6 8.8 %attend_backward.7 = (bf16[512,768]{1,0:T(8,128)(2,1)S(1)}, f32[1,768]{1,0:T(1,128)S(1)}, f32[256,1024]{1,0:T(8,128)S(1)}, bf16[256,1024]{1,0:T(8,128)(2,1)}) custom-call(bf16[256,1024]{1,0:T(8,128)(2,1)S(1)} %copy-done.30, bf16[256,1024]{1,0:T(8,128)(2,1)} %collective-permute-done.63.refs_1_.refs_3_, bf16[1024,1024]{1,0:T(8,128)(2,1)S(1)} %copy-done.20, ...), custom_call_target="tpu_custom_call" | custom-call | flops 1000 | bytes 1000 | tf_op jit(solution)/shard_map/attend_backward/pallas_call | solution.py:364
  498.4 7.2 %collective-permute-done.82.refs_0_ = bf16[128,1024]{1,0:T(8,128)(2,1)S(1)} collective-permute-done((bf16[128,1024]{1,0:T(8,128)(2,1)S(1)}, bf16[128,1024]{1,0:T(8,128)(2,1)S(1)}, u32[]{:S(2)}, u32[]{:S(2)}) %collective-permute-start.82) | collective-permute-done | bytes 262176 | tf_op jit(solution)/shard_map/ppermute | solution.py:64
  525.0 5.4 collective-permute-done.78
  (656 shorter events, 360.3 us)
Async XLA Ops:
  18.0 34.7 %all-to-all-start = ((bf16[16,16,1024]{2,1,0:T(8,128)(2,1)}), bf16[16,16,1024]{2,1,0:T(8,128)(2,1)}, u32[]{:S(2)}, u32[]{:S(2)}) async-start(bf16[16,16,1024]{2,1,0:T(8,128)(2,1)} %bitcast.13), calls=%async_computation | async-start | bytes 1048576 | tf_op jit(solution)/shard_map/all_to_all | solution.py:155
  26.7 20.2 %collective-permute-start.8 = (bf16[64,2048]{1,0:T(8,128)(2,1)S(1)}, bf16[64,2048]{1,0:T(8,128)(2,1)S(1)}, u32[]{:S(2)}, u32[]{:S(2)}) collective-permute-start(bf16[64,2048]{1,0:T(8,128)(2,1)S(1)} %pad_maximum_fusion), channel_id=1, source_target_pairs={{0,2},{2,0},{4,6},{6,4},{8,10},{10,8},{12,14},{14,12},{16,18},{18,... | collective-permute-start | bytes 786440 | tf_op jit(solution)/shard_map/ppermute | solution.py:67
  52.8 17.4 %collective-permute-start.12 = (bf16[128,2048]{1,0:T(8,128)(2,1)S(1)}, bf16[128,2048]{1,0:T(8,128)(2,1)}, u32[]{:S(2)}, u32[]{:S(2)}) collective-permute-start(bf16[128,2048]{1,0:T(8,128)(2,1)S(1)} %maximum_select_fusion.refs_0_), channel_id=1, source_target_pairs={{8,0},{6,2},{0,4},{14,6},{16,8},{2,10},{4,12},{22,14},{24,16},{10,... | collective-permute-start | bytes 1572872 | tf_op jit(solution)/shard_map/ppermute | solution.py:64
  114.9 16.5 %collective-permute-start.25 = (bf16[1024,2048]{1,0:T(8,128)(2,1)S(1)}, bf16[1024,2048]{1,0:T(8,128)(2,1)S(1)}, u32[]{:S(2)}, u32[]{:S(2)}) collective-permute-start(bf16[1024,2048]{1,0:T(8,128)(2,1)S(1)} %place_pieces.11.refs_2_), channel_id=1, source_target_pairs={{0,2},{2,0},{4,6},{6,4},{8,10},{10,8},{12,14},{14,12},{16,18},{18,... | collective-permute-start | bytes 12582920 | tf_op jit(solution)/shard_map/ppermute | solution.py:67
  141.1 17.0 %collective-permute-start.29 = (bf16[128,1024]{1,0:T(8,128)(2,1)S(1)}, bf16[128,1024]{1,0:T(8,128)(2,1)S(1)}, u32[]{:S(2)}, u32[]{:S(2)}) collective-permute-start(bf16[128,1024]{1,0:T(8,128)(2,1)S(1)} %collective-permute-done.26.refs_2_), channel_id=1, source_target_pairs={{0,8},{2,6},{4,0},{6,14},{8,16},{10,2},{12,4},{14,22},{16,24},{18,... | collective-permute-start | bytes 786440 | tf_op jit(solution)/shard_map/ppermute | solution.py:64
  159.4 17.8 %collective-permute-start.33 = (bf16[256,1024]{1,0:T(8,128)(2,1)S(1)}, bf16[256,1024]{1,0:T(8,128)(2,1)S(1)}, u32[]{:S(2)}, u32[]{:S(2)}) collective-permute-start(bf16[256,1024]{1,0:T(8,128)(2,1)S(1)} %fusion.6.refs_0_), channel_id=1, source_target_pairs={{0,1},{1,0},{2,3},{3,2},{4,5},{5,4},{6,7},{7,6},{8,9},{9,8},{10,11... | collective-permute-start | bytes 1572872 | tf_op jit(solution)/shard_map/ppermute | solution.py:70
  161.0 16.2 %collective-permute-start.35 = (bf16[128,2048]{1,0:T(8,128)(2,1)S(1)}, bf16[128,2048]{1,0:T(8,128)(2,1)S(1)}, u32[]{:S(2)}, u32[]{:S(2)}) collective-permute-start(bf16[128,2048]{1,0:T(8,128)(2,1)S(1)} %collective-permute-done.31.refs_1_), channel_id=1, source_target_pairs={{0,8},{2,6},{4,0},{6,14},{8,16},{10,2},{12,4},{14,22},{16,24},{18,... | collective-permute-start | bytes 1572872 | tf_op jit(solution)/shard_map/ppermute | solution.py:64
  238.1 18.9 %all-to-all-start.1 = ((bf16[16,16,1024]{2,1,0:T(8,128)(2,1)}), bf16[16,16,1024]{2,1,0:T(8,128)(2,1)}, u32[]{:S(2)}, u32[]{:S(2)}) async-start(bf16[16,16,1024]{2,1,0:T(8,128)(2,1)} %bitcast.182), calls=%async_computation.1 | async-start | bytes 1048576 | tf_op jit(solution)/shard_map/all_to_all | solution.py:155
  321.1 16.3 %collective-permute-start.51 = (bf16[128,2048]{1,0:T(8,128)(2,1)S(1)}, bf16[128,2048]{1,0:T(8,128)(2,1)S(1)}, u32[]{:S(2)}, u32[]{:S(2)}) collective-permute-start(bf16[128,2048]{1,0:T(8,128)(2,1)S(1)} %get-tuple-element.273), channel_id=1, source_target_pairs={{0,8},{2,6},{4,0},{6,14},{8,16},{10,2},{12,4},{14,22},{16,24},{18,... | collective-permute-start | bytes 1572872 | tf_op jit(solution)/shard_map/ppermute | solution.py:64
  331.0 28.1 %collective-permute-start.56 = (bf16[1024,1024]{1,0:T(8,128)(2,1)S(1)}, bf16[1024,1024]{1,0:T(8,128)(2,1)S(1)}, u32[]{:S(2)}, u32[]{:S(2)}) collective-permute-start(bf16[1024,1024]{1,0:T(8,128)(2,1)S(1)} %weight_gradients.11), channel_id=1, source_target_pairs={{0,2},{2,0},{4,6},{6,4},{8,10},{10,8},{12,14},{14,12},{16,18},{18,... | collective-permute-start | bytes 6291464 | tf_op jit(solution)/shard_map/ppermute | solution.py:67
  387.1 25.0 %collective-permute-start.62 = (bf16[1024,2048]{1,0:T(8,128)(2,1)}, bf16[1024,2048]{1,0:T(8,128)(2,1)}, u32[]{:S(2)}, u32[]{:S(2)}) collective-permute-start(bf16[1024,2048]{1,0:T(8,128)(2,1)} %weight_gradients.13), channel_id=1, source_target_pairs={{0,2},{2,0},{4,6},{6,4},{8,10},{10,8},{12,14},{14,12},{16,18},{18,... | collective-permute-start | bytes 12582920 | tf_op jit(solution)/shard_map/ppermute | solution.py:67
  387.2 21.9 %collective-permute-start.61 = (bf16[256,1024]{1,0:T(8,128)(2,1)}, bf16[256,1024]{1,0:T(8,128)(2,1)}, u32[]{:S(2)}, u32[]{:S(2)}) collective-permute-start(bf16[256,1024]{1,0:T(8,128)(2,1)} %get-tuple-element.291), channel_id=1, source_target_pairs={{0,1},{1,0},{2,3},{3,2},{4,5},{5,4},{6,7},{7,6},{8,9},{9,8},{10,11... | collective-permute-start | bytes 1572872 | tf_op jit(solution)/shard_map/ppermute | solution.py:70
  389.8 27.7 %all-to-all-start.2 = ((bf16[16,16,1024]{2,1,0:T(8,128)(2,1)}), bf16[16,16,1024]{2,1,0:T(8,128)(2,1)}, u32[]{:S(2)}, u32[]{:S(2)}) async-start(bf16[16,16,1024]{2,1,0:T(8,128)(2,1)} %bitcast.180), calls=%async_computation.2 | async-start | bytes 1048576 | tf_op jit(solution)/shard_map/all_to_all | solution.py:155
  435.0 29.5 %collective-permute-start.68 = (bf16[128,2048]{1,0:T(8,128)(2,1)S(1)}, bf16[128,2048]{1,0:T(8,128)(2,1)S(1)}, u32[]{:S(2)}, u32[]{:S(2)}) collective-permute-start(bf16[128,2048]{1,0:T(8,128)(2,1)S(1)} %get-tuple-element.314), channel_id=1, source_target_pairs={{0,8},{2,6},{4,0},{6,14},{8,16},{10,2},{12,4},{14,22},{16,24},{18,... | collective-permute-start | bytes 1572872 | tf_op jit(solution)/shard_map/ppermute | solution.py:64
  436.1 28.5 %collective-permute-start.69 = (bf16[128,2048]{1,0:T(8,128)(2,1)S(1)}, bf16[128,2048]{1,0:T(8,128)(2,1)S(1)}, u32[]{:S(2)}, u32[]{:S(2)}) collective-permute-start(bf16[128,2048]{1,0:T(8,128)(2,1)S(1)} %get-tuple-element.315), channel_id=1, source_target_pairs={{8,0},{6,2},{0,4},{14,6},{16,8},{2,10},{4,12},{22,14},{24,16},{10,... | collective-permute-start | bytes 1572872 | tf_op jit(solution)/shard_map/ppermute | solution.py:64
  448.8 44.6 %collective-permute-start.81 = (bf16[1024,1024]{1,0:T(8,128)(2,1)}, bf16[1024,1024]{1,0:T(8,128)(2,1)}, u32[]{:S(2)}, u32[]{:S(2)}) collective-permute-start(bf16[1024,1024]{1,0:T(8,128)(2,1)} %weight_gradients.15), channel_id=1, source_target_pairs={{0,2},{2,0},{4,6},{6,4},{8,10},{10,8},{12,14},{14,12},{16,18},{18,... | collective-permute-start | bytes 6291464 | tf_op jit(solution)/shard_map/ppermute | solution.py:67
  464.4 19.3 %collective-permute-start.75 = (bf16[64,2048]{1,0:T(8,128)(2,1)}, bf16[64,2048]{1,0:T(8,128)(2,1)}, u32[]{:S(2)}, u32[]{:S(2)}) collective-permute-start(bf16[64,2048]{1,0:T(8,128)(2,1)} %get-tuple-element.328), channel_id=1, source_target_pairs={{0,2},{2,0},{4,6},{6,4},{8,10},{10,8},{12,14},{14,12},{16,18},{18,... | collective-permute-start | bytes 786440 | tf_op jit(solution)/shard_map/ppermute | solution.py:67
  470.5 17.5 %collective-permute-start.90 = (bf16[128,2048]{1,0:T(8,128)(2,1)}, bf16[128,2048]{1,0:T(8,128)(2,1)}, u32[]{:S(2)}, u32[]{:S(2)}) collective-permute-start(bf16[128,2048]{1,0:T(8,128)(2,1)} %get-tuple-element.354), channel_id=1, source_target_pairs={{0,8},{2,6},{4,0},{6,14},{8,16},{10,2},{12,4},{14,22},{16,24},{18,... | collective-permute-start | bytes 1572872 | tf_op jit(solution)/shard_map/ppermute | solution.py:64
  471.9 19.3 %collective-permute-start.72 = (bf16[256,1024]{1,0:T(8,128)(2,1)}, bf16[256,1024]{1,0:T(8,128)(2,1)}, u32[]{:S(2)}, u32[]{:S(2)}) collective-permute-start(bf16[256,1024]{1,0:T(8,128)(2,1)} %get-tuple-element.320), channel_id=1, source_target_pairs={{0,1},{1,0},{2,3},{3,2},{4,5},{5,4},{6,7},{7,6},{8,9},{9,8},{10,11... | collective-permute-start | bytes 1572872 | tf_op jit(solution)/shard_map/ppermute | solution.py:70
  483.7 55.4 %collective-permute-start.92 = (bf16[128,2048]{1,0:T(8,128)(2,1)}, bf16[128,2048]{1,0:T(8,128)(2,1)S(1)}, u32[]{:S(2)}, u32[]{:S(2)}) collective-permute-start(bf16[128,2048]{1,0:T(8,128)(2,1)} %get-tuple-element.355), channel_id=1, source_target_pairs={{8,0},{6,2},{0,4},{14,6},{16,8},{2,10},{4,12},{22,14},{24,16},{10,... | collective-permute-start | bytes 1572872 | tf_op jit(solution)/shard_map/ppermute | solution.py:64
  490.6 48.5 %collective-permute-start.91 = (bf16[128,2048]{1,0:T(8,128)(2,1)}, bf16[128,2048]{1,0:T(8,128)(2,1)}, u32[]{:S(2)}, u32[]{:S(2)}) collective-permute-start(bf16[128,2048]{1,0:T(8,128)(2,1)} %add_portions.31), channel_id=1, source_target_pairs={{0,8},{2,6},{4,0},{6,14},{8,16},{10,2},{12,4},{14,22},{16,24},{18,... | collective-permute-start | bytes 1572872 | tf_op jit(solution)/shard_map/ppermute | solution.py:63
  511.3 47.0 %all-to-all-start.3 = ((bf16[16,16,1024]{2,1,0:T(8,128)(2,1)}), bf16[16,16,1024]{2,1,0:T(8,128)(2,1)}, u32[]{:S(2)}, u32[]{:S(2)}) async-start(bf16[16,16,1024]{2,1,0:T(8,128)(2,1)} %bitcast.181), calls=%async_computation.3 | async-start | bytes 1048576 | tf_op jit(solution)/shard_map/all_to_all | solution.py:155
  520.8 25.8 %collective-permute-start.86 = (bf16[128,1024]{1,0:T(8,128)(2,1)}, bf16[128,1024]{1,0:T(8,128)(2,1)S(1)}, u32[]{:S(2)}, u32[]{:S(2)}) collective-permute-start(bf16[128,1024]{1,0:T(8,128)(2,1)} %get-tuple-element.348), channel_id=1, source_target_pairs={{0,8},{2,6},{4,0},{6,14},{8,16},{10,2},{12,4},{14,22},{16,24},{18,... | collective-permute-start | bytes 786440 | tf_op jit(solution)/shard_map/ppermute | solution.py:64
  544.3 17.7 %collective-permute-start.93 = (bf16[64,2048]{1,0:T(8,128)(2,1)}, bf16[64,2048]{1,0:T(8,128)(2,1)S(1)}, u32[]{:S(2)}, u32[]{:S(2)}) collective-permute-start(bf16[64,2048]{1,0:T(8,128)(2,1)} %get-tuple-element.357), channel_id=1, source_target_pairs={{0,2},{2,0},{4,6},{6,4},{8,10},{10,8},{12,14},{14,12},{16,18},{18,... | collective-permute-start | bytes 786440 | tf_op jit(solution)/shard_map/ppermute | solution.py:67
  (214 other events, 2108.0 us)

commit v10 on v9

--- a/solution.py
+++ b/solution.py
@@ -225,7 +225,7 @@
         out_specs=[pl.BlockSpec(memory_space=pl.ANY)] * len(shapes),
         scratch_shapes=[pltpu.SemaphoreType.DMA((count, 2))],
         input_output_aliases={1 + count + i: i for i in range(given)},
-        compiler_params=pltpu.CompilerParams(vmem_limit_bytes=16 << 20),
+        compiler_params=pltpu.CompilerParams(vmem_limit_bytes=8 << 20),
         cost_estimate=pl.CostEstimate(
             flops=0, bytes_accessed=1 << 26, transcendentals=0
         ),
@@ -285,7 +285,7 @@
     outs = pl.pallas_call(
         kernel,
         out_shape=shapes,
-        compiler_params=pltpu.CompilerParams(vmem_limit_bytes=32 << 20),
+        compiler_params=pltpu.CompilerParams(vmem_limit_bytes=20 << 20),
         cost_estimate=SMALL_COST,
         name="attend_forward",
     )(*blocks, weight, bias[None], segment[:, None], segment[None], *(earlier or ()))
@@ -365,7 +365,7 @@
         kernel,
         out_shape=shapes,
         scratch_shapes=[pltpu.VMEM((rows, inner), BF16)],
-        compiler_params=pltpu.CompilerParams(vmem_limit_bytes=32 << 20),
+        compiler_params=pltpu.CompilerParams(vmem_limit_bytes=24 << 20),
         cost_estimate=SMALL_COST,
         name="attend_backward",
     )(*blocks, weight, qkv, mixture, log_total, segment[:, None], segment[None], *(earlier or ()))
@@ -444,7 +444,7 @@
         out_shape=sum_shapes(blocks)
         + [wide, wide if forward else jax.ShapeDtypeStruct((1, 2 * hidden), F32)],
         scratch_shapes=[pltpu.VMEM((2, rows, tile), F32)],
-        compiler_params=pltpu.CompilerParams(vmem_limit_bytes=32 << 20),
+        compiler_params=pltpu.CompilerParams(vmem_limit_bytes=24 << 20),
         cost_estimate=SMALL_COST,
         name="feed_forward" if forward else "feed_backward",
     )(*blocks, *weights, side)
@@ -507,7 +507,7 @@
         in_specs=specs,
         out_specs=over,
         scratch_shapes=[pltpu.VMEM((2, D, rows), BF16)],
-        compiler_params=pltpu.CompilerParams(vmem_limit_bytes=24 << 20),
+        compiler_params=pltpu.CompilerParams(vmem_limit_bytes=16 << 20),
         cost_estimate=SMALL_COST,
         name="weight_gradients",
     )(*blocks_flat, pairs[0][1], pairs[1][1])
@@ -540,7 +540,7 @@
             out_specs=[whole] * count,
         ),
         out_shape=[jax.ShapeDtypeStruct(shape, BF16)] * count,
-        compiler_params=pltpu.CompilerParams(vmem_limit_bytes=24 << 20),
+        compiler_params=pltpu.CompilerParams(vmem_limit_bytes=8 << 20),
         cost_estimate=SMALL_COST,
         name="add_portions",
     )(spot, *came[:given], *(list(sums) * count))
@@ -573,7 +573,7 @@
             jax.ShapeDtypeStruct((rows, shape[1]), F32),
             jax.ShapeDtypeStruct((rows, shape[1]), BF16),
         ],
-        compiler_params=pltpu.CompilerParams(vmem_limit_bytes=24 << 20),
+        compiler_params=pltpu.CompilerParams(vmem_limit_bytes=8 << 20),
         cost_estimate=SMALL_COST,
         name="last_portion",
     )(spot, *came, *sums)
@@ -618,7 +618,7 @@
         ),
         out_shape=[jax.ShapeDtypeStruct(shape, F32) for shape in shapes],
         input_output_aliases={5 + i: i for i in range(given)},
-        compiler_params=pltpu.CompilerParams(vmem_limit_bytes=24 << 20),
+        compiler_params=pltpu.CompilerParams(vmem_limit_bytes=12 << 20),
         cost_estimate=SMALL_COST,
         name="matrix_outputs",
     )(spot, *ins, *(filled or ()))

time: 574 us -> 572 us (level)
  no operation moved by 1% of the time
where the time goes in v10:
time: 572 us; the launch traced here: 562 us
  waiting for transfers between devices  210 us (37%)
  Pallas kernels  152 us (27%)
  starting transfers between devices  112 us (20%)
  local copies, waits for them, and re-layouts  56.7 us (10%)
  other arithmetic  27.4 us (5%)
    ppermute x16, waiting for transfers between devices, across(): return lax.ppermute(array, 'tensor', [(0, 1), (1, 0)])  97.4 us
    ppermute x24, waiting for transfers between devices, round(): lax.ppermute(forth, 'dp', self.ahead)  47.1 us
    pallas_call x8, Pallas kernels, weight_gradients(): pl.pallas_call(kernel, grid=(sum(counts),), out_shape=jax.ShapeDtypeStruc...  36.4 us
    unnamed x291, local copies, waits for them, and re-layouts  32.6 us
    ppermute x24, starting transfers between devices, round(): lax.ppermute(forth, 'dp', self.ahead)  30.5 us
    ppermute x8, waiting for transfers between devices, round(): return [lax.ppermute(forth, 'dp', self.ahead)]  29.2 us
    pallas_call x16, Pallas kernels, add_portions(): pl.pallas_call(kernel, grid_spec=pltpu.PrefetchScalarGridSpec(num_scalar_...  27.9 us
    pallas_call x4, Pallas kernels, attend_backward(): pl.pallas_call(kernel, out_shape=shapes, scratch_shapes=[pltpu.VMEM((rows...  26.3 us
  transfers between devices with their start and end apart: 98, of which 43 were waited for; matrix products, arithmetic and copies ran while one was open for 8% of the time, Pallas kernels for 20%

profile of v10, /device:TPU:0, one launch (start us, length us, event | category | flops | bytes accessed | tf_op | source)
XLA Modules:
  0.0 562.1 jit_solution(12839407498513630529)
XLA Ops:
  9.1 6.3 %collective-permute-done.3.refs_4_ = bf16[136,1024]{1,0:T(8,128)(2,1)S(1)} collective-permute-done((bf16[136,1024]{1,0:T(8,128)(2,1)S(1)}, bf16[136,1024]{1,0:T(8,128)(2,1)S(1)}, u32[]{:S(2)}, u32[]{:S(2)}) %collective-permute-start.3) | collective-permute-done | bytes 278560 | tf_op jit(solution)/shard_map/ppermute | solution.py:64
  18.0 6.4 %all-to-all-start = ((bf16[16,16,1024]{2,1,0:T(8,128)(2,1)}), bf16[16,16,1024]{2,1,0:T(8,128)(2,1)}, u32[]{:S(2)}, u32[]{:S(2)}) async-start(bf16[16,16,1024]{2,1,0:T(8,128)(2,1)} %bitcast.13), calls=%async_computation | async-start | bytes 1048576 | tf_op jit(solution)/shard_map/all_to_all | solution.py:155
  26.8 13.1 %collective-permute-done.4.refs_2_ = bf16[136,1024]{1,0:T(8,128)(2,1)S(1)} collective-permute-done((bf16[136,1024]{1,0:T(8,128)(2,1)S(1)}, bf16[136,1024]{1,0:T(8,128)(2,1)S(1)}, u32[]{:S(2)}, u32[]{:S(2)}) %collective-permute-start.4) | collective-permute-done | bytes 278560 | tf_op jit(solution)/shard_map/ppermute | solution.py:64
  81.2 5.6 attend_forward.5
  91.3 10.5 %collective-permute-done.18 = bf16[256,1024]{1,0:T(8,128)(2,1)S(1)} collective-permute-done((bf16[256,1024]{1,0:T(8,128)(2,1)S(1)}, bf16[256,1024]{1,0:T(8,128)(2,1)S(1)}, u32[]{:S(2)}, u32[]{:S(2)}) %collective-permute-start.18) | collective-permute-done | bytes 524320 | tf_op jit(solution)/shard_map/ppermute | solution.py:70
  117.6 6.9 %collective-permute-done.23.refs_4_ = bf16[128,1024]{1,0:T(8,128)(2,1)S(1)} collective-permute-done((bf16[128,1024]{1,0:T(8,128)(2,1)S(1)}, bf16[128,1024]{1,0:T(8,128)(2,1)S(1)}, u32[]{:S(2)}, u32[]{:S(2)}) %collective-permute-start.23) | collective-permute-done | bytes 262176 | tf_op jit(solution)/shard_map/ppermute | solution.py:64
  131.5 6.9 %feed_forward.2 = (f32[256,1024]{1,0:T(8,128)S(1)}, bf16[256,1024]{1,0:T(8,128)(2,1)S(1)}, bf16[512,2048]{1,0:T(8,128)(2,1)S(1)}, bf16[512,2048]{1,0:T(8,128)(2,1)S(1)}) custom-call(bf16[256,1024]{1,0:T(8,128)(2,1)S(1)} %fusion.5.refs_0_, bf16[256,1024]{1,0:T(8,128)(2,1)S(1)} %collective-permute-done.21.refs_1_, ...), custom_call_target="tpu_custom_call" | custom-call | flops 1000 | bytes 1000 | tf_op jit(solution)/shard_map/feed_forward/pallas_call | solution.py:442
  143.1 9.1 %collective-permute-done.28 = bf16[256,1024]{1,0:T(8,128)(2,1)S(1)} collective-permute-done((bf16[256,1024]{1,0:T(8,128)(2,1)S(1)}, bf16[256,1024]{1,0:T(8,128)(2,1)S(1)}, u32[]{:S(2)}, u32[]{:S(2)}) %collective-permute-start.28) | collective-permute-done | bytes 524320 | tf_op jit(solution)/shard_map/ppermute | solution.py:70
  165.2 11.9 %collective-permute-done.34.refs_0_ = bf16[128,1024]{1,0:T(8,128)(2,1)S(1)} collective-permute-done((bf16[128,1024]{1,0:T(8,128)(2,1)S(1)}, bf16[128,1024]{1,0:T(8,128)(2,1)S(1)}, u32[]{:S(2)}, u32[]{:S(2)}) %collective-permute-start.34) | collective-permute-done | bytes 262176 | tf_op jit(solution)/shard_map/ppermute | solution.py:63
  194.8 11.6 %collective-permute-done.40 = bf16[256,1024]{1,0:T(8,128)(2,1)S(1)} collective-permute-done((bf16[256,1024]{1,0:T(8,128)(2,1)S(1)}, bf16[256,1024]{1,0:T(8,128)(2,1)S(1)}, u32[]{:S(2)}, u32[]{:S(2)}) %collective-permute-start.40) | collective-permute-done | bytes 524320 | tf_op jit(solution)/shard_map/ppermute | solution.py:70
  208.8 13.8 %collective-permute-done.42.refs_1_ = bf16[256,1024]{1,0:T(8,128)(2,1)S(1)} collective-permute-done((bf16[256,1024]{1,0:T(8,128)(2,1)S(1)}, bf16[256,1024]{1,0:T(8,128)(2,1)S(1)}, u32[]{:S(2)}, u32[]{:S(2)}) %collective-permute-start.42) | collective-permute-done | bytes 524320 | tf_op jit(solution)/shard_map/ppermute | solution.py:70
  222.6 7.8 %feed_forward.3 = (f32[256,1024]{1,0:T(8,128)S(1)}, bf16[256,1024]{1,0:T(8,128)(2,1)}, bf16[512,2048]{1,0:T(8,128)(2,1)S(1)}, bf16[512,2048]{1,0:T(8,128)(2,1)S(1)}) custom-call(bf16[256,1024]{1,0:T(8,128)(2,1)S(1)} %fusion.7.refs_0_, bf16[256,1024]{1,0:T(8,128)(2,1)S(1)} %collective-permute-done.42.refs_1_, bf16[1024,2048]{1,0:T(8,128)(2,1)S(1)} %place_pieces.15.refs_2_, ...), custom_call_target="tpu_custom_call" | custom-call | flops 1000 | bytes 1000 | tf_op jit(solution)/shard_map/feed_forward/pallas_call | solution.py:442
  263.5 12.4 %collective-permute-done.45.refs_1_.refs_3_ = bf16[256,1024]{1,0:T(8,128)(2,1)S(1)} collective-permute-done((bf16[256,1024]{1,0:T(8,128)(2,1)S(1)}, bf16[256,1024]{1,0:T(8,128)(2,1)S(1)}, u32[]{:S(2)}, u32[]{:S(2)}) %collective-permute-start.45) | collective-permute-done | bytes 524320 | tf_op jit(solution)/shard_map/ppermute | solution.py:70
  294.8 7.6 %collective-permute-done.46 = bf16[256,1024]{1,0:T(8,128)(2,1)S(1)} collective-permute-done((bf16[256,1024]{1,0:T(8,128)(2,1)S(1)}, bf16[256,1024]{1,0:T(8,128)(2,1)S(1)}, u32[]{:S(2)}, u32[]{:S(2)}) %collective-permute-start.46) | collective-permute-done | bytes 524320 | tf_op jit(solution)/shard_map/ppermute | solution.py:70
  308.2 9.1 %collective-permute-done.48.refs_1_.refs_3_ = bf16[256,1024]{1,0:T(8,128)(2,1)S(1)} collective-permute-done((bf16[256,1024]{1,0:T(8,128)(2,1)S(1)}, bf16[256,1024]{1,0:T(8,128)(2,1)S(1)}, u32[]{:S(2)}, u32[]{:S(2)}) %collective-permute-start.48) | collective-permute-done | bytes 524320 | tf_op jit(solution)/shard_map/ppermute | solution.py:70
  331.2 6.2 %attend_backward.5 = (bf16[512,768]{1,0:T(8,128)(2,1)S(1)}, f32[1,768]{1,0:T(1,128)S(1)}, f32[256,1024]{1,0:T(8,128)S(1)}, bf16[256,1024]{1,0:T(8,128)(2,1)S(1)}) custom-call(bf16[256,1024]{1,0:T(8,128)(2,1)S(1)} %get-tuple-element.257.refs_0_.refs_2_, bf16[256,1024]{1,0:T(8,128)(2,1)S(1)} %collective-permute-done.48.refs_1_.refs_3_, ...), custom_call_target="tpu_custom_call" | custom-call | flops 1000 | bytes 1000 | tf_op jit(solution)/shard_map/attend_backward/pallas_call | solution.py:364
  343.9 8.0 %collective-permute-done.53 = bf16[256,1024]{1,0:T(8,128)(2,1)S(1)} collective-permute-done((bf16[256,1024]{1,0:T(8,128)(2,1)S(1)}, bf16[256,1024]{1,0:T(8,128)(2,1)S(1)}, u32[]{:S(2)}, u32[]{:S(2)}) %collective-permute-start.53) | collective-permute-done | bytes 524320 | tf_op jit(solution)/shard_map/ppermute | solution.py:70
  362.8 6.3 %collective-permute-done.58.refs_0_ = bf16[128,2048]{1,0:T(8,128)(2,1)S(1)} collective-permute-done((bf16[128,2048]{1,0:T(8,128)(2,1)S(1)}, bf16[128,2048]{1,0:T(8,128)(2,1)S(1)}, u32[]{:S(2)}, u32[]{:S(2)}) %collective-permute-start.58) | collective-permute-done | bytes 524320 | tf_op jit(solution)/shard_map/ppermute | solution.py:63
  373.4 5.5 feed_backward.3
  379.0 6.5 %weight_gradients.13 = bf16[1024,2048]{1,0:T(8,128)(2,1)} custom-call(bf16[256,1024]{1,0:T(8,128)(2,1)S(1)} %copy-done.42, bf16[256,1024]{1,0:T(8,128)(2,1)S(1)} %copy-done.49, bf16[256,1024]{1,0:T(8,128)(2,1)S(1)} %get-tuple-element.282.refs_0_.refs_2_, bf16[256,1024]{1,0:T(8,128)(2,1)S(1)} %collective-permute-done.57.refs_1_.refs_3_, ...), custom_call_target="tpu_custom_call" | custom-call | flops 1000 | bytes 1000 | tf_op jit(solution)/shard_map/weight_gradients/pallas_call | solution.py:503
  435.2 6.6 %attend_backward.6 = (bf16[512,768]{1,0:T(8,128)(2,1)S(1)}, f32[1,768]{1,0:T(1,128)S(1)}) custom-call(bf16[256,1024]{1,0:T(8,128)(2,1)S(1)} %copy-done.30, bf16[256,1024]{1,0:T(8,128)(2,1)} %collective-permute-done.63.refs_1_.refs_3_, bf16[1024,1024]{1,0:T(8,128)(2,1)} %collective-permute-done.15.refs_2_.refs_9_, bf16[512,768]{1,0:T(8,128)(2,1)S(1)} %copy-done.80, ...), custom_call_target="tpu_custom_call" | custom-call | flops 1000 | bytes 1000 | tf_op jit(solution)/shard_map/attend_backward/pallas_call | solution.py:364
  453.4 8.8 %attend_backward.7 = (bf16[512,768]{1,0:T(8,128)(2,1)S(1)}, f32[1,768]{1,0:T(1,128)S(1)}, f32[256,1024]{1,0:T(8,128)S(1)}, bf16[256,1024]{1,0:T(8,128)(2,1)}) custom-call(bf16[256,1024]{1,0:T(8,128)(2,1)S(1)} %copy-done.30, bf16[256,1024]{1,0:T(8,128)(2,1)} %collective-permute-done.63.refs_1_.refs_3_, bf16[1024,1024]{1,0:T(8,128)(2,1)S(1)} %copy-done.20, ...), custom_call_target="tpu_custom_call" | custom-call | flops 1000 | bytes 1000 | tf_op jit(solution)/shard_map/attend_backward/pallas_call | solution.py:364
  496.2 7.3 %collective-permute-done.82.refs_0_ = bf16[128,1024]{1,0:T(8,128)(2,1)S(1)} collective-permute-done((bf16[128,1024]{1,0:T(8,128)(2,1)S(1)}, bf16[128,1024]{1,0:T(8,128)(2,1)S(1)}, u32[]{:S(2)}, u32[]{:S(2)}) %collective-permute-start.82) | collective-permute-done | bytes 262176 | tf_op jit(solution)/shard_map/ppermute | solution.py:64
  522.9 5.4 collective-permute-done.78
  (656 shorter events, 358.4 us)
Async XLA Ops:
  18.0 34.7 %all-to-all-start = ((bf16[16,16,1024]{2,1,0:T(8,128)(2,1)}), bf16[16,16,1024]{2,1,0:T(8,128)(2,1)}, u32[]{:S(2)}, u32[]{:S(2)}) async-start(bf16[16,16,1024]{2,1,0:T(8,128)(2,1)} %bitcast.13), calls=%async_computation | async-start | bytes 1048576 | tf_op jit(solution)/shard_map/all_to_all | solution.py:155
  26.7 20.2 %collective-permute-start.8 = (bf16[64,2048]{1,0:T(8,128)(2,1)S(1)}, bf16[64,2048]{1,0:T(8,128)(2,1)S(1)}, u32[]{:S(2)}, u32[]{:S(2)}) collective-permute-start(bf16[64,2048]{1,0:T(8,128)(2,1)S(1)} %pad_maximum_fusion), channel_id=1, source_target_pairs={{0,2},{2,0},{4,6},{6,4},{8,10},{10,8},{12,14},{14,12},{16,18},{18,... | collective-permute-start | bytes 786440 | tf_op jit(solution)/shard_map/ppermute | solution.py:67
  52.8 17.4 %collective-permute-start.12 = (bf16[128,2048]{1,0:T(8,128)(2,1)S(1)}, bf16[128,2048]{1,0:T(8,128)(2,1)}, u32[]{:S(2)}, u32[]{:S(2)}) collective-permute-start(bf16[128,2048]{1,0:T(8,128)(2,1)S(1)} %maximum_select_fusion.refs_0_), channel_id=1, source_target_pairs={{8,0},{6,2},{0,4},{14,6},{16,8},{2,10},{4,12},{22,14},{24,16},{10,... | collective-permute-start | bytes 1572872 | tf_op jit(solution)/shard_map/ppermute | solution.py:64
  114.9 16.5 %collective-permute-start.25 = (bf16[1024,2048]{1,0:T(8,128)(2,1)S(1)}, bf16[1024,2048]{1,0:T(8,128)(2,1)S(1)}, u32[]{:S(2)}, u32[]{:S(2)}) collective-permute-start(bf16[1024,2048]{1,0:T(8,128)(2,1)S(1)} %place_pieces.11.refs_2_), channel_id=1, source_target_pairs={{0,2},{2,0},{4,6},{6,4},{8,10},{10,8},{12,14},{14,12},{16,18},{18,... | collective-permute-start | bytes 12582920 | tf_op jit(solution)/shard_map/ppermute | solution.py:67
  141.1 17.0 %collective-permute-start.29 = (bf16[128,1024]{1,0:T(8,128)(2,1)S(1)}, bf16[128,1024]{1,0:T(8,128)(2,1)S(1)}, u32[]{:S(2)}, u32[]{:S(2)}) collective-permute-start(bf16[128,1024]{1,0:T(8,128)(2,1)S(1)} %collective-permute-done.26.refs_2_), channel_id=1, source_target_pairs={{0,8},{2,6},{4,0},{6,14},{8,16},{10,2},{12,4},{14,22},{16,24},{18,... | collective-permute-start | bytes 786440 | tf_op jit(solution)/shard_map/ppermute | solution.py:64
  159.4 17.8 %collective-permute-start.33 = (bf16[256,1024]{1,0:T(8,128)(2,1)S(1)}, bf16[256,1024]{1,0:T(8,128)(2,1)S(1)}, u32[]{:S(2)}, u32[]{:S(2)}) collective-permute-start(bf16[256,1024]{1,0:T(8,128)(2,1)S(1)} %fusion.6.refs_0_), channel_id=1, source_target_pairs={{0,1},{1,0},{2,3},{3,2},{4,5},{5,4},{6,7},{7,6},{8,9},{9,8},{10,11... | collective-permute-start | bytes 1572872 | tf_op jit(solution)/shard_map/ppermute | solution.py:70
  161.0 16.2 %collective-permute-start.35 = (bf16[128,2048]{1,0:T(8,128)(2,1)S(1)}, bf16[128,2048]{1,0:T(8,128)(2,1)S(1)}, u32[]{:S(2)}, u32[]{:S(2)}) collective-permute-start(bf16[128,2048]{1,0:T(8,128)(2,1)S(1)} %collective-permute-done.31.refs_1_), channel_id=1, source_target_pairs={{0,8},{2,6},{4,0},{6,14},{8,16},{10,2},{12,4},{14,22},{16,24},{18,... | collective-permute-start | bytes 1572872 | tf_op jit(solution)/shard_map/ppermute | solution.py:64
  238.1 18.9 %all-to-all-start.1 = ((bf16[16,16,1024]{2,1,0:T(8,128)(2,1)}), bf16[16,16,1024]{2,1,0:T(8,128)(2,1)}, u32[]{:S(2)}, u32[]{:S(2)}) async-start(bf16[16,16,1024]{2,1,0:T(8,128)(2,1)} %bitcast.182), calls=%async_computation.1 | async-start | bytes 1048576 | tf_op jit(solution)/shard_map/all_to_all | solution.py:155
  321.1 16.3 %collective-permute-start.51 = (bf16[128,2048]{1,0:T(8,128)(2,1)S(1)}, bf16[128,2048]{1,0:T(8,128)(2,1)S(1)}, u32[]{:S(2)}, u32[]{:S(2)}) collective-permute-start(bf16[128,2048]{1,0:T(8,128)(2,1)S(1)} %get-tuple-element.273), channel_id=1, source_target_pairs={{0,8},{2,6},{4,0},{6,14},{8,16},{10,2},{12,4},{14,22},{16,24},{18,... | collective-permute-start | bytes 1572872 | tf_op jit(solution)/shard_map/ppermute | solution.py:64
  331.1 27.3 %collective-permute-start.56 = (bf16[1024,1024]{1,0:T(8,128)(2,1)S(1)}, bf16[1024,1024]{1,0:T(8,128)(2,1)S(1)}, u32[]{:S(2)}, u32[]{:S(2)}) collective-permute-start(bf16[1024,1024]{1,0:T(8,128)(2,1)S(1)} %weight_gradients.11), channel_id=1, source_target_pairs={{0,2},{2,0},{4,6},{6,4},{8,10},{10,8},{12,14},{14,12},{16,18},{18,... | collective-permute-start | bytes 6291464 | tf_op jit(solution)/shard_map/ppermute | solution.py:67
  385.5 24.3 %collective-permute-start.62 = (bf16[1024,2048]{1,0:T(8,128)(2,1)}, bf16[1024,2048]{1,0:T(8,128)(2,1)}, u32[]{:S(2)}, u32[]{:S(2)}) collective-permute-start(bf16[1024,2048]{1,0:T(8,128)(2,1)} %weight_gradients.13), channel_id=1, source_target_pairs={{0,2},{2,0},{4,6},{6,4},{8,10},{10,8},{12,14},{14,12},{16,18},{18,... | collective-permute-start | bytes 12582920 | tf_op jit(solution)/shard_map/ppermute | solution.py:67
  385.5 22.0 %collective-permute-start.61 = (bf16[256,1024]{1,0:T(8,128)(2,1)}, bf16[256,1024]{1,0:T(8,128)(2,1)}, u32[]{:S(2)}, u32[]{:S(2)}) collective-permute-start(bf16[256,1024]{1,0:T(8,128)(2,1)} %get-tuple-element.291), channel_id=1, source_target_pairs={{0,1},{1,0},{2,3},{3,2},{4,5},{5,4},{6,7},{7,6},{8,9},{9,8},{10,11... | collective-permute-start | bytes 1572872 | tf_op jit(solution)/shard_map/ppermute | solution.py:70
  388.2 27.1 %all-to-all-start.2 = ((bf16[16,16,1024]{2,1,0:T(8,128)(2,1)}), bf16[16,16,1024]{2,1,0:T(8,128)(2,1)}, u32[]{:S(2)}, u32[]{:S(2)}) async-start(bf16[16,16,1024]{2,1,0:T(8,128)(2,1)} %bitcast.180), calls=%async_computation.2 | async-start | bytes 1048576 | tf_op jit(solution)/shard_map/all_to_all | solution.py:155
  432.9 29.5 %collective-permute-start.68 = (bf16[128,2048]{1,0:T(8,128)(2,1)S(1)}, bf16[128,2048]{1,0:T(8,128)(2,1)S(1)}, u32[]{:S(2)}, u32[]{:S(2)}) collective-permute-start(bf16[128,2048]{1,0:T(8,128)(2,1)S(1)} %get-tuple-element.314), channel_id=1, source_target_pairs={{0,8},{2,6},{4,0},{6,14},{8,16},{10,2},{12,4},{14,22},{16,24},{18,... | collective-permute-start | bytes 1572872 | tf_op jit(solution)/shard_map/ppermute | solution.py:64
  433.9 28.5 %collective-permute-start.69 = (bf16[128,2048]{1,0:T(8,128)(2,1)S(1)}, bf16[128,2048]{1,0:T(8,128)(2,1)S(1)}, u32[]{:S(2)}, u32[]{:S(2)}) collective-permute-start(bf16[128,2048]{1,0:T(8,128)(2,1)S(1)} %get-tuple-element.315), channel_id=1, source_target_pairs={{8,0},{6,2},{0,4},{14,6},{16,8},{2,10},{4,12},{22,14},{24,16},{10,... | collective-permute-start | bytes 1572872 | tf_op jit(solution)/shard_map/ppermute | solution.py:64
  446.7 44.6 %collective-permute-start.81 = (bf16[1024,1024]{1,0:T(8,128)(2,1)}, bf16[1024,1024]{1,0:T(8,128)(2,1)}, u32[]{:S(2)}, u32[]{:S(2)}) collective-permute-start(bf16[1024,1024]{1,0:T(8,128)(2,1)} %weight_gradients.15), channel_id=1, source_target_pairs={{0,2},{2,0},{4,6},{6,4},{8,10},{10,8},{12,14},{14,12},{16,18},{18,... | collective-permute-start | bytes 6291464 | tf_op jit(solution)/shard_map/ppermute | solution.py:67
  462.2 19.3 %collective-permute-start.75 = (bf16[64,2048]{1,0:T(8,128)(2,1)}, bf16[64,2048]{1,0:T(8,128)(2,1)}, u32[]{:S(2)}, u32[]{:S(2)}) collective-permute-start(bf16[64,2048]{1,0:T(8,128)(2,1)} %get-tuple-element.328), channel_id=1, source_target_pairs={{0,2},{2,0},{4,6},{6,4},{8,10},{10,8},{12,14},{14,12},{16,18},{18,... | collective-permute-start | bytes 786440 | tf_op jit(solution)/shard_map/ppermute | solution.py:67
  468.3 17.5 %collective-permute-start.90 = (bf16[128,2048]{1,0:T(8,128)(2,1)}, bf16[128,2048]{1,0:T(8,128)(2,1)}, u32[]{:S(2)}, u32[]{:S(2)}) collective-permute-start(bf16[128,2048]{1,0:T(8,128)(2,1)} %get-tuple-element.354), channel_id=1, source_target_pairs={{0,8},{2,6},{4,0},{6,14},{8,16},{10,2},{12,4},{14,22},{16,24},{18,... | collective-permute-start | bytes 1572872 | tf_op jit(solution)/shard_map/ppermute | solution.py:64
  469.7 19.3 %collective-permute-start.72 = (bf16[256,1024]{1,0:T(8,128)(2,1)}, bf16[256,1024]{1,0:T(8,128)(2,1)}, u32[]{:S(2)}, u32[]{:S(2)}) collective-permute-start(bf16[256,1024]{1,0:T(8,128)(2,1)} %get-tuple-element.320), channel_id=1, source_target_pairs={{0,1},{1,0},{2,3},{3,2},{4,5},{5,4},{6,7},{7,6},{8,9},{9,8},{10,11... | collective-permute-start | bytes 1572872 | tf_op jit(solution)/shard_map/ppermute | solution.py:70
  481.5 55.5 %collective-permute-start.92 = (bf16[128,2048]{1,0:T(8,128)(2,1)}, bf16[128,2048]{1,0:T(8,128)(2,1)S(1)}, u32[]{:S(2)}, u32[]{:S(2)}) collective-permute-start(bf16[128,2048]{1,0:T(8,128)(2,1)} %get-tuple-element.355), channel_id=1, source_target_pairs={{8,0},{6,2},{0,4},{14,6},{16,8},{2,10},{4,12},{22,14},{24,16},{10,... | collective-permute-start | bytes 1572872 | tf_op jit(solution)/shard_map/ppermute | solution.py:64
  488.5 48.5 %collective-permute-start.91 = (bf16[128,2048]{1,0:T(8,128)(2,1)}, bf16[128,2048]{1,0:T(8,128)(2,1)}, u32[]{:S(2)}, u32[]{:S(2)}) collective-permute-start(bf16[128,2048]{1,0:T(8,128)(2,1)} %add_portions.31), channel_id=1, source_target_pairs={{0,8},{2,6},{4,0},{6,14},{8,16},{10,2},{12,4},{14,22},{16,24},{18,... | collective-permute-start | bytes 1572872 | tf_op jit(solution)/shard_map/ppermute | solution.py:63
  509.1 47.0 %all-to-all-start.3 = ((bf16[16,16,1024]{2,1,0:T(8,128)(2,1)}), bf16[16,16,1024]{2,1,0:T(8,128)(2,1)}, u32[]{:S(2)}, u32[]{:S(2)}) async-start(bf16[16,16,1024]{2,1,0:T(8,128)(2,1)} %bitcast.181), calls=%async_computation.3 | async-start | bytes 1048576 | tf_op jit(solution)/shard_map/all_to_all | solution.py:155
  518.7 25.8 %collective-permute-start.86 = (bf16[128,1024]{1,0:T(8,128)(2,1)}, bf16[128,1024]{1,0:T(8,128)(2,1)S(1)}, u32[]{:S(2)}, u32[]{:S(2)}) collective-permute-start(bf16[128,1024]{1,0:T(8,128)(2,1)} %get-tuple-element.348), channel_id=1, source_target_pairs={{0,8},{2,6},{4,0},{6,14},{8,16},{10,2},{12,4},{14,22},{16,24},{18,... | collective-permute-start | bytes 786440 | tf_op jit(solution)/shard_map/ppermute | solution.py:64
  542.1 17.7 %collective-permute-start.93 = (bf16[64,2048]{1,0:T(8,128)(2,1)}, bf16[64,2048]{1,0:T(8,128)(2,1)S(1)}, u32[]{:S(2)}, u32[]{:S(2)}) collective-permute-start(bf16[64,2048]{1,0:T(8,128)(2,1)} %get-tuple-element.357), channel_id=1, source_target_pairs={{0,2},{2,0},{4,6},{6,4},{8,10},{10,8},{12,14},{14,12},{16,18},{18,... | collective-permute-start | bytes 786440 | tf_op jit(solution)/shard_map/ppermute | solution.py:67
  (214 other events, 2100.2 us)

commit v11 on v10

--- a/solution.py
+++ b/solution.py
@@ -453,7 +453,7 @@
 
 def weight_gradients(pairs, half):
     widths = [width for _, _, width in pairs]
-    tile = math.gcd(256, *widths)
+    tile = math.gcd(512, *widths)
     if tile % 128:
         terms = [
             contract_rows(join(blocks), _columns(right, half, width))

time: 572 us -> 568 us (level)
  no operation moved by 1% of the time
where the time goes in v11:
time: 568 us; the launch traced here: 558 us
  waiting for transfers between devices  212 us (37%)
  Pallas kernels  147 us (26%)
  starting transfers between devices  112 us (20%)
  local copies, waits for them, and re-layouts  56.7 us (10%)
  other arithmetic  27.4 us (5%)
    ppermute x16, waiting for transfers between devices, across(): return lax.ppermute(array, 'tensor', [(0, 1), (1, 0)])  98.5 us
    ppermute x24, waiting for transfers between devices, round(): lax.ppermute(forth, 'dp', self.ahead)  47 us
    unnamed x291, local copies, waits for them, and re-layouts  32.6 us
    pallas_call x8, Pallas kernels, weight_gradients(): pl.pallas_call(kernel, grid=(sum(counts),), out_shape=jax.ShapeDtypeStruc...  31.6 us
    ppermute x24, starting transfers between devices, round(): lax.ppermute(forth, 'dp', self.ahead)  30.4 us
    ppermute x8, waiting for transfers between devices, round(): return [lax.ppermute(forth, 'dp', self.ahead)]  29.2 us
    pallas_call x16, Pallas kernels, add_portions(): pl.pallas_call(kernel, grid_spec=pltpu.PrefetchScalarGridSpec(num_scalar_...  27.9 us
    pallas_call x4, Pallas kernels, attend_backward(): pl.pallas_call(kernel, out_shape=shapes, scratch_shapes=[pltpu.VMEM((rows...  26.3 us
  transfers between devices with their start and end apart: 98, of which 43 were waited for; matrix products, arithmetic and copies ran while one was open for 8% of the time, Pallas kernels for 20%

profile of v11, /device:TPU:0, one launch (start us, length us, event | category | flops | bytes accessed | tf_op | source)
XLA Modules:
  0.0 558.4 jit_solution(13747705287866367682)
XLA Ops:
  9.1 6.3 %collective-permute-done.3.refs_4_ = bf16[136,1024]{1,0:T(8,128)(2,1)S(1)} collective-permute-done((bf16[136,1024]{1,0:T(8,128)(2,1)S(1)}, bf16[136,1024]{1,0:T(8,128)(2,1)S(1)}, u32[]{:S(2)}, u32[]{:S(2)}) %collective-permute-start.3) | collective-permute-done | bytes 278560 | tf_op jit(solution)/shard_map/ppermute | solution.py:64
  18.0 6.4 %all-to-all-start = ((bf16[16,16,1024]{2,1,0:T(8,128)(2,1)}), bf16[16,16,1024]{2,1,0:T(8,128)(2,1)}, u32[]{:S(2)}, u32[]{:S(2)}) async-start(bf16[16,16,1024]{2,1,0:T(8,128)(2,1)} %bitcast.13), calls=%async_computation | async-start | bytes 1048576 | tf_op jit(solution)/shard_map/all_to_all | solution.py:155
  26.8 13.1 %collective-permute-done.4.refs_2_ = bf16[136,1024]{1,0:T(8,128)(2,1)S(1)} collective-permute-done((bf16[136,1024]{1,0:T(8,128)(2,1)S(1)}, bf16[136,1024]{1,0:T(8,128)(2,1)S(1)}, u32[]{:S(2)}, u32[]{:S(2)}) %collective-permute-start.4) | collective-permute-done | bytes 278560 | tf_op jit(solution)/shard_map/ppermute | solution.py:64
  81.2 5.6 attend_forward.5
  91.3 10.5 %collective-permute-done.18 = bf16[256,1024]{1,0:T(8,128)(2,1)S(1)} collective-permute-done((bf16[256,1024]{1,0:T(8,128)(2,1)S(1)}, bf16[256,1024]{1,0:T(8,128)(2,1)S(1)}, u32[]{:S(2)}, u32[]{:S(2)}) %collective-permute-start.18) | collective-permute-done | bytes 524320 | tf_op jit(solution)/shard_map/ppermute | solution.py:70
  117.6 6.9 %collective-permute-done.23.refs_4_ = bf16[128,1024]{1,0:T(8,128)(2,1)S(1)} collective-permute-done((bf16[128,1024]{1,0:T(8,128)(2,1)S(1)}, bf16[128,1024]{1,0:T(8,128)(2,1)S(1)}, u32[]{:S(2)}, u32[]{:S(2)}) %collective-permute-start.23) | collective-permute-done | bytes 262176 | tf_op jit(solution)/shard_map/ppermute | solution.py:64
  131.5 6.9 %feed_forward.2 = (f32[256,1024]{1,0:T(8,128)S(1)}, bf16[256,1024]{1,0:T(8,128)(2,1)S(1)}, bf16[512,2048]{1,0:T(8,128)(2,1)S(1)}, bf16[512,2048]{1,0:T(8,128)(2,1)S(1)}) custom-call(bf16[256,1024]{1,0:T(8,128)(2,1)S(1)} %fusion.5.refs_0_, bf16[256,1024]{1,0:T(8,128)(2,1)S(1)} %collective-permute-done.21.refs_1_, ...), custom_call_target="tpu_custom_call" | custom-call | flops 1000 | bytes 1000 | tf_op jit(solution)/shard_map/feed_forward/pallas_call | solution.py:442
  143.1 9.1 %collective-permute-done.28 = bf16[256,1024]{1,0:T(8,128)(2,1)S(1)} collective-permute-done((bf16[256,1024]{1,0:T(8,128)(2,1)S(1)}, bf16[256,1024]{1,0:T(8,128)(2,1)S(1)}, u32[]{:S(2)}, u32[]{:S(2)}) %collective-permute-start.28) | collective-permute-done | bytes 524320 | tf_op jit(solution)/shard_map/ppermute | solution.py:70
  165.2 11.9 %collective-permute-done.34.refs_0_ = bf16[128,1024]{1,0:T(8,128)(2,1)S(1)} collective-permute-done((bf16[128,1024]{1,0:T(8,128)(2,1)S(1)}, bf16[128,1024]{1,0:T(8,128)(2,1)S(1)}, u32[]{:S(2)}, u32[]{:S(2)}) %collective-permute-start.34) | collective-permute-done | bytes 262176 | tf_op jit(solution)/shard_map/ppermute | solution.py:63
  194.8 11.6 %collective-permute-done.40 = bf16[256,1024]{1,0:T(8,128)(2,1)S(1)} collective-permute-done((bf16[256,1024]{1,0:T(8,128)(2,1)S(1)}, bf16[256,1024]{1,0:T(8,128)(2,1)S(1)}, u32[]{:S(2)}, u32[]{:S(2)}) %collective-permute-start.40) | collective-permute-done | bytes 524320 | tf_op jit(solution)/shard_map/ppermute | solution.py:70
  208.8 13.8 %collective-permute-done.42.refs_1_ = bf16[256,1024]{1,0:T(8,128)(2,1)S(1)} collective-permute-done((bf16[256,1024]{1,0:T(8,128)(2,1)S(1)}, bf16[256,1024]{1,0:T(8,128)(2,1)S(1)}, u32[]{:S(2)}, u32[]{:S(2)}) %collective-permute-start.42) | collective-permute-done | bytes 524320 | tf_op jit(solution)/shard_map/ppermute | solution.py:70
  222.6 7.8 %feed_forward.3 = (f32[256,1024]{1,0:T(8,128)S(1)}, bf16[256,1024]{1,0:T(8,128)(2,1)}, bf16[512,2048]{1,0:T(8,128)(2,1)S(1)}, bf16[512,2048]{1,0:T(8,128)(2,1)S(1)}) custom-call(bf16[256,1024]{1,0:T(8,128)(2,1)S(1)} %fusion.7.refs_0_, bf16[256,1024]{1,0:T(8,128)(2,1)S(1)} %collective-permute-done.42.refs_1_, bf16[1024,2048]{1,0:T(8,128)(2,1)S(1)} %place_pieces.15.refs_2_, ...), custom_call_target="tpu_custom_call" | custom-call | flops 1000 | bytes 1000 | tf_op jit(solution)/shard_map/feed_forward/pallas_call | solution.py:442
  242.6 5.4 collective-permute-done.44
  263.5 12.4 %collective-permute-done.45.refs_1_.refs_3_ = bf16[256,1024]{1,0:T(8,128)(2,1)S(1)} collective-permute-done((bf16[256,1024]{1,0:T(8,128)(2,1)S(1)}, bf16[256,1024]{1,0:T(8,128)(2,1)S(1)}, u32[]{:S(2)}, u32[]{:S(2)}) %collective-permute-start.45) | collective-permute-done | bytes 524320 | tf_op jit(solution)/shard_map/ppermute | solution.py:70
  292.6 8.7 %collective-permute-done.46 = bf16[256,1024]{1,0:T(8,128)(2,1)S(1)} collective-permute-done((bf16[256,1024]{1,0:T(8,128)(2,1)S(1)}, bf16[256,1024]{1,0:T(8,128)(2,1)S(1)}, u32[]{:S(2)}, u32[]{:S(2)}) %collective-permute-start.46) | collective-permute-done | bytes 524320 | tf_op jit(solution)/shard_map/ppermute | solution.py:70
  307.1 9.1 %collective-permute-done.48.refs_1_.refs_3_ = bf16[256,1024]{1,0:T(8,128)(2,1)S(1)} collective-permute-done((bf16[256,1024]{1,0:T(8,128)(2,1)S(1)}, bf16[256,1024]{1,0:T(8,128)(2,1)S(1)}, u32[]{:S(2)}, u32[]{:S(2)}) %collective-permute-start.48) | collective-permute-done | bytes 524320 | tf_op jit(solution)/shard_map/ppermute | solution.py:70
  330.1 6.2 %attend_backward.5 = (bf16[512,768]{1,0:T(8,128)(2,1)S(1)}, f32[1,768]{1,0:T(1,128)S(1)}, f32[256,1024]{1,0:T(8,128)S(1)}, bf16[256,1024]{1,0:T(8,128)(2,1)S(1)}) custom-call(bf16[256,1024]{1,0:T(8,128)(2,1)S(1)} %get-tuple-element.257.refs_0_.refs_2_, bf16[256,1024]{1,0:T(8,128)(2,1)S(1)} %collective-permute-done.48.refs_1_.refs_3_, ...), custom_call_target="tpu_custom_call" | custom-call | flops 1000 | bytes 1000 | tf_op jit(solution)/shard_map/attend_backward/pallas_call | solution.py:364
  342.8 8.0 %collective-permute-done.53 = bf16[256,1024]{1,0:T(8,128)(2,1)S(1)} collective-permute-done((bf16[256,1024]{1,0:T(8,128)(2,1)S(1)}, bf16[256,1024]{1,0:T(8,128)(2,1)S(1)}, u32[]{:S(2)}, u32[]{:S(2)}) %collective-permute-start.53) | collective-permute-done | bytes 524320 | tf_op jit(solution)/shard_map/ppermute | solution.py:70
  361.7 6.3 %collective-permute-done.58.refs_0_ = bf16[128,2048]{1,0:T(8,128)(2,1)S(1)} collective-permute-done((bf16[128,2048]{1,0:T(8,128)(2,1)S(1)}, bf16[128,2048]{1,0:T(8,128)(2,1)S(1)}, u32[]{:S(2)}, u32[]{:S(2)}) %collective-permute-start.58) | collective-permute-done | bytes 524320 | tf_op jit(solution)/shard_map/ppermute | solution.py:63
  372.3 5.5 feed_backward.3
  431.5 6.6 %attend_backward.6 = (bf16[512,768]{1,0:T(8,128)(2,1)S(1)}, f32[1,768]{1,0:T(1,128)S(1)}) custom-call(bf16[256,1024]{1,0:T(8,128)(2,1)S(1)} %copy-done.30, bf16[256,1024]{1,0:T(8,128)(2,1)} %collective-permute-done.63.refs_1_.refs_3_, bf16[1024,1024]{1,0:T(8,128)(2,1)} %collective-permute-done.15.refs_2_.refs_9_, bf16[512,768]{1,0:T(8,128)(2,1)S(1)} %copy-done.80, ...), custom_call_target="tpu_custom_call" | custom-call | flops 1000 | bytes 1000 | tf_op jit(solution)/shard_map/attend_backward/pallas_call | solution.py:364
  449.8 8.8 %attend_backward.7 = (bf16[512,768]{1,0:T(8,128)(2,1)S(1)}, f32[1,768]{1,0:T(1,128)S(1)}, f32[256,1024]{1,0:T(8,128)S(1)}, bf16[256,1024]{1,0:T(8,128)(2,1)}) custom-call(bf16[256,1024]{1,0:T(8,128)(2,1)S(1)} %copy-done.30, bf16[256,1024]{1,0:T(8,128)(2,1)} %collective-permute-done.63.refs_1_.refs_3_, bf16[1024,1024]{1,0:T(8,128)(2,1)S(1)} %copy-done.20, ...), custom_call_target="tpu_custom_call" | custom-call | flops 1000 | bytes 1000 | tf_op jit(solution)/shard_map/attend_backward/pallas_call | solution.py:364
  492.6 7.2 %collective-permute-done.82.refs_0_ = bf16[128,1024]{1,0:T(8,128)(2,1)S(1)} collective-permute-done((bf16[128,1024]{1,0:T(8,128)(2,1)S(1)}, bf16[128,1024]{1,0:T(8,128)(2,1)S(1)}, u32[]{:S(2)}, u32[]{:S(2)}) %collective-permute-start.82) | collective-permute-done | bytes 262176 | tf_op jit(solution)/shard_map/ppermute | solution.py:64
  519.2 5.4 collective-permute-done.78
  (656 shorter events, 354.8 us)
Async XLA Ops:
  18.0 34.7 %all-to-all-start = ((bf16[16,16,1024]{2,1,0:T(8,128)(2,1)}), bf16[16,16,1024]{2,1,0:T(8,128)(2,1)}, u32[]{:S(2)}, u32[]{:S(2)}) async-start(bf16[16,16,1024]{2,1,0:T(8,128)(2,1)} %bitcast.13), calls=%async_computation | async-start | bytes 1048576 | tf_op jit(solution)/shard_map/all_to_all | solution.py:155
  26.7 20.2 %collective-permute-start.8 = (bf16[64,2048]{1,0:T(8,128)(2,1)S(1)}, bf16[64,2048]{1,0:T(8,128)(2,1)S(1)}, u32[]{:S(2)}, u32[]{:S(2)}) collective-permute-start(bf16[64,2048]{1,0:T(8,128)(2,1)S(1)} %pad_maximum_fusion), channel_id=1, source_target_pairs={{0,2},{2,0},{4,6},{6,4},{8,10},{10,8},{12,14},{14,12},{16,18},{18,... | collective-permute-start | bytes 786440 | tf_op jit(solution)/shard_map/ppermute | solution.py:67
  52.8 17.4 %collective-permute-start.12 = (bf16[128,2048]{1,0:T(8,128)(2,1)S(1)}, bf16[128,2048]{1,0:T(8,128)(2,1)}, u32[]{:S(2)}, u32[]{:S(2)}) collective-permute-start(bf16[128,2048]{1,0:T(8,128)(2,1)S(1)} %maximum_select_fusion.refs_0_), channel_id=1, source_target_pairs={{8,0},{6,2},{0,4},{14,6},{16,8},{2,10},{4,12},{22,14},{24,16},{10,... | collective-permute-start | bytes 1572872 | tf_op jit(solution)/shard_map/ppermute | solution.py:64
  114.9 16.5 %collective-permute-start.25 = (bf16[1024,2048]{1,0:T(8,128)(2,1)S(1)}, bf16[1024,2048]{1,0:T(8,128)(2,1)S(1)}, u32[]{:S(2)}, u32[]{:S(2)}) collective-permute-start(bf16[1024,2048]{1,0:T(8,128)(2,1)S(1)} %place_pieces.11.refs_2_), channel_id=1, source_target_pairs={{0,2},{2,0},{4,6},{6,4},{8,10},{10,8},{12,14},{14,12},{16,18},{18,... | collective-permute-start | bytes 12582920 | tf_op jit(solution)/shard_map/ppermute | solution.py:67
  141.1 17.0 %collective-permute-start.29 = (bf16[128,1024]{1,0:T(8,128)(2,1)S(1)}, bf16[128,1024]{1,0:T(8,128)(2,1)S(1)}, u32[]{:S(2)}, u32[]{:S(2)}) collective-permute-start(bf16[128,1024]{1,0:T(8,128)(2,1)S(1)} %collective-permute-done.26.refs_2_), channel_id=1, source_target_pairs={{0,8},{2,6},{4,0},{6,14},{8,16},{10,2},{12,4},{14,22},{16,24},{18,... | collective-permute-start | bytes 786440 | tf_op jit(solution)/shard_map/ppermute | solution.py:64
  159.4 17.8 %collective-permute-start.33 = (bf16[256,1024]{1,0:T(8,128)(2,1)S(1)}, bf16[256,1024]{1,0:T(8,128)(2,1)S(1)}, u32[]{:S(2)}, u32[]{:S(2)}) collective-permute-start(bf16[256,1024]{1,0:T(8,128)(2,1)S(1)} %fusion.6.refs_0_), channel_id=1, source_target_pairs={{0,1},{1,0},{2,3},{3,2},{4,5},{5,4},{6,7},{7,6},{8,9},{9,8},{10,11... | collective-permute-start | bytes 1572872 | tf_op jit(solution)/shard_map/ppermute | solution.py:70
  161.0 16.2 %collective-permute-start.35 = (bf16[128,2048]{1,0:T(8,128)(2,1)S(1)}, bf16[128,2048]{1,0:T(8,128)(2,1)S(1)}, u32[]{:S(2)}, u32[]{:S(2)}) collective-permute-start(bf16[128,2048]{1,0:T(8,128)(2,1)S(1)} %collective-permute-done.31.refs_1_), channel_id=1, source_target_pairs={{0,8},{2,6},{4,0},{6,14},{8,16},{10,2},{12,4},{14,22},{16,24},{18,... | collective-permute-start | bytes 1572872 | tf_op jit(solution)/shard_map/ppermute | solution.py:64
  238.1 18.9 %all-to-all-start.1 = ((bf16[16,16,1024]{2,1,0:T(8,128)(2,1)}), bf16[16,16,1024]{2,1,0:T(8,128)(2,1)}, u32[]{:S(2)}, u32[]{:S(2)}) async-start(bf16[16,16,1024]{2,1,0:T(8,128)(2,1)} %bitcast.182), calls=%async_computation.1 | async-start | bytes 1048576 | tf_op jit(solution)/shard_map/all_to_all | solution.py:155
  320.0 16.3 %collective-permute-start.51 = (bf16[128,2048]{1,0:T(8,128)(2,1)S(1)}, bf16[128,2048]{1,0:T(8,128)(2,1)S(1)}, u32[]{:S(2)}, u32[]{:S(2)}) collective-permute-start(bf16[128,2048]{1,0:T(8,128)(2,1)S(1)} %get-tuple-element.273), channel_id=1, source_target_pairs={{0,8},{2,6},{4,0},{6,14},{8,16},{10,2},{12,4},{14,22},{16,24},{18,... | collective-permute-start | bytes 1572872 | tf_op jit(solution)/shard_map/ppermute | solution.py:64
  330.0 27.3 %collective-permute-start.56 = (bf16[1024,1024]{1,0:T(8,128)(2,1)S(1)}, bf16[1024,1024]{1,0:T(8,128)(2,1)S(1)}, u32[]{:S(2)}, u32[]{:S(2)}) collective-permute-start(bf16[1024,1024]{1,0:T(8,128)(2,1)S(1)} %weight_gradients.11), channel_id=1, source_target_pairs={{0,2},{2,0},{4,6},{6,4},{8,10},{10,8},{12,14},{14,12},{16,18},{18,... | collective-permute-start | bytes 6291464 | tf_op jit(solution)/shard_map/ppermute | solution.py:67
  383.0 23.2 %collective-permute-start.62 = (bf16[1024,2048]{1,0:T(8,128)(2,1)}, bf16[1024,2048]{1,0:T(8,128)(2,1)}, u32[]{:S(2)}, u32[]{:S(2)}) collective-permute-start(bf16[1024,2048]{1,0:T(8,128)(2,1)} %weight_gradients.13), channel_id=1, source_target_pairs={{0,2},{2,0},{4,6},{6,4},{8,10},{10,8},{12,14},{14,12},{16,18},{18,... | collective-permute-start | bytes 12582920 | tf_op jit(solution)/shard_map/ppermute | solution.py:67
  383.0 20.9 %collective-permute-start.61 = (bf16[256,1024]{1,0:T(8,128)(2,1)}, bf16[256,1024]{1,0:T(8,128)(2,1)}, u32[]{:S(2)}, u32[]{:S(2)}) collective-permute-start(bf16[256,1024]{1,0:T(8,128)(2,1)} %get-tuple-element.291), channel_id=1, source_target_pairs={{0,1},{1,0},{2,3},{3,2},{4,5},{5,4},{6,7},{7,6},{8,9},{9,8},{10,11... | collective-permute-start | bytes 1572872 | tf_op jit(solution)/shard_map/ppermute | solution.py:70
  385.7 26.0 %all-to-all-start.2 = ((bf16[16,16,1024]{2,1,0:T(8,128)(2,1)}), bf16[16,16,1024]{2,1,0:T(8,128)(2,1)}, u32[]{:S(2)}, u32[]{:S(2)}) async-start(bf16[16,16,1024]{2,1,0:T(8,128)(2,1)} %bitcast.180), calls=%async_computation.2 | async-start | bytes 1048576 | tf_op jit(solution)/shard_map/all_to_all | solution.py:155
  429.2 29.5 %collective-permute-start.68 = (bf16[128,2048]{1,0:T(8,128)(2,1)S(1)}, bf16[128,2048]{1,0:T(8,128)(2,1)S(1)}, u32[]{:S(2)}, u32[]{:S(2)}) collective-permute-start(bf16[128,2048]{1,0:T(8,128)(2,1)S(1)} %get-tuple-element.314), channel_id=1, source_target_pairs={{0,8},{2,6},{4,0},{6,14},{8,16},{10,2},{12,4},{14,22},{16,24},{18,... | collective-permute-start | bytes 1572872 | tf_op jit(solution)/shard_map/ppermute | solution.py:64
  430.3 28.5 %collective-permute-start.69 = (bf16[128,2048]{1,0:T(8,128)(2,1)S(1)}, bf16[128,2048]{1,0:T(8,128)(2,1)S(1)}, u32[]{:S(2)}, u32[]{:S(2)}) collective-permute-start(bf16[128,2048]{1,0:T(8,128)(2,1)S(1)} %get-tuple-element.315), channel_id=1, source_target_pairs={{8,0},{6,2},{0,4},{14,6},{16,8},{2,10},{4,12},{22,14},{24,16},{10,... | collective-permute-start | bytes 1572872 | tf_op jit(solution)/shard_map/ppermute | solution.py:64
  443.0 44.6 %collective-permute-start.81 = (bf16[1024,1024]{1,0:T(8,128)(2,1)}, bf16[1024,1024]{1,0:T(8,128)(2,1)}, u32[]{:S(2)}, u32[]{:S(2)}) collective-permute-start(bf16[1024,1024]{1,0:T(8,128)(2,1)} %weight_gradients.15), channel_id=1, source_target_pairs={{0,2},{2,0},{4,6},{6,4},{8,10},{10,8},{12,14},{14,12},{16,18},{18,... | collective-permute-start | bytes 6291464 | tf_op jit(solution)/shard_map/ppermute | solution.py:67
  458.6 19.3 %collective-permute-start.75 = (bf16[64,2048]{1,0:T(8,128)(2,1)}, bf16[64,2048]{1,0:T(8,128)(2,1)}, u32[]{:S(2)}, u32[]{:S(2)}) collective-permute-start(bf16[64,2048]{1,0:T(8,128)(2,1)} %get-tuple-element.328), channel_id=1, source_target_pairs={{0,2},{2,0},{4,6},{6,4},{8,10},{10,8},{12,14},{14,12},{16,18},{18,... | collective-permute-start | bytes 786440 | tf_op jit(solution)/shard_map/ppermute | solution.py:67
  464.6 17.5 %collective-permute-start.90 = (bf16[128,2048]{1,0:T(8,128)(2,1)}, bf16[128,2048]{1,0:T(8,128)(2,1)}, u32[]{:S(2)}, u32[]{:S(2)}) collective-permute-start(bf16[128,2048]{1,0:T(8,128)(2,1)} %get-tuple-element.354), channel_id=1, source_target_pairs={{0,8},{2,6},{4,0},{6,14},{8,16},{10,2},{12,4},{14,22},{16,24},{18,... | collective-permute-start | bytes 1572872 | tf_op jit(solution)/shard_map/ppermute | solution.py:64
  466.0 19.3 %collective-permute-start.72 = (bf16[256,1024]{1,0:T(8,128)(2,1)}, bf16[256,1024]{1,0:T(8,128)(2,1)}, u32[]{:S(2)}, u32[]{:S(2)}) collective-permute-start(bf16[256,1024]{1,0:T(8,128)(2,1)} %get-tuple-element.320), channel_id=1, source_target_pairs={{0,1},{1,0},{2,3},{3,2},{4,5},{5,4},{6,7},{7,6},{8,9},{9,8},{10,11... | collective-permute-start | bytes 1572872 | tf_op jit(solution)/shard_map/ppermute | solution.py:70
  477.9 55.4 %collective-permute-start.92 = (bf16[128,2048]{1,0:T(8,128)(2,1)}, bf16[128,2048]{1,0:T(8,128)(2,1)S(1)}, u32[]{:S(2)}, u32[]{:S(2)}) collective-permute-start(bf16[128,2048]{1,0:T(8,128)(2,1)} %get-tuple-element.355), channel_id=1, source_target_pairs={{8,0},{6,2},{0,4},{14,6},{16,8},{2,10},{4,12},{22,14},{24,16},{10,... | collective-permute-start | bytes 1572872 | tf_op jit(solution)/shard_map/ppermute | solution.py:64
  484.8 48.5 %collective-permute-start.91 = (bf16[128,2048]{1,0:T(8,128)(2,1)}, bf16[128,2048]{1,0:T(8,128)(2,1)}, u32[]{:S(2)}, u32[]{:S(2)}) collective-permute-start(bf16[128,2048]{1,0:T(8,128)(2,1)} %add_portions.31), channel_id=1, source_target_pairs={{0,8},{2,6},{4,0},{6,14},{8,16},{10,2},{12,4},{14,22},{16,24},{18,... | collective-permute-start | bytes 1572872 | tf_op jit(solution)/shard_map/ppermute | solution.py:63
  505.5 47.0 %all-to-all-start.3 = ((bf16[16,16,1024]{2,1,0:T(8,128)(2,1)}), bf16[16,16,1024]{2,1,0:T(8,128)(2,1)}, u32[]{:S(2)}, u32[]{:S(2)}) async-start(bf16[16,16,1024]{2,1,0:T(8,128)(2,1)} %bitcast.181), calls=%async_computation.3 | async-start | bytes 1048576 | tf_op jit(solution)/shard_map/all_to_all | solution.py:155
  515.0 25.8 %collective-permute-start.86 = (bf16[128,1024]{1,0:T(8,128)(2,1)}, bf16[128,1024]{1,0:T(8,128)(2,1)S(1)}, u32[]{:S(2)}, u32[]{:S(2)}) collective-permute-start(bf16[128,1024]{1,0:T(8,128)(2,1)} %get-tuple-element.348), channel_id=1, source_target_pairs={{0,8},{2,6},{4,0},{6,14},{8,16},{10,2},{12,4},{14,22},{16,24},{18,... | collective-permute-start | bytes 786440 | tf_op jit(solution)/shard_map/ppermute | solution.py:64
  538.4 17.7 %collective-permute-start.93 = (bf16[64,2048]{1,0:T(8,128)(2,1)}, bf16[64,2048]{1,0:T(8,128)(2,1)S(1)}, u32[]{:S(2)}, u32[]{:S(2)}) collective-permute-start(bf16[64,2048]{1,0:T(8,128)(2,1)} %get-tuple-element.357), channel_id=1, source_target_pairs={{0,2},{2,0},{4,6},{6,4},{8,10},{10,8},{12,14},{14,12},{16,18},{18,... | collective-permute-start | bytes 786440 | tf_op jit(solution)/shard_map/ppermute | solution.py:67
  (214 other events, 2092.4 us)
